TPU v7x, 256 devices: a whole 4x4x8 slice. The times are simulated.
256 devices in a mesh: band: 64 (over z, y, core), sub: 4 (over x).
Axes of the slice: x: 4, y: 4, z: 8, core: 2. Of those that a mesh axis runs over, the one named last changes fastest.
Arguments:
- grid_x: bfloat16 [227, 131072], P(None, ('band', 'sub')), may hold values from -6 to 6
- mesh_in: bfloat16 [16384, 512], P(('band', 'sub')), may hold values from -6 to 6
- w_embed: bfloat16 [227, 512], replicated, may hold values from -0.375 to 0.375
- w_src: bfloat16 [512, 512], replicated, may hold values from -0.25 to 0.25
- w_dst: bfloat16 [512, 512], replicated, may hold values from -0.25 to 0.25
- w_edge: bfloat16 [512, 512], replicated, may hold values from -0.25 to 0.25
- w_proc: bfloat16 [512, 512], replicated, may hold values from -0.25 to 0.25
- w_recv: bfloat16 [512, 512], replicated, may hold values from -0.25 to 0.25
- g2m_src: int32 [16384, 40], P(('band', 'sub')), may hold values from 0 to 131071, as said below
- mesh_src: int32 [16384, 6], P(('band', 'sub')), may hold values from 0 to 16383, as said below
- cotangent: bfloat16 [16384, 512], P(('band', 'sub')), may hold values from -6 to 6
Outputs:
- mesh_out: bfloat16 [16384, 512], P(('band', 'sub'))
- grid_grad: float32 [227, 131072], P(None, ('band', 'sub'))
- src_grad: float32 [512, 512], replicated
- edge_grad: float32 [512, 512], replicated
Inputs may be any that keep to these rules, and one draw needn't show every extreme that they name: Grid node g belongs to band g // (512 * 4), mesh node m to band m // (64 * 4); g2m_src[m, k] lies in the band of mesh node m, or among the 512 grid nodes of an adjacent band that stand next to that band in index order. mesh_src[m, j] lies in the band of mesh node m, or among the 64 mesh nodes of an adjacent band that stand next to that band in index order.
All inputs are finite; a program needn't handle non-finite values.
Results may differ from a plain program's by a relative error of at most 0.015.
Values may be sent and summed in bfloat16 or wider, within the bound.
No kernel may reach another device: no remote copies, remote signals or barrier semaphores. Data moves between devices by JAX's collectives and lax.ppermute only.
A program may use at most 128 MiB of HBM per device.

v0:
```python
import math

import jax
import jax.numpy as jnp
from jax import lax
from jax.sharding import Mesh
from jax.sharding import PartitionSpec as P

BAND = ("band_0", "band_1", "band_2")
BAND_SUB = ("band_0", "band_1", "band_2", "sub")


EPSILON = 1e-05


def from_everyone(shard, axis):
    devices = lax.axis_size(axis)
    return lax.all_to_all(
        jnp.broadcast_to(shard[None], (devices, *shard.shape)), axis, 0, 0, tiled=True
    )


def in_order(parts, dim):
    lengths = list(parts.shape[1:])
    lengths[dim] *= parts.shape[0]
    return jnp.moveaxis(parts, 0, dim).reshape(lengths)


def collect(shard, axis, dim):
    parts = from_everyone(shard, axis)
    return in_order(parts, dim)


def padded(shard, sides, width, wrap):
    for axis, dim in sides:
        devices, length = (lax.axis_size(axis), shard.shape[dim])
        up = [(i, (i + 1) % devices) for i in range(devices if wrap else devices - 1)]
        down = [(j, i) for i, j in up]
        last = lax.slice_in_dim(shard, length - width, length, axis=dim)
        first = lax.slice_in_dim(shard, 0, width, axis=dim)
        before = lax.ppermute(last, axis, up)
        after = lax.ppermute(first, axis, down)
        shard = jnp.concatenate([before, shard, after], axis=dim)
    return shard


def from_behind(value, axis, steps):
    count = lax.axis_size(axis)
    first, last = (max(0, -steps), min(count, count - steps))
    return lax.ppermute(value, axis, [(source, source + steps) for source in range(first, last)])


def cut_along(shard, dim, devices):
    before, after = (shard.shape[:dim], shard.shape[dim + 1 :])
    return jnp.moveaxis(shard.reshape(*before, devices, -1, *after), dim, 0)


def sent_and_summed(shard, axis, dim):
    devices = lax.axis_size(axis)
    parts = lax.all_to_all(cut_along(shard, dim, devices), axis, 0, 0, tiled=True)
    return jnp.sum(parts.astype(jnp.float32), axis=0)


def filled_up(lines, devices):
    spare = -lines.shape[0] % devices
    if not spare:
        return lines
    return jnp.concatenate([lines, jnp.zeros((spare, *lines.shape[1:]), lines.dtype)])


def gather_axes(shard, axes, dim):
    far, near = axes
    first = from_everyone(shard, far)
    parts = jnp.swapaxes(from_everyone(first, near), 0, 1)
    return in_order(parts.reshape(-1, *shard.shape), dim)


def sent_and_summed_2(shard, axis, dim):
    devices = lax.axis_size(axis)
    parts = lax.all_to_all(cut_along(shard, dim, devices), axis, 0, 0, tiled=True)
    return jnp.sum(parts, axis=0)


def summed_rows(shard, axes, dim):
    far, near = axes
    parts = cut_along(shard, dim, lax.axis_size(far))
    nearer = sent_and_summed_2(parts, near, dim + 1)
    arrived = lax.all_to_all(nearer, far, split_axis=0, concat_axis=0, tiled=True)
    return arrived.sum(axis=0)


def nested_sum(shard, axes):
    padded = filled_up(shard, lax.axis_size(axes[0]) * lax.axis_size(axes[1]))
    whole = gather_axes(summed_rows(padded, axes, 0), axes, 0)
    return lax.slice_in_dim(whole, 0, len(shard)).reshape(shard.shape)


def together(arrays, axis):
    ravelled, at, done = (jnp.concatenate([a.reshape(-1) for a in arrays]), 0, [])
    so_far = nested_sum(ravelled, axis)
    for a in arrays:
        done.append(so_far[at : at + a.size].reshape(a.shape))
        at += a.size
    return tuple(done)


def silu_slope(value):
    sigma = jax.nn.sigmoid(value)
    return sigma * (1.0 + value * (1.0 - sigma))


def normalize(value):
    centred = value - jnp.mean(value, axis=-1, keepdims=True)
    spread = jnp.sqrt(jnp.mean(centred * centred, axis=-1, keepdims=True) + EPSILON)
    return (centred / spread, spread)


def times_transpose(left, right):
    return lax.dot_general(
        left, right, (((1,), (1,)), ((), ())), preferred_element_type=jnp.float32
    )


def first_contract(left, right):
    return lax.dot_general(
        left, right, (((0,), (0,)), ((), ())), preferred_element_type=jnp.float32
    )


def fetch_grid(projected):
    border = projected.shape[0]
    block = collect(projected, "sub", 0)
    return padded(block, ((BAND, 0),), border, False)


def return_grid(window_grad, border):
    middle = window_grad[border:-border]
    from_above = from_behind(window_grad[:border].astype(jnp.bfloat16), BAND, -1).astype(
        jnp.float32
    )
    from_below = from_behind(window_grad[-border:].astype(jnp.bfloat16), BAND, 1).astype(
        jnp.float32
    )
    middle = middle.at[:border].add(from_below)
    middle = middle.at[middle.shape[0] - border :].add(from_above)
    return sent_and_summed(middle.astype(jnp.bfloat16), "sub", 0)


def return_mesh(window_grad, border):
    middle = window_grad[border:-border]
    from_above = from_behind(window_grad[:border].astype(jnp.bfloat16), BAND, -1).astype(
        jnp.float32
    )
    from_below = from_behind(window_grad[-border:].astype(jnp.bfloat16), BAND, 1).astype(
        jnp.float32
    )
    middle = middle.at[:border].add(from_below)
    middle = middle.at[middle.shape[0] - border :].add(from_above)
    return sent_and_summed(middle.astype(jnp.bfloat16), "sub", 0)


def body(
    grid_x, mesh_in, w_embed, w_src, w_dst, w_edge, w_proc, w_recv, g2m_src, mesh_src, cotangent
):
    latent = w_src.shape[0]
    mesh_rows, enc_count = g2m_src.shape
    mesh_count = mesh_src.shape[1]
    band_index = lax.axis_index(BAND)
    groups = lax.axis_size("sub")
    hidden_pre = first_contract(grid_x, w_embed)
    hidden_grid = jax.nn.silu(hidden_pre).astype(jnp.bfloat16)
    projected = jnp.dot(hidden_grid, w_src, preferred_element_type=jnp.float32).astype(jnp.bfloat16)
    dest_term = jnp.dot(mesh_in, w_dst, preferred_element_type=jnp.float32)
    grid_border = projected.shape[0]
    grid_window = fetch_grid(projected)
    grid_base = band_index * (grid_border * groups) - grid_border
    grid_local = (g2m_src - grid_base).reshape(-1)
    before = jnp.take(grid_window, grid_local, axis=0).astype(jnp.float32)
    before = (before.reshape(mesh_rows, enc_count, latent) + dest_term[:, None, :]).reshape(
        -1, latent
    )
    active = jax.nn.silu(before).astype(jnp.bfloat16)
    normed, spread = normalize(jnp.dot(active, w_edge, preferred_element_type=jnp.float32))
    encoded = jnp.sum(normed.reshape(mesh_rows, enc_count, latent), axis=1)
    hidden_mesh = (mesh_in.astype(jnp.float32) + encoded / math.sqrt(enc_count)).astype(
        jnp.bfloat16
    )
    query = jnp.dot(hidden_mesh, w_proc, preferred_element_type=jnp.float32).astype(jnp.bfloat16)
    receiver = jnp.dot(hidden_mesh, w_recv, preferred_element_type=jnp.float32)
    mesh_border = query.shape[0]
    mesh_block = collect(query, "sub", 0)
    mesh_window = padded(mesh_block, ((BAND, 0),), mesh_border, False)
    mesh_base = band_index * mesh_block.shape[0] - mesh_border
    mesh_local = (mesh_src - mesh_base).reshape(-1)
    mesh_before = jnp.take(mesh_window, mesh_local, axis=0).astype(jnp.float32)
    mesh_before = mesh_before.reshape(mesh_rows, mesh_count, latent) + receiver[:, None, :]
    summed = jnp.sum(jax.nn.silu(mesh_before), axis=1)
    mesh_out = (hidden_mesh.astype(jnp.float32) + summed / math.sqrt(mesh_count)).astype(
        jnp.bfloat16
    )
    upstream = cotangent.astype(jnp.float32)
    mesh_slope = (upstream / math.sqrt(mesh_count))[:, None, :] * silu_slope(mesh_before)
    receiver_grad = jnp.sum(mesh_slope, axis=1)
    window_grad = jnp.zeros((mesh_window.shape[0], latent), jnp.float32)
    window_grad = window_grad.at[mesh_local].add(mesh_slope.reshape(-1, latent))
    query_grad = return_mesh(window_grad, mesh_border)
    mesh_grad = upstream + times_transpose(query_grad.astype(jnp.bfloat16), w_proc)
    mesh_grad = mesh_grad + times_transpose(receiver_grad.astype(jnp.bfloat16), w_recv)
    upper = mesh_grad / math.sqrt(enc_count)
    incoming = jnp.broadcast_to(upper[:, None, :], (mesh_rows, enc_count, latent)).reshape(
        -1, latent
    )
    centred_grad = incoming - jnp.mean(incoming, axis=-1, keepdims=True)
    centred_grad = centred_grad - normed * jnp.mean(incoming * normed, axis=-1, keepdims=True)
    norm_grad = (centred_grad / spread).astype(jnp.bfloat16)
    edge_part = first_contract(active, norm_grad)
    before_grad = times_transpose(norm_grad, w_edge) * silu_slope(before)
    grid_window_grad = (
        jnp.zeros((grid_window.shape[0], latent), jnp.float32).at[grid_local].add(before_grad)
    )
    projected_grad = return_grid(grid_window_grad, grid_border)
    projected_low = projected_grad.astype(jnp.bfloat16)
    src_part = first_contract(hidden_grid, projected_low)
    hidden_grad = (times_transpose(projected_low, w_src) * silu_slope(hidden_pre)).astype(
        jnp.bfloat16
    )
    grid_grad = times_transpose(w_embed, hidden_grad)
    src_grad, edge_grad = together((src_part, edge_part), (("band_0", "band_1"), ("band_2", "sub")))
    return (mesh_out, grid_grad, src_grad, edge_grad)


def solution(mesh):
    torus = Mesh(
        mesh.devices.reshape(8, 4, 2, mesh.shape["sub"]), ("band_0", "band_1", "band_2", "sub")
    )
    return jax.shard_map(
        body,
        mesh=torus,
        in_specs=(
            P(None, BAND_SUB),
            P(BAND_SUB, None),
            P(),
            P(),
            P(),
            P(),
            P(),
            P(),
            P(BAND_SUB, None),
            P(BAND_SUB, None),
            P(BAND_SUB, None),
        ),
        out_specs=(P(BAND_SUB, None), P(None, BAND_SUB), P(), P()),
        check_vma=False,
    )
```

profile of v0, /device:TPU:1, one launch (start us, length us, event | category | flops | bytes accessed | tf_op | source)
XLA Modules:
  0.0 344.8 jit_solution(1889162275128251789)
XLA Ops:
  6.1 5.0 %all-to-all-start = ((bf16[4,512,512]{2,1,0:T(8,128)(2,1)}), bf16[4,512,512]{2,1,0:T(8,128)(2,1)S(1)}, u32[]{:S(2)}, u32[]{:S(2)}) async-start(bf16[4,512,512]{2,1,0:T(8,128)(2,1)} %broadcast_in_dim.41), calls=%async_computation | async-start | bytes 4194304 | tf_op jit(solution)/shard_map/all_to_all | solution.py:18
  17.0 18.4 %all-to-all-done = bf16[4,512,512]{2,1,0:T(8,128)(2,1)S(1)} async-done(((bf16[4,512,512]{2,1,0:T(8,128)(2,1)}), bf16[4,512,512]{2,1,0:T(8,128)(2,1)S(1)}, u32[]{:S(2)}, u32[]{:S(2)}) %all-to-all-start) | async-done | bytes 2097184 | tf_op jit(solution)/shard_map/all_to_all | solution.py:18
  35.5 6.0 %collective-permute-start = (bf16[512,512]{1,0:T(8,128)(2,1)S(1)}, bf16[512,512]{1,0:T(8,128)(2,1)S(1)}, u32[]{:S(2)}, u32[]{:S(2)}) collective-permute-start(bf16[512,512]{1,0:T(8,128)(2,1)S(1)} %get-tuple-element.62), channel_id=1, source_target_pairs={{0,4},{4,8},{8,12},{12,16},{16,20},{20,24},{24,28},{28,32},{32,36}... | collective-permute-start | bytes 1572872 | tf_op jit(solution)/shard_map/ppermute | solution.py:41
  47.6 4.4 %collective-permute-done.1 = bf16[512,512]{1,0:T(8,128)(2,1)S(1)} collective-permute-done((bf16[512,512]{1,0:T(8,128)(2,1)S(1)}, bf16[512,512]{1,0:T(8,128)(2,1)S(1)}, u32[]{:S(2)}, u32[]{:S(2)}) %collective-permute-start.1) | collective-permute-done | bytes 524320 | tf_op jit(solution)/shard_map/ppermute | solution.py:42
  53.8 10.7 %gather_fusion = bf16[2560,512]{1,0:T(8,128)(2,1)} fusion(bf16[3072,512]{1,0:T(8,128)(2,1)} %pad_maximum_fusion, s32[3072]{0:T(1024)S(1)} %pad_clamp_fusion), kind=kCustom, calls=%fused_computation | custom fusion | bytes 5253120 | tf_op jit(solution)/shard_map/jit(_take)/gather | solution.py:178
  64.5 5.7 %bitcast_add_fusion = (f32[2560,512]{1,0:T(8,128)}, bf16[2560,512]{1,0:T(8,128)(2,1)S(1)}) fusion(f32[64,512]{1,0:T(8,128)S(1)} %copy-done.13, bf16[2560,512]{1,0:T(8,128)(2,1)} %gather_fusion, pred[2560]{0:T(1024)(128)(4,1)S(1)} %compare_and_fusion), kind=kLoop, calls=%fused_computation.10 | loop fusion | flops 10485760 | bytes 10619392 | tf_op jit(solution)/shard_map/add | solution.py:179
  86.2 5.0 %all-to-all-done.1 = bf16[4,64,512]{2,1,0:T(8,128)(2,1)S(1)} async-done(((bf16[4,64,512]{2,1,0:T(8,128)(2,1)}), bf16[4,64,512]{2,1,0:T(8,128)(2,1)S(1)}, u32[]{:S(2)}, u32[]{:S(2)}) %all-to-all-start.1) | async-done | bytes 262176 | tf_op jit(solution)/shard_map/all_to_all | solution.py:18
  105.7 5.1 %scatter_custom_fusion = f32[384,512]{1,0:T(8,128)} fusion(s32[384]{0:T(512)} %copy-done.23, f32[384,512]{1,0:T(8,128)} %mul.90, f32[384,512]{1,0:T(8,128)} %add.192, bf16[384,512]{1,0:T(8,128)(2,1)} %gather_fusion.1, f32[]{:T(128)} %constant.188.clone.1, f32[]{:T(128)} %constant.190.clone.1, pred[384]{0:T(512)(128)(4,1)} %compare_and_fusion.2, ...), kind=kCustom, calls=%fused_computation.48 | custom fusion | flops 2359296 | bytes 2754560 | tf_op jit(solution)/shard_map/scatter-add | solution.py:205
  112.7 3.6 %collective-permute-start.4 = (bf16[64,512]{1,0:T(8,128)(2,1)}, bf16[64,512]{1,0:T(8,128)(2,1)S(1)}, u32[]{:S(2)}, u32[]{:S(2)}) collective-permute-start(bf16[64,512]{1,0:T(8,128)(2,1)} %get-tuple-element.65), channel_id=1, source_target_pairs={{0,4},{4,8},{8,12},{12,16},{16,20},{20,24},{24,28},{28,32},{32,36}... | collective-permute-start | bytes 196616 | tf_op jit(solution)/shard_map/ppermute | solution.py:50
  127.3 4.0 %all-to-all-start.2 = ((bf16[4,64,512]{2,1,0:T(8,128)(2,1)}), bf16[4,64,512]{2,1,0:T(8,128)(2,1)}, u32[]{:S(2)}, u32[]{:S(2)}) async-start(bf16[4,64,512]{2,1,0:T(8,128)(2,1)} %bitcast.64), calls=%async_computation.2 | async-start | bytes 524288 | tf_op jit(solution)/shard_map/all_to_all | solution.py:60
  144.5 3.9 %fusion.2 = bf16[2560,512]{1,0:T(8,128)(2,1)S(1)} fusion(f32[2560]{0:T(1024)S(1)} %broadcast_multiply_fusion, f32[2560]{0:T(1024)S(1)} %div.71, f32[64,512]{1,0:T(8,128)S(1)} %get-tuple-element.71, f32[2560]{0:T(1024)} %copy-done.20, f32[2560,512]{1,0:T(8,128)} %copy-done.2, f32[2560]{0:T(1024)S(1)} %broadcast_multiply_fusion.1), kind=kLoop, calls=%fused_computation.8 | loop fusion | flops 9175040 | bytes 8036352 | tf_op jit(solution)/shard_map/convert_element_type | solution.py:215
  148.5 4.0 %fusion.55 = f32[2560,512]{1,0:T(8,128)} fusion(bf16[2560,512]{1,0:T(8,128)(2,1)S(1)} %fusion.2, bf16[512,512]{1,0:T(8,128)(2,1)S(1)} %copy-done), kind=kOutput, calls=%fused_computation.109 | convolution fusion | flops 1342177280 | bytes 8388608 | tf_op jit(solution)/shard_map/dot_general | solution.py:119
  152.4 21.5 %scatter_custom_fusion.1 = f32[3072,512]{1,0:T(8,128)} fusion(s32[2560]{0:T(1024)} %copy-done.21, f32[2560,512]{1,0:T(8,128)} %fusion.55, f32[2560,512]{1,0:T(8,128)} %get-tuple-element.58, f32[]{:T(128)} %constant.190.clone.1, f32[]{:T(128)} %constant.188.clone.1), kind=kCustom, calls=%fused_computation.11 | custom fusion | flops 11796480 | bytes 16778240 | tf_op jit(solution)/shard_map/scatter-add | solution.py:219
  177.3 3.8 %collective-permute-start.6 = (bf16[512,512]{1,0:T(8,128)(2,1)S(1)}, bf16[512,512]{1,0:T(8,128)(2,1)S(1)}, u32[]{:S(2)}, u32[]{:S(2)}) collective-permute-start(bf16[512,512]{1,0:T(8,128)(2,1)S(1)} %get-tuple-element.57), channel_id=1, source_target_pairs={{0,4},{4,8},{8,12},{12,16},{16,20},{20,24},{24,28},{28,32},{32,36}... | collective-permute-start | bytes 1572872 | tf_op jit(solution)/shard_map/ppermute | solution.py:50
  183.0 4.2 %collective-permute-done.6 = bf16[512,512]{1,0:T(8,128)(2,1)S(1)} collective-permute-done((bf16[512,512]{1,0:T(8,128)(2,1)S(1)}, bf16[512,512]{1,0:T(8,128)(2,1)S(1)}, u32[]{:S(2)}, u32[]{:S(2)}) %collective-permute-start.6) | collective-permute-done | bytes 524320 | tf_op jit(solution)/shard_map/ppermute | solution.py:50
  187.4 4.2 %collective-permute-done.7 = bf16[512,512]{1,0:T(8,128)(2,1)S(1)} collective-permute-done((bf16[512,512]{1,0:T(8,128)(2,1)S(1)}, bf16[512,512]{1,0:T(8,128)(2,1)S(1)}, u32[]{:S(2)}, u32[]{:S(2)}) %collective-permute-start.7) | collective-permute-done | bytes 524320 | tf_op jit(solution)/shard_map/ppermute | solution.py:50
  193.5 4.7 %all-to-all-start.3 = ((bf16[4,512,512]{2,1,0:T(8,128)(2,1)}), bf16[4,512,512]{2,1,0:T(8,128)(2,1)}, u32[]{:S(2)}, u32[]{:S(2)}) async-start(bf16[4,512,512]{2,1,0:T(8,128)(2,1)} %bitcast.61), calls=%async_computation.3 | async-start | bytes 4194304 | tf_op jit(solution)/shard_map/all_to_all | solution.py:60
  198.1 4.3 %fusion.56 = f32[512,512]{1,0:T(8,128)} fusion(bf16[2560,512]{1,0:T(8,128)(2,1)S(1)} %get-tuple-element.59, bf16[2560,512]{1,0:T(8,128)(2,1)} %copy-done.4), kind=kOutput, calls=%fused_computation.110 | convolution fusion | flops 1342177280 | bytes 6291456 | tf_op jit(solution)/shard_map/dot_general | solution.py:125
  204.7 13.6 %all-to-all-done.3 = bf16[4,512,512]{2,1,0:T(8,128)(2,1)} async-done(((bf16[4,512,512]{2,1,0:T(8,128)(2,1)}), bf16[4,512,512]{2,1,0:T(8,128)(2,1)}, u32[]{:S(2)}, u32[]{:S(2)}) %all-to-all-start.3) | async-done | bytes 2097184 | tf_op jit(solution)/shard_map/all_to_all | solution.py:60
  225.7 28.6 %all_to_all.45 = f32[8,32,2048]{2,1,0:T(8,128)S(1)} all-to-all(f32[8,32,2048]{2,1,0:T(8,128)S(1)} %maximum_bitcast_fusion), channel_id=1, replica_groups=mesh['band_0'=8,'band_1'=4,'band_2'=2,'sub'=4] {'band_2','sub'}, dimensions={0} | all-to-all | bytes 4194304 | tf_op jit(solution)/shard_map/all_to_all | solution.py:80
  254.6 34.1 %all_to_all.46 = f32[32,1,2048]{2,1,0:T(1,128)S(1)} all-to-all(f32[32,1,2048]{2,1,0:T(1,128)S(1)} %all_to_all.33), channel_id=1, replica_groups=mesh['band_0'=8,'band_1'=4,'band_2'=2,'sub'=4] {'band_0','band_1'}, dimensions={0} | all-to-all | bytes 524288 | tf_op jit(solution)/shard_map/all_to_all | solution.py:88
  289.0 15.0 %all_to_all.47 = f32[32,1,2048]{2,1,0:T(1,128)S(1)} all-to-all(f32[32,1,2048]{2,1,0:T(1,128)S(1)} %broadcast_in_dim.82), channel_id=1, replica_groups=mesh['band_0'=8,'band_1'=4,'band_2'=2,'sub'=4] {'band_0','band_1'}, dimensions={0} | all-to-all | bytes 524288 | tf_op jit(solution)/shard_map/all_to_all | solution.py:18
  305.7 6.8 %all-to-all-start.7 = ((f32[8,32,2048]{2,1,0:T(8,128)}), f32[8,32,2048]{2,1,0:T(8,128)S(1)}, u32[]{:S(2)}, u32[]{:S(2)}) async-start(f32[8,32,2048]{2,1,0:T(8,128)} %broadcast_in_dim.84), calls=%async_computation.7 | async-start | bytes 4194304 | tf_op jit(solution)/shard_map/all_to_all | solution.py:18
  316.2 22.5 %all-to-all-done.7 = f32[8,32,2048]{2,1,0:T(8,128)S(1)} async-done(((f32[8,32,2048]{2,1,0:T(8,128)}), f32[8,32,2048]{2,1,0:T(8,128)S(1)}, u32[]{:S(2)}, u32[]{:S(2)}) %all-to-all-start.7) | async-done | bytes 2097184 | tf_op jit(solution)/shard_map/all_to_all | solution.py:18
  (146 shorter events, 104.6 us)
Async XLA Ops:
  0.6 69.5 %copy-start = (bf16[512,512]{1,0:T(8,128)(2,1)S(1)}, bf16[512,512]{1,0:T(8,128)(2,1)}, u32[]{:S(2)}) copy-start(bf16[512,512]{1,0:T(8,128)(2,1)} %param.24) | copy-start | bytes 1572868
  6.1 37.4 %copy-start.15 = (bf16[512,512]{1,0:T(8,128)(2,1)S(1)}, bf16[512,512]{1,0:T(8,128)(2,1)}, u32[]{:S(2)}) copy-start(bf16[512,512]{1,0:T(8,128)(2,1)} %param.23) | copy-start | bytes 1572868
  6.1 37.4 %copy-start.18 = (bf16[64,512]{1,0:T(8,128)(2,1)S(1)}, bf16[64,512]{1,0:T(8,128)(2,1)}, u32[]{:S(2)}) copy-start(bf16[64,512]{1,0:T(8,128)(2,1)} %param.20) | copy-start | bytes 196612
  6.1 29.4 %all-to-all-start = ((bf16[4,512,512]{2,1,0:T(8,128)(2,1)}), bf16[4,512,512]{2,1,0:T(8,128)(2,1)S(1)}, u32[]{:S(2)}, u32[]{:S(2)}) async-start(bf16[4,512,512]{2,1,0:T(8,128)(2,1)} %broadcast_in_dim.41), calls=%async_computation | async-start | bytes 4194304 | tf_op jit(solution)/shard_map/all_to_all | solution.py:18
  17.0 36.8 %copy-start.21 = (s32[2560]{0:T(1024)}, s32[2560]{0:T(1024)S(1)}, u32[]{:S(2)}) copy-start(s32[2560]{0:T(1024)S(1)} %fusion.43) | copy-start | bytes 30724
  17.0 36.8 %copy-start.23 = (s32[384]{0:T(512)}, s32[384]{0:T(512)S(1)}, u32[]{:S(2)}) copy-start(s32[384]{0:T(512)S(1)} %fusion.44) | copy-start | bytes 4612
  35.5 12.1 %collective-permute-start = (bf16[512,512]{1,0:T(8,128)(2,1)S(1)}, bf16[512,512]{1,0:T(8,128)(2,1)S(1)}, u32[]{:S(2)}, u32[]{:S(2)}) collective-permute-start(bf16[512,512]{1,0:T(8,128)(2,1)S(1)} %get-tuple-element.62), channel_id=1, source_target_pairs={{0,4},{4,8},{8,12},{12,16},{16,20},{20,24},{24,28},{28,32},{32,36}... | collective-permute-start | bytes 1572872 | tf_op jit(solution)/shard_map/ppermute | solution.py:41
  41.5 10.5 %collective-permute-start.1 = (bf16[512,512]{1,0:T(8,128)(2,1)S(1)}, bf16[512,512]{1,0:T(8,128)(2,1)S(1)}, u32[]{:S(2)}, u32[]{:S(2)}) collective-permute-start(bf16[512,512]{1,0:T(8,128)(2,1)S(1)} %get-tuple-element.63), channel_id=1, source_target_pairs={{4,0},{8,4},{12,8},{16,12},{20,16},{24,20},{28,24},{32,28},{36,32}... | collective-permute-start | bytes 1572872 | tf_op jit(solution)/shard_map/ppermute | solution.py:42
  82.2 8.9 %all-to-all-start.1 = ((bf16[4,64,512]{2,1,0:T(8,128)(2,1)}), bf16[4,64,512]{2,1,0:T(8,128)(2,1)S(1)}, u32[]{:S(2)}, u32[]{:S(2)}) async-start(bf16[4,64,512]{2,1,0:T(8,128)(2,1)} %broadcast_in_dim.75), calls=%async_computation.1 | async-start | bytes 524288 | tf_op jit(solution)/shard_map/all_to_all | solution.py:18
  91.2 10.9 %copy-start.5 = (bf16[4,64,512]{2,1,0:T(8,128)(2,1)}, bf16[4,64,512]{2,1,0:T(8,128)(2,1)S(1)}, u32[]{:S(2)}) copy-start(bf16[4,64,512]{2,1,0:T(8,128)(2,1)S(1)} %all-to-all-done.1) | copy-start | bytes 786436
  91.9 10.2 %collective-permute-start.2 = (bf16[64,512]{1,0:T(8,128)(2,1)}, bf16[64,512]{1,0:T(8,128)(2,1)}, u32[]{:S(2)}, u32[]{:S(2)}) collective-permute-start(bf16[64,512]{1,0:T(8,128)(2,1)} %get-tuple-element.66), channel_id=1, source_target_pairs={{0,4},{4,8},{8,12},{12,16},{16,20},{20,24},{24,28},{28,32},{32,36}... | collective-permute-start | bytes 196616 | tf_op jit(solution)/shard_map/ppermute | solution.py:41
  95.3 6.8 %collective-permute-start.3 = (bf16[64,512]{1,0:T(8,128)(2,1)}, bf16[64,512]{1,0:T(8,128)(2,1)}, u32[]{:S(2)}, u32[]{:S(2)}) collective-permute-start(bf16[64,512]{1,0:T(8,128)(2,1)} %get-tuple-element.67), channel_id=1, source_target_pairs={{4,0},{8,4},{12,8},{16,12},{20,16},{24,20},{28,24},{32,28},{36,32}... | collective-permute-start | bytes 196616 | tf_op jit(solution)/shard_map/ppermute | solution.py:42
  105.7 25.6 %copy-start.7 = (f32[64,512]{1,0:T(8,128)S(1)}, f32[64,512]{1,0:T(8,128)}, u32[]{:S(2)}) copy-start(f32[64,512]{1,0:T(8,128)} %copy-done.6) | copy-start | bytes 393220
  105.7 25.6 %copy-start.9 = (f32[64,512]{1,0:T(8,128)S(1)}, f32[64,512]{1,0:T(8,128)}, u32[]{:S(2)}) copy-start(f32[64,512]{1,0:T(8,128)} %copy-done.8) | copy-start | bytes 393220
  105.7 32.2 %copy-start.17 = (bf16[64,512]{1,0:T(8,128)(2,1)S(1)}, bf16[64,512]{1,0:T(8,128)(2,1)}, u32[]{:S(2)}) copy-start(bf16[64,512]{1,0:T(8,128)(2,1)} %param.29) | copy-start | bytes 196612
  112.7 10.0 %collective-permute-start.4 = (bf16[64,512]{1,0:T(8,128)(2,1)}, bf16[64,512]{1,0:T(8,128)(2,1)S(1)}, u32[]{:S(2)}, u32[]{:S(2)}) collective-permute-start(bf16[64,512]{1,0:T(8,128)(2,1)} %get-tuple-element.65), channel_id=1, source_target_pairs={{0,4},{4,8},{8,12},{12,16},{16,20},{20,24},{24,28},{28,32},{32,36}... | collective-permute-start | bytes 196616 | tf_op jit(solution)/shard_map/ppermute | solution.py:50
  120.7 5.8 %collective-permute-start.5 = (bf16[64,512]{1,0:T(8,128)(2,1)}, bf16[64,512]{1,0:T(8,128)(2,1)S(1)}, u32[]{:S(2)}, u32[]{:S(2)}) collective-permute-start(bf16[64,512]{1,0:T(8,128)(2,1)} %get-tuple-element.64), channel_id=1, source_target_pairs={{4,0},{8,4},{12,8},{16,12},{20,16},{24,20},{28,24},{32,28},{36,32}... | collective-permute-start | bytes 196616 | tf_op jit(solution)/shard_map/ppermute | solution.py:50
  127.3 9.6 %all-to-all-start.2 = ((bf16[4,64,512]{2,1,0:T(8,128)(2,1)}), bf16[4,64,512]{2,1,0:T(8,128)(2,1)}, u32[]{:S(2)}, u32[]{:S(2)}) async-start(bf16[4,64,512]{2,1,0:T(8,128)(2,1)} %bitcast.64), calls=%async_computation.2 | async-start | bytes 524288 | tf_op jit(solution)/shard_map/all_to_all | solution.py:60
  177.3 9.9 %collective-permute-start.6 = (bf16[512,512]{1,0:T(8,128)(2,1)S(1)}, bf16[512,512]{1,0:T(8,128)(2,1)S(1)}, u32[]{:S(2)}, u32[]{:S(2)}) collective-permute-start(bf16[512,512]{1,0:T(8,128)(2,1)S(1)} %get-tuple-element.57), channel_id=1, source_target_pairs={{0,4},{4,8},{8,12},{12,16},{16,20},{20,24},{24,28},{28,32},{32,36}... | collective-permute-start | bytes 1572872 | tf_op jit(solution)/shard_map/ppermute | solution.py:50
  181.1 10.5 %collective-permute-start.7 = (bf16[512,512]{1,0:T(8,128)(2,1)S(1)}, bf16[512,512]{1,0:T(8,128)(2,1)S(1)}, u32[]{:S(2)}, u32[]{:S(2)}) collective-permute-start(bf16[512,512]{1,0:T(8,128)(2,1)S(1)} %get-tuple-element.56), channel_id=1, source_target_pairs={{4,0},{8,4},{12,8},{16,12},{20,16},{24,20},{28,24},{32,28},{36,32}... | collective-permute-start | bytes 1572872 | tf_op jit(solution)/shard_map/ppermute | solution.py:50
  193.5 24.9 %all-to-all-start.3 = ((bf16[4,512,512]{2,1,0:T(8,128)(2,1)}), bf16[4,512,512]{2,1,0:T(8,128)(2,1)}, u32[]{:S(2)}, u32[]{:S(2)}) async-start(bf16[4,512,512]{2,1,0:T(8,128)(2,1)} %bitcast.61), calls=%async_computation.3 | async-start | bytes 4194304 | tf_op jit(solution)/shard_map/all_to_all | solution.py:60
  254.3 58.2 %copy-start.12 = (bf16[64,512]{1,0:T(8,128)(2,1)S(1)}, bf16[64,512]{1,0:T(8,128)(2,1)}, u32[]{:S(2)}) copy-start(bf16[64,512]{1,0:T(8,128)(2,1)} %copy-done.11) | copy-start | bytes 196612
  254.3 58.2 %copy-start.14 = (f32[64,512]{1,0:T(8,128)S(1)}, f32[64,512]{1,0:T(8,128)}, u32[]{:S(2)}) copy-start(f32[64,512]{1,0:T(8,128)} %get-tuple-element.53) | copy-start | bytes 393220
  305.7 33.0 %all-to-all-start.7 = ((f32[8,32,2048]{2,1,0:T(8,128)}), f32[8,32,2048]{2,1,0:T(8,128)S(1)}, u32[]{:S(2)}, u32[]{:S(2)}) async-start(f32[8,32,2048]{2,1,0:T(8,128)} %broadcast_in_dim.84), calls=%async_computation.7 | async-start | bytes 4194304 | tf_op jit(solution)/shard_map/all_to_all | solution.py:18
  (16 other events, 93.4 us)
where the time goes:
time: 347 us; the launch traced here: 345 us
  waiting for transfers between devices  81.2 us (23%)
  blocking collectives  77.7 us (22%)
  other arithmetic  66.8 us (19%)
  starting transfers between devices  48.7 us (14%)
  local copies, waits for them, and re-layouts  44.5 us (13%)
  matrix products  24.7 us (7%)
    all_to_all x3, waiting for transfers between devices, from_everyone(): lax.all_to_all(jnp.broadcast_to(shard[None], (devices, *shard.shape)), ax...  45.9 us
    all_to_all x1, blocking collectives, summed_rows(): lax.all_to_all(nearer, far, split_axis=0, concat_axis=0, tiled=True)  34.1 us
    all_to_all x1, blocking collectives, sent_and_summed_2(): lax.all_to_all(cut_along(shard, dim, devices), axis, 0, 0, tiled=True)  28.6 us
    scatter-add x1, other arithmetic, body(): jnp.zeros((grid_window.shape[0], latent), jnp.float32).at[grid_local]  21.5 us
    all_to_all x2, waiting for transfers between devices, sent_and_summed(): lax.all_to_all(cut_along(shard, dim, devices), axis, 0, 0, tiled=True)  16.4 us
    all_to_all x3, starting transfers between devices, from_everyone(): lax.all_to_all(jnp.broadcast_to(shard[None], (devices, *shard.shape)), ax...  15.2 us
    all_to_all x1, blocking collectives, from_everyone(): lax.all_to_all(jnp.broadcast_to(shard[None], (devices, *shard.shape)), ax...  15 us
    ppermute x4, waiting for transfers between devices, from_behind(): lax.ppermute(value, axis, [(source, source + steps) for source in range(f...  11.3 us
  transfers between devices with their start and end apart: 13, of which 10 were waited for; matrix products, arithmetic and copies ran while one was open for 9% of the time, Pallas kernels for 0%

commit v1 on v0

v1 whole, which is shorter than its diff:
```python
import functools
import math

import jax
import jax.numpy as jnp
from jax import lax
from jax.experimental import pallas as pl
from jax.experimental.pallas import tpu as pltpu
from jax.sharding import Mesh
from jax.sharding import PartitionSpec as P

BAND = ("band_0", "band_1", "band_2")
ALL = ("band_0", "band_1", "band_2", "sub")
NEAR = ("band_1", "band_2", "sub")
FAR = "band_0"

EPSILON = 1e-05
BF = jnp.bfloat16
F32 = jnp.float32
VMEM = 48 * 1024 * 1024


def sigmoid(value):
    return 0.5 * jnp.tanh(0.5 * value) + 0.5


def silu_and_slope(value):
    sigma = sigmoid(value)
    active = value * sigma
    return active, sigma + active * (1.0 - sigma)


def dot(left, right):
    return jnp.dot(left, right, preferred_element_type=F32)


def dot_t(left, right):
    return lax.dot_general(left, right, (((1,), (1,)), ((), ())), preferred_element_type=F32)


def t_dot(left, right):
    return lax.dot_general(left, right, (((0,), (0,)), ((), ())), preferred_element_type=F32)


def selection(column, width, base):
    lanes = lax.broadcasted_iota(jnp.int32, (column.shape[0], width), 1)
    return jnp.where(column - base == lanes, 1.0, 0.0).astype(BF)


def selection_t(row, height):
    lines = lax.broadcasted_iota(jnp.int32, (height, row.shape[1]), 0)
    return jnp.where(row == lines, 1.0, 0.0).astype(BF)


def padded_rows(ref, scratch):
    rows = ref.shape[0]
    scratch[...] = jnp.zeros_like(scratch)
    scratch[:rows, :] = ref[...]
    return scratch[...]


def forward_kernel(
    scale,
    index_ref, low_ref, band_ref, high_ref, mesh_ref, embed_ref, src_ref, dst_ref, edge_ref,
    hidden_ref, hslope_ref, active_ref, bslope_ref, normed_ref, inverse_ref, mesh_out_ref,
    table, pad, embed, dest, total,
):
    step = pl.program_id(0)
    nodes = low_ref.shape[1]
    blocks = band_ref.shape[0] + 2
    rows = mesh_ref.shape[0]

    @pl.when(step == 0)
    def _():
        for block in range(blocks):
            if block == 0:
                source = low_ref
            elif block == blocks - 1:
                source = high_ref
            else:
                source = band_ref.at[block - 1]
            table[block * nodes : (block + 1) * nodes, :] = padded_rows(source, pad).T
        embed[...] = padded_rows(embed_ref, pad)
        dest[...] = dot(mesh_ref[...], dst_ref[...])
        total[...] = jnp.zeros_like(total)

    column = index_ref[...]
    edges = column.shape[0]
    picked = jnp.zeros((edges, table.shape[1]), F32)
    for block in range(blocks):
        part = table[block * nodes : (block + 1) * nodes, :]
        picked += dot(selection(column, nodes, block * nodes), part)
    hidden, hslope = silu_and_slope(dot(picked.astype(BF), embed[...]))
    hidden = hidden.astype(BF)
    hidden_ref[...] = hidden
    hslope_ref[...] = hslope.astype(BF)
    projected = dot(hidden, src_ref[...]).astype(BF).astype(F32)
    before = (projected.reshape(-1, rows, projected.shape[1]) + dest[...][None]).reshape(projected.shape)
    active, bslope = silu_and_slope(before)
    active = active.astype(BF)
    active_ref[...] = active
    bslope_ref[...] = bslope.astype(BF)
    out = dot(active, edge_ref[...])
    centred = out - jnp.mean(out, axis=-1, keepdims=True)
    inverse = lax.rsqrt(jnp.mean(centred * centred, axis=-1, keepdims=True) + EPSILON)
    normed = centred * inverse
    normed_ref[...] = normed.astype(BF)
    inverse_ref[...] = inverse
    total[...] += jnp.sum(normed.reshape(-1, rows, normed.shape[1]), axis=0)

    @pl.when(step == pl.num_programs(0) - 1)
    def _():
        mesh_out_ref[...] = (mesh_ref[...].astype(F32) + total[...] * scale).astype(BF)


def mesh_kernel(
    mesh_scale, scale,
    own_ref, band_ref, far_ref, edge_ref, cot_ref, cots_ref, index_ref, column_ref, row_ref,
    proc_ref, recv_ref, active_ref, normed_ref, inverse_ref,
    out_ref, ngrad_ref, wgrad_ref,
    receiver_all, query_grad, upper_ref, total,
):
    step = pl.program_id(0)
    own = own_ref[...]
    rows, latent = own_ref.shape

    @pl.when(step == 0)
    def _():
        proc = proc_ref[...]
        recv = recv_ref[...]
        window = jnp.concatenate([band_ref[...], far_ref[...], edge_ref[...]], axis=0)
        query = dot(window, proc).astype(BF)
        receiver = dot(own, recv)
        count = index_ref.shape[0] // rows
        sent = dot(selection(index_ref[...], window.shape[0], 0), query)
        before = sent.reshape(count, rows, latent) + receiver[None]
        active, slope = silu_and_slope(before)
        summed = jnp.sum(active, axis=0)
        out_ref[...] = (own.astype(F32) + summed * mesh_scale).astype(BF)
        upstream = cot_ref[...].astype(F32)
        receiver_grad = upstream * mesh_scale * jnp.sum(slope, axis=0)

        wide = band_ref.shape[0]
        receiver_all[:wide, :] = dot(band_ref[...], recv)
        receiver_all[wide:, :] = dot(far_ref[...], recv)
        own_query = dot(own, proc).astype(BF)
        query_grad[...] = jnp.zeros_like(query_grad)

        def one(j, carry):
            value = dot(selection(column_ref[j], rows, 0), own_query) + receiver_all[...]
            _, slopes = silu_and_slope(value)
            slopes = (cots_ref[...].astype(F32) * mesh_scale * slopes).astype(BF)
            query_grad[...] += dot(selection_t(row_ref[j], rows), slopes)
            return carry

        lax.fori_loop(0, count, one, 0)
        mesh_grad = upstream + dot_t(query_grad[...].astype(BF), proc)
        mesh_grad = mesh_grad + dot_t(receiver_grad.astype(BF), recv)
        upper_ref[...] = mesh_grad * scale
        total[...] = jnp.zeros_like(total)

    upper = upper_ref[...]
    centred = upper - jnp.mean(upper, axis=-1, keepdims=True)
    normed = normed_ref[...].astype(F32).reshape(-1, rows, latent)
    inverse = inverse_ref[...].reshape(-1, rows, 1)
    along = jnp.mean(upper[None] * normed, axis=-1, keepdims=True)
    ngrad = ((centred[None] - normed * along) * inverse).reshape(-1, latent).astype(BF)
    ngrad_ref[...] = ngrad
    total[...] += t_dot(active_ref[...], ngrad)

    @pl.when(step == pl.num_programs(0) - 1)
    def _():
        wgrad_ref[...] = total[...].astype(BF)


def source_kernel(
    edge_ref, ngrad_ref, bslope_ref, hidden_ref,
    bgrad_ref, wgrad_ref,
    total,
):
    step = pl.program_id(0)

    @pl.when(step == 0)
    def _():
        total[...] = jnp.zeros_like(total)

    bgrad = (dot_t(ngrad_ref[...], edge_ref[...]) * bslope_ref[...].astype(F32)).astype(BF)
    bgrad_ref[...] = bgrad
    total[...] += t_dot(hidden_ref[...], bgrad)

    @pl.when(step == pl.num_programs(0) - 1)
    def _():
        wgrad_ref[...] = total[...].astype(BF)


def grid_kernel(
    index_ref, src_ref, embed_ref, bgrad_ref, hslope_ref,
    low_ref, band_ref, high_ref,
    pad, total,
):
    step = pl.program_id(0)
    channels, nodes = low_ref.shape
    blocks = band_ref.shape[0] + 2

    @pl.when(step == 0)
    def _():
        padded_rows(embed_ref, pad)
        total[...] = jnp.zeros_like(total)

    hgrad = (dot_t(bgrad_ref[...], src_ref[...]) * hslope_ref[...].astype(F32)).astype(BF)
    ggrad = dot_t(pad[...], hgrad).astype(BF)
    column = index_ref[...]
    for block in range(blocks):
        total[block] += dot(ggrad, selection(column, nodes, block * nodes))

    @pl.when(step == pl.num_programs(0) - 1)
    def _():
        for block in range(blocks):
            done = total[block][:channels].astype(BF)
            if block == 0:
                low_ref[...] = done
            elif block == blocks - 1:
                high_ref[...] = done
            else:
                band_ref[block - 1] = done


def whole(shape):
    return pl.BlockSpec(shape, lambda i, n=len(shape): (0,) * n)


def tiled(edges, width):
    return pl.BlockSpec((edges, width), lambda i: (i, 0))


def params():
    return pltpu.CompilerParams(dimension_semantics=("arbitrary",), vmem_limit_bytes=VMEM)


def from_everyone(shard, axis):
    devices = lax.axis_size(axis)
    return lax.all_to_all(
        jnp.broadcast_to(shard[None], (devices, *shard.shape)), axis, 0, 0, tiled=True
    )


def bands_up(value):
    count = lax.axis_size(BAND)
    return lax.ppermute(value, BAND, [(i, i + 1) for i in range(count - 1)])


def bands_down(value):
    count = lax.axis_size(BAND)
    return lax.ppermute(value, BAND, [(i + 1, i) for i in range(count - 1)])


def outwards(value, near):
    bands, subs = lax.axis_size(BAND), lax.axis_size("sub")
    pairs = []
    for band in range(bands):
        for sub in range(subs):
            up = (sub < subs // 2) == near
            to = band + 1 if up else band - 1
            if 0 <= to < bands:
                pairs.append((band * subs + sub, to * subs + sub))
    return lax.ppermute(value, ALL, pairs)


def weight_sum(part):
    near = lax.axis_size(NEAR)
    rows, width = part.shape
    parts = lax.all_to_all(part.reshape(near, rows // near, width), NEAR, 0, 0, tiled=True)
    mine = jnp.sum(parts.astype(F32), axis=0).astype(BF)
    mine = jnp.sum(from_everyone(mine, FAR).astype(F32), axis=0).astype(BF)
    return from_everyone(mine, NEAR).reshape(rows, width).astype(F32)


def body(
    grid_x, mesh_in, w_embed, w_src, w_dst, w_edge, w_proc, w_recv, g2m_src, mesh_src, cotangent
):
    channels, nodes = grid_x.shape
    latent = w_src.shape[0]
    rows, enc_count = g2m_src.shape
    mesh_count = mesh_src.shape[1]
    subs = lax.axis_size("sub")
    band = lax.axis_index(BAND)
    sub = lax.axis_index("sub")
    wide = -(-channels // 128) * 128
    blocks = subs + 2
    edges = rows * enc_count
    steps = 4
    tile = edges // steps
    scale = 1.0 / math.sqrt(enc_count)
    mesh_scale = 1.0 / math.sqrt(mesh_count)

    grid_band = lax.all_gather(grid_x, "sub", axis=0)
    grid_low = bands_up(grid_band[subs - 1])
    grid_high = bands_down(grid_band[0])
    grid_local = (g2m_src - (band * (nodes * subs) - nodes)).T.reshape(edges, 1)

    band_cot = from_everyone(cotangent, "sub").reshape(subs * rows, latent)
    band_src = from_everyone(mesh_src, "sub").reshape(subs * rows, mesh_count)
    far_cot = outwards(band_cot, True)
    far_src = outwards(band_src, True)
    all_cot = jnp.concatenate([band_cot, far_cot])
    own_base = (band * subs + sub) * rows
    all_src = (jnp.concatenate([band_src, far_src]) - own_base).T
    column_src = all_src[:, :, None]
    row_src = all_src[:, None, :]
    lower = sub < subs // 2
    local = mesh_src - band * (rows * subs)
    width = rows * subs
    below = jnp.where(lower, local + 2 * width, local + rows + 2 * width)
    above = jnp.where(lower, local - width + 2 * width, local)
    place = jnp.where(local < 0, below, jnp.where(local >= width, above, local))
    place = place.T.reshape(rows * mesh_count, 1)

    hidden, hslope, active, bslope, normed, inverse, hidden_mesh = pl.pallas_call(
        functools.partial(forward_kernel, scale),
        grid=(steps,),
        in_specs=[
            tiled(tile, 1),
            whole((channels, nodes)),
            whole((subs, channels, nodes)),
            whole((channels, nodes)),
            whole((rows, latent)),
            whole((channels, latent)),
            whole((latent, latent)),
            whole((latent, latent)),
            whole((latent, latent)),
        ],
        out_specs=[tiled(tile, latent)] * 5 + [tiled(tile, 1), whole((rows, latent))],
        out_shape=[jax.ShapeDtypeStruct((edges, latent), BF)] * 5
        + [jax.ShapeDtypeStruct((edges, 1), F32), jax.ShapeDtypeStruct((rows, latent), BF)],
        scratch_shapes=[
            pltpu.VMEM((blocks * nodes, wide), BF),
            pltpu.VMEM((wide, nodes), BF),
            pltpu.VMEM((wide, latent), BF),
            pltpu.VMEM((rows, latent), F32),
            pltpu.VMEM((rows, latent), F32),
        ],
        compiler_params=params(),
        name="encode",
    )(grid_local, grid_low, grid_band, grid_high, mesh_in, w_embed, w_src, w_dst, w_edge)

    mesh_band = from_everyone(hidden_mesh, "sub").reshape(subs * rows, latent)
    mesh_far = outwards(mesh_band, True)
    border = jnp.where(lower, mesh_band[:rows], mesh_band[-rows:])
    mesh_edge = outwards(border, False)

    mesh_out, ngrad, edge_part = pl.pallas_call(
        functools.partial(mesh_kernel, mesh_scale, scale),
        grid=(steps,),
        in_specs=[
            whole((rows, latent)),
            whole((width, latent)),
            whole((width, latent)),
            whole((rows, latent)),
            whole((rows, latent)),
            whole((2 * width, latent)),
            whole((rows * mesh_count, 1)),
            whole((mesh_count, 2 * width, 1)),
            whole((mesh_count, 1, 2 * width)),
            whole((latent, latent)),
            whole((latent, latent)),
            tiled(tile, latent),
            tiled(tile, latent),
            tiled(tile, 1),
        ],
        out_specs=[whole((rows, latent)), tiled(tile, latent), whole((latent, latent))],
        out_shape=[
            jax.ShapeDtypeStruct((rows, latent), BF),
            jax.ShapeDtypeStruct((edges, latent), BF),
            jax.ShapeDtypeStruct((latent, latent), BF),
        ],
        scratch_shapes=[
            pltpu.VMEM((2 * width, latent), F32),
            pltpu.VMEM((rows, latent), F32),
            pltpu.VMEM((rows, latent), F32),
            pltpu.VMEM((latent, latent), F32),
        ],
        compiler_params=params(),
        name="process",
    )(
        hidden_mesh, mesh_band, mesh_far, mesh_edge, cotangent, all_cot, place, column_src, row_src,
        w_proc, w_recv, active, normed, inverse,
    )

    bgrad, src_part = pl.pallas_call(
        source_kernel,
        grid=(steps,),
        in_specs=[whole((latent, latent))] + [tiled(tile, latent)] * 3,
        out_specs=[tiled(tile, latent), whole((latent, latent))],
        out_shape=[
            jax.ShapeDtypeStruct((edges, latent), BF),
            jax.ShapeDtypeStruct((latent, latent), BF),
        ],
        scratch_shapes=[pltpu.VMEM((latent, latent), F32)],
        compiler_params=params(),
        name="source",
    )(w_edge, ngrad, bslope, hidden)

    part_low, part_band, part_high = pl.pallas_call(
        grid_kernel,
        grid=(steps,),
        in_specs=[
            tiled(tile, 1),
            whole((latent, latent)),
            whole((channels, latent)),
            tiled(tile, latent),
            tiled(tile, latent),
        ],
        out_specs=[
            whole((channels, nodes)),
            whole((subs, channels, nodes)),
            whole((channels, nodes)),
        ],
        out_shape=[
            jax.ShapeDtypeStruct((channels, nodes), BF),
            jax.ShapeDtypeStruct((subs, channels, nodes), BF),
            jax.ShapeDtypeStruct((channels, nodes), BF),
        ],
        scratch_shapes=[pltpu.VMEM((wide, latent), BF), pltpu.VMEM((blocks, wide, nodes), F32)],
        compiler_params=params(),
        name="channels",
    )(grid_local, w_src, w_embed, bgrad, hslope)

    edge_grad = weight_sum(edge_part)
    src_grad = weight_sum(src_part)
    from_above = bands_down(part_low)
    from_below = bands_up(part_high)
    first = (part_band[0].astype(F32) + from_below.astype(F32)).astype(BF)
    last = (part_band[subs - 1].astype(F32) + from_above.astype(F32)).astype(BF)
    part = jnp.concatenate([first[None], part_band[1 : subs - 1], last[None]])
    arrived = lax.all_to_all(part, "sub", 0, 0, tiled=True)
    grid_grad = jnp.sum(arrived.astype(F32), axis=0)
    return (mesh_out, grid_grad, src_grad, edge_grad)


def solution(mesh):
    torus = Mesh(mesh.devices.reshape(8, 4, 2, mesh.shape["sub"]), ALL)
    return jax.shard_map(
        body,
        mesh=torus,
        in_specs=(
            P(None, ALL),
            P(ALL, None),
            P(),
            P(),
            P(),
            P(),
            P(),
            P(),
            P(ALL, None),
            P(ALL, None),
            P(ALL, None),
        ),
        out_specs=(P(ALL, None), P(None, ALL), P(), P()),
        check_vma=False,
    )
```

time: 347 us -> 244 us (0.70)
  blocking collectives: 77.7 us -> 14 us
  other arithmetic: 66.8 us -> 11.8 us
  Pallas kernels: 0 us -> 49.1 us
  starting transfers between devices: 48.7 us -> 81.2 us
  waiting for transfers between devices: 81.2 us -> 54.5 us
  matrix products: 24.7 us -> 0 us
  local copies, waits for them, and re-layouts: 44.5 us -> 30.4 us
    all_to_all x3 -> x0, blocking collectives: 77.7 us -> none  [the longest x1 34.1 us: summed_rows(): lax.all_to_all(nearer, far, split_axis=0, concat_axis=0, tiled=True)]
    pallas_call x0 -> x4, Pallas kernels: none -> 49.1 us  [the longest x1 19.3 us: body(): pl.pallas_call(functools.partial(forward_kernel, scale), grid=(steps,), i...]
    scatter-add x6 -> x0, other arithmetic: 28 us -> none  [the longest x1 21.5 us: body(): jnp.zeros((grid_window.shape[0], latent), jnp.float32).at[grid_local]]
    all_to_all x3 -> x7, starting transfers between devices: 15.2 us -> 40.9 us  [from_everyone(): lax.all_to_all(jnp.broadcast_to(shard[None], (devices, *shard.shape)), ax...]
    dot_general x12 -> x0, matrix products: 24.7 us -> none  [the longest x4 9.82 us: times_transpose(): lax.dot_general(left, right, (((1,), (1,)), ((), ())), preferred_element_...]
    ppermute x8, waiting for transfers between devices: 19 us -> 2.6 us  [the longest x4 2.58 us: outwards(): return lax.ppermute(value, ALL, pairs)]
    gather x3 -> x0, local copies, waits for them, and re-layouts: 15.2 us -> none  [the longest x1 10.7 us: body(): before = jnp.take(grid_window, grid_local, axis=0).astype(jnp.float32)]
    unnamed x53 -> x43, local copies, waits for them, and re-layouts: 2.41 us -> 17.6 us
  transfers between devices with their start and end apart: 13 -> 18, of which waited for: 10 -> 9; matrix products, arithmetic and copies ran while one was open for 9% -> 10% of each run, Pallas kernels for 0% -> 15%
where the time goes in v1:
time: 244 us; the launch traced here: 242 us
  starting transfers between devices  81.2 us (33%)
  waiting for transfers between devices  54.5 us (22%)
  Pallas kernels  49.1 us (20%)
  local copies, waits for them, and re-layouts  30.4 us (12%)
  blocking collectives  14 us (6%)
  other arithmetic  11.8 us (5%)
    all_to_all x7, starting transfers between devices, from_everyone(): lax.all_to_all(jnp.broadcast_to(shard[None], (devices, *shard.shape)), ax...  40.9 us
    all_to_all x7, waiting for transfers between devices, from_everyone(): lax.all_to_all(jnp.broadcast_to(shard[None], (devices, *shard.shape)), ax...  39.9 us
    pallas_call x1, Pallas kernels, body(): pl.pallas_call(functools.partial(forward_kernel, scale), grid=(steps,), i...  19.3 us
    unnamed x43, local copies, waits for them, and re-layouts  17.6 us
    all_gather x1, blocking collectives, body(): grid_band = lax.all_gather(grid_x, 'sub', axis=0)  14 us
    pallas_call x1, Pallas kernels, body(): pl.pallas_call(functools.partial(mesh_kernel, mesh_scale, scale), grid=(s...  13 us
    all_to_all x2, starting transfers between devices, weight_sum(): lax.all_to_all(part.reshape(near, rows // near, width), NEAR, 0, 0, tiled...  11.8 us
    ppermute x4, starting transfers between devices, outwards(): return lax.ppermute(value, ALL, pairs)  11.2 us
  transfers between devices with their start and end apart: 18, of which 9 were waited for; matrix products, arithmetic and copies ran while one was open for 10% of the time, Pallas kernels for 15%

profile of v1, /device:TPU:1, one launch (start us, length us, event | category | flops | bytes accessed | tf_op | source)
XLA Modules:
  0.0 242.1 jit_solution(760196174738464334)
XLA Ops:
  0.7 14.0 %all-gather.1.band_ref = bf16[4,227,512]{2,1,0:T(8,128)(2,1)S(1)} all-gather(bf16[1,227,512]{2,1,0:T(8,128)(2,1)} %bitcast.42), channel_id=2, replica_groups=mesh['band_0'=8,'band_1'=4,'band_2'=2,'sub'=4] {'sub'}, dimensions={0}, use_global_device_ids=true | all-gather | bytes 1162240 | tf_op jit(solution)/shard_map/all_gather | solution.py:296
  15.4 5.9 %collective-permute-start.1 = (bf16[227,512]{1,0:T(8,128)(2,1)}, bf16[227,512]{1,0:T(8,128)(2,1)S(1)}, u32[]{:S(2)}, u32[]{:S(2)}) collective-permute-start(bf16[227,512]{1,0:T(8,128)(2,1)} %get-tuple-element.36), channel_id=1, source_target_pairs={{4,0},{8,4},{12,8},{16,12},{20,16},{24,20},{28,24},{32,28},{36,32}... | collective-permute-start | bytes 697352 | tf_op jit(solution)/shard_map/ppermute | solution.py:254
  24.6 3.7 %all-to-all-start.2 = ((s32[4,1,384]{2,1,0:T(1,128)}), s32[4,1,384]{2,1,0:T(1,128)S(1)}, u32[]{:S(2)}, u32[]{:S(2)}) async-start(s32[4,1,384]{2,1,0:T(1,128)} %reshape.73), calls=%async_computation.2 | async-start | bytes 12288 | tf_op jit(solution)/shard_map/all_to_all | solution.py:242
  28.3 4.2 %all-to-all-done.2 = s32[4,1,384]{2,1,0:T(1,128)S(1)} async-done(((s32[4,1,384]{2,1,0:T(1,128)}), s32[4,1,384]{2,1,0:T(1,128)S(1)}, u32[]{:S(2)}, u32[]{:S(2)}) %all-to-all-start.2) | async-done | bytes 6176 | tf_op jit(solution)/shard_map/all_to_all | solution.py:242
  34.0 4.0 %all-to-all-start.1 = ((bf16[4,64,512]{2,1,0:T(8,128)(2,1)}), bf16[4,64,512]{2,1,0:T(8,128)(2,1)}, u32[]{:S(2)}, u32[]{:S(2)}) async-start(bf16[4,64,512]{2,1,0:T(8,128)(2,1)} %broadcast_in_dim.23), calls=%async_computation.1 | async-start | bytes 524288 | tf_op jit(solution)/shard_map/all_to_all | solution.py:242
  45.9 3.8 %collective-permute-start.5 = (s32[256,6]{0,1:T(8,128)S(1)}, s32[256,6]{0,1:T(8,128)}, u32[]{:S(2)}, u32[]{:S(2)}) collective-permute-start(s32[256,6]{0,1:T(8,128)S(1)} %reshape.54), channel_id=1, source_target_pairs={{0,4},{1,5},{4,8},{5,9},{6,2},{7,3},{8,12},{9,13},{10,6},{11,7},{1... | collective-permute-start | bytes 18440 | tf_op jit(solution)/shard_map/ppermute | solution.py:266
  54.3 19.3 %encode.1 = (bf16[2560,512]{1,0:T(8,128)(2,1)}, bf16[2560,512]{1,0:T(8,128)(2,1)}, bf16[2560,512]{1,0:T(8,128)(2,1)}, bf16[2560,512]{1,0:T(8,128)(2,1)}, bf16[25...) custom-call(s32[2560,1]{1,0:T(8,128)S(1)} %reshape.71.index_ref, ...), custom_call_target="tpu_custom_call" | custom-call | tf_op jit(solution)/shard_map/encode/pallas_call | solution.py:318
  75.4 4.4 %all-to-all-start = ((bf16[4,64,512]{2,1,0:T(8,128)(2,1)}), bf16[4,64,512]{2,1,0:T(8,128)(2,1)}, u32[]{:S(2)}, u32[]{:S(2)}) async-start(bf16[4,64,512]{2,1,0:T(8,128)(2,1)} %broadcast_in_dim.22), calls=%async_computation | async-start | bytes 524288 | tf_op jit(solution)/shard_map/all_to_all | solution.py:242
  101.0 13.0 %process.1 = (bf16[64,512]{1,0:T(8,128)(2,1)}, bf16[2560,512]{1,0:T(8,128)(2,1)}, bf16[512,512]{1,0:T(8,128)(2,1)S(1)}) custom-call(bf16[64,512]{1,0:T(8,128)(2,1)S(1)} %get-tuple-element.19.own_ref, bf16[256,512]{1,0:T(8,128)(2,1)} %bitcast.4.band_ref, bf16[256,512]{1,0:T(8,128)(2,1)S(1)} %collective-permute-done.2.far_ref, ...), custom_call_target="tpu_custom_call" | custom-call | tf_op jit(solution)/shard_map/process/pallas_call | solution.py:351
  114.8 7.0 %all-to-all-start.7 = ((bf16[32,16,512]{2,1,0:T(8,128)(2,1)}), bf16[32,16,512]{2,1,0:T(8,128)(2,1)}, u32[]{:S(2)}, u32[]{:S(2)}) async-start(bf16[32,16,512]{2,1,0:T(8,128)(2,1)} %bitcast.41), calls=%async_computation.7 | async-start | bytes 1048576 | tf_op jit(solution)/shard_map/all_to_all | solution.py:272
  121.8 7.0 %source.1 = (bf16[2560,512]{1,0:T(8,128)(2,1)S(1)}, bf16[512,512]{1,0:T(8,128)(2,1)}) custom-call(bf16[512,512]{1,0:T(8,128)(2,1)S(1)} %copy-done.2, bf16[2560,512]{1,0:T(8,128)(2,1)} %get-tuple-element.24.ngrad_ref, bf16[2560,512]{1,0:T(8,128)(2,1)} %get-tuple-element.25.bslope_ref, bf16[2560,512]{1,0:T(8,128)(2,1)} %get-tuple-element.26.hidden_ref), custom_call_target="tpu_custom_call" | custom-call | tf_op jit(solution)/shard_map/source/pallas_call | solution.py:389
  133.3 4.8 %all-to-all-start.4 = ((bf16[32,16,512]{2,1,0:T(8,128)(2,1)}), bf16[32,16,512]{2,1,0:T(8,128)(2,1)}, u32[]{:S(2)}, u32[]{:S(2)}) async-start(bf16[32,16,512]{2,1,0:T(8,128)(2,1)} %bitcast.14), calls=%async_computation.4 | async-start | bytes 1048576 | tf_op jit(solution)/shard_map/all_to_all | solution.py:272
  140.7 9.8 %channels.1 = (bf16[227,512]{1,0:T(8,128)(2,1)S(1)}, bf16[4,227,512]{2,1,0:T(8,128)(2,1)S(1)}, bf16[227,512]{1,0:T(8,128)(2,1)S(1)}) custom-call(s32[2560,1]{1,0:T(8,128)S(1)} %reshape.71.index_ref, bf16[512,512]{1,0:T(8,128)(2,1)S(1)} %copy-done.4, bf16[227,512]{1,0:T(8,128)(2,1)S(1)} %copy-done.8, bf16[2560,512]{1,0:T(8,128)(2,1)S(1)} %copy-done.1, ...), custom_call_target="tpu_custom_call" | custom-call | tf_op jit(solution)/shard_map/channels/pallas_call | solution.py:403
  150.6 3.6 %collective-permute-start.6 = (bf16[227,512]{1,0:T(8,128)(2,1)S(1)}, bf16[227,512]{1,0:T(8,128)(2,1)S(1)}, u32[]{:S(2)}, u32[]{:S(2)}) collective-permute-start(bf16[227,512]{1,0:T(8,128)(2,1)S(1)} %get-tuple-element.30), channel_id=1, source_target_pairs={{0,4},{4,8},{8,12},{12,16},{16,20},{20,24},{24,28},{28,32},{32,36}... | collective-permute-start | bytes 697352 | tf_op jit(solution)/shard_map/ppermute | solution.py:249
  157.9 9.5 %all-to-all-start.8 = ((bf16[8,16,512]{2,1,0:T(8,128)(2,1)}), bf16[8,16,512]{2,1,0:T(8,128)(2,1)S(1)}, u32[]{:S(2)}, u32[]{:S(2)}) async-start(bf16[8,16,512]{2,1,0:T(8,128)(2,1)} %broadcast_in_dim.31), calls=%async_computation.8 | async-start | bytes 262144 | tf_op jit(solution)/shard_map/all_to_all | solution.py:242
  168.6 6.8 %all-to-all-done.8 = bf16[8,16,512]{2,1,0:T(8,128)(2,1)S(1)} async-done(((bf16[8,16,512]{2,1,0:T(8,128)(2,1)}), bf16[8,16,512]{2,1,0:T(8,128)(2,1)S(1)}, u32[]{:S(2)}, u32[]{:S(2)}) %all-to-all-start.8) | async-done | bytes 131104 | tf_op jit(solution)/shard_map/all_to_all | solution.py:242
  176.1 3.4 %all-to-all-start.5 = ((bf16[8,16,512]{2,1,0:T(8,128)(2,1)}), bf16[8,16,512]{2,1,0:T(8,128)(2,1)S(1)}, u32[]{:S(2)}, u32[]{:S(2)}) async-start(bf16[8,16,512]{2,1,0:T(8,128)(2,1)} %broadcast_in_dim.29), calls=%async_computation.5 | async-start | bytes 262144 | tf_op jit(solution)/shard_map/all_to_all | solution.py:242
  180.6 6.6 %all-to-all-done.5 = bf16[8,16,512]{2,1,0:T(8,128)(2,1)S(1)} async-done(((bf16[8,16,512]{2,1,0:T(8,128)(2,1)}), bf16[8,16,512]{2,1,0:T(8,128)(2,1)S(1)}, u32[]{:S(2)}, u32[]{:S(2)}) %all-to-all-start.5) | async-done | bytes 131104 | tf_op jit(solution)/shard_map/all_to_all | solution.py:242
  187.3 3.9 %all-to-all-start.3 = ((bf16[4,227,512]{2,1,0:T(8,128)(2,1)}), bf16[4,227,512]{2,1,0:T(8,128)(2,1)S(1)}, u32[]{:S(2)}, u32[]{:S(2)}) async-start(bf16[4,227,512]{2,1,0:T(8,128)(2,1)} %pad_maximum_fusion), calls=%async_computation.3 | async-start | bytes 1900544 | tf_op jit(solution)/shard_map/all_to_all | solution.py:435
  191.3 9.2 %all-to-all-done.3 = bf16[4,227,512]{2,1,0:T(8,128)(2,1)S(1)} async-done(((bf16[4,227,512]{2,1,0:T(8,128)(2,1)}), bf16[4,227,512]{2,1,0:T(8,128)(2,1)S(1)}, u32[]{:S(2)}, u32[]{:S(2)}) %all-to-all-start.3) | async-done | bytes 929824 | tf_op jit(solution)/shard_map/all_to_all | solution.py:435
  201.3 11.5 %all-to-all-start.9 = ((bf16[32,16,512]{2,1,0:T(8,128)(2,1)}), bf16[32,16,512]{2,1,0:T(8,128)(2,1)S(1)}, u32[]{:S(2)}, u32[]{:S(2)}) async-start(bf16[32,16,512]{2,1,0:T(8,128)(2,1)} %broadcast_in_dim.64), calls=%async_computation.9 | async-start | bytes 1048576 | tf_op jit(solution)/shard_map/all_to_all | solution.py:242
  212.9 11.4 %all-to-all-done.9 = bf16[32,16,512]{2,1,0:T(8,128)(2,1)S(1)} async-done(((bf16[32,16,512]{2,1,0:T(8,128)(2,1)}), bf16[32,16,512]{2,1,0:T(8,128)(2,1)S(1)}, u32[]{:S(2)}, u32[]{:S(2)}) %all-to-all-start.9) | async-done | bytes 524320 | tf_op jit(solution)/shard_map/all_to_all | solution.py:242
  225.2 4.3 %all-to-all-start.6 = ((bf16[32,16,512]{2,1,0:T(8,128)(2,1)}), bf16[32,16,512]{2,1,0:T(8,128)(2,1)S(1)}, u32[]{:S(2)}, u32[]{:S(2)}) async-start(bf16[32,16,512]{2,1,0:T(8,128)(2,1)} %broadcast_in_dim.30), calls=%async_computation.6 | async-start | bytes 1048576 | tf_op jit(solution)/shard_map/all_to_all | solution.py:242
  231.6 9.3 %all-to-all-done.6 = bf16[32,16,512]{2,1,0:T(8,128)(2,1)S(1)} async-done(((bf16[32,16,512]{2,1,0:T(8,128)(2,1)}), bf16[32,16,512]{2,1,0:T(8,128)(2,1)S(1)}, u32[]{:S(2)}, u32[]{:S(2)}) %all-to-all-start.6) | async-done | bytes 524320 | tf_op jit(solution)/shard_map/all_to_all | solution.py:242
  (90 shorter events, 60.5 us)
Async XLA Ops:
  0.6 37.4 %copy-start.18 = (s32[64,40]{0,1:T(8,128)S(1)}, s32[64,40]{0,1:T(8,128)}, u32[]{:S(2)}) copy-start(s32[64,40]{0,1:T(8,128)} %param.19) | copy-start | bytes 30724
  0.6 49.8 %copy-start.2 = (bf16[512,512]{1,0:T(8,128)(2,1)S(1)}, bf16[512,512]{1,0:T(8,128)(2,1)}, u32[]{:S(2)}) copy-start(bf16[512,512]{1,0:T(8,128)(2,1)} %edge_ref.3) | copy-start | bytes 1572868
  0.7 49.8 %copy-start.3 = (bf16[512,512]{1,0:T(8,128)(2,1)S(1)}, bf16[512,512]{1,0:T(8,128)(2,1)}, u32[]{:S(2)}) copy-start(bf16[512,512]{1,0:T(8,128)(2,1)} %src_ref.3) | copy-start | bytes 1572868
  15.4 34.3 %collective-permute-start.1 = (bf16[227,512]{1,0:T(8,128)(2,1)}, bf16[227,512]{1,0:T(8,128)(2,1)S(1)}, u32[]{:S(2)}, u32[]{:S(2)}) collective-permute-start(bf16[227,512]{1,0:T(8,128)(2,1)} %get-tuple-element.36), channel_id=1, source_target_pairs={{4,0},{8,4},{12,8},{16,12},{20,16},{24,20},{28,24},{32,28},{36,32}... | collective-permute-start | bytes 697352 | tf_op jit(solution)/shard_map/ppermute | solution.py:254
  21.3 29.2 %collective-permute-start = (bf16[227,512]{1,0:T(8,128)(2,1)}, bf16[227,512]{1,0:T(8,128)(2,1)}, u32[]{:S(2)}, u32[]{:S(2)}) collective-permute-start(bf16[227,512]{1,0:T(8,128)(2,1)} %get-tuple-element.37), channel_id=1, source_target_pairs={{0,4},{4,8},{8,12},{12,16},{16,20},{20,24},{24,28},{28,32},{32,36}... | collective-permute-start | bytes 697352 | tf_op jit(solution)/shard_map/ppermute | solution.py:249
  24.6 7.9 %all-to-all-start.2 = ((s32[4,1,384]{2,1,0:T(1,128)}), s32[4,1,384]{2,1,0:T(1,128)S(1)}, u32[]{:S(2)}, u32[]{:S(2)}) async-start(s32[4,1,384]{2,1,0:T(1,128)} %reshape.73), calls=%async_computation.2 | async-start | bytes 12288 | tf_op jit(solution)/shard_map/all_to_all | solution.py:242
  34.0 40.6 %all-to-all-start.1 = ((bf16[4,64,512]{2,1,0:T(8,128)(2,1)}), bf16[4,64,512]{2,1,0:T(8,128)(2,1)}, u32[]{:S(2)}, u32[]{:S(2)}) async-start(bf16[4,64,512]{2,1,0:T(8,128)(2,1)} %broadcast_in_dim.23), calls=%async_computation.1 | async-start | bytes 524288 | tf_op jit(solution)/shard_map/all_to_all | solution.py:242
  45.9 37.0 %collective-permute-start.5 = (s32[256,6]{0,1:T(8,128)S(1)}, s32[256,6]{0,1:T(8,128)}, u32[]{:S(2)}, u32[]{:S(2)}) collective-permute-start(s32[256,6]{0,1:T(8,128)S(1)} %reshape.54), channel_id=1, source_target_pairs={{0,4},{1,5},{4,8},{5,9},{6,2},{7,3},{8,12},{9,13},{10,6},{11,7},{1... | collective-permute-start | bytes 18440 | tf_op jit(solution)/shard_map/ppermute | solution.py:266
  54.3 25.5 %copy-start.19 = (s32[64,6]{0,1:T(8,128)S(1)}, s32[64,6]{0,1:T(8,128)}, u32[]{:S(2)}) copy-start(s32[64,6]{0,1:T(8,128)} %param.20) | copy-start | bytes 4612
  74.6 22.0 %copy-start.14 = (bf16[64,512]{1,0:T(8,128)(2,1)S(1)}, bf16[64,512]{1,0:T(8,128)(2,1)}, u32[]{:S(2)}) copy-start(bf16[64,512]{1,0:T(8,128)(2,1)} %cot_ref.1) | copy-start | bytes 196612
  75.4 11.6 %all-to-all-start = ((bf16[4,64,512]{2,1,0:T(8,128)(2,1)}), bf16[4,64,512]{2,1,0:T(8,128)(2,1)}, u32[]{:S(2)}, u32[]{:S(2)}) async-start(bf16[4,64,512]{2,1,0:T(8,128)(2,1)} %broadcast_in_dim.22), calls=%async_computation | async-start | bytes 524288 | tf_op jit(solution)/shard_map/all_to_all | solution.py:242
  80.6 12.4 %collective-permute-start.4 = (bf16[256,512]{1,0:T(8,128)(2,1)}, bf16[256,512]{1,0:T(8,128)(2,1)}, u32[]{:S(2)}, u32[]{:S(2)}) collective-permute-start(bf16[256,512]{1,0:T(8,128)(2,1)} %bitcast.6), channel_id=1, source_target_pairs={{0,4},{1,5},{4,8},{5,9},{6,2},{7,3},{8,12},{9,13},{10,6},{11,7},{1... | collective-permute-start | bytes 786440 | tf_op jit(solution)/shard_map/ppermute | solution.py:266
  87.0 9.7 %collective-permute-start.2 = (bf16[256,512]{1,0:T(8,128)(2,1)}, bf16[256,512]{1,0:T(8,128)(2,1)S(1)}, u32[]{:S(2)}, u32[]{:S(2)}) collective-permute-start(bf16[256,512]{1,0:T(8,128)(2,1)} %bitcast.4.band_ref), channel_id=1, source_target_pairs={{0,4},{1,5},{4,8},{5,9},{6,2},{7,3},{8,12},{9,13},{10,6},{11,7},{1... | collective-permute-start | bytes 786440 | tf_op jit(solution)/shard_map/ppermute | solution.py:266
  91.1 5.6 %collective-permute-start.3 = (bf16[64,512]{1,0:T(8,128)(2,1)S(1)}, bf16[64,512]{1,0:T(8,128)(2,1)S(1)}, u32[]{:S(2)}, u32[]{:S(2)}) collective-permute-start(bf16[64,512]{1,0:T(8,128)(2,1)S(1)} %fusion.4), channel_id=1, source_target_pairs={{2,6},{3,7},{4,0},{5,1},{6,10},{7,11},{8,4},{9,5},{10,14},{11,15},... | collective-permute-start | bytes 196616 | tf_op jit(solution)/shard_map/ppermute | solution.py:266
  114.8 18.5 %all-to-all-start.7 = ((bf16[32,16,512]{2,1,0:T(8,128)(2,1)}), bf16[32,16,512]{2,1,0:T(8,128)(2,1)}, u32[]{:S(2)}, u32[]{:S(2)}) async-start(bf16[32,16,512]{2,1,0:T(8,128)(2,1)} %bitcast.41), calls=%async_computation.7 | async-start | bytes 1048576 | tf_op jit(solution)/shard_map/all_to_all | solution.py:272
  121.8 16.2 %copy-start.4 = (bf16[512,512]{1,0:T(8,128)(2,1)S(1)}, bf16[512,512]{1,0:T(8,128)(2,1)}, u32[]{:S(2)}) copy-start(bf16[512,512]{1,0:T(8,128)(2,1)} %src_ref.3) | copy-start | bytes 1572868
  133.3 24.0 %all-to-all-start.4 = ((bf16[32,16,512]{2,1,0:T(8,128)(2,1)}), bf16[32,16,512]{2,1,0:T(8,128)(2,1)}, u32[]{:S(2)}, u32[]{:S(2)}) async-start(bf16[32,16,512]{2,1,0:T(8,128)(2,1)} %bitcast.14), calls=%async_computation.4 | async-start | bytes 1048576 | tf_op jit(solution)/shard_map/all_to_all | solution.py:272
  150.6 28.9 %collective-permute-start.6 = (bf16[227,512]{1,0:T(8,128)(2,1)S(1)}, bf16[227,512]{1,0:T(8,128)(2,1)S(1)}, u32[]{:S(2)}, u32[]{:S(2)}) collective-permute-start(bf16[227,512]{1,0:T(8,128)(2,1)S(1)} %get-tuple-element.30), channel_id=1, source_target_pairs={{0,4},{4,8},{8,12},{12,16},{16,20},{20,24},{24,28},{28,32},{32,36}... | collective-permute-start | bytes 697352 | tf_op jit(solution)/shard_map/ppermute | solution.py:249
  154.2 25.3 %collective-permute-start.7 = (bf16[227,512]{1,0:T(8,128)(2,1)S(1)}, bf16[227,512]{1,0:T(8,128)(2,1)S(1)}, u32[]{:S(2)}, u32[]{:S(2)}) collective-permute-start(bf16[227,512]{1,0:T(8,128)(2,1)S(1)} %get-tuple-element.31), channel_id=1, source_target_pairs={{4,0},{8,4},{12,8},{16,12},{20,16},{24,20},{28,24},{32,28},{36,32}... | collective-permute-start | bytes 697352 | tf_op jit(solution)/shard_map/ppermute | solution.py:254
  157.9 17.5 %all-to-all-start.8 = ((bf16[8,16,512]{2,1,0:T(8,128)(2,1)}), bf16[8,16,512]{2,1,0:T(8,128)(2,1)S(1)}, u32[]{:S(2)}, u32[]{:S(2)}) async-start(bf16[8,16,512]{2,1,0:T(8,128)(2,1)} %broadcast_in_dim.31), calls=%async_computation.8 | async-start | bytes 262144 | tf_op jit(solution)/shard_map/all_to_all | solution.py:242
  176.1 11.2 %all-to-all-start.5 = ((bf16[8,16,512]{2,1,0:T(8,128)(2,1)}), bf16[8,16,512]{2,1,0:T(8,128)(2,1)S(1)}, u32[]{:S(2)}, u32[]{:S(2)}) async-start(bf16[8,16,512]{2,1,0:T(8,128)(2,1)} %broadcast_in_dim.29), calls=%async_computation.5 | async-start | bytes 262144 | tf_op jit(solution)/shard_map/all_to_all | solution.py:242
  187.3 13.2 %all-to-all-start.3 = ((bf16[4,227,512]{2,1,0:T(8,128)(2,1)}), bf16[4,227,512]{2,1,0:T(8,128)(2,1)S(1)}, u32[]{:S(2)}, u32[]{:S(2)}) async-start(bf16[4,227,512]{2,1,0:T(8,128)(2,1)} %pad_maximum_fusion), calls=%async_computation.3 | async-start | bytes 1900544 | tf_op jit(solution)/shard_map/all_to_all | solution.py:435
  201.3 23.0 %all-to-all-start.9 = ((bf16[32,16,512]{2,1,0:T(8,128)(2,1)}), bf16[32,16,512]{2,1,0:T(8,128)(2,1)S(1)}, u32[]{:S(2)}, u32[]{:S(2)}) async-start(bf16[32,16,512]{2,1,0:T(8,128)(2,1)} %broadcast_in_dim.64), calls=%async_computation.9 | async-start | bytes 1048576 | tf_op jit(solution)/shard_map/all_to_all | solution.py:242
  225.2 15.7 %all-to-all-start.6 = ((bf16[32,16,512]{2,1,0:T(8,128)(2,1)}), bf16[32,16,512]{2,1,0:T(8,128)(2,1)S(1)}, u32[]{:S(2)}, u32[]{:S(2)}) async-start(bf16[32,16,512]{2,1,0:T(8,128)(2,1)} %broadcast_in_dim.30), calls=%async_computation.6 | async-start | bytes 1048576 | tf_op jit(solution)/shard_map/all_to_all | solution.py:242
  (14 other events, 14.9 us)

commit v2 on v1

v2 whole, which is shorter than its diff:
```python
import functools
import math

import jax
import jax.numpy as jnp
from jax import lax
from jax.experimental import pallas as pl
from jax.experimental.pallas import tpu as pltpu
from jax.sharding import Mesh
from jax.sharding import PartitionSpec as P

BAND = ("band_0", "band_1", "band_2")
ALL = ("band_0", "band_1", "band_2", "sub")
NEAR = ("band_1", "band_2", "sub")
FAR = "band_0"
SUBS = 4

EPSILON = 1e-05
BF = jnp.bfloat16
F32 = jnp.float32
VMEM = 60 * 1024 * 1024


def sigmoid(value):
    return 0.5 * jnp.tanh(0.5 * value) + 0.5


def silu_and_slope(value):
    sigma = sigmoid(value)
    active = value * sigma
    return active, sigma + active * (1.0 - sigma)


def dot(left, right):
    return jnp.dot(left, right, preferred_element_type=F32)


def dot_t(left, right):
    return lax.dot_general(left, right, (((1,), (1,)), ((), ())), preferred_element_type=F32)


def t_dot(left, right):
    return lax.dot_general(left, right, (((0,), (0,)), ((), ())), preferred_element_type=F32)


def selection(column, width):
    lanes = lax.broadcasted_iota(jnp.int32, (column.shape[0], width), 1)
    return jnp.where(column == lanes, 1.0, 0.0).astype(BF)


def selection_t(row, height):
    lines = lax.broadcasted_iota(jnp.int32, (height, row.shape[1]), 0)
    return jnp.where(row == lines, 1.0, 0.0).astype(BF)


def padded_rows(ref, scratch):
    rows = ref.shape[0]
    scratch[...] = jnp.zeros_like(scratch)
    scratch[:rows, :] = ref[...]
    return scratch[...]


def forward_kernel(
    scale,
    sub_ref, index_ref, own_ref, one_ref, two_ref, three_ref, low_ref, high_ref,
    mesh_ref, embed_ref, src_ref, dst_ref, edge_ref,
    hidden_ref, hslope_ref, active_ref, bslope_ref, normed_ref, inverse_ref, mesh_out_ref,
    table, pad, embed, dest, total,
):
    step = pl.program_id(0)
    sources = (own_ref, one_ref, two_ref, three_ref, low_ref, high_ref)
    nodes = low_ref.shape[1]
    rows = mesh_ref.shape[0]
    sub = sub_ref[0]
    bases = [(lax.rem(sub + SUBS - k, SUBS) + 1) * nodes for k in range(SUBS)]
    bases += [0, (SUBS + 1) * nodes]

    @pl.when(step == 0)
    def _():
        for block, source in enumerate(sources):
            table[block * nodes : (block + 1) * nodes, :] = padded_rows(source, pad).T
        embed[...] = padded_rows(embed_ref, pad)
        dest[...] = dot(mesh_ref[...], dst_ref[...])
        total[...] = jnp.zeros_like(total)

    column = index_ref[...]
    edges = column.shape[0]
    picked = jnp.zeros((edges, table.shape[1]), F32)
    for block, base in enumerate(bases):
        part = table[block * nodes : (block + 1) * nodes, :]
        picked += dot(selection(column - base, nodes), part)
    hidden, hslope = silu_and_slope(dot(picked.astype(BF), embed[...]))
    hidden = hidden.astype(BF)
    hidden_ref[...] = hidden
    hslope_ref[...] = hslope.astype(BF)
    projected = dot(hidden, src_ref[...]).astype(BF).astype(F32)
    before = (projected.reshape(-1, rows, projected.shape[1]) + dest[...][None]).reshape(projected.shape)
    active, bslope = silu_and_slope(before)
    active = active.astype(BF)
    active_ref[...] = active
    bslope_ref[...] = bslope.astype(BF)
    out = dot(active, edge_ref[...])
    centred = out - jnp.mean(out, axis=-1, keepdims=True)
    inverse = lax.rsqrt(jnp.mean(centred * centred, axis=-1, keepdims=True) + EPSILON)
    normed = centred * inverse
    normed_ref[...] = normed.astype(BF)
    inverse_ref[...] = inverse
    total[...] += jnp.sum(normed.reshape(-1, rows, normed.shape[1]), axis=0)

    @pl.when(step == pl.num_programs(0) - 1)
    def _():
        mesh_out_ref[...] = (mesh_ref[...].astype(F32) + total[...] * scale).astype(BF)


def mesh_kernel(
    mesh_scale, scale, count,
    sub_ref, band_ref, far_ref, side_ref, pay_ref, far_pay_ref, proc_ref, recv_ref, edge_ref,
    active_ref, normed_ref, inverse_ref, bslope_ref, hidden_ref,
    out_ref, bgrad_ref, wgrad_ref,
    receiver_all, cots, columns, lines, query_grad, upper_ref, edge_total, src_total,
):
    step = pl.program_id(0)
    rows, latent = side_ref.shape
    wide = band_ref.shape[0]

    @pl.when(step == 0)
    def _():
        sub = sub_ref[0]
        lower = sub < SUBS // 2
        proc = proc_ref[...]
        recv = recv_ref[...]
        own = band_ref[:rows, :]
        window = jnp.concatenate([band_ref[...], far_ref[...], side_ref[...]], axis=0)
        query = dot(window, proc).astype(BF)
        receiver_all[:wide, :] = dot(band_ref[...], recv)
        receiver_all[wide:, :] = dot(far_ref[...], recv)
        receiver = receiver_all[:rows, :]

        tail = pay_ref[:, latent:].astype(F32).astype(jnp.int32)
        far_tail = far_pay_ref[:, latent:].astype(F32).astype(jnp.int32)
        turn = tail.shape[1] // 2
        block, line = tail[:, :turn], tail[:, turn:]
        far_block, far_line = far_tail[:, :turn], far_tail[:, turn:]
        far_wanted = jnp.where(lower, SUBS + 1 + sub, sub - SUBS + 1)
        columns[:wide, :turn] = (block - (sub + 1)) * rows + line
        columns[wide:, :turn] = (far_block - far_wanted) * rows + far_line
        own_block, own_line = block[:rows], line[:rows]
        inside = lax.rem(sub + SUBS + 1 - own_block, SUBS) * rows
        below = jnp.where(lower, wide + lax.rem(sub + 1, SUBS) * rows, 2 * wide)
        above = jnp.where(lower, 2 * wide, wide + sub * rows)
        place = jnp.where(own_block == 0, below, jnp.where(own_block == SUBS + 1, above, inside))
        place = place + own_line
        columns[:, turn:] = jnp.zeros_like(columns[:, turn:])
        lines[...] = columns[...].T
        cots[:wide, :] = pay_ref[:, :latent].astype(F32) * mesh_scale
        cots[wide:, :] = far_pay_ref[:, :latent].astype(F32) * mesh_scale

        summed = jnp.zeros((rows, latent), F32)
        slopes = jnp.zeros((rows, latent), F32)
        for j in range(count):
            sent = dot(selection(place[:, j : j + 1], window.shape[0]), query)
            active, slope = silu_and_slope(sent + receiver)
            summed += active
            slopes += slope
        out_ref[...] = (own.astype(F32) + summed * mesh_scale).astype(BF)
        receiver_grad = cots[:rows, :] * slopes

        own_query = query[:rows]
        query_grad[...] = jnp.zeros_like(query_grad)
        lanes = lax.broadcasted_iota(jnp.int32, columns.shape, 1)

        def one(j, carry):
            column = jnp.sum(jnp.where(lanes == j, columns[...], 0), axis=1, keepdims=True)
            value = dot(selection(column, rows), own_query) + receiver_all[...]
            _, slopes = silu_and_slope(value)
            slopes = (cots[...] * slopes).astype(BF)
            query_grad[...] += dot(selection_t(lines[pl.ds(j, 1), :], rows), slopes)
            return carry

        lax.fori_loop(0, count, one, 0)
        mesh_grad = pay_ref[:rows, :latent].astype(F32) + dot_t(query_grad[...].astype(BF), proc)
        mesh_grad = mesh_grad + dot_t(receiver_grad.astype(BF), recv)
        upper_ref[...] = mesh_grad * scale
        edge_total[...] = jnp.zeros_like(edge_total)
        src_total[...] = jnp.zeros_like(src_total)

    upper = upper_ref[...]
    centred = upper - jnp.mean(upper, axis=-1, keepdims=True)
    normed = normed_ref[...].astype(F32).reshape(-1, rows, latent)
    inverse = inverse_ref[...].reshape(-1, rows, 1)
    along = jnp.mean(upper[None] * normed, axis=-1, keepdims=True)
    ngrad = ((centred[None] - normed * along) * inverse).reshape(-1, latent).astype(BF)
    edge_total[...] += t_dot(active_ref[...], ngrad)
    bgrad = (dot_t(ngrad, edge_ref[...]) * bslope_ref[...].astype(F32)).astype(BF)
    bgrad_ref[...] = bgrad
    src_total[...] += t_dot(hidden_ref[...], bgrad)

    @pl.when(step == pl.num_programs(0) - 1)
    def _():
        wgrad_ref[:latent, :] = edge_total[...].astype(BF)
        wgrad_ref[latent:, :] = src_total[...].astype(BF)


def grid_kernel(
    sub_ref, index_ref, src_ref, embed_ref, bgrad_ref, hslope_ref,
    own_ref, one_ref, two_ref, three_ref, low_ref, high_ref,
    pad, total,
):
    step = pl.program_id(0)
    channels, nodes = low_ref.shape
    targets = (own_ref, one_ref, two_ref, three_ref, low_ref, high_ref)
    sub = sub_ref[0]
    bases = [(lax.rem(sub + k, SUBS) + 1) * nodes for k in range(SUBS)]
    bases += [0, (SUBS + 1) * nodes]

    @pl.when(step == 0)
    def _():
        padded_rows(embed_ref, pad)
        total[...] = jnp.zeros_like(total)

    hgrad = (dot_t(bgrad_ref[...], src_ref[...]) * hslope_ref[...].astype(F32)).astype(BF)
    ggrad = dot_t(pad[...], hgrad).astype(BF)
    column = index_ref[...]
    for block, base in enumerate(bases):
        total[block] += dot(ggrad, selection(column - base, nodes))

    @pl.when(step == pl.num_programs(0) - 1)
    def _():
        for block, target in enumerate(targets):
            target[...] = total[block][:channels].astype(BF)


def whole(shape):
    return pl.BlockSpec(shape, lambda i, n=len(shape): (0,) * n)


def tiled(edges, width):
    return pl.BlockSpec((edges, width), lambda i: (i, 0))


def scalar():
    return pl.BlockSpec(memory_space=pltpu.SMEM)


def params():
    return pltpu.CompilerParams(dimension_semantics=("arbitrary",), vmem_limit_bytes=VMEM)


def from_everyone(shard, axis):
    devices = lax.axis_size(axis)
    return lax.all_to_all(
        jnp.broadcast_to(shard[None], (devices, *shard.shape)), axis, 0, 0, tiled=True
    )


def bands_up(value):
    count = lax.axis_size(BAND)
    return lax.ppermute(value, BAND, [(i, i + 1) for i in range(count - 1)])


def bands_down(value):
    count = lax.axis_size(BAND)
    return lax.ppermute(value, BAND, [(i + 1, i) for i in range(count - 1)])


def outwards(value, near):
    bands, subs = lax.axis_size(BAND), lax.axis_size("sub")
    pairs = []
    for band in range(bands):
        for sub in range(subs):
            up = (sub < subs // 2) == near
            to = band + 1 if up else band - 1
            if 0 <= to < bands:
                pairs.append((band * subs + sub, to * subs + sub))
    return lax.ppermute(value, ALL, pairs)


def along_sub(value, steps):
    count = lax.axis_size("sub")
    return lax.ppermute(value, "sub", [(i, (i + steps) % count) for i in range(count)])


def weight_sum(part):
    near = lax.axis_size(NEAR)
    rows, width = part.shape
    parts = lax.all_to_all(part.reshape(near, rows // near, width), NEAR, 0, 0, tiled=True)
    mine = jnp.sum(parts.astype(F32), axis=0).astype(BF)
    mine = jnp.sum(from_everyone(mine, FAR).astype(F32), axis=0).astype(BF)
    return from_everyone(mine, NEAR).reshape(rows, width)


def body(
    grid_x, mesh_in, w_embed, w_src, w_dst, w_edge, w_proc, w_recv, g2m_src, mesh_src, cotangent
):
    channels, nodes = grid_x.shape
    latent = w_src.shape[0]
    rows, enc_count = g2m_src.shape
    mesh_count = mesh_src.shape[1]
    band = lax.axis_index(BAND)
    sub = lax.axis_index("sub")
    sub_scalar = sub.astype(jnp.int32).reshape(1)
    wide = -(-channels // 128) * 128
    edges = rows * enc_count
    steps = 4
    tile = edges // steps
    width = SUBS * rows
    scale = 1.0 / math.sqrt(enc_count)
    mesh_scale = 1.0 / math.sqrt(mesh_count)

    grid = [grid_x] + [along_sub(grid_x, k) for k in range(1, SUBS)]
    last = lax.select_n(lax.rem(sub + 1, SUBS), *grid)
    first = lax.select_n(sub, *grid)
    grid_low = bands_up(last)
    grid_high = bands_down(first)
    grid_local = (g2m_src - (band * (nodes * SUBS) - nodes)).T.reshape(edges, 1)

    place = mesh_src - (band * width - rows)
    half = 64
    spare = jnp.zeros((rows, half - mesh_count), BF)
    pay = jnp.concatenate(
        [cotangent, (place // rows).astype(BF), spare, (place % rows).astype(BF), spare], axis=1
    )
    pay, _ = lax.optimization_barrier((pay, last))
    pay = jnp.concatenate([pay] + [along_sub(pay, k) for k in range(1, SUBS)])
    far_pay = outwards(pay, True)

    hidden, hslope, active, bslope, normed, inverse, hidden_mesh = pl.pallas_call(
        functools.partial(forward_kernel, scale),
        grid=(steps,),
        in_specs=[scalar(), tiled(tile, 1)]
        + [whole((channels, nodes))] * (SUBS + 2)
        + [
            whole((rows, latent)),
            whole((channels, latent)),
            whole((latent, latent)),
            whole((latent, latent)),
            whole((latent, latent)),
        ],
        out_specs=[tiled(tile, latent)] * 5 + [tiled(tile, 1), whole((rows, latent))],
        out_shape=[jax.ShapeDtypeStruct((edges, latent), BF)] * 5
        + [jax.ShapeDtypeStruct((edges, 1), F32), jax.ShapeDtypeStruct((rows, latent), BF)],
        scratch_shapes=[
            pltpu.VMEM(((SUBS + 2) * nodes, wide), BF),
            pltpu.VMEM((wide, nodes), BF),
            pltpu.VMEM((wide, latent), BF),
            pltpu.VMEM((rows, latent), F32),
            pltpu.VMEM((rows, latent), F32),
        ],
        compiler_params=params(),
        name="encode",
    )(sub_scalar, grid_local, *grid, grid_low, grid_high, mesh_in, w_embed, w_src, w_dst, w_edge)

    mesh_band = jnp.concatenate([hidden_mesh] + [along_sub(hidden_mesh, k) for k in range(1, SUBS)])
    mesh_far = outwards(mesh_band, True)
    at = jnp.where(sub < SUBS // 2, sub, lax.rem(sub + 1, SUBS)) * rows
    mesh_side = outwards(lax.dynamic_slice_in_dim(mesh_band, at, rows), False)

    mesh_out, bgrad, part = pl.pallas_call(
        functools.partial(mesh_kernel, mesh_scale, scale, mesh_count),
        grid=(steps,),
        in_specs=[
            scalar(),
            whole((width, latent)),
            whole((width, latent)),
            whole((rows, latent)),
            whole((width, latent + 2 * half)),
            whole((width, latent + 2 * half)),
            whole((latent, latent)),
            whole((latent, latent)),
            whole((latent, latent)),
            tiled(tile, latent),
            tiled(tile, latent),
            tiled(tile, 1),
            tiled(tile, latent),
            tiled(tile, latent),
        ],
        out_specs=[whole((rows, latent)), tiled(tile, latent), whole((2 * latent, latent))],
        out_shape=[
            jax.ShapeDtypeStruct((rows, latent), BF),
            jax.ShapeDtypeStruct((edges, latent), BF),
            jax.ShapeDtypeStruct((2 * latent, latent), BF),
        ],
        scratch_shapes=[
            pltpu.VMEM((2 * width, latent), F32),
            pltpu.VMEM((2 * width, latent), F32),
            pltpu.VMEM((2 * width, 2 * half), jnp.int32),
            pltpu.VMEM((2 * half, 2 * width), jnp.int32),
            pltpu.VMEM((rows, latent), F32),
            pltpu.VMEM((rows, latent), F32),
            pltpu.VMEM((latent, latent), F32),
            pltpu.VMEM((latent, latent), F32),
        ],
        compiler_params=params(),
        name="process",
    )(
        sub_scalar, mesh_band, mesh_far, mesh_side, pay, far_pay, w_proc, w_recv, w_edge,
        active, normed, inverse, bslope, hidden,
    )

    *parts, part_low, part_high = pl.pallas_call(
        grid_kernel,
        grid=(steps,),
        in_specs=[
            scalar(),
            tiled(tile, 1),
            whole((latent, latent)),
            whole((channels, latent)),
            tiled(tile, latent),
            tiled(tile, latent),
        ],
        out_specs=[whole((channels, nodes))] * (SUBS + 2),
        out_shape=[jax.ShapeDtypeStruct((channels, nodes), BF)] * (SUBS + 2),
        scratch_shapes=[pltpu.VMEM((wide, latent), BF), pltpu.VMEM((SUBS + 2, wide, nodes), F32)],
        compiler_params=params(),
        name="channels",
    )(sub_scalar, grid_local, w_src, w_embed, bgrad, hslope)

    weights = weight_sum(part)
    from_above = bands_down(part_low)
    from_below = bands_up(part_high)
    arrived = None
    for k in range(SUBS):
        block = lax.rem(sub + k, SUBS)
        value = parts[k].astype(F32)
        value += jnp.where(block == 0, from_below, jnp.zeros_like(from_below)).astype(F32)
        value += jnp.where(block == SUBS - 1, from_above, jnp.zeros_like(from_above)).astype(F32)
        if k == 0:
            arrived = value
        else:
            arrived += along_sub(value.astype(BF), k).astype(F32)
    src_grad, edge_grad = weights[latent:].astype(F32), weights[:latent].astype(F32)
    return (mesh_out, arrived, src_grad, edge_grad)


def solution(mesh):
    torus = Mesh(mesh.devices.reshape(8, 4, 2, mesh.shape["sub"]), ALL)
    return jax.shard_map(
        body,
        mesh=torus,
        in_specs=(
            P(None, ALL),
            P(ALL, None),
            P(),
            P(),
            P(),
            P(),
            P(),
            P(),
            P(ALL, None),
            P(ALL, None),
            P(ALL, None),
        ),
        out_specs=(P(ALL, None), P(None, ALL), P(), P()),
        check_vma=False,
    )
```

time: 244 us -> 187 us (0.77)
  starting transfers between devices: 81.2 us -> 48.2 us
  blocking collectives: 14 us -> 45.6 us
  waiting for transfers between devices: 54.5 us -> 23.2 us
  local copies, waits for them, and re-layouts: 30.4 us -> 7.72 us
  other arithmetic: 11.8 us -> 7.21 us
    all_to_all x0 -> x2, blocking collectives: none -> 45.6 us  [the longest x1 24.5 us: weight_sum(): lax.all_to_all(part.reshape(near, rows // near, width), NEAR, 0, 0, tiled...]
    all_to_all x7 -> x1, waiting for transfers between devices: 39.9 us -> 0.01 us  [from_everyone(): lax.all_to_all(jnp.broadcast_to(shard[None], (devices, *shard.shape)), ax...]
    all_to_all x7 -> x1, starting transfers between devices: 40.9 us -> 7.26 us  [from_everyone(): lax.all_to_all(jnp.broadcast_to(shard[None], (devices, *shard.shape)), ax...]
    ppermute x0 -> x12, starting transfers between devices: none -> 18.7 us  [along_sub(): lax.ppermute(value, 'sub', [(i, (i + steps) % count) for i in range(count)])]
    all_to_all x3 -> x0, starting transfers between devices: 15.8 us -> none  [the longest x2 11.8 us: weight_sum(): lax.all_to_all(part.reshape(near, rows // near, width), NEAR, 0, 0, tiled...]
    unnamed x43 -> x27, local copies, waits for them, and re-layouts: 17.6 us -> 3.2 us
    all_gather x1 -> x0, blocking collectives: 14 us -> none  [body(): grid_band = lax.all_gather(grid_x, 'sub', axis=0)]
    ppermute x0 -> x12, waiting for transfers between devices: none -> 13.2 us  [along_sub(): lax.ppermute(value, 'sub', [(i, (i + steps) % count) for i in range(count)])]
  transfers between devices with their start and end apart: 18 -> 20, of which waited for: 9 -> 12; matrix products, arithmetic and copies ran while one was open for 10% -> 5% of each run, Pallas kernels for 15% -> 18%
where the time goes in v2:
time: 187 us; the launch traced here: 183 us
  Pallas kernels  50.4 us (27%)
  starting transfers between devices  48.2 us (26%)
  blocking collectives  45.6 us (24%)
  waiting for transfers between devices  23.2 us (12%)
  local copies, waits for them, and re-layouts  7.72 us (4%)
  other arithmetic  7.21 us (4%)
    all_to_all x1, blocking collectives, weight_sum(): lax.all_to_all(part.reshape(near, rows // near, width), NEAR, 0, 0, tiled...  24.5 us
    all_to_all x1, blocking collectives, from_everyone(): lax.all_to_all(jnp.broadcast_to(shard[None], (devices, *shard.shape)), ax...  21.1 us
    pallas_call x1, Pallas kernels, body(): pl.pallas_call(functools.partial(forward_kernel, scale), grid=(steps,), i...  20.7 us
    ppermute x12, starting transfers between devices, along_sub(): lax.ppermute(value, 'sub', [(i, (i + steps) % count) for i in range(count)])  18.7 us
    pallas_call x1, Pallas kernels, body(): pl.pallas_call(functools.partial(mesh_kernel, mesh_scale, scale, mesh_cou...  17.9 us
    ppermute x12, waiting for transfers between devices, along_sub(): lax.ppermute(value, 'sub', [(i, (i + steps) % count) for i in range(count)])  13.2 us
    pallas_call x1, Pallas kernels, body(): pl.pallas_call(grid_kernel, grid=(steps,), in_specs=[scalar(), tiled(tile...  11.8 us
    ppermute x3, starting transfers between devices, outwards(): return lax.ppermute(value, ALL, pairs)  10.2 us
  transfers between devices with their start and end apart: 20, of which 12 were waited for; matrix products, arithmetic and copies ran while one was open for 5% of the time, Pallas kernels for 18%

profile of v2, /device:TPU:1, one launch (start us, length us, event | category | flops | bytes accessed | tf_op | source)
XLA Modules:
  0.0 183.2 jit_solution(3767713374543371335)
XLA Ops:
  0.6 2.1 %collective-permute-start = (bf16[227,512]{1,0:T(8,128)(2,1)}, bf16[227,512]{1,0:T(8,128)(2,1)S(1)}, u32[]{:S(2)}, u32[]{:S(2)}) collective-permute-start(bf16[227,512]{1,0:T(8,128)(2,1)} %own_ref.1), channel_id=1, source_target_pairs={{0,1},{1,2},{2,3},{3,0},{4,5},{5,6},{6,7},{7,4},{8,9},{9,10},{10,1... | collective-permute-start | bytes 697352 | tf_op jit(solution)/shard_map/ppermute | solution.py:280
  2.7 2.5 %collective-permute-start.1 = (bf16[227,512]{1,0:T(8,128)(2,1)}, bf16[227,512]{1,0:T(8,128)(2,1)S(1)}, u32[]{:S(2)}, u32[]{:S(2)}) collective-permute-start(bf16[227,512]{1,0:T(8,128)(2,1)} %own_ref.1), channel_id=1, source_target_pairs={{0,2},{1,3},{2,0},{3,1},{4,6},{5,7},{6,4},{7,5},{8,10},{9,11},{10,... | collective-permute-start | bytes 697352 | tf_op jit(solution)/shard_map/ppermute | solution.py:280
  7.1 2.3 %reshape.31.index_ref = s32[2560,1]{1,0:T(8,128)} reshape(s32[40,64]{1,0:T(8,128)S(1)} %subtract_bitcast_fusion) | data formatting | bytes 20480 | tf_op jit(solution)/shard_map/reshape | solution.py:315
  11.2 4.5 %collective-permute-done.1.two_ref = bf16[227,512]{1,0:T(8,128)(2,1)S(1)} collective-permute-done((bf16[227,512]{1,0:T(8,128)(2,1)}, bf16[227,512]{1,0:T(8,128)(2,1)S(1)}, u32[]{:S(2)}, u32[]{:S(2)}) %collective-permute-start.1) | collective-permute-done | bytes 232480 | tf_op jit(solution)/shard_map/ppermute | solution.py:280
  16.9 4.6 %collective-permute-start.3 = (bf16[227,512]{1,0:T(8,128)(2,1)S(1)}, bf16[227,512]{1,0:T(8,128)(2,1)S(1)}, u32[]{:S(2)}, u32[]{:S(2)}) collective-permute-start(bf16[227,512]{1,0:T(8,128)(2,1)S(1)} %get-tuple-element.41), channel_id=1, source_target_pairs={{0,4},{4,8},{8,12},{12,16},{16,20},{20,24},{24,28},{28,32},{32,36}... | collective-permute-start | bytes 697352 | tf_op jit(solution)/shard_map/ppermute | solution.py:258
  22.6 2.1 %collective-permute-start.11 = (bf16[64,640]{1,0:T(8,128)(2,1)S(1)}, bf16[64,640]{1,0:T(8,128)(2,1)S(1)}, u32[]{:S(2)}, u32[]{:S(2)}) collective-permute-start(bf16[64,640]{1,0:T(8,128)(2,1)S(1)} %concatenate.10), channel_id=1, source_target_pairs={{0,2},{1,3},{2,0},{3,1},{4,6},{5,7},{6,4},{7,5},{8,10},{9,11},{10,... | collective-permute-start | bytes 245768 | tf_op jit(solution)/shard_map/ppermute | solution.py:280
  28.5 4.1 %collective-permute-start.13 = (bf16[256,640]{1,0:T(8,128)(2,1)S(1)}, bf16[256,640]{1,0:T(8,128)(2,1)S(1)}, u32[]{:S(2)}, u32[]{:S(2)}) collective-permute-start(bf16[256,640]{1,0:T(8,128)(2,1)S(1)} %constant_dynamic-update-slice_fusion.4.pay_ref), channel_id=1, source_target_pairs={{0,4},{1,5},{4,8},{5,9},{6,2},{7,3},{8,12},{9,13},{10,6},{11,7},{1... | collective-permute-start | bytes 983048 | tf_op jit(solution)/shard_map/ppermute | solution.py:275
  34.1 20.7 %encode.1 = (bf16[2560,512]{1,0:T(8,128)(2,1)}, bf16[2560,512]{1,0:T(8,128)(2,1)}, bf16[2560,512]{1,0:T(8,128)(2,1)}, bf16[2560,512]{1,0:T(8,128)(2,1)}, bf16[25...) custom-call(s32[1]{0:T(128)} %bitcast.sub_ref, s32[2560,1]{1,0:T(8,128)} %reshape.31.index_ref, ...), custom_call_target="tpu_custom_call" | custom-call | tf_op jit(solution)/shard_map/encode/pallas_call | solution.py:327
  56.0 2.4 %collective-permute-start.7 = (bf16[64,512]{1,0:T(8,128)(2,1)}, bf16[64,512]{1,0:T(8,128)(2,1)S(1)}, u32[]{:S(2)}, u32[]{:S(2)}) collective-permute-start(bf16[64,512]{1,0:T(8,128)(2,1)} %get-tuple-element.21), channel_id=1, source_target_pairs={{0,3},{1,0},{2,1},{3,2},{4,7},{5,4},{6,5},{7,6},{8,11},{9,8},{10,9... | collective-permute-start | bytes 196616 | tf_op jit(solution)/shard_map/ppermute | solution.py:280
  61.1 4.1 %collective-permute-start.8 = (bf16[256,512]{1,0:T(8,128)(2,1)S(1)}, bf16[256,512]{1,0:T(8,128)(2,1)S(1)}, u32[]{:S(2)}, u32[]{:S(2)}) collective-permute-start(bf16[256,512]{1,0:T(8,128)(2,1)S(1)} %constant_dynamic-update-slice_fusion.band_ref), channel_id=1, source_target_pairs={{0,4},{1,5},{4,8},{5,9},{6,2},{7,3},{8,12},{9,13},{10,6},{11,7},{1... | collective-permute-start | bytes 786440 | tf_op jit(solution)/shard_map/ppermute | solution.py:275
  65.3 2.1 %collective-permute-start.9 = (bf16[64,512]{1,0:T(8,128)(2,1)S(1)}, bf16[64,512]{1,0:T(8,128)(2,1)S(1)}, u32[]{:S(2)}, u32[]{:S(2)}) collective-permute-start(bf16[64,512]{1,0:T(8,128)(2,1)S(1)} %constant_dynamic-slice_fusion), channel_id=1, source_target_pairs={{2,6},{3,7},{4,0},{5,1},{6,10},{7,11},{8,4},{9,5},{10,14},{11,15},... | collective-permute-start | bytes 196616 | tf_op jit(solution)/shard_map/ppermute | solution.py:275
  67.4 3.5 %collective-permute-done.9.side_ref = bf16[64,512]{1,0:T(8,128)(2,1)S(1)} collective-permute-done((bf16[64,512]{1,0:T(8,128)(2,1)S(1)}, bf16[64,512]{1,0:T(8,128)(2,1)S(1)}, u32[]{:S(2)}, u32[]{:S(2)}) %collective-permute-start.9) | collective-permute-done | bytes 65568 | tf_op jit(solution)/shard_map/ppermute | solution.py:275
  71.7 17.9 %process.1 = (bf16[64,512]{1,0:T(8,128)(2,1)}, bf16[2560,512]{1,0:T(8,128)(2,1)}, bf16[1024,512]{1,0:T(8,128)(2,1)}) custom-call(s32[1]{0:T(128)} %bitcast.sub_ref, bf16[256,512]{1,0:T(8,128)(2,1)} %copy-done.3, bf16[256,512]{1,0:T(8,128)(2,1)} %copy-done.6, bf16[64,512]{1,0:T(8,128)(2,1)} %copy-done.9, bf16[256,640]{1,0:T(8,128)(2,1)} %copy-done.4, ...), custom_call_target="tpu_custom_call" | custom-call | tf_op jit(solution)/shard_map/process/pallas_call | solution.py:358
  89.6 24.5 %all_to_all.15 = bf16[32,32,512]{2,1,0:T(8,128)(2,1)S(1)} all-to-all(bf16[32,32,512]{2,1,0:T(8,128)(2,1)} %bitcast.10), channel_id=1, replica_groups=mesh['band_0'=8,'band_1'=4,'band_2'=2,'sub'=4] {'band_1','band_2','sub'}, dimensions={0} | all-to-all | bytes 2097152 | tf_op jit(solution)/shard_map/all_to_all | solution.py:286
  114.3 21.1 %all_to_all.16 = bf16[8,32,512]{2,1,0:T(8,128)(2,1)S(1)} all-to-all(bf16[8,32,512]{2,1,0:T(8,128)(2,1)S(1)} %broadcast_in_dim.7), channel_id=1, replica_groups=mesh['band_0'=8,'band_1'=4,'band_2'=2,'sub'=4] {'band_0'}, dimensions={0} | all-to-all | bytes 524288 | tf_op jit(solution)/shard_map/all_to_all | solution.py:251
  136.6 7.3 %all-to-all-start.2 = ((bf16[32,32,512]{2,1,0:T(8,128)(2,1)}), bf16[32,32,512]{2,1,0:T(8,128)(2,1)S(1)}, u32[]{:S(2)}, u32[]{:S(2)}) async-start(bf16[32,32,512]{2,1,0:T(8,128)(2,1)} %broadcast_in_dim.8), calls=%async_computation.2 | async-start | bytes 2097152 | tf_op jit(solution)/shard_map/all_to_all | solution.py:251
  143.8 11.8 %channels.1 = (bf16[227,512]{1,0:T(8,128)(2,1)}, bf16[227,512]{1,0:T(8,128)(2,1)}, bf16[227,512]{1,0:T(8,128)(2,1)}, bf16[227,512]{1,0:T(8,128)(2,1)}, bf16[227,...) custom-call(s32[1]{0:T(128)} %bitcast.sub_ref, s32[2560,1]{1,0:T(8,128)} %reshape.31.index_ref, bf16[512,512]{1,0:T(8,128)(2,1)} %src_ref.3, ...), custom_call_target="tpu_custom_call" | custom-call | tf_op jit(solution)/shard_map/channels/pallas_call | solution.py:400
  155.6 3.5 %collective-permute-start.14 = (bf16[227,512]{1,0:T(8,128)(2,1)}, bf16[227,512]{1,0:T(8,128)(2,1)S(1)}, u32[]{:S(2)}, u32[]{:S(2)}) collective-permute-start(bf16[227,512]{1,0:T(8,128)(2,1)} %get-tuple-element.32), channel_id=1, source_target_pairs={{0,4},{4,8},{8,12},{12,16},{16,20},{20,24},{24,28},{28,32},{32,36}... | collective-permute-start | bytes 697352 | tf_op jit(solution)/shard_map/ppermute | solution.py:258
  159.2 1.9 %collective-permute-start.15 = (bf16[227,512]{1,0:T(8,128)(2,1)}, bf16[227,512]{1,0:T(8,128)(2,1)S(1)}, u32[]{:S(2)}, u32[]{:S(2)}) collective-permute-start(bf16[227,512]{1,0:T(8,128)(2,1)} %get-tuple-element.33), channel_id=1, source_target_pairs={{4,0},{8,4},{12,8},{16,12},{20,16},{24,20},{28,24},{32,28},{36,32}... | collective-permute-start | bytes 697352 | tf_op jit(solution)/shard_map/ppermute | solution.py:263
  162.5 4.3 %collective-permute-done.15 = bf16[227,512]{1,0:T(8,128)(2,1)S(1)} collective-permute-done((bf16[227,512]{1,0:T(8,128)(2,1)}, bf16[227,512]{1,0:T(8,128)(2,1)S(1)}, u32[]{:S(2)}, u32[]{:S(2)}) %collective-permute-start.15) | collective-permute-done | bytes 232480 | tf_op jit(solution)/shard_map/ppermute | solution.py:263
  169.5 2.4 %collective-permute-start.17 = (bf16[227,512]{1,0:T(8,128)(2,1)S(1)}, bf16[227,512]{1,0:T(8,128)(2,1)S(1)}, u32[]{:S(2)}, u32[]{:S(2)}) collective-permute-start(bf16[227,512]{1,0:T(8,128)(2,1)S(1)} %get-tuple-element.44), channel_id=1, source_target_pairs={{0,2},{1,3},{2,0},{3,1},{4,6},{5,7},{6,4},{7,5},{8,10},{9,11},{10,... | collective-permute-start | bytes 697352 | tf_op jit(solution)/shard_map/ppermute | solution.py:280
  173.1 3.8 %collective-permute-done.16 = bf16[227,512]{1,0:T(8,128)(2,1)S(1)} collective-permute-done((bf16[227,512]{1,0:T(8,128)(2,1)S(1)}, bf16[227,512]{1,0:T(8,128)(2,1)S(1)}, u32[]{:S(2)}, u32[]{:S(2)}) %collective-permute-start.16) | collective-permute-done | bytes 232480 | tf_op jit(solution)/shard_map/ppermute | solution.py:280
  176.9 2.5 %collective-permute-done.17 = bf16[227,512]{1,0:T(8,128)(2,1)S(1)} collective-permute-done((bf16[227,512]{1,0:T(8,128)(2,1)S(1)}, bf16[227,512]{1,0:T(8,128)(2,1)S(1)}, u32[]{:S(2)}, u32[]{:S(2)}) %collective-permute-start.17) | collective-permute-done | bytes 232480 | tf_op jit(solution)/shard_map/ppermute | solution.py:280
  179.5 1.9 %convert_add_fusion = f32[227,512]{1,0:T(8,128)} fusion(bf16[227,512]{1,0:T(8,128)(2,1)S(1)} %collective-permute-done.18, bf16[227,512]{1,0:T(8,128)(2,1)S(1)} %collective-permute-done.17, bf16[227,512]{1,0:T(8,128)(2,1)S(1)} %collective-permute-done.16, bf16[227,512]{1,0:T(8,128)(2,1)} %get-tuple-element.31, ...), kind=kLoop, calls=%fused_computation.2 | loop fusion | flops 1510912 | bytes 1859586 | tf_op jit(solution)/shard_map/add | solution.py:430
  (65 shorter events, 24.3 us)
Async XLA Ops:
  0.6 10.6 %collective-permute-start = (bf16[227,512]{1,0:T(8,128)(2,1)}, bf16[227,512]{1,0:T(8,128)(2,1)S(1)}, u32[]{:S(2)}, u32[]{:S(2)}) collective-permute-start(bf16[227,512]{1,0:T(8,128)(2,1)} %own_ref.1), channel_id=1, source_target_pairs={{0,1},{1,2},{2,3},{3,0},{4,5},{5,6},{6,7},{7,4},{8,9},{9,10},{10,1... | collective-permute-start | bytes 697352 | tf_op jit(solution)/shard_map/ppermute | solution.py:280
  2.7 12.9 %collective-permute-start.1 = (bf16[227,512]{1,0:T(8,128)(2,1)}, bf16[227,512]{1,0:T(8,128)(2,1)S(1)}, u32[]{:S(2)}, u32[]{:S(2)}) collective-permute-start(bf16[227,512]{1,0:T(8,128)(2,1)} %own_ref.1), channel_id=1, source_target_pairs={{0,2},{1,3},{2,0},{3,1},{4,6},{5,7},{6,4},{7,5},{8,10},{9,11},{10,... | collective-permute-start | bytes 697352 | tf_op jit(solution)/shard_map/ppermute | solution.py:280
  5.2 10.5 %collective-permute-start.2 = (bf16[227,512]{1,0:T(8,128)(2,1)}, bf16[227,512]{1,0:T(8,128)(2,1)S(1)}, u32[]{:S(2)}, u32[]{:S(2)}) collective-permute-start(bf16[227,512]{1,0:T(8,128)(2,1)} %own_ref.1), channel_id=1, source_target_pairs={{0,3},{1,0},{2,1},{3,2},{4,7},{5,4},{6,5},{7,6},{8,11},{9,8},{10,9... | collective-permute-start | bytes 697352 | tf_op jit(solution)/shard_map/ppermute | solution.py:280
  11.2 22.2 %copy-start = (bf16[227,512]{1,0:T(8,128)(2,1)}, bf16[227,512]{1,0:T(8,128)(2,1)S(1)}, u32[]{:S(2)}) copy-start(bf16[227,512]{1,0:T(8,128)(2,1)S(1)} %collective-permute-done.one_ref) | copy-start | bytes 697348
  15.7 17.7 %copy-start.1 = (bf16[227,512]{1,0:T(8,128)(2,1)}, bf16[227,512]{1,0:T(8,128)(2,1)S(1)}, u32[]{:S(2)}) copy-start(bf16[227,512]{1,0:T(8,128)(2,1)S(1)} %collective-permute-done.1.two_ref) | copy-start | bytes 697348
  15.7 17.7 %copy-start.2 = (bf16[227,512]{1,0:T(8,128)(2,1)}, bf16[227,512]{1,0:T(8,128)(2,1)S(1)}, u32[]{:S(2)}) copy-start(bf16[227,512]{1,0:T(8,128)(2,1)S(1)} %collective-permute-done.2.three_ref) | copy-start | bytes 697348
  16.9 15.7 %collective-permute-start.3 = (bf16[227,512]{1,0:T(8,128)(2,1)S(1)}, bf16[227,512]{1,0:T(8,128)(2,1)S(1)}, u32[]{:S(2)}, u32[]{:S(2)}) collective-permute-start(bf16[227,512]{1,0:T(8,128)(2,1)S(1)} %get-tuple-element.41), channel_id=1, source_target_pairs={{0,4},{4,8},{8,12},{12,16},{16,20},{20,24},{24,28},{28,32},{32,36}... | collective-permute-start | bytes 697352 | tf_op jit(solution)/shard_map/ppermute | solution.py:258
  21.5 6.4 %collective-permute-start.10 = (bf16[64,640]{1,0:T(8,128)(2,1)S(1)}, bf16[64,640]{1,0:T(8,128)(2,1)S(1)}, u32[]{:S(2)}, u32[]{:S(2)}) collective-permute-start(bf16[64,640]{1,0:T(8,128)(2,1)S(1)} %concatenate.10), channel_id=1, source_target_pairs={{0,1},{1,2},{2,3},{3,0},{4,5},{5,6},{6,7},{7,4},{8,9},{9,10},{10,1... | collective-permute-start | bytes 245768 | tf_op jit(solution)/shard_map/ppermute | solution.py:280
  22.6 5.4 %collective-permute-start.11 = (bf16[64,640]{1,0:T(8,128)(2,1)S(1)}, bf16[64,640]{1,0:T(8,128)(2,1)S(1)}, u32[]{:S(2)}, u32[]{:S(2)}) collective-permute-start(bf16[64,640]{1,0:T(8,128)(2,1)S(1)} %concatenate.10), channel_id=1, source_target_pairs={{0,2},{1,3},{2,0},{3,1},{4,6},{5,7},{6,4},{7,5},{8,10},{9,11},{10,... | collective-permute-start | bytes 245768 | tf_op jit(solution)/shard_map/ppermute | solution.py:280
  24.7 3.8 %collective-permute-start.12 = (bf16[64,640]{1,0:T(8,128)(2,1)S(1)}, bf16[64,640]{1,0:T(8,128)(2,1)S(1)}, u32[]{:S(2)}, u32[]{:S(2)}) collective-permute-start(bf16[64,640]{1,0:T(8,128)(2,1)S(1)} %concatenate.10), channel_id=1, source_target_pairs={{0,3},{1,0},{2,1},{3,2},{4,7},{5,4},{6,5},{7,6},{8,11},{9,8},{10,9... | collective-permute-start | bytes 245768 | tf_op jit(solution)/shard_map/ppermute | solution.py:280
  26.0 7.4 %collective-permute-start.4 = (bf16[227,512]{1,0:T(8,128)(2,1)S(1)}, bf16[227,512]{1,0:T(8,128)(2,1)S(1)}, u32[]{:S(2)}, u32[]{:S(2)}) collective-permute-start(bf16[227,512]{1,0:T(8,128)(2,1)S(1)} %get-tuple-element.40), channel_id=1, source_target_pairs={{4,0},{8,4},{12,8},{16,12},{20,16},{24,20},{28,24},{32,28},{36,32}... | collective-permute-start | bytes 697352 | tf_op jit(solution)/shard_map/ppermute | solution.py:263
  28.4 36.8 %copy-start.4 = (bf16[256,640]{1,0:T(8,128)(2,1)}, bf16[256,640]{1,0:T(8,128)(2,1)S(1)}, u32[]{:S(2)}) copy-start(bf16[256,640]{1,0:T(8,128)(2,1)S(1)} %constant_dynamic-update-slice_fusion.4.pay_ref) | copy-start | bytes 983044
  28.5 42.4 %collective-permute-start.13 = (bf16[256,640]{1,0:T(8,128)(2,1)S(1)}, bf16[256,640]{1,0:T(8,128)(2,1)S(1)}, u32[]{:S(2)}, u32[]{:S(2)}) collective-permute-start(bf16[256,640]{1,0:T(8,128)(2,1)S(1)} %constant_dynamic-update-slice_fusion.4.pay_ref), channel_id=1, source_target_pairs={{0,4},{1,5},{4,8},{5,9},{6,2},{7,3},{8,12},{9,13},{10,6},{11,7},{1... | collective-permute-start | bytes 983048 | tf_op jit(solution)/shard_map/ppermute | solution.py:275
  54.7 5.3 %collective-permute-start.5 = (bf16[64,512]{1,0:T(8,128)(2,1)}, bf16[64,512]{1,0:T(8,128)(2,1)S(1)}, u32[]{:S(2)}, u32[]{:S(2)}) collective-permute-start(bf16[64,512]{1,0:T(8,128)(2,1)} %get-tuple-element.21), channel_id=1, source_target_pairs={{0,1},{1,2},{2,3},{3,0},{4,5},{5,6},{6,7},{7,4},{8,9},{9,10},{10,1... | collective-permute-start | bytes 196616 | tf_op jit(solution)/shard_map/ppermute | solution.py:280
  55.9 4.8 %collective-permute-start.6 = (bf16[64,512]{1,0:T(8,128)(2,1)}, bf16[64,512]{1,0:T(8,128)(2,1)S(1)}, u32[]{:S(2)}, u32[]{:S(2)}) collective-permute-start(bf16[64,512]{1,0:T(8,128)(2,1)} %get-tuple-element.21), channel_id=1, source_target_pairs={{0,2},{1,3},{2,0},{3,1},{4,6},{5,7},{6,4},{7,5},{8,10},{9,11},{10,... | collective-permute-start | bytes 196616 | tf_op jit(solution)/shard_map/ppermute | solution.py:280
  56.0 5.1 %collective-permute-start.7 = (bf16[64,512]{1,0:T(8,128)(2,1)}, bf16[64,512]{1,0:T(8,128)(2,1)S(1)}, u32[]{:S(2)}, u32[]{:S(2)}) collective-permute-start(bf16[64,512]{1,0:T(8,128)(2,1)} %get-tuple-element.21), channel_id=1, source_target_pairs={{0,3},{1,0},{2,1},{3,2},{4,7},{5,4},{6,5},{7,6},{8,11},{9,8},{10,9... | collective-permute-start | bytes 196616 | tf_op jit(solution)/shard_map/ppermute | solution.py:280
  61.1 9.7 %collective-permute-start.8 = (bf16[256,512]{1,0:T(8,128)(2,1)S(1)}, bf16[256,512]{1,0:T(8,128)(2,1)S(1)}, u32[]{:S(2)}, u32[]{:S(2)}) collective-permute-start(bf16[256,512]{1,0:T(8,128)(2,1)S(1)} %constant_dynamic-update-slice_fusion.band_ref), channel_id=1, source_target_pairs={{0,4},{1,5},{4,8},{5,9},{6,2},{7,3},{8,12},{9,13},{10,6},{11,7},{1... | collective-permute-start | bytes 786440 | tf_op jit(solution)/shard_map/ppermute | solution.py:275
  65.3 5.6 %collective-permute-start.9 = (bf16[64,512]{1,0:T(8,128)(2,1)S(1)}, bf16[64,512]{1,0:T(8,128)(2,1)S(1)}, u32[]{:S(2)}, u32[]{:S(2)}) collective-permute-start(bf16[64,512]{1,0:T(8,128)(2,1)S(1)} %constant_dynamic-slice_fusion), channel_id=1, source_target_pairs={{2,6},{3,7},{4,0},{5,1},{6,10},{7,11},{8,4},{9,5},{10,14},{11,15},... | collective-permute-start | bytes 196616 | tf_op jit(solution)/shard_map/ppermute | solution.py:275
  136.6 44.8 %all-to-all-start.2 = ((bf16[32,32,512]{2,1,0:T(8,128)(2,1)}), bf16[32,32,512]{2,1,0:T(8,128)(2,1)S(1)}, u32[]{:S(2)}, u32[]{:S(2)}) async-start(bf16[32,32,512]{2,1,0:T(8,128)(2,1)} %broadcast_in_dim.8), calls=%async_computation.2 | async-start | bytes 2097152 | tf_op jit(solution)/shard_map/all_to_all | solution.py:251
  155.6 6.9 %collective-permute-start.14 = (bf16[227,512]{1,0:T(8,128)(2,1)}, bf16[227,512]{1,0:T(8,128)(2,1)S(1)}, u32[]{:S(2)}, u32[]{:S(2)}) collective-permute-start(bf16[227,512]{1,0:T(8,128)(2,1)} %get-tuple-element.32), channel_id=1, source_target_pairs={{0,4},{4,8},{8,12},{12,16},{16,20},{20,24},{24,28},{28,32},{32,36}... | collective-permute-start | bytes 697352 | tf_op jit(solution)/shard_map/ppermute | solution.py:258
  159.2 7.6 %collective-permute-start.15 = (bf16[227,512]{1,0:T(8,128)(2,1)}, bf16[227,512]{1,0:T(8,128)(2,1)S(1)}, u32[]{:S(2)}, u32[]{:S(2)}) collective-permute-start(bf16[227,512]{1,0:T(8,128)(2,1)} %get-tuple-element.33), channel_id=1, source_target_pairs={{4,0},{8,4},{12,8},{16,12},{20,16},{24,20},{28,24},{32,28},{36,32}... | collective-permute-start | bytes 697352 | tf_op jit(solution)/shard_map/ppermute | solution.py:263
  168.3 8.7 %collective-permute-start.16 = (bf16[227,512]{1,0:T(8,128)(2,1)S(1)}, bf16[227,512]{1,0:T(8,128)(2,1)S(1)}, u32[]{:S(2)}, u32[]{:S(2)}) collective-permute-start(bf16[227,512]{1,0:T(8,128)(2,1)S(1)} %get-tuple-element.42), channel_id=1, source_target_pairs={{0,1},{1,2},{2,3},{3,0},{4,5},{5,6},{6,7},{7,4},{8,9},{9,10},{10,1... | collective-permute-start | bytes 697352 | tf_op jit(solution)/shard_map/ppermute | solution.py:280
  169.5 10.0 %collective-permute-start.17 = (bf16[227,512]{1,0:T(8,128)(2,1)S(1)}, bf16[227,512]{1,0:T(8,128)(2,1)S(1)}, u32[]{:S(2)}, u32[]{:S(2)}) collective-permute-start(bf16[227,512]{1,0:T(8,128)(2,1)S(1)} %get-tuple-element.44), channel_id=1, source_target_pairs={{0,2},{1,3},{2,0},{3,1},{4,6},{5,7},{6,4},{7,5},{8,10},{9,11},{10,... | collective-permute-start | bytes 697352 | tf_op jit(solution)/shard_map/ppermute | solution.py:280
  171.9 7.6 %collective-permute-start.18 = (bf16[227,512]{1,0:T(8,128)(2,1)S(1)}, bf16[227,512]{1,0:T(8,128)(2,1)S(1)}, u32[]{:S(2)}, u32[]{:S(2)}) collective-permute-start(bf16[227,512]{1,0:T(8,128)(2,1)S(1)} %get-tuple-element.43), channel_id=1, source_target_pairs={{0,3},{1,0},{2,1},{3,2},{4,7},{5,4},{6,5},{7,6},{8,11},{9,8},{10,9... | collective-permute-start | bytes 697352 | tf_op jit(solution)/shard_map/ppermute | solution.py:280
  (6 other events, 13.5 us)

commit v3 on v2

--- a/solution.py
+++ b/solution.py
@@ -280,13 +280,8 @@
     return lax.ppermute(value, "sub", [(i, (i + steps) % count) for i in range(count)])
 
 
-def weight_sum(part):
-    near = lax.axis_size(NEAR)
-    rows, width = part.shape
-    parts = lax.all_to_all(part.reshape(near, rows // near, width), NEAR, 0, 0, tiled=True)
-    mine = jnp.sum(parts.astype(F32), axis=0).astype(BF)
-    mine = jnp.sum(from_everyone(mine, FAR).astype(F32), axis=0).astype(BF)
-    return from_everyone(mine, NEAR).reshape(rows, width)
+def summed(parts):
+    return jnp.sum(parts.astype(F32), axis=0).astype(BF)
 
 
 def body(
@@ -415,21 +410,25 @@
         name="channels",
     )(sub_scalar, grid_local, w_src, w_embed, bgrad, hslope)
 
-    weights = weight_sum(part)
+    near = lax.axis_size(NEAR)
+    pieces = lax.all_to_all(part.reshape(near, -1, latent), NEAR, 0, 0, tiled=True)
+    pieces, parts, part_low, part_high = lax.optimization_barrier((pieces, parts, part_low, part_high))
+    pieces = from_everyone(summed(pieces), FAR)
     from_above = bands_down(part_low)
     from_below = bands_up(part_high)
-    arrived = None
+    pieces, from_above, from_below = lax.optimization_barrier((pieces, from_above, from_below))
+    weights = from_everyone(summed(pieces), NEAR).reshape(2 * latent, latent)
+    arrived = []
     for k in range(SUBS):
         block = lax.rem(sub + k, SUBS)
         value = parts[k].astype(F32)
         value += jnp.where(block == 0, from_below, jnp.zeros_like(from_below)).astype(F32)
         value += jnp.where(block == SUBS - 1, from_above, jnp.zeros_like(from_above)).astype(F32)
-        if k == 0:
-            arrived = value
-        else:
-            arrived += along_sub(value.astype(BF), k).astype(F32)
+        arrived.append(along_sub(value.astype(BF), k) if k else value)
+    weights, *arrived = lax.optimization_barrier((weights, *arrived))
+    grid_grad = functools.reduce(jnp.add, [value.astype(F32) for value in arrived])
     src_grad, edge_grad = weights[latent:].astype(F32), weights[:latent].astype(F32)
-    return (mesh_out, arrived, src_grad, edge_grad)
+    return (mesh_out, grid_grad, src_grad, edge_grad)
 
 
 def solution(mesh):

time: 187 us -> 173 us (0.925); the launches traced: 183 us -> 172 us
  blocking collectives: 45.6 us -> 0 us
  starting transfers between devices: 48.2 us -> 68.8 us
  waiting for transfers between devices: 23.2 us -> 39 us
  other arithmetic: 7.21 us -> 5.03 us
    all_to_all x2 -> x0, blocking collectives: 45.6 us -> none  [the longest x1 24.5 us: weight_sum(): lax.all_to_all(part.reshape(near, rows // near, width), NEAR, 0, 0, tiled...]
    ppermute x12, waiting for transfers between devices: 13.2 us -> 26.5 us  [along_sub(): lax.ppermute(value, 'sub', [(i, (i + steps) % count) for i in range(count)])]
    all_to_all x1 -> x2, starting transfers between devices: 7.26 us -> 18.7 us  [from_everyone(): lax.all_to_all(jnp.broadcast_to(shard[None], (devices, *shard.shape)), ax...]
    all_to_all x0 -> x1, starting transfers between devices: none -> 8.45 us  [body(): lax.all_to_all(part.reshape(near, -1, latent), NEAR, 0, 0, tiled=True)]
    all_to_all x0 -> x1, waiting for transfers between devices: none -> 4.22 us  [body(): lax.all_to_all(part.reshape(near, -1, latent), NEAR, 0, 0, tiled=True)]
    ppermute x2, waiting for transfers between devices: 5.12 us -> 3.18 us  [bands_down(): return lax.ppermute(value, BAND, [(i + 1, i) for i in range(count - 1)])]
  transfers between devices with their start and end apart: 20 -> 22, of which waited for: 12 -> 14; matrix products, arithmetic and copies ran while one was open for 5% -> 4% of each run, Pallas kernels for 18% -> 19%
where the time goes in v3:
time: 173 us; the launch traced here: 172 us
  starting transfers between devices  68.8 us (40%)
  Pallas kernels  50.4 us (29%)
  waiting for transfers between devices  39 us (23%)
  local copies, waits for them, and re-layouts  8.35 us (5%)
  other arithmetic  5.03 us (3%)
    ppermute x12, waiting for transfers between devices, along_sub(): lax.ppermute(value, 'sub', [(i, (i + steps) % count) for i in range(count)])  26.5 us
    pallas_call x1, Pallas kernels, body(): pl.pallas_call(functools.partial(forward_kernel, scale), grid=(steps,), i...  20.7 us
    ppermute x12, starting transfers between devices, along_sub(): lax.ppermute(value, 'sub', [(i, (i + steps) % count) for i in range(count)])  18.8 us
    all_to_all x2, starting transfers between devices, from_everyone(): lax.all_to_all(jnp.broadcast_to(shard[None], (devices, *shard.shape)), ax...  18.7 us
    pallas_call x1, Pallas kernels, body(): pl.pallas_call(functools.partial(mesh_kernel, mesh_scale, scale, mesh_cou...  17.9 us
    pallas_call x1, Pallas kernels, body(): pl.pallas_call(grid_kernel, grid=(steps,), in_specs=[scalar(), tiled(tile...  11.8 us
    ppermute x3, starting transfers between devices, outwards(): return lax.ppermute(value, ALL, pairs)  10.3 us
    all_to_all x1, starting transfers between devices, body(): lax.all_to_all(part.reshape(near, -1, latent), NEAR, 0, 0, tiled=True)  8.45 us
  transfers between devices with their start and end apart: 22, of which 14 were waited for; matrix products, arithmetic and copies ran while one was open for 4% of the time, Pallas kernels for 19%

profile of v3, /device:TPU:1, one launch (start us, length us, event | category | flops | bytes accessed | tf_op | source)
XLA Modules:
  0.0 172.4 jit_solution(8909330108712519661)
XLA Ops:
  0.6 2.1 %collective-permute-start = (bf16[227,512]{1,0:T(8,128)(2,1)}, bf16[227,512]{1,0:T(8,128)(2,1)S(1)}, u32[]{:S(2)}, u32[]{:S(2)}) collective-permute-start(bf16[227,512]{1,0:T(8,128)(2,1)} %own_ref.1), channel_id=1, source_target_pairs={{0,1},{1,2},{2,3},{3,0},{4,5},{5,6},{6,7},{7,4},{8,9},{9,10},{10,1... | collective-permute-start | bytes 697352 | tf_op jit(solution)/shard_map/ppermute | solution.py:280
  2.7 2.5 %collective-permute-start.1 = (bf16[227,512]{1,0:T(8,128)(2,1)}, bf16[227,512]{1,0:T(8,128)(2,1)S(1)}, u32[]{:S(2)}, u32[]{:S(2)}) collective-permute-start(bf16[227,512]{1,0:T(8,128)(2,1)} %own_ref.1), channel_id=1, source_target_pairs={{0,2},{1,3},{2,0},{3,1},{4,6},{5,7},{6,4},{7,5},{8,10},{9,11},{10,... | collective-permute-start | bytes 697352 | tf_op jit(solution)/shard_map/ppermute | solution.py:280
  7.1 2.4 %reshape.26.index_ref = s32[2560,1]{1,0:T(8,128)} reshape(s32[40,64]{1,0:T(8,128)S(1)} %subtract_bitcast_fusion) | data formatting | bytes 20480 | tf_op jit(solution)/shard_map/reshape | solution.py:310
  11.2 4.5 %collective-permute-done.1.two_ref = bf16[227,512]{1,0:T(8,128)(2,1)S(1)} collective-permute-done((bf16[227,512]{1,0:T(8,128)(2,1)}, bf16[227,512]{1,0:T(8,128)(2,1)S(1)}, u32[]{:S(2)}, u32[]{:S(2)}) %collective-permute-start.1) | collective-permute-done | bytes 232480 | tf_op jit(solution)/shard_map/ppermute | solution.py:280
  16.9 4.6 %collective-permute-start.3 = (bf16[227,512]{1,0:T(8,128)(2,1)S(1)}, bf16[227,512]{1,0:T(8,128)(2,1)S(1)}, u32[]{:S(2)}, u32[]{:S(2)}) collective-permute-start(bf16[227,512]{1,0:T(8,128)(2,1)S(1)} %get-tuple-element.71), channel_id=1, source_target_pairs={{0,4},{4,8},{8,12},{12,16},{16,20},{20,24},{24,28},{28,32},{32,36}... | collective-permute-start | bytes 697352 | tf_op jit(solution)/shard_map/ppermute | solution.py:258
  22.6 2.1 %collective-permute-start.11 = (bf16[64,640]{1,0:T(8,128)(2,1)S(1)}, bf16[64,640]{1,0:T(8,128)(2,1)S(1)}, u32[]{:S(2)}, u32[]{:S(2)}) collective-permute-start(bf16[64,640]{1,0:T(8,128)(2,1)S(1)} %concatenate.10), channel_id=1, source_target_pairs={{0,2},{1,3},{2,0},{3,1},{4,6},{5,7},{6,4},{7,5},{8,10},{9,11},{10,... | collective-permute-start | bytes 245768 | tf_op jit(solution)/shard_map/ppermute | solution.py:280
  28.5 4.1 %collective-permute-start.13 = (bf16[256,640]{1,0:T(8,128)(2,1)S(1)}, bf16[256,640]{1,0:T(8,128)(2,1)S(1)}, u32[]{:S(2)}, u32[]{:S(2)}) collective-permute-start(bf16[256,640]{1,0:T(8,128)(2,1)S(1)} %constant_dynamic-update-slice_fusion.4.pay_ref), channel_id=1, source_target_pairs={{0,4},{1,5},{4,8},{5,9},{6,2},{7,3},{8,12},{9,13},{10,6},{11,7},{1... | collective-permute-start | bytes 983048 | tf_op jit(solution)/shard_map/ppermute | solution.py:275
  34.1 20.7 %encode.1 = (bf16[2560,512]{1,0:T(8,128)(2,1)}, bf16[2560,512]{1,0:T(8,128)(2,1)}, bf16[2560,512]{1,0:T(8,128)(2,1)}, bf16[2560,512]{1,0:T(8,128)(2,1)}, bf16[25...) custom-call(s32[1]{0:T(128)} %bitcast.sub_ref, s32[2560,1]{1,0:T(8,128)} %reshape.26.index_ref, ...), custom_call_target="tpu_custom_call" | custom-call | tf_op jit(solution)/shard_map/encode/pallas_call | solution.py:322
  56.0 2.4 %collective-permute-start.7 = (bf16[64,512]{1,0:T(8,128)(2,1)}, bf16[64,512]{1,0:T(8,128)(2,1)S(1)}, u32[]{:S(2)}, u32[]{:S(2)}) collective-permute-start(bf16[64,512]{1,0:T(8,128)(2,1)} %get-tuple-element.36), channel_id=1, source_target_pairs={{0,3},{1,0},{2,1},{3,2},{4,7},{5,4},{6,5},{7,6},{8,11},{9,8},{10,9... | collective-permute-start | bytes 196616 | tf_op jit(solution)/shard_map/ppermute | solution.py:280
  61.1 4.1 %collective-permute-start.8 = (bf16[256,512]{1,0:T(8,128)(2,1)S(1)}, bf16[256,512]{1,0:T(8,128)(2,1)S(1)}, u32[]{:S(2)}, u32[]{:S(2)}) collective-permute-start(bf16[256,512]{1,0:T(8,128)(2,1)S(1)} %constant_dynamic-update-slice_fusion.band_ref), channel_id=1, source_target_pairs={{0,4},{1,5},{4,8},{5,9},{6,2},{7,3},{8,12},{9,13},{10,6},{11,7},{1... | collective-permute-start | bytes 786440 | tf_op jit(solution)/shard_map/ppermute | solution.py:275
  65.3 2.1 %collective-permute-start.9 = (bf16[64,512]{1,0:T(8,128)(2,1)S(1)}, bf16[64,512]{1,0:T(8,128)(2,1)S(1)}, u32[]{:S(2)}, u32[]{:S(2)}) collective-permute-start(bf16[64,512]{1,0:T(8,128)(2,1)S(1)} %constant_dynamic-slice_fusion), channel_id=1, source_target_pairs={{2,6},{3,7},{4,0},{5,1},{6,10},{7,11},{8,4},{9,5},{10,14},{11,15},... | collective-permute-start | bytes 196616 | tf_op jit(solution)/shard_map/ppermute | solution.py:275
  67.4 3.5 %collective-permute-done.9.side_ref = bf16[64,512]{1,0:T(8,128)(2,1)S(1)} collective-permute-done((bf16[64,512]{1,0:T(8,128)(2,1)S(1)}, bf16[64,512]{1,0:T(8,128)(2,1)S(1)}, u32[]{:S(2)}, u32[]{:S(2)}) %collective-permute-start.9) | collective-permute-done | bytes 65568 | tf_op jit(solution)/shard_map/ppermute | solution.py:275
  71.7 17.9 %process.1 = (bf16[64,512]{1,0:T(8,128)(2,1)}, bf16[2560,512]{1,0:T(8,128)(2,1)}, bf16[1024,512]{1,0:T(8,128)(2,1)}) custom-call(s32[1]{0:T(128)} %bitcast.sub_ref, bf16[256,512]{1,0:T(8,128)(2,1)} %copy-done.3, bf16[256,512]{1,0:T(8,128)(2,1)} %copy-done.6, bf16[64,512]{1,0:T(8,128)(2,1)} %copy-done.13, bf16[256,640]{1,0:T(8,128)(2,1)} %copy-done.4, ...), custom_call_target="tpu_custom_call" | custom-call | tf_op jit(solution)/shard_map/process/pallas_call | solution.py:353
  89.6 8.4 %all-to-all-start = ((bf16[32,32,512]{2,1,0:T(8,128)(2,1)}), bf16[32,32,512]{2,1,0:T(8,128)(2,1)S(1)}, u32[]{:S(2)}, u32[]{:S(2)}) async-start(bf16[32,32,512]{2,1,0:T(8,128)(2,1)} %bitcast.6), calls=%async_computation | async-start | bytes 2097152 | tf_op jit(solution)/shard_map/all_to_all | solution.py:414
  98.1 11.8 %channels.1 = (bf16[227,512]{1,0:T(8,128)(2,1)}, bf16[227,512]{1,0:T(8,128)(2,1)}, bf16[227,512]{1,0:T(8,128)(2,1)}, bf16[227,512]{1,0:T(8,128)(2,1)}, bf16[227,...) custom-call(s32[1]{0:T(128)} %bitcast.sub_ref, s32[2560,1]{1,0:T(8,128)} %reshape.26.index_ref, bf16[512,512]{1,0:T(8,128)(2,1)} %src_ref.3, ...), custom_call_target="tpu_custom_call" | custom-call | tf_op jit(solution)/shard_map/channels/pallas_call | solution.py:395
  109.9 4.2 %all-to-all-done = bf16[32,32,512]{2,1,0:T(8,128)(2,1)S(1)} async-done(((bf16[32,32,512]{2,1,0:T(8,128)(2,1)}), bf16[32,32,512]{2,1,0:T(8,128)(2,1)S(1)}, u32[]{:S(2)}, u32[]{:S(2)}) %all-to-all-start) | async-done | bytes 1048608 | tf_op jit(solution)/shard_map/all_to_all | solution.py:414
  115.0 11.5 %all-to-all-start.1 = ((bf16[8,32,512]{2,1,0:T(8,128)(2,1)}), bf16[8,32,512]{2,1,0:T(8,128)(2,1)S(1)}, u32[]{:S(2)}, u32[]{:S(2)}) async-start(bf16[8,32,512]{2,1,0:T(8,128)(2,1)} %broadcast_in_dim.7), calls=%async_computation.1 | async-start | bytes 524288 | tf_op jit(solution)/shard_map/all_to_all | solution.py:251
  126.5 3.4 %collective-permute-start.14 = (bf16[227,512]{1,0:T(8,128)(2,1)}, bf16[227,512]{1,0:T(8,128)(2,1)S(1)}, u32[]{:S(2)}, u32[]{:S(2)}) collective-permute-start(bf16[227,512]{1,0:T(8,128)(2,1)} %get-tuple-element.54), channel_id=1, source_target_pairs={{4,0},{8,4},{12,8},{16,12},{20,16},{24,20},{28,24},{32,28},{36,32}... | collective-permute-start | bytes 697352 | tf_op jit(solution)/shard_map/ppermute | solution.py:263
  129.9 2.5 %collective-permute-start.15 = (bf16[227,512]{1,0:T(8,128)(2,1)}, bf16[227,512]{1,0:T(8,128)(2,1)S(1)}, u32[]{:S(2)}, u32[]{:S(2)}) collective-permute-start(bf16[227,512]{1,0:T(8,128)(2,1)} %get-tuple-element.55), channel_id=1, source_target_pairs={{0,4},{4,8},{8,12},{12,16},{16,20},{20,24},{24,28},{28,32},{32,36}... | collective-permute-start | bytes 697352 | tf_op jit(solution)/shard_map/ppermute | solution.py:258
  132.4 2.4 %collective-permute-done.14 = bf16[227,512]{1,0:T(8,128)(2,1)S(1)} collective-permute-done((bf16[227,512]{1,0:T(8,128)(2,1)}, bf16[227,512]{1,0:T(8,128)(2,1)S(1)}, u32[]{:S(2)}, u32[]{:S(2)}) %collective-permute-start.14) | collective-permute-done | bytes 232480 | tf_op jit(solution)/shard_map/ppermute | solution.py:263
  137.5 7.3 %all-to-all-start.2 = ((bf16[32,32,512]{2,1,0:T(8,128)(2,1)}), bf16[32,32,512]{2,1,0:T(8,128)(2,1)S(1)}, u32[]{:S(2)}, u32[]{:S(2)}) async-start(bf16[32,32,512]{2,1,0:T(8,128)(2,1)} %broadcast_in_dim.8), calls=%async_computation.2 | async-start | bytes 2097152 | tf_op jit(solution)/shard_map/all_to_all | solution.py:251
  146.7 2.4 %collective-permute-start.17 = (bf16[227,512]{1,0:T(8,128)(2,1)S(1)}, bf16[227,512]{1,0:T(8,128)(2,1)S(1)}, u32[]{:S(2)}, u32[]{:S(2)}) collective-permute-start(bf16[227,512]{1,0:T(8,128)(2,1)S(1)} %get-tuple-element.73), channel_id=1, source_target_pairs={{0,2},{1,3},{2,0},{3,1},{4,6},{5,7},{6,4},{7,5},{8,10},{9,11},{10,... | collective-permute-start | bytes 697352 | tf_op jit(solution)/shard_map/ppermute | solution.py:280
  150.2 14.3 %collective-permute-done.16 = bf16[227,512]{1,0:T(8,128)(2,1)S(1)} collective-permute-done((bf16[227,512]{1,0:T(8,128)(2,1)S(1)}, bf16[227,512]{1,0:T(8,128)(2,1)S(1)}, u32[]{:S(2)}, u32[]{:S(2)}) %collective-permute-start.16) | collective-permute-done | bytes 232480 | tf_op jit(solution)/shard_map/ppermute | solution.py:280
  164.5 5.4 %collective-permute-done.17 = bf16[227,512]{1,0:T(8,128)(2,1)S(1)} collective-permute-done((bf16[227,512]{1,0:T(8,128)(2,1)S(1)}, bf16[227,512]{1,0:T(8,128)(2,1)S(1)}, u32[]{:S(2)}, u32[]{:S(2)}) %collective-permute-start.17) | collective-permute-done | bytes 232480 | tf_op jit(solution)/shard_map/ppermute | solution.py:280
  (74 shorter events, 25.1 us)
Async XLA Ops:
  0.6 10.6 %collective-permute-start = (bf16[227,512]{1,0:T(8,128)(2,1)}, bf16[227,512]{1,0:T(8,128)(2,1)S(1)}, u32[]{:S(2)}, u32[]{:S(2)}) collective-permute-start(bf16[227,512]{1,0:T(8,128)(2,1)} %own_ref.1), channel_id=1, source_target_pairs={{0,1},{1,2},{2,3},{3,0},{4,5},{5,6},{6,7},{7,4},{8,9},{9,10},{10,1... | collective-permute-start | bytes 697352 | tf_op jit(solution)/shard_map/ppermute | solution.py:280
  2.7 12.9 %collective-permute-start.1 = (bf16[227,512]{1,0:T(8,128)(2,1)}, bf16[227,512]{1,0:T(8,128)(2,1)S(1)}, u32[]{:S(2)}, u32[]{:S(2)}) collective-permute-start(bf16[227,512]{1,0:T(8,128)(2,1)} %own_ref.1), channel_id=1, source_target_pairs={{0,2},{1,3},{2,0},{3,1},{4,6},{5,7},{6,4},{7,5},{8,10},{9,11},{10,... | collective-permute-start | bytes 697352 | tf_op jit(solution)/shard_map/ppermute | solution.py:280
  5.2 10.5 %collective-permute-start.2 = (bf16[227,512]{1,0:T(8,128)(2,1)}, bf16[227,512]{1,0:T(8,128)(2,1)S(1)}, u32[]{:S(2)}, u32[]{:S(2)}) collective-permute-start(bf16[227,512]{1,0:T(8,128)(2,1)} %own_ref.1), channel_id=1, source_target_pairs={{0,3},{1,0},{2,1},{3,2},{4,7},{5,4},{6,5},{7,6},{8,11},{9,8},{10,9... | collective-permute-start | bytes 697352 | tf_op jit(solution)/shard_map/ppermute | solution.py:280
  16.9 15.7 %collective-permute-start.3 = (bf16[227,512]{1,0:T(8,128)(2,1)S(1)}, bf16[227,512]{1,0:T(8,128)(2,1)S(1)}, u32[]{:S(2)}, u32[]{:S(2)}) collective-permute-start(bf16[227,512]{1,0:T(8,128)(2,1)S(1)} %get-tuple-element.71), channel_id=1, source_target_pairs={{0,4},{4,8},{8,12},{12,16},{16,20},{20,24},{24,28},{28,32},{32,36}... | collective-permute-start | bytes 697352 | tf_op jit(solution)/shard_map/ppermute | solution.py:258
  21.5 6.4 %collective-permute-start.10 = (bf16[64,640]{1,0:T(8,128)(2,1)S(1)}, bf16[64,640]{1,0:T(8,128)(2,1)S(1)}, u32[]{:S(2)}, u32[]{:S(2)}) collective-permute-start(bf16[64,640]{1,0:T(8,128)(2,1)S(1)} %concatenate.10), channel_id=1, source_target_pairs={{0,1},{1,2},{2,3},{3,0},{4,5},{5,6},{6,7},{7,4},{8,9},{9,10},{10,1... | collective-permute-start | bytes 245768 | tf_op jit(solution)/shard_map/ppermute | solution.py:280
  22.6 5.4 %collective-permute-start.11 = (bf16[64,640]{1,0:T(8,128)(2,1)S(1)}, bf16[64,640]{1,0:T(8,128)(2,1)S(1)}, u32[]{:S(2)}, u32[]{:S(2)}) collective-permute-start(bf16[64,640]{1,0:T(8,128)(2,1)S(1)} %concatenate.10), channel_id=1, source_target_pairs={{0,2},{1,3},{2,0},{3,1},{4,6},{5,7},{6,4},{7,5},{8,10},{9,11},{10,... | collective-permute-start | bytes 245768 | tf_op jit(solution)/shard_map/ppermute | solution.py:280
  24.7 3.8 %collective-permute-start.12 = (bf16[64,640]{1,0:T(8,128)(2,1)S(1)}, bf16[64,640]{1,0:T(8,128)(2,1)S(1)}, u32[]{:S(2)}, u32[]{:S(2)}) collective-permute-start(bf16[64,640]{1,0:T(8,128)(2,1)S(1)} %concatenate.10), channel_id=1, source_target_pairs={{0,3},{1,0},{2,1},{3,2},{4,7},{5,4},{6,5},{7,6},{8,11},{9,8},{10,9... | collective-permute-start | bytes 245768 | tf_op jit(solution)/shard_map/ppermute | solution.py:280
  26.0 7.4 %collective-permute-start.4 = (bf16[227,512]{1,0:T(8,128)(2,1)S(1)}, bf16[227,512]{1,0:T(8,128)(2,1)S(1)}, u32[]{:S(2)}, u32[]{:S(2)}) collective-permute-start(bf16[227,512]{1,0:T(8,128)(2,1)S(1)} %get-tuple-element.70), channel_id=1, source_target_pairs={{4,0},{8,4},{12,8},{16,12},{20,16},{24,20},{28,24},{32,28},{36,32}... | collective-permute-start | bytes 697352 | tf_op jit(solution)/shard_map/ppermute | solution.py:263
  28.4 36.8 %copy-start.4 = (bf16[256,640]{1,0:T(8,128)(2,1)}, bf16[256,640]{1,0:T(8,128)(2,1)S(1)}, u32[]{:S(2)}) copy-start(bf16[256,640]{1,0:T(8,128)(2,1)S(1)} %constant_dynamic-update-slice_fusion.4.pay_ref) | copy-start | bytes 983044
  28.5 42.4 %collective-permute-start.13 = (bf16[256,640]{1,0:T(8,128)(2,1)S(1)}, bf16[256,640]{1,0:T(8,128)(2,1)S(1)}, u32[]{:S(2)}, u32[]{:S(2)}) collective-permute-start(bf16[256,640]{1,0:T(8,128)(2,1)S(1)} %constant_dynamic-update-slice_fusion.4.pay_ref), channel_id=1, source_target_pairs={{0,4},{1,5},{4,8},{5,9},{6,2},{7,3},{8,12},{9,13},{10,6},{11,7},{1... | collective-permute-start | bytes 983048 | tf_op jit(solution)/shard_map/ppermute | solution.py:275
  54.7 5.6 %collective-permute-start.5 = (bf16[64,512]{1,0:T(8,128)(2,1)}, bf16[64,512]{1,0:T(8,128)(2,1)S(1)}, u32[]{:S(2)}, u32[]{:S(2)}) collective-permute-start(bf16[64,512]{1,0:T(8,128)(2,1)} %get-tuple-element.36), channel_id=1, source_target_pairs={{0,1},{1,2},{2,3},{3,0},{4,5},{5,6},{6,7},{7,4},{8,9},{9,10},{10,1... | collective-permute-start | bytes 196616 | tf_op jit(solution)/shard_map/ppermute | solution.py:280
  55.9 4.9 %collective-permute-start.6 = (bf16[64,512]{1,0:T(8,128)(2,1)}, bf16[64,512]{1,0:T(8,128)(2,1)S(1)}, u32[]{:S(2)}, u32[]{:S(2)}) collective-permute-start(bf16[64,512]{1,0:T(8,128)(2,1)} %get-tuple-element.36), channel_id=1, source_target_pairs={{0,2},{1,3},{2,0},{3,1},{4,6},{5,7},{6,4},{7,5},{8,10},{9,11},{10,... | collective-permute-start | bytes 196616 | tf_op jit(solution)/shard_map/ppermute | solution.py:280
  56.0 5.1 %collective-permute-start.7 = (bf16[64,512]{1,0:T(8,128)(2,1)}, bf16[64,512]{1,0:T(8,128)(2,1)S(1)}, u32[]{:S(2)}, u32[]{:S(2)}) collective-permute-start(bf16[64,512]{1,0:T(8,128)(2,1)} %get-tuple-element.36), channel_id=1, source_target_pairs={{0,3},{1,0},{2,1},{3,2},{4,7},{5,4},{6,5},{7,6},{8,11},{9,8},{10,9... | collective-permute-start | bytes 196616 | tf_op jit(solution)/shard_map/ppermute | solution.py:280
  61.1 9.8 %collective-permute-start.8 = (bf16[256,512]{1,0:T(8,128)(2,1)S(1)}, bf16[256,512]{1,0:T(8,128)(2,1)S(1)}, u32[]{:S(2)}, u32[]{:S(2)}) collective-permute-start(bf16[256,512]{1,0:T(8,128)(2,1)S(1)} %constant_dynamic-update-slice_fusion.band_ref), channel_id=1, source_target_pairs={{0,4},{1,5},{4,8},{5,9},{6,2},{7,3},{8,12},{9,13},{10,6},{11,7},{1... | collective-permute-start | bytes 786440 | tf_op jit(solution)/shard_map/ppermute | solution.py:275
  65.3 5.6 %collective-permute-start.9 = (bf16[64,512]{1,0:T(8,128)(2,1)S(1)}, bf16[64,512]{1,0:T(8,128)(2,1)S(1)}, u32[]{:S(2)}, u32[]{:S(2)}) collective-permute-start(bf16[64,512]{1,0:T(8,128)(2,1)S(1)} %constant_dynamic-slice_fusion), channel_id=1, source_target_pairs={{2,6},{3,7},{4,0},{5,1},{6,10},{7,11},{8,4},{9,5},{10,14},{11,15},... | collective-permute-start | bytes 196616 | tf_op jit(solution)/shard_map/ppermute | solution.py:275
  89.6 24.5 %all-to-all-start = ((bf16[32,32,512]{2,1,0:T(8,128)(2,1)}), bf16[32,32,512]{2,1,0:T(8,128)(2,1)S(1)}, u32[]{:S(2)}, u32[]{:S(2)}) async-start(bf16[32,32,512]{2,1,0:T(8,128)(2,1)} %bitcast.6), calls=%async_computation | async-start | bytes 2097152 | tf_op jit(solution)/shard_map/all_to_all | solution.py:414
  114.1 30.7 %copy-start.10 = (bf16[227,512]{1,0:T(8,128)(2,1)S(1)}, bf16[227,512]{1,0:T(8,128)(2,1)}, u32[]{:S(2)}) copy-start(bf16[227,512]{1,0:T(8,128)(2,1)} %get-tuple-element.62) | copy-start | bytes 697348
  115.0 21.4 %all-to-all-start.1 = ((bf16[8,32,512]{2,1,0:T(8,128)(2,1)}), bf16[8,32,512]{2,1,0:T(8,128)(2,1)S(1)}, u32[]{:S(2)}, u32[]{:S(2)}) async-start(bf16[8,32,512]{2,1,0:T(8,128)(2,1)} %broadcast_in_dim.7), calls=%async_computation.1 | async-start | bytes 524288 | tf_op jit(solution)/shard_map/all_to_all | solution.py:251
  126.5 8.3 %collective-permute-start.14 = (bf16[227,512]{1,0:T(8,128)(2,1)}, bf16[227,512]{1,0:T(8,128)(2,1)S(1)}, u32[]{:S(2)}, u32[]{:S(2)}) collective-permute-start(bf16[227,512]{1,0:T(8,128)(2,1)} %get-tuple-element.54), channel_id=1, source_target_pairs={{4,0},{8,4},{12,8},{16,12},{20,16},{24,20},{28,24},{32,28},{36,32}... | collective-permute-start | bytes 697352 | tf_op jit(solution)/shard_map/ppermute | solution.py:263
  129.9 5.8 %collective-permute-start.15 = (bf16[227,512]{1,0:T(8,128)(2,1)}, bf16[227,512]{1,0:T(8,128)(2,1)S(1)}, u32[]{:S(2)}, u32[]{:S(2)}) collective-permute-start(bf16[227,512]{1,0:T(8,128)(2,1)} %get-tuple-element.55), channel_id=1, source_target_pairs={{0,4},{4,8},{8,12},{12,16},{16,20},{20,24},{24,28},{28,32},{32,36}... | collective-permute-start | bytes 697352 | tf_op jit(solution)/shard_map/ppermute | solution.py:258
  137.5 32.4 %all-to-all-start.2 = ((bf16[32,32,512]{2,1,0:T(8,128)(2,1)}), bf16[32,32,512]{2,1,0:T(8,128)(2,1)S(1)}, u32[]{:S(2)}, u32[]{:S(2)}) async-start(bf16[32,32,512]{2,1,0:T(8,128)(2,1)} %broadcast_in_dim.8), calls=%async_computation.2 | async-start | bytes 2097152 | tf_op jit(solution)/shard_map/all_to_all | solution.py:251
  145.2 19.3 %collective-permute-start.16 = (bf16[227,512]{1,0:T(8,128)(2,1)S(1)}, bf16[227,512]{1,0:T(8,128)(2,1)S(1)}, u32[]{:S(2)}, u32[]{:S(2)}) collective-permute-start(bf16[227,512]{1,0:T(8,128)(2,1)S(1)} %get-tuple-element.74), channel_id=1, source_target_pairs={{0,1},{1,2},{2,3},{3,0},{4,5},{5,6},{6,7},{7,4},{8,9},{9,10},{10,1... | collective-permute-start | bytes 697352 | tf_op jit(solution)/shard_map/ppermute | solution.py:280
  146.7 23.3 %collective-permute-start.17 = (bf16[227,512]{1,0:T(8,128)(2,1)S(1)}, bf16[227,512]{1,0:T(8,128)(2,1)S(1)}, u32[]{:S(2)}, u32[]{:S(2)}) collective-permute-start(bf16[227,512]{1,0:T(8,128)(2,1)S(1)} %get-tuple-element.73), channel_id=1, source_target_pairs={{0,2},{1,3},{2,0},{3,1},{4,6},{5,7},{6,4},{7,5},{8,10},{9,11},{10,... | collective-permute-start | bytes 697352 | tf_op jit(solution)/shard_map/ppermute | solution.py:280
  149.1 20.9 %collective-permute-start.18 = (bf16[227,512]{1,0:T(8,128)(2,1)S(1)}, bf16[227,512]{1,0:T(8,128)(2,1)S(1)}, u32[]{:S(2)}, u32[]{:S(2)}) collective-permute-start(bf16[227,512]{1,0:T(8,128)(2,1)S(1)} %get-tuple-element.72), channel_id=1, source_target_pairs={{0,3},{1,0},{2,1},{3,2},{4,7},{5,4},{6,5},{7,6},{8,11},{9,8},{10,9... | collective-permute-start | bytes 697352 | tf_op jit(solution)/shard_map/ppermute | solution.py:280
  (12 other events, 163.2 us)

commit v4 on v3

--- a/solution.py
+++ b/solution.py
@@ -112,12 +112,16 @@
         mesh_out_ref[...] = (mesh_ref[...].astype(F32) + total[...] * scale).astype(BF)
 
 
+def product_kernel(edge_ref, normed_ref, product_ref):
+    product_ref[...] = dot_t(normed_ref[...], edge_ref[...]).astype(BF)
+
+
 def mesh_kernel(
     mesh_scale, scale, count,
     sub_ref, band_ref, far_ref, side_ref, pay_ref, far_pay_ref, proc_ref, recv_ref, edge_ref,
-    active_ref, normed_ref, inverse_ref, bslope_ref, hidden_ref,
+    active_ref, normed_ref, product_ref, inverse_ref, bslope_ref, hidden_ref,
     out_ref, bgrad_ref, wgrad_ref,
-    receiver_all, cots, columns, lines, query_grad, upper_ref, edge_total, src_total,
+    receiver_all, cots, columns, lines, query_grad, centred_ref, upper_ref, through_ref, edge_total, src_total,
 ):
     step = pl.program_id(0)
     rows, latent = side_ref.shape
@@ -180,18 +184,21 @@
         lax.fori_loop(0, count, one, 0)
         mesh_grad = pay_ref[:rows, :latent].astype(F32) + dot_t(query_grad[...].astype(BF), proc)
         mesh_grad = mesh_grad + dot_t(receiver_grad.astype(BF), recv)
-        upper_ref[...] = mesh_grad * scale
+        upper = mesh_grad * scale
+        upper_ref[...] = upper
+        centred_ref[...] = upper - jnp.mean(upper, axis=-1, keepdims=True)
+        through_ref[...] = dot_t(centred_ref[...].astype(BF), edge_ref[...])
         edge_total[...] = jnp.zeros_like(edge_total)
         src_total[...] = jnp.zeros_like(src_total)
 
-    upper = upper_ref[...]
-    centred = upper - jnp.mean(upper, axis=-1, keepdims=True)
     normed = normed_ref[...].astype(F32).reshape(-1, rows, latent)
+    product = product_ref[...].astype(F32).reshape(-1, rows, latent)
     inverse = inverse_ref[...].reshape(-1, rows, 1)
-    along = jnp.mean(upper[None] * normed, axis=-1, keepdims=True)
-    ngrad = ((centred[None] - normed * along) * inverse).reshape(-1, latent).astype(BF)
+    along = jnp.mean(upper_ref[...][None] * normed, axis=-1, keepdims=True)
+    ngrad = ((centred_ref[...][None] - normed * along) * inverse).reshape(-1, latent).astype(BF)
     edge_total[...] += t_dot(active_ref[...], ngrad)
-    bgrad = (dot_t(ngrad, edge_ref[...]) * bslope_ref[...].astype(F32)).astype(BF)
+    bgrad = ((through_ref[...][None] - product * along) * inverse).reshape(-1, latent)
+    bgrad = (bgrad * bslope_ref[...].astype(F32)).astype(BF)
     bgrad_ref[...] = bgrad
     src_total[...] += t_dot(hidden_ref[...], bgrad)
 
@@ -312,12 +319,11 @@
     place = mesh_src - (band * width - rows)
     half = 64
     spare = jnp.zeros((rows, half - mesh_count), BF)
+    cot_then, _ = lax.optimization_barrier((cotangent, last))
     pay = jnp.concatenate(
-        [cotangent, (place // rows).astype(BF), spare, (place % rows).astype(BF), spare], axis=1
+        [cot_then, (place // rows).astype(BF), spare, (place % rows).astype(BF), spare], axis=1
     )
-    pay, _ = lax.optimization_barrier((pay, last))
     pay = jnp.concatenate([pay] + [along_sub(pay, k) for k in range(1, SUBS)])
-    far_pay = outwards(pay, True)
 
     hidden, hslope, active, bslope, normed, inverse, hidden_mesh = pl.pallas_call(
         functools.partial(forward_kernel, scale),
@@ -345,10 +351,26 @@
         name="encode",
     )(sub_scalar, grid_local, *grid, grid_low, grid_high, mesh_in, w_embed, w_src, w_dst, w_edge)
 
+    pay, _ = lax.optimization_barrier((pay, hidden_mesh))
+    far_pay = outwards(pay, True)
     mesh_band = jnp.concatenate([hidden_mesh] + [along_sub(hidden_mesh, k) for k in range(1, SUBS)])
     mesh_far = outwards(mesh_band, True)
     at = jnp.where(sub < SUBS // 2, sub, lax.rem(sub + 1, SUBS)) * rows
     mesh_side = outwards(lax.dynamic_slice_in_dim(mesh_band, at, rows), False)
+
+    normed_then, _ = lax.optimization_barrier((normed, mesh_band))
+    product = pl.pallas_call(
+        product_kernel,
+        grid=(2,),
+        in_specs=[whole((latent, latent)), tiled(edges // 2, latent)],
+        out_specs=tiled(edges // 2, latent),
+        out_shape=jax.ShapeDtypeStruct((edges, latent), BF),
+        compiler_params=params(),
+        cost_estimate=pl.CostEstimate(
+            flops=2 * edges * latent * latent, bytes_accessed=4 * edges * latent, transcendentals=0
+        ),
+        name="product",
+    )(w_edge, normed_then)
 
     mesh_out, bgrad, part = pl.pallas_call(
         functools.partial(mesh_kernel, mesh_scale, scale, mesh_count),
@@ -365,6 +387,7 @@
             whole((latent, latent)),
             tiled(tile, latent),
             tiled(tile, latent),
+            tiled(tile, latent),
             tiled(tile, 1),
             tiled(tile, latent),
             tiled(tile, latent),
@@ -382,6 +405,8 @@
             pltpu.VMEM((2 * half, 2 * width), jnp.int32),
             pltpu.VMEM((rows, latent), F32),
             pltpu.VMEM((rows, latent), F32),
+            pltpu.VMEM((rows, latent), F32),
+            pltpu.VMEM((rows, latent), F32),
             pltpu.VMEM((latent, latent), F32),
             pltpu.VMEM((latent, latent), F32),
         ],
@@ -389,7 +414,7 @@
         name="process",
     )(
         sub_scalar, mesh_band, mesh_far, mesh_side, pay, far_pay, w_proc, w_recv, w_edge,
-        active, normed, inverse, bslope, hidden,
+        active, normed, product, inverse, bslope, hidden,
     )
 
     *parts, part_low, part_high = pl.pallas_call(
@@ -412,12 +437,10 @@
 
     near = lax.axis_size(NEAR)
     pieces = lax.all_to_all(part.reshape(near, -1, latent), NEAR, 0, 0, tiled=True)
-    pieces, parts, part_low, part_high = lax.optimization_barrier((pieces, parts, part_low, part_high))
-    pieces = from_everyone(summed(pieces), FAR)
     from_above = bands_down(part_low)
     from_below = bands_up(part_high)
     pieces, from_above, from_below = lax.optimization_barrier((pieces, from_above, from_below))
-    weights = from_everyone(summed(pieces), NEAR).reshape(2 * latent, latent)
+    pieces = from_everyone(summed(pieces), FAR)
     arrived = []
     for k in range(SUBS):
         block = lax.rem(sub + k, SUBS)
@@ -425,7 +448,8 @@
         value += jnp.where(block == 0, from_below, jnp.zeros_like(from_below)).astype(F32)
         value += jnp.where(block == SUBS - 1, from_above, jnp.zeros_like(from_above)).astype(F32)
         arrived.append(along_sub(value.astype(BF), k) if k else value)
-    weights, *arrived = lax.optimization_barrier((weights, *arrived))
+    pieces, *arrived = lax.optimization_barrier((pieces, *arrived))
+    weights = from_everyone(summed(pieces), NEAR).reshape(2 * latent, latent)
     grid_grad = functools.reduce(jnp.add, [value.astype(F32) for value in arrived])
     src_grad, edge_grad = weights[latent:].astype(F32), weights[:latent].astype(F32)
     return (mesh_out, grid_grad, src_grad, edge_grad)

time: 173 us -> 178 us (1.029)
  waiting for transfers between devices: 39 us -> 34.2 us
  Pallas kernels: 50.4 us -> 54.6 us
  starting transfers between devices: 68.8 us -> 72.7 us
    all_to_all x2, waiting for transfers between devices: 0.62 us -> 15.1 us  [from_everyone(): lax.all_to_all(jnp.broadcast_to(shard[None], (devices, *shard.shape)), ax...]
    ppermute x12, waiting for transfers between devices: 26.5 us -> 13.4 us  [along_sub(): lax.ppermute(value, 'sub', [(i, (i + steps) % count) for i in range(count)])]
    all_to_all x2, starting transfers between devices: 18.7 us -> 24.2 us  [from_everyone(): lax.all_to_all(jnp.broadcast_to(shard[None], (devices, *shard.shape)), ax...]
    pallas_call x0 -> x1, Pallas kernels: none -> 4.33 us  [body(): pl.pallas_call(product_kernel, grid=(2,), in_specs=[whole((latent, latent...]
    all_to_all x1, waiting for transfers between devices: 4.22 us -> 0.01 us  [body(): lax.all_to_all(part.reshape(near, -1, latent), NEAR, 0, 0, tiled=True)]
    ppermute x3, waiting for transfers between devices: 3.48 us -> 0.01 us  [outwards(): return lax.ppermute(value, ALL, pairs)]
    ppermute x3, starting transfers between devices: 10.3 us -> 8.28 us  [outwards(): return lax.ppermute(value, ALL, pairs)]
    all_to_all x1, starting transfers between devices: 8.45 us -> 10.3 us  [body(): lax.all_to_all(part.reshape(near, -1, latent), NEAR, 0, 0, tiled=True)]
  transfers between devices with their start and end apart: 22 -> 22, of which waited for: 14 -> 8; matrix products, arithmetic and copies ran while one was open for 4% -> 5% of each run, Pallas kernels for 19% -> 9%
where the time goes in v4:
time: 178 us; the launch traced here: 177 us
  starting transfers between devices  72.7 us (41%)
  Pallas kernels  54.6 us (31%)
  waiting for transfers between devices  34.2 us (19%)
  local copies, waits for them, and re-layouts  8.31 us (5%)
  other arithmetic  6.41 us (4%)
    all_to_all x2, starting transfers between devices, from_everyone(): lax.all_to_all(jnp.broadcast_to(shard[None], (devices, *shard.shape)), ax...  24.2 us
    pallas_call x1, Pallas kernels, body(): pl.pallas_call(functools.partial(forward_kernel, scale), grid=(steps,), i...  20.7 us
    ppermute x12, starting transfers between devices, along_sub(): lax.ppermute(value, 'sub', [(i, (i + steps) % count) for i in range(count)])  17.8 us
    pallas_call x1, Pallas kernels, body(): pl.pallas_call(functools.partial(mesh_kernel, mesh_scale, scale, mesh_cou...  17.8 us
    all_to_all x2, waiting for transfers between devices, from_everyone(): lax.all_to_all(jnp.broadcast_to(shard[None], (devices, *shard.shape)), ax...  15.1 us
    ppermute x12, waiting for transfers between devices, along_sub(): lax.ppermute(value, 'sub', [(i, (i + steps) % count) for i in range(count)])  13.4 us
    pallas_call x1, Pallas kernels, body(): pl.pallas_call(grid_kernel, grid=(steps,), in_specs=[scalar(), tiled(tile...  11.8 us
    all_to_all x1, starting transfers between devices, body(): lax.all_to_all(part.reshape(near, -1, latent), NEAR, 0, 0, tiled=True)  10.3 us
  transfers between devices with their start and end apart: 22, of which 8 were waited for; matrix products, arithmetic and copies ran while one was open for 5% of the time, Pallas kernels for 9%

profile of v4, /device:TPU:1, one launch (start us, length us, event | category | flops | bytes accessed | tf_op | source)
XLA Modules:
  0.0 177.1 jit_solution(15813782347869205861)
XLA Ops:
  0.6 2.1 %collective-permute-start = (bf16[227,512]{1,0:T(8,128)(2,1)}, bf16[227,512]{1,0:T(8,128)(2,1)S(1)}, u32[]{:S(2)}, u32[]{:S(2)}) collective-permute-start(bf16[227,512]{1,0:T(8,128)(2,1)} %own_ref.1), channel_id=1, source_target_pairs={{0,1},{1,2},{2,3},{3,0},{4,5},{5,6},{6,7},{7,4},{8,9},{9,10},{10,1... | collective-permute-start | bytes 697352 | tf_op jit(solution)/shard_map/ppermute | solution.py:287
  2.7 2.5 %collective-permute-start.1 = (bf16[227,512]{1,0:T(8,128)(2,1)}, bf16[227,512]{1,0:T(8,128)(2,1)S(1)}, u32[]{:S(2)}, u32[]{:S(2)}) collective-permute-start(bf16[227,512]{1,0:T(8,128)(2,1)} %own_ref.1), channel_id=1, source_target_pairs={{0,2},{1,3},{2,0},{3,1},{4,6},{5,7},{6,4},{7,5},{8,10},{9,11},{10,... | collective-permute-start | bytes 697352 | tf_op jit(solution)/shard_map/ppermute | solution.py:287
  7.7 8.0 %collective-permute-done.1.two_ref = bf16[227,512]{1,0:T(8,128)(2,1)S(1)} collective-permute-done((bf16[227,512]{1,0:T(8,128)(2,1)}, bf16[227,512]{1,0:T(8,128)(2,1)S(1)}, u32[]{:S(2)}, u32[]{:S(2)}) %collective-permute-start.1) | collective-permute-done | bytes 232480 | tf_op jit(solution)/shard_map/ppermute | solution.py:287
  16.9 4.6 %collective-permute-start.3 = (bf16[227,512]{1,0:T(8,128)(2,1)S(1)}, bf16[227,512]{1,0:T(8,128)(2,1)S(1)}, u32[]{:S(2)}, u32[]{:S(2)}) collective-permute-start(bf16[227,512]{1,0:T(8,128)(2,1)S(1)} %get-tuple-element.61), channel_id=1, source_target_pairs={{0,4},{4,8},{8,12},{12,16},{16,20},{20,24},{24,28},{28,32},{32,36}... | collective-permute-start | bytes 697352 | tf_op jit(solution)/shard_map/ppermute | solution.py:265
  23.5 2.1 %collective-permute-start.11 = (bf16[64,640]{1,0:T(8,128)(2,1)S(1)}, bf16[64,640]{1,0:T(8,128)(2,1)S(1)}, u32[]{:S(2)}, u32[]{:S(2)}) collective-permute-start(bf16[64,640]{1,0:T(8,128)(2,1)S(1)} %concatenate.10), channel_id=1, source_target_pairs={{0,2},{1,3},{2,0},{3,1},{4,6},{5,7},{6,4},{7,5},{8,10},{9,11},{10,... | collective-permute-start | bytes 245768 | tf_op jit(solution)/shard_map/ppermute | solution.py:287
  26.9 1.9 %collective-permute-start.4 = (bf16[227,512]{1,0:T(8,128)(2,1)S(1)}, bf16[227,512]{1,0:T(8,128)(2,1)S(1)}, u32[]{:S(2)}, u32[]{:S(2)}) collective-permute-start(bf16[227,512]{1,0:T(8,128)(2,1)S(1)} %get-tuple-element.60), channel_id=1, source_target_pairs={{4,0},{8,4},{12,8},{16,12},{20,16},{24,20},{28,24},{32,28},{36,32}... | collective-permute-start | bytes 697352 | tf_op jit(solution)/shard_map/ppermute | solution.py:270
  29.6 2.3 %reshape.31.index_ref = s32[2560,1]{1,0:T(8,128)} reshape(s32[40,64]{1,0:T(8,128)S(1)} %subtract_bitcast_fusion) | data formatting | bytes 20480 | tf_op jit(solution)/shard_map/reshape | solution.py:317
  32.0 2.3 %collective-permute-done.4.high_ref = bf16[227,512]{1,0:T(8,128)(2,1)S(1)} collective-permute-done((bf16[227,512]{1,0:T(8,128)(2,1)S(1)}, bf16[227,512]{1,0:T(8,128)(2,1)S(1)}, u32[]{:S(2)}, u32[]{:S(2)}) %collective-permute-start.4) | collective-permute-done | bytes 232480 | tf_op jit(solution)/shard_map/ppermute | solution.py:270
  35.0 20.7 %encode.1 = (bf16[2560,512]{1,0:T(8,128)(2,1)}, bf16[2560,512]{1,0:T(8,128)(2,1)}, bf16[2560,512]{1,0:T(8,128)(2,1)}, bf16[2560,512]{1,0:T(8,128)(2,1)}, bf16[25...) custom-call(s32[1]{0:T(128)} %bitcast.sub_ref, s32[2560,1]{1,0:T(8,128)} %reshape.31.index_ref, ...), custom_call_target="tpu_custom_call" | custom-call | tf_op jit(solution)/shard_map/encode/pallas_call | solution.py:328
  58.5 2.6 %collective-permute-start.13 = (bf16[256,640]{1,0:T(8,128)(2,1)S(1)}, bf16[256,640]{1,0:T(8,128)(2,1)S(1)}, u32[]{:S(2)}, u32[]{:S(2)}) collective-permute-start(bf16[256,640]{1,0:T(8,128)(2,1)S(1)} %pad_maximum_fusion.pay_ref), channel_id=1, source_target_pairs={{0,4},{1,5},{4,8},{5,9},{6,2},{7,3},{8,12},{9,13},{10,6},{11,7},{1... | collective-permute-start | bytes 983048 | tf_op jit(solution)/shard_map/ppermute | solution.py:282
  62.0 3.6 %collective-permute-start.8 = (bf16[256,512]{1,0:T(8,128)(2,1)S(1)}, bf16[256,512]{1,0:T(8,128)(2,1)S(1)}, u32[]{:S(2)}, u32[]{:S(2)}) collective-permute-start(bf16[256,512]{1,0:T(8,128)(2,1)S(1)} %constant_dynamic-update-slice_fusion.band_ref), channel_id=1, source_target_pairs={{0,4},{1,5},{4,8},{5,9},{6,2},{7,3},{8,12},{9,13},{10,6},{11,7},{1... | collective-permute-start | bytes 786440 | tf_op jit(solution)/shard_map/ppermute | solution.py:282
  65.7 2.1 %collective-permute-start.9 = (bf16[64,512]{1,0:T(8,128)(2,1)S(1)}, bf16[64,512]{1,0:T(8,128)(2,1)S(1)}, u32[]{:S(2)}, u32[]{:S(2)}) collective-permute-start(bf16[64,512]{1,0:T(8,128)(2,1)S(1)} %constant_dynamic-slice_fusion), channel_id=1, source_target_pairs={{2,6},{3,7},{4,0},{5,1},{6,10},{7,11},{8,4},{9,5},{10,14},{11,15},... | collective-permute-start | bytes 196616 | tf_op jit(solution)/shard_map/ppermute | solution.py:282
  67.8 4.3 %product.1.product_ref = bf16[2560,512]{1,0:T(8,128)(2,1)} custom-call(bf16[512,512]{1,0:T(8,128)(2,1)} %edge_ref.5, bf16[2560,512]{1,0:T(8,128)(2,1)} %get-tuple-element.36.normed_ref), custom_call_target="tpu_custom_call" | custom-call | flops 1342177280 | bytes 5242880 | tf_op jit(solution)/shard_map/product/pallas_call | solution.py:362
  72.9 17.8 %process.1 = (bf16[64,512]{1,0:T(8,128)(2,1)}, bf16[2560,512]{1,0:T(8,128)(2,1)}, bf16[1024,512]{1,0:T(8,128)(2,1)}) custom-call(s32[1]{0:T(128)} %bitcast.sub_ref, bf16[256,512]{1,0:T(8,128)(2,1)} %copy-done.4, bf16[256,512]{1,0:T(8,128)(2,1)} %copy-done.6, bf16[64,512]{1,0:T(8,128)(2,1)} %copy-done.9, bf16[256,640]{1,0:T(8,128)(2,1)} %copy-done, ...), custom_call_target="tpu_custom_call" | custom-call | tf_op jit(solution)/shard_map/process/pallas_call | solution.py:375
  90.7 10.3 %all-to-all-start = ((bf16[32,32,512]{2,1,0:T(8,128)(2,1)}), bf16[32,32,512]{2,1,0:T(8,128)(2,1)S(1)}, u32[]{:S(2)}, u32[]{:S(2)}) async-start(bf16[32,32,512]{2,1,0:T(8,128)(2,1)} %bitcast.10), calls=%async_computation | async-start | bytes 2097152 | tf_op jit(solution)/shard_map/all_to_all | solution.py:439
  101.0 11.8 %channels.1 = (bf16[227,512]{1,0:T(8,128)(2,1)}, bf16[227,512]{1,0:T(8,128)(2,1)}, bf16[227,512]{1,0:T(8,128)(2,1)}, bf16[227,512]{1,0:T(8,128)(2,1)}, bf16[227,...) custom-call(s32[1]{0:T(128)} %bitcast.sub_ref, s32[2560,1]{1,0:T(8,128)} %reshape.31.index_ref, bf16[512,512]{1,0:T(8,128)(2,1)} %src_ref.3, ...), custom_call_target="tpu_custom_call" | custom-call | tf_op jit(solution)/shard_map/channels/pallas_call | solution.py:420
  112.8 2.1 %collective-permute-start.14 = (bf16[227,512]{1,0:T(8,128)(2,1)}, bf16[227,512]{1,0:T(8,128)(2,1)S(1)}, u32[]{:S(2)}, u32[]{:S(2)}) collective-permute-start(bf16[227,512]{1,0:T(8,128)(2,1)} %get-tuple-element.44), channel_id=1, source_target_pairs={{4,0},{8,4},{12,8},{16,12},{20,16},{24,20},{28,24},{32,28},{36,32}... | collective-permute-start | bytes 697352 | tf_op jit(solution)/shard_map/ppermute | solution.py:270
  115.0 3.4 %collective-permute-start.15 = (bf16[227,512]{1,0:T(8,128)(2,1)}, bf16[227,512]{1,0:T(8,128)(2,1)S(1)}, u32[]{:S(2)}, u32[]{:S(2)}) collective-permute-start(bf16[227,512]{1,0:T(8,128)(2,1)} %get-tuple-element.45), channel_id=1, source_target_pairs={{0,4},{4,8},{8,12},{12,16},{16,20},{20,24},{24,28},{28,32},{32,36}... | collective-permute-start | bytes 697352 | tf_op jit(solution)/shard_map/ppermute | solution.py:265
  118.4 2.0 %collective-permute-done.14 = bf16[227,512]{1,0:T(8,128)(2,1)S(1)} collective-permute-done((bf16[227,512]{1,0:T(8,128)(2,1)}, bf16[227,512]{1,0:T(8,128)(2,1)S(1)}, u32[]{:S(2)}, u32[]{:S(2)}) %collective-permute-start.14) | collective-permute-done | bytes 232480 | tf_op jit(solution)/shard_map/ppermute | solution.py:270
  122.6 10.5 %all-to-all-start.1 = ((bf16[8,32,512]{2,1,0:T(8,128)(2,1)}), bf16[8,32,512]{2,1,0:T(8,128)(2,1)S(1)}, u32[]{:S(2)}, u32[]{:S(2)}) async-start(bf16[8,32,512]{2,1,0:T(8,128)(2,1)} %broadcast_in_dim.7), calls=%async_computation.1 | async-start | bytes 524288 | tf_op jit(solution)/shard_map/all_to_all | solution.py:258
  136.1 2.4 %collective-permute-start.17 = (bf16[227,512]{1,0:T(8,128)(2,1)S(1)}, bf16[227,512]{1,0:T(8,128)(2,1)S(1)}, u32[]{:S(2)}, u32[]{:S(2)}) collective-permute-start(bf16[227,512]{1,0:T(8,128)(2,1)S(1)} %get-tuple-element.63), channel_id=1, source_target_pairs={{0,2},{1,3},{2,0},{3,1},{4,6},{5,7},{6,4},{7,5},{8,10},{9,11},{10,... | collective-permute-start | bytes 697352 | tf_op jit(solution)/shard_map/ppermute | solution.py:287
  141.0 3.5 %collective-permute-done.17 = bf16[227,512]{1,0:T(8,128)(2,1)S(1)} collective-permute-done((bf16[227,512]{1,0:T(8,128)(2,1)S(1)}, bf16[227,512]{1,0:T(8,128)(2,1)S(1)}, u32[]{:S(2)}, u32[]{:S(2)}) %collective-permute-start.17) | collective-permute-done | bytes 232480 | tf_op jit(solution)/shard_map/ppermute | solution.py:287
  145.6 13.7 %all-to-all-start.2 = ((bf16[32,32,512]{2,1,0:T(8,128)(2,1)}), bf16[32,32,512]{2,1,0:T(8,128)(2,1)S(1)}, u32[]{:S(2)}, u32[]{:S(2)}) async-start(bf16[32,32,512]{2,1,0:T(8,128)(2,1)} %broadcast_in_dim.8), calls=%async_computation.2 | async-start | bytes 2097152 | tf_op jit(solution)/shard_map/all_to_all | solution.py:258
  160.2 15.1 %all-to-all-done.2 = bf16[32,32,512]{2,1,0:T(8,128)(2,1)S(1)} async-done(((bf16[32,32,512]{2,1,0:T(8,128)(2,1)}), bf16[32,32,512]{2,1,0:T(8,128)(2,1)S(1)}, u32[]{:S(2)}, u32[]{:S(2)}) %all-to-all-start.2) | async-done | bytes 1048608 | tf_op jit(solution)/shard_map/all_to_all | solution.py:258
  (65 shorter events, 24.4 us)
Async XLA Ops:
  0.6 7.1 %collective-permute-start = (bf16[227,512]{1,0:T(8,128)(2,1)}, bf16[227,512]{1,0:T(8,128)(2,1)S(1)}, u32[]{:S(2)}, u32[]{:S(2)}) collective-permute-start(bf16[227,512]{1,0:T(8,128)(2,1)} %own_ref.1), channel_id=1, source_target_pairs={{0,1},{1,2},{2,3},{3,0},{4,5},{5,6},{6,7},{7,4},{8,9},{9,10},{10,1... | collective-permute-start | bytes 697352 | tf_op jit(solution)/shard_map/ppermute | solution.py:287
  2.7 12.9 %collective-permute-start.1 = (bf16[227,512]{1,0:T(8,128)(2,1)}, bf16[227,512]{1,0:T(8,128)(2,1)S(1)}, u32[]{:S(2)}, u32[]{:S(2)}) collective-permute-start(bf16[227,512]{1,0:T(8,128)(2,1)} %own_ref.1), channel_id=1, source_target_pairs={{0,2},{1,3},{2,0},{3,1},{4,6},{5,7},{6,4},{7,5},{8,10},{9,11},{10,... | collective-permute-start | bytes 697352 | tf_op jit(solution)/shard_map/ppermute | solution.py:287
  5.2 10.5 %collective-permute-start.2 = (bf16[227,512]{1,0:T(8,128)(2,1)}, bf16[227,512]{1,0:T(8,128)(2,1)S(1)}, u32[]{:S(2)}, u32[]{:S(2)}) collective-permute-start(bf16[227,512]{1,0:T(8,128)(2,1)} %own_ref.1), channel_id=1, source_target_pairs={{0,3},{1,0},{2,1},{3,2},{4,7},{5,4},{6,5},{7,6},{8,11},{9,8},{10,9... | collective-permute-start | bytes 697352 | tf_op jit(solution)/shard_map/ppermute | solution.py:287
  7.7 26.6 %copy-start.1 = (bf16[227,512]{1,0:T(8,128)(2,1)}, bf16[227,512]{1,0:T(8,128)(2,1)S(1)}, u32[]{:S(2)}) copy-start(bf16[227,512]{1,0:T(8,128)(2,1)S(1)} %collective-permute-done.one_ref) | copy-start | bytes 697348
  16.9 15.1 %collective-permute-start.3 = (bf16[227,512]{1,0:T(8,128)(2,1)S(1)}, bf16[227,512]{1,0:T(8,128)(2,1)S(1)}, u32[]{:S(2)}, u32[]{:S(2)}) collective-permute-start(bf16[227,512]{1,0:T(8,128)(2,1)S(1)} %get-tuple-element.61), channel_id=1, source_target_pairs={{0,4},{4,8},{8,12},{12,16},{16,20},{20,24},{24,28},{28,32},{32,36}... | collective-permute-start | bytes 697352 | tf_op jit(solution)/shard_map/ppermute | solution.py:265
  22.5 9.4 %collective-permute-start.10 = (bf16[64,640]{1,0:T(8,128)(2,1)S(1)}, bf16[64,640]{1,0:T(8,128)(2,1)S(1)}, u32[]{:S(2)}, u32[]{:S(2)}) collective-permute-start(bf16[64,640]{1,0:T(8,128)(2,1)S(1)} %concatenate.10), channel_id=1, source_target_pairs={{0,1},{1,2},{2,3},{3,0},{4,5},{5,6},{6,7},{7,4},{8,9},{9,10},{10,1... | collective-permute-start | bytes 245768 | tf_op jit(solution)/shard_map/ppermute | solution.py:287
  23.5 8.4 %collective-permute-start.11 = (bf16[64,640]{1,0:T(8,128)(2,1)S(1)}, bf16[64,640]{1,0:T(8,128)(2,1)S(1)}, u32[]{:S(2)}, u32[]{:S(2)}) collective-permute-start(bf16[64,640]{1,0:T(8,128)(2,1)S(1)} %concatenate.10), channel_id=1, source_target_pairs={{0,2},{1,3},{2,0},{3,1},{4,6},{5,7},{6,4},{7,5},{8,10},{9,11},{10,... | collective-permute-start | bytes 245768 | tf_op jit(solution)/shard_map/ppermute | solution.py:287
  25.6 6.3 %collective-permute-start.12 = (bf16[64,640]{1,0:T(8,128)(2,1)S(1)}, bf16[64,640]{1,0:T(8,128)(2,1)S(1)}, u32[]{:S(2)}, u32[]{:S(2)}) collective-permute-start(bf16[64,640]{1,0:T(8,128)(2,1)S(1)} %concatenate.10), channel_id=1, source_target_pairs={{0,3},{1,0},{2,1},{3,2},{4,7},{5,4},{6,5},{7,6},{8,11},{9,8},{10,9... | collective-permute-start | bytes 245768 | tf_op jit(solution)/shard_map/ppermute | solution.py:287
  26.9 7.4 %collective-permute-start.4 = (bf16[227,512]{1,0:T(8,128)(2,1)S(1)}, bf16[227,512]{1,0:T(8,128)(2,1)S(1)}, u32[]{:S(2)}, u32[]{:S(2)}) collective-permute-start(bf16[227,512]{1,0:T(8,128)(2,1)S(1)} %get-tuple-element.60), channel_id=1, source_target_pairs={{4,0},{8,4},{12,8},{16,12},{20,16},{24,20},{28,24},{32,28},{36,32}... | collective-permute-start | bytes 697352 | tf_op jit(solution)/shard_map/ppermute | solution.py:270
  32.0 33.7 %copy-start = (bf16[256,640]{1,0:T(8,128)(2,1)}, bf16[256,640]{1,0:T(8,128)(2,1)S(1)}, u32[]{:S(2)}) copy-start(bf16[256,640]{1,0:T(8,128)(2,1)S(1)} %pad_maximum_fusion.pay_ref) | copy-start | bytes 983044
  55.7 6.3 %collective-permute-start.5 = (bf16[64,512]{1,0:T(8,128)(2,1)}, bf16[64,512]{1,0:T(8,128)(2,1)S(1)}, u32[]{:S(2)}, u32[]{:S(2)}) collective-permute-start(bf16[64,512]{1,0:T(8,128)(2,1)} %get-tuple-element.31), channel_id=1, source_target_pairs={{0,1},{1,2},{2,3},{3,0},{4,5},{5,6},{6,7},{7,4},{8,9},{9,10},{10,1... | collective-permute-start | bytes 196616 | tf_op jit(solution)/shard_map/ppermute | solution.py:287
  55.9 6.0 %collective-permute-start.6 = (bf16[64,512]{1,0:T(8,128)(2,1)}, bf16[64,512]{1,0:T(8,128)(2,1)S(1)}, u32[]{:S(2)}, u32[]{:S(2)}) collective-permute-start(bf16[64,512]{1,0:T(8,128)(2,1)} %get-tuple-element.31), channel_id=1, source_target_pairs={{0,2},{1,3},{2,0},{3,1},{4,6},{5,7},{6,4},{7,5},{8,10},{9,11},{10,... | collective-permute-start | bytes 196616 | tf_op jit(solution)/shard_map/ppermute | solution.py:287
  56.9 5.0 %collective-permute-start.7 = (bf16[64,512]{1,0:T(8,128)(2,1)}, bf16[64,512]{1,0:T(8,128)(2,1)S(1)}, u32[]{:S(2)}, u32[]{:S(2)}) collective-permute-start(bf16[64,512]{1,0:T(8,128)(2,1)} %get-tuple-element.31), channel_id=1, source_target_pairs={{0,3},{1,0},{2,1},{3,2},{4,7},{5,4},{6,5},{7,6},{8,11},{9,8},{10,9... | collective-permute-start | bytes 196616 | tf_op jit(solution)/shard_map/ppermute | solution.py:287
  58.5 13.6 %collective-permute-start.13 = (bf16[256,640]{1,0:T(8,128)(2,1)S(1)}, bf16[256,640]{1,0:T(8,128)(2,1)S(1)}, u32[]{:S(2)}, u32[]{:S(2)}) collective-permute-start(bf16[256,640]{1,0:T(8,128)(2,1)S(1)} %pad_maximum_fusion.pay_ref), channel_id=1, source_target_pairs={{0,4},{1,5},{4,8},{5,9},{6,2},{7,3},{8,12},{9,13},{10,6},{11,7},{1... | collective-permute-start | bytes 983048 | tf_op jit(solution)/shard_map/ppermute | solution.py:282
  62.0 10.1 %collective-permute-start.8 = (bf16[256,512]{1,0:T(8,128)(2,1)S(1)}, bf16[256,512]{1,0:T(8,128)(2,1)S(1)}, u32[]{:S(2)}, u32[]{:S(2)}) collective-permute-start(bf16[256,512]{1,0:T(8,128)(2,1)S(1)} %constant_dynamic-update-slice_fusion.band_ref), channel_id=1, source_target_pairs={{0,4},{1,5},{4,8},{5,9},{6,2},{7,3},{8,12},{9,13},{10,6},{11,7},{1... | collective-permute-start | bytes 786440 | tf_op jit(solution)/shard_map/ppermute | solution.py:282
  65.7 6.4 %collective-permute-start.9 = (bf16[64,512]{1,0:T(8,128)(2,1)S(1)}, bf16[64,512]{1,0:T(8,128)(2,1)S(1)}, u32[]{:S(2)}, u32[]{:S(2)}) collective-permute-start(bf16[64,512]{1,0:T(8,128)(2,1)S(1)} %constant_dynamic-slice_fusion), channel_id=1, source_target_pairs={{2,6},{3,7},{4,0},{5,1},{6,10},{7,11},{8,4},{9,5},{10,14},{11,15},... | collective-permute-start | bytes 196616 | tf_op jit(solution)/shard_map/ppermute | solution.py:282
  90.7 31.0 %all-to-all-start = ((bf16[32,32,512]{2,1,0:T(8,128)(2,1)}), bf16[32,32,512]{2,1,0:T(8,128)(2,1)S(1)}, u32[]{:S(2)}, u32[]{:S(2)}) async-start(bf16[32,32,512]{2,1,0:T(8,128)(2,1)} %bitcast.10), calls=%async_computation | async-start | bytes 2097152 | tf_op jit(solution)/shard_map/all_to_all | solution.py:439
  112.8 7.6 %collective-permute-start.14 = (bf16[227,512]{1,0:T(8,128)(2,1)}, bf16[227,512]{1,0:T(8,128)(2,1)S(1)}, u32[]{:S(2)}, u32[]{:S(2)}) collective-permute-start(bf16[227,512]{1,0:T(8,128)(2,1)} %get-tuple-element.44), channel_id=1, source_target_pairs={{4,0},{8,4},{12,8},{16,12},{20,16},{24,20},{28,24},{32,28},{36,32}... | collective-permute-start | bytes 697352 | tf_op jit(solution)/shard_map/ppermute | solution.py:270
  115.0 6.8 %collective-permute-start.15 = (bf16[227,512]{1,0:T(8,128)(2,1)}, bf16[227,512]{1,0:T(8,128)(2,1)S(1)}, u32[]{:S(2)}, u32[]{:S(2)}) collective-permute-start(bf16[227,512]{1,0:T(8,128)(2,1)} %get-tuple-element.45), channel_id=1, source_target_pairs={{0,4},{4,8},{8,12},{12,16},{16,20},{20,24},{24,28},{28,32},{32,36}... | collective-permute-start | bytes 697352 | tf_op jit(solution)/shard_map/ppermute | solution.py:265
  122.6 21.9 %all-to-all-start.1 = ((bf16[8,32,512]{2,1,0:T(8,128)(2,1)}), bf16[8,32,512]{2,1,0:T(8,128)(2,1)S(1)}, u32[]{:S(2)}, u32[]{:S(2)}) async-start(bf16[8,32,512]{2,1,0:T(8,128)(2,1)} %broadcast_in_dim.7), calls=%async_computation.1 | async-start | bytes 524288 | tf_op jit(solution)/shard_map/all_to_all | solution.py:258
  134.8 6.2 %collective-permute-start.16 = (bf16[227,512]{1,0:T(8,128)(2,1)S(1)}, bf16[227,512]{1,0:T(8,128)(2,1)S(1)}, u32[]{:S(2)}, u32[]{:S(2)}) collective-permute-start(bf16[227,512]{1,0:T(8,128)(2,1)S(1)} %get-tuple-element.64), channel_id=1, source_target_pairs={{0,1},{1,2},{2,3},{3,0},{4,5},{5,6},{6,7},{7,4},{8,9},{9,10},{10,1... | collective-permute-start | bytes 697352 | tf_op jit(solution)/shard_map/ppermute | solution.py:287
  136.1 8.4 %collective-permute-start.17 = (bf16[227,512]{1,0:T(8,128)(2,1)S(1)}, bf16[227,512]{1,0:T(8,128)(2,1)S(1)}, u32[]{:S(2)}, u32[]{:S(2)}) collective-permute-start(bf16[227,512]{1,0:T(8,128)(2,1)S(1)} %get-tuple-element.63), channel_id=1, source_target_pairs={{0,2},{1,3},{2,0},{3,1},{4,6},{5,7},{6,4},{7,5},{8,10},{9,11},{10,... | collective-permute-start | bytes 697352 | tf_op jit(solution)/shard_map/ppermute | solution.py:287
  138.5 6.0 %collective-permute-start.18 = (bf16[227,512]{1,0:T(8,128)(2,1)S(1)}, bf16[227,512]{1,0:T(8,128)(2,1)S(1)}, u32[]{:S(2)}, u32[]{:S(2)}) collective-permute-start(bf16[227,512]{1,0:T(8,128)(2,1)S(1)} %get-tuple-element.62), channel_id=1, source_target_pairs={{0,3},{1,0},{2,1},{3,2},{4,7},{5,4},{6,5},{7,6},{8,11},{9,8},{10,9... | collective-permute-start | bytes 697352 | tf_op jit(solution)/shard_map/ppermute | solution.py:287
  145.6 29.7 %all-to-all-start.2 = ((bf16[32,32,512]{2,1,0:T(8,128)(2,1)}), bf16[32,32,512]{2,1,0:T(8,128)(2,1)S(1)}, u32[]{:S(2)}, u32[]{:S(2)}) async-start(bf16[32,32,512]{2,1,0:T(8,128)(2,1)} %broadcast_in_dim.8), calls=%async_computation.2 | async-start | bytes 2097152 | tf_op jit(solution)/shard_map/all_to_all | solution.py:258
  (8 other events, 52.6 us)

commit v5 on v4

--- a/solution.py
+++ b/solution.py
@@ -60,20 +60,36 @@
     return scratch[...]
 
 
+def gather_kernel(blocks, sub_ref, index_ref, *refs):
+    *sources, picked_ref, table, pad = refs
+    nodes = sources[0].shape[1]
+    sub = sub_ref[0]
+
+    @pl.when(pl.program_id(0) == 0)
+    def _():
+        for place, source in enumerate(sources):
+            table[place * nodes : (place + 1) * nodes, :] = padded_rows(source, pad).T
+
+    column = index_ref[...]
+    chosen = [
+        selection(column - (lax.rem(sub + SUBS - k, SUBS) + 1) * nodes, nodes) for k in blocks
+    ]
+    picked_ref[...] = dot(jnp.concatenate(chosen, axis=1), table[...]).astype(BF)
+
+
 def forward_kernel(
     scale,
-    sub_ref, index_ref, own_ref, one_ref, two_ref, three_ref, low_ref, high_ref,
+    sub_ref, index_ref, picked_ref, two_ref, low_ref, high_ref,
     mesh_ref, embed_ref, src_ref, dst_ref, edge_ref,
     hidden_ref, hslope_ref, active_ref, bslope_ref, normed_ref, inverse_ref, mesh_out_ref,
     table, pad, embed, dest, total,
 ):
     step = pl.program_id(0)
-    sources = (own_ref, one_ref, two_ref, three_ref, low_ref, high_ref)
+    sources = (two_ref, low_ref, high_ref)
     nodes = low_ref.shape[1]
     rows = mesh_ref.shape[0]
     sub = sub_ref[0]
-    bases = [(lax.rem(sub + SUBS - k, SUBS) + 1) * nodes for k in range(SUBS)]
-    bases += [0, (SUBS + 1) * nodes]
+    bases = [(lax.rem(sub + SUBS - 2, SUBS) + 1) * nodes, 0, (SUBS + 1) * nodes]
 
     @pl.when(step == 0)
     def _():
@@ -84,12 +100,9 @@
         total[...] = jnp.zeros_like(total)
 
     column = index_ref[...]
-    edges = column.shape[0]
-    picked = jnp.zeros((edges, table.shape[1]), F32)
-    for block, base in enumerate(bases):
-        part = table[block * nodes : (block + 1) * nodes, :]
-        picked += dot(selection(column - base, nodes), part)
-    hidden, hslope = silu_and_slope(dot(picked.astype(BF), embed[...]))
+    chosen = [selection(column - base, nodes) for base in bases]
+    picked = dot(jnp.concatenate(chosen, axis=1), table[...]).astype(BF) + picked_ref[...]
+    hidden, hslope = silu_and_slope(dot(picked, embed[...]))
     hidden = hidden.astype(BF)
     hidden_ref[...] = hidden
     hslope_ref[...] = hslope.astype(BF)
@@ -118,14 +131,16 @@
 
 def mesh_kernel(
     mesh_scale, scale, count,
-    sub_ref, band_ref, far_ref, side_ref, pay_ref, far_pay_ref, proc_ref, recv_ref, edge_ref,
+    sub_ref, band_all, far_all, side_ref, proc_ref, recv_ref, edge_ref,
     active_ref, normed_ref, product_ref, inverse_ref, bslope_ref, hidden_ref,
     out_ref, bgrad_ref, wgrad_ref,
     receiver_all, cots, columns, lines, query_grad, centred_ref, upper_ref, through_ref, edge_total, src_total,
 ):
     step = pl.program_id(0)
     rows, latent = side_ref.shape
-    wide = band_ref.shape[0]
+    wide = band_all.shape[0]
+    band_ref, far_ref = band_all.at[:, :latent], far_all.at[:, :latent]
+    pay_ref, far_pay_ref = band_all.at[:, latent:], far_all.at[:, latent:]
 
     @pl.when(step == 0)
     def _():
@@ -310,11 +325,33 @@
     mesh_scale = 1.0 / math.sqrt(mesh_count)
 
     grid = [grid_x] + [along_sub(grid_x, k) for k in range(1, SUBS)]
+    grid_local = (g2m_src - (band * (nodes * SUBS) - nodes)).T.reshape(edges, 1)
+
+    nearest = (0, 1, 3)
+    picked = pl.pallas_call(
+        functools.partial(gather_kernel, nearest),
+        grid=(2,),
+        in_specs=[scalar(), tiled(edges // 2, 1)] + [whole((channels, nodes))] * len(nearest),
+        out_specs=tiled(edges // 2, wide),
+        out_shape=jax.ShapeDtypeStruct((edges, wide), BF),
+        scratch_shapes=[
+            pltpu.VMEM((len(nearest) * nodes, wide), BF),
+            pltpu.VMEM((wide, nodes), BF),
+        ],
+        compiler_params=params(),
+        cost_estimate=pl.CostEstimate(
+            flops=2 * edges * wide * nodes * len(nearest),
+            bytes_accessed=2 * edges * wide,
+            transcendentals=0,
+        ),
+        name="gather",
+    )(sub_scalar, grid_local, *[grid[k] for k in nearest])
+
+    grid[2], picked = lax.optimization_barrier((grid[2], picked))
     last = lax.select_n(lax.rem(sub + 1, SUBS), *grid)
     first = lax.select_n(sub, *grid)
     grid_low = bands_up(last)
     grid_high = bands_down(first)
-    grid_local = (g2m_src - (band * (nodes * SUBS) - nodes)).T.reshape(edges, 1)
 
     place = mesh_src - (band * width - rows)
     half = 64
@@ -328,8 +365,8 @@
     hidden, hslope, active, bslope, normed, inverse, hidden_mesh = pl.pallas_call(
         functools.partial(forward_kernel, scale),
         grid=(steps,),
-        in_specs=[scalar(), tiled(tile, 1)]
-        + [whole((channels, nodes))] * (SUBS + 2)
+        in_specs=[scalar(), tiled(tile, 1), tiled(tile, wide)]
+        + [whole((channels, nodes))] * 3
         + [
             whole((rows, latent)),
             whole((channels, latent)),
@@ -341,7 +378,7 @@
         out_shape=[jax.ShapeDtypeStruct((edges, latent), BF)] * 5
         + [jax.ShapeDtypeStruct((edges, 1), F32), jax.ShapeDtypeStruct((rows, latent), BF)],
         scratch_shapes=[
-            pltpu.VMEM(((SUBS + 2) * nodes, wide), BF),
+            pltpu.VMEM((3 * nodes, wide), BF),
             pltpu.VMEM((wide, nodes), BF),
             pltpu.VMEM((wide, latent), BF),
             pltpu.VMEM((rows, latent), F32),
@@ -349,14 +386,13 @@
         ],
         compiler_params=params(),
         name="encode",
-    )(sub_scalar, grid_local, *grid, grid_low, grid_high, mesh_in, w_embed, w_src, w_dst, w_edge)
-
-    pay, _ = lax.optimization_barrier((pay, hidden_mesh))
-    far_pay = outwards(pay, True)
+    )(sub_scalar, grid_local, picked, grid[2], grid_low, grid_high, mesh_in, w_embed, w_src, w_dst, w_edge)
+
     mesh_band = jnp.concatenate([hidden_mesh] + [along_sub(hidden_mesh, k) for k in range(1, SUBS)])
+    mesh_band = jnp.concatenate([mesh_band, pay], axis=1)
     mesh_far = outwards(mesh_band, True)
     at = jnp.where(sub < SUBS // 2, sub, lax.rem(sub + 1, SUBS)) * rows
-    mesh_side = outwards(lax.dynamic_slice_in_dim(mesh_band, at, rows), False)
+    mesh_side = outwards(lax.dynamic_slice(mesh_band, (at, 0), (rows, latent)), False)
 
     normed_then, _ = lax.optimization_barrier((normed, mesh_band))
     product = pl.pallas_call(
@@ -377,11 +413,9 @@
         grid=(steps,),
         in_specs=[
             scalar(),
-            whole((width, latent)),
-            whole((width, latent)),
+            whole((width, 2 * latent + 2 * half)),
+            whole((width, 2 * latent + 2 * half)),
             whole((rows, latent)),
-            whole((width, latent + 2 * half)),
-            whole((width, latent + 2 * half)),
             whole((latent, latent)),
             whole((latent, latent)),
             whole((latent, latent)),
@@ -413,7 +447,7 @@
         compiler_params=params(),
         name="process",
     )(
-        sub_scalar, mesh_band, mesh_far, mesh_side, pay, far_pay, w_proc, w_recv, w_edge,
+        sub_scalar, mesh_band, mesh_far, mesh_side, w_proc, w_recv, w_edge,
         active, normed, product, inverse, bslope, hidden,
     )
 
@@ -439,16 +473,16 @@
     pieces = lax.all_to_all(part.reshape(near, -1, latent), NEAR, 0, 0, tiled=True)
     from_above = bands_down(part_low)
     from_below = bands_up(part_high)
-    pieces, from_above, from_below = lax.optimization_barrier((pieces, from_above, from_below))
-    pieces = from_everyone(summed(pieces), FAR)
-    arrived = []
+    values = []
     for k in range(SUBS):
         block = lax.rem(sub + k, SUBS)
         value = parts[k].astype(F32)
         value += jnp.where(block == 0, from_below, jnp.zeros_like(from_below)).astype(F32)
         value += jnp.where(block == SUBS - 1, from_above, jnp.zeros_like(from_above)).astype(F32)
-        arrived.append(along_sub(value.astype(BF), k) if k else value)
-    pieces, *arrived = lax.optimization_barrier((pieces, *arrived))
+        values.append(value.astype(BF) if k else value)
+    arrived = values[:1] + [along_sub(values[k], k) for k in range(1, SUBS)]
+    pieces = from_everyone(summed(pieces), FAR)
+    pieces, arrived[1], arrived[3] = lax.optimization_barrier((pieces, arrived[1], arrived[3]))
     weights = from_everyone(summed(pieces), NEAR).reshape(2 * latent, latent)
     grid_grad = functools.reduce(jnp.add, [value.astype(F32) for value in arrived])
     src_grad, edge_grad = weights[latent:].astype(F32), weights[:latent].astype(F32)

time: 178 us -> 171 us (0.961)
  waiting for transfers between devices: 34.2 us -> 28.6 us
    all_to_all x2, waiting for transfers between devices: 15.1 us -> 2.75 us  [from_everyone(): lax.all_to_all(jnp.broadcast_to(shard[None], (devices, *shard.shape)), ax...]
    ppermute x12, waiting for transfers between devices: 13.4 us -> 24.8 us  [along_sub(): lax.ppermute(value, 'sub', [(i, (i + steps) % count) for i in range(count)])]
    pallas_call x1, Pallas kernels: 20.7 us -> 15.4 us  [body(): pl.pallas_call(functools.partial(forward_kernel, scale), grid=(steps,), i...]
    pallas_call x0 -> x1, Pallas kernels: none -> 5.05 us  [body(): pl.pallas_call(functools.partial(gather_kernel, nearest), grid=(2,), in_s...]
    all_to_all x2, starting transfers between devices: 24.2 us -> 19.6 us  [from_everyone(): lax.all_to_all(jnp.broadcast_to(shard[None], (devices, *shard.shape)), ax...]
    ppermute x2, starting transfers between devices: 8.04 us -> 12.5 us  [bands_up(): return lax.ppermute(value, BAND, [(i, i + 1) for i in range(count - 1)])]
    ppermute x2, waiting for transfers between devices: 4.38 us -> 0.69 us  [bands_down(): return lax.ppermute(value, BAND, [(i + 1, i) for i in range(count - 1)])]
    ppermute x12, starting transfers between devices: 17.8 us -> 20 us  [along_sub(): lax.ppermute(value, 'sub', [(i, (i + steps) % count) for i in range(count)])]
  transfers between devices with their start and end apart: 22 -> 21, of which waited for: 8 -> 9; matrix products, arithmetic and copies ran while one was open for 5% -> 3% of each run, Pallas kernels for 9% -> 22%
where the time goes in v5:
time: 171 us; the launch traced here: 170 us
  starting transfers between devices  73.4 us (43%)
  Pallas kernels  54.4 us (32%)
  waiting for transfers between devices  28.6 us (17%)
  local copies, waits for them, and re-layouts  6.78 us (4%)
  other arithmetic  6.01 us (4%)
    ppermute x12, waiting for transfers between devices, along_sub(): lax.ppermute(value, 'sub', [(i, (i + steps) % count) for i in range(count)])  24.8 us
    ppermute x12, starting transfers between devices, along_sub(): lax.ppermute(value, 'sub', [(i, (i + steps) % count) for i in range(count)])  20 us
    all_to_all x2, starting transfers between devices, from_everyone(): lax.all_to_all(jnp.broadcast_to(shard[None], (devices, *shard.shape)), ax...  19.6 us
    pallas_call x1, Pallas kernels, body(): pl.pallas_call(functools.partial(mesh_kernel, mesh_scale, scale, mesh_cou...  17.8 us
    pallas_call x1, Pallas kernels, body(): pl.pallas_call(functools.partial(forward_kernel, scale), grid=(steps,), i...  15.4 us
    ppermute x2, starting transfers between devices, bands_up(): return lax.ppermute(value, BAND, [(i, i + 1) for i in range(count - 1)])  12.5 us
    pallas_call x1, Pallas kernels, body(): pl.pallas_call(grid_kernel, grid=(steps,), in_specs=[scalar(), tiled(tile...  11.8 us
    all_to_all x1, starting transfers between devices, body(): lax.all_to_all(part.reshape(near, -1, latent), NEAR, 0, 0, tiled=True)  10.4 us
  transfers between devices with their start and end apart: 21, of which 9 were waited for; matrix products, arithmetic and copies ran while one was open for 3% of the time, Pallas kernels for 22%

profile of v5, /device:TPU:1, one launch (start us, length us, event | category | flops | bytes accessed | tf_op | source)
XLA Modules:
  0.0 170.1 jit_solution(9867506849615105701)
XLA Ops:
  0.6 2.1 %collective-permute-start.1 = (bf16[227,512]{1,0:T(8,128)(2,1)}, bf16[227,512]{1,0:T(8,128)(2,1)S(1)}, u32[]{:S(2)}, u32[]{:S(2)}) collective-permute-start(bf16[227,512]{1,0:T(8,128)(2,1)} %refs_0_.1), channel_id=1, source_target_pairs={{0,1},{1,2},{2,3},{3,0},{4,5},{5,6},{6,7},{7,4},{8,9},{9,10},{10,1... | collective-permute-start | bytes 697352 | tf_op jit(solution)/shard_map/ppermute | solution.py:302
  6.5 2.4 %reshape.31.index_ref = s32[2560,1]{1,0:T(8,128)} reshape(s32[40,64]{1,0:T(8,128)S(1)} %subtract_bitcast_fusion) | data formatting | bytes 20480 | tf_op jit(solution)/shard_map/reshape | solution.py:328
  9.7 5.0 %gather.1.picked_ref = bf16[2560,256]{1,0:T(8,128)(2,1)} custom-call(s32[1]{0:T(128)} %bitcast.sub_ref, s32[2560,1]{1,0:T(8,128)} %reshape.31.index_ref, bf16[227,512]{1,0:T(8,128)(2,1)} %refs_0_.1, bf16[227,512]{1,0:T(8,128)(2,1)} %copy-done.5, bf16[227,512]{1,0:T(8,128)(2,1)} %copy-done.6), custom_call_target="tpu_custom_call" | custom-call | flops 2013265920 | bytes 1310720 | tf_op jit(solution)/shard_map/gather/pallas_call | solution.py:331
  16.9 8.8 %collective-permute-start.3 = (bf16[227,512]{1,0:T(8,128)(2,1)S(1)}, bf16[227,512]{1,0:T(8,128)(2,1)S(1)}, u32[]{:S(2)}, u32[]{:S(2)}) collective-permute-start(bf16[227,512]{1,0:T(8,128)(2,1)S(1)} %get-tuple-element.53), channel_id=1, source_target_pairs={{0,4},{4,8},{8,12},{12,16},{16,20},{20,24},{24,28},{28,32},{32,36}... | collective-permute-start | bytes 697352 | tf_op jit(solution)/shard_map/ppermute | solution.py:280
  25.7 1.9 %collective-permute-start.4 = (bf16[227,512]{1,0:T(8,128)(2,1)S(1)}, bf16[227,512]{1,0:T(8,128)(2,1)S(1)}, u32[]{:S(2)}, u32[]{:S(2)}) collective-permute-start(bf16[227,512]{1,0:T(8,128)(2,1)S(1)} %get-tuple-element.52), channel_id=1, source_target_pairs={{4,0},{8,4},{12,8},{16,12},{20,16},{24,20},{28,24},{32,28},{36,32}... | collective-permute-start | bytes 697352 | tf_op jit(solution)/shard_map/ppermute | solution.py:285
  27.8 3.4 %collective-permute-start.10 = (bf16[64,640]{1,0:T(8,128)(2,1)S(1)}, bf16[64,640]{1,0:T(8,128)(2,1)S(1)}, u32[]{:S(2)}, u32[]{:S(2)}) collective-permute-start(bf16[64,640]{1,0:T(8,128)(2,1)S(1)} %concatenate.13), channel_id=1, source_target_pairs={{0,3},{1,0},{2,1},{3,2},{4,7},{5,4},{6,5},{7,6},{8,11},{9,8},{10,9... | collective-permute-start | bytes 245768 | tf_op jit(solution)/shard_map/ppermute | solution.py:302
  33.8 15.4 %encode.1 = (bf16[2560,512]{1,0:T(8,128)(2,1)}, bf16[2560,512]{1,0:T(8,128)(2,1)}, bf16[2560,512]{1,0:T(8,128)(2,1)}, bf16[2560,512]{1,0:T(8,128)(2,1)}, bf16[25...) custom-call(s32[1]{0:T(128)} %bitcast.sub_ref, s32[2560,1]{1,0:T(8,128)} %reshape.31.index_ref, ...), custom_call_target="tpu_custom_call" | custom-call | tf_op jit(solution)/shard_map/encode/pallas_call | solution.py:365
  49.3 2.1 %collective-permute-start.5 = (bf16[64,512]{1,0:T(8,128)(2,1)}, bf16[64,512]{1,0:T(8,128)(2,1)S(1)}, u32[]{:S(2)}, u32[]{:S(2)}) collective-permute-start(bf16[64,512]{1,0:T(8,128)(2,1)} %get-tuple-element.29), channel_id=1, source_target_pairs={{0,1},{1,2},{2,3},{3,0},{4,5},{5,6},{6,7},{7,4},{8,9},{9,10},{10,1... | collective-permute-start | bytes 196616 | tf_op jit(solution)/shard_map/ppermute | solution.py:302
  51.3 2.5 %collective-permute-start.6 = (bf16[64,512]{1,0:T(8,128)(2,1)}, bf16[64,512]{1,0:T(8,128)(2,1)S(1)}, u32[]{:S(2)}, u32[]{:S(2)}) collective-permute-start(bf16[64,512]{1,0:T(8,128)(2,1)} %get-tuple-element.29), channel_id=1, source_target_pairs={{0,2},{1,3},{2,0},{3,1},{4,6},{5,7},{6,4},{7,5},{8,10},{9,11},{10,... | collective-permute-start | bytes 196616 | tf_op jit(solution)/shard_map/ppermute | solution.py:302
  54.5 2.6 %collective-permute-done.6 = bf16[64,512]{1,0:T(8,128)(2,1)S(1)} collective-permute-done((bf16[64,512]{1,0:T(8,128)(2,1)}, bf16[64,512]{1,0:T(8,128)(2,1)S(1)}, u32[]{:S(2)}, u32[]{:S(2)}) %collective-permute-start.6) | collective-permute-done | bytes 65568 | tf_op jit(solution)/shard_map/ppermute | solution.py:302
  58.0 4.9 %collective-permute-start.11 = (bf16[256,1152]{1,0:T(8,128)(2,1)S(1)}, bf16[256,1152]{1,0:T(8,128)(2,1)S(1)}, u32[]{:S(2)}, u32[]{:S(2)}) collective-permute-start(bf16[256,1152]{1,0:T(8,128)(2,1)S(1)} %maximum_maximum_fusion.band_all), channel_id=1, source_target_pairs={{0,4},{1,5},{4,8},{5,9},{6,2},{7,3},{8,12},{9,13},{10,6},{11,7},{1... | collective-permute-start | bytes 1769480 | tf_op jit(solution)/shard_map/ppermute | solution.py:297
  63.0 2.1 %collective-permute-start.12 = (bf16[64,512]{1,0:T(8,128)(2,1)S(1)}, bf16[64,512]{1,0:T(8,128)(2,1)S(1)}, u32[]{:S(2)}, u32[]{:S(2)}) collective-permute-start(bf16[64,512]{1,0:T(8,128)(2,1)S(1)} %constant_dynamic-slice_fusion), channel_id=1, source_target_pairs={{2,6},{3,7},{4,0},{5,1},{6,10},{7,11},{8,4},{9,5},{10,14},{11,15},... | collective-permute-start | bytes 196616 | tf_op jit(solution)/shard_map/ppermute | solution.py:297
  65.1 4.3 %product.1.product_ref = bf16[2560,512]{1,0:T(8,128)(2,1)} custom-call(bf16[512,512]{1,0:T(8,128)(2,1)} %edge_ref.5, bf16[2560,512]{1,0:T(8,128)(2,1)} %get-tuple-element.33.normed_ref), custom_call_target="tpu_custom_call" | custom-call | flops 1342177280 | bytes 5242880 | tf_op jit(solution)/shard_map/product/pallas_call | solution.py:398
  70.6 17.8 %process.1 = (bf16[64,512]{1,0:T(8,128)(2,1)}, bf16[2560,512]{1,0:T(8,128)(2,1)}, bf16[1024,512]{1,0:T(8,128)(2,1)}) custom-call(s32[1]{0:T(128)} %bitcast.sub_ref, bf16[256,1152]{1,0:T(8,128)(2,1)} %copy-done, bf16[256,1152]{1,0:T(8,128)(2,1)} %copy-done.2, bf16[64,512]{1,0:T(8,128)(2,1)} %copy-done.12, bf16[512,512]{1,0:T(8,128)(2,1)} %proc_ref.1, ...), custom_call_target="tpu_custom_call" | custom-call | tf_op jit(solution)/shard_map/process/pallas_call | solution.py:411
  88.4 10.4 %all-to-all-start = ((bf16[32,32,512]{2,1,0:T(8,128)(2,1)}), bf16[32,32,512]{2,1,0:T(8,128)(2,1)S(1)}, u32[]{:S(2)}, u32[]{:S(2)}) async-start(bf16[32,32,512]{2,1,0:T(8,128)(2,1)} %bitcast.10), calls=%async_computation | async-start | bytes 2097152 | tf_op jit(solution)/shard_map/all_to_all | solution.py:473
  98.8 11.8 %channels.1 = (bf16[227,512]{1,0:T(8,128)(2,1)}, bf16[227,512]{1,0:T(8,128)(2,1)}, bf16[227,512]{1,0:T(8,128)(2,1)}, bf16[227,512]{1,0:T(8,128)(2,1)}, bf16[227,...) custom-call(s32[1]{0:T(128)} %bitcast.sub_ref, s32[2560,1]{1,0:T(8,128)} %reshape.31.index_ref, bf16[512,512]{1,0:T(8,128)(2,1)} %src_ref.3, ...), custom_call_target="tpu_custom_call" | custom-call | tf_op jit(solution)/shard_map/channels/pallas_call | solution.py:454
  110.6 3.7 %collective-permute-start.13 = (bf16[227,512]{1,0:T(8,128)(2,1)}, bf16[227,512]{1,0:T(8,128)(2,1)S(1)}, u32[]{:S(2)}, u32[]{:S(2)}) collective-permute-start(bf16[227,512]{1,0:T(8,128)(2,1)} %get-tuple-element.41), channel_id=1, source_target_pairs={{0,4},{4,8},{8,12},{12,16},{16,20},{20,24},{24,28},{28,32},{32,36}... | collective-permute-start | bytes 697352 | tf_op jit(solution)/shard_map/ppermute | solution.py:280
  114.3 1.9 %collective-permute-start.14 = (bf16[227,512]{1,0:T(8,128)(2,1)}, bf16[227,512]{1,0:T(8,128)(2,1)S(1)}, u32[]{:S(2)}, u32[]{:S(2)}) collective-permute-start(bf16[227,512]{1,0:T(8,128)(2,1)} %get-tuple-element.42), channel_id=1, source_target_pairs={{4,0},{8,4},{12,8},{16,12},{20,16},{24,20},{28,24},{32,28},{36,32}... | collective-permute-start | bytes 697352 | tf_op jit(solution)/shard_map/ppermute | solution.py:285
  117.1 9.3 %all-to-all-start.1 = ((bf16[8,32,512]{2,1,0:T(8,128)(2,1)}), bf16[8,32,512]{2,1,0:T(8,128)(2,1)S(1)}, u32[]{:S(2)}, u32[]{:S(2)}) async-start(bf16[8,32,512]{2,1,0:T(8,128)(2,1)} %broadcast_in_dim.7), calls=%async_computation.1 | async-start | bytes 524288 | tf_op jit(solution)/shard_map/all_to_all | solution.py:273
  129.6 3.5 %collective-permute-done.15 = bf16[227,512]{1,0:T(8,128)(2,1)S(1)} collective-permute-done((bf16[227,512]{1,0:T(8,128)(2,1)S(1)}, bf16[227,512]{1,0:T(8,128)(2,1)S(1)}, u32[]{:S(2)}, u32[]{:S(2)}) %collective-permute-start.15) | collective-permute-done | bytes 232480 | tf_op jit(solution)/shard_map/ppermute | solution.py:302
  133.1 2.7 %all-to-all-done.1 = bf16[8,32,512]{2,1,0:T(8,128)(2,1)S(1)} async-done(((bf16[8,32,512]{2,1,0:T(8,128)(2,1)}), bf16[8,32,512]{2,1,0:T(8,128)(2,1)S(1)}, u32[]{:S(2)}, u32[]{:S(2)}) %all-to-all-start.1) | async-done | bytes 262176 | tf_op jit(solution)/shard_map/all_to_all | solution.py:273
  137.0 10.2 %all-to-all-start.2 = ((bf16[32,32,512]{2,1,0:T(8,128)(2,1)}), bf16[32,32,512]{2,1,0:T(8,128)(2,1)S(1)}, u32[]{:S(2)}, u32[]{:S(2)}) async-start(bf16[32,32,512]{2,1,0:T(8,128)(2,1)} %broadcast_in_dim.8), calls=%async_computation.2 | async-start | bytes 2097152 | tf_op jit(solution)/shard_map/all_to_all | solution.py:273
  147.2 3.0 %collective-permute-start.17 = (bf16[227,512]{1,0:T(8,128)(2,1)S(1)}, bf16[227,512]{1,0:T(8,128)(2,1)S(1)}, u32[]{:S(2)}, u32[]{:S(2)}) collective-permute-start(bf16[227,512]{1,0:T(8,128)(2,1)S(1)} %get-tuple-element.54), channel_id=1, source_target_pairs={{0,2},{1,3},{2,0},{3,1},{4,6},{5,7},{6,4},{7,5},{8,10},{9,11},{10,... | collective-permute-start | bytes 697352 | tf_op jit(solution)/shard_map/ppermute | solution.py:302
  150.2 17.1 %collective-permute-done.17 = bf16[227,512]{1,0:T(8,128)(2,1)S(1)} collective-permute-done((bf16[227,512]{1,0:T(8,128)(2,1)S(1)}, bf16[227,512]{1,0:T(8,128)(2,1)S(1)}, u32[]{:S(2)}, u32[]{:S(2)}) %collective-permute-start.17) | collective-permute-done | bytes 232480 | tf_op jit(solution)/shard_map/ppermute | solution.py:302
  (70 shorter events, 20.2 us)
Async XLA Ops:
  0.6 8.3 %collective-permute-start.1 = (bf16[227,512]{1,0:T(8,128)(2,1)}, bf16[227,512]{1,0:T(8,128)(2,1)S(1)}, u32[]{:S(2)}, u32[]{:S(2)}) collective-permute-start(bf16[227,512]{1,0:T(8,128)(2,1)} %refs_0_.1), channel_id=1, source_target_pairs={{0,1},{1,2},{2,3},{3,0},{4,5},{5,6},{6,7},{7,4},{8,9},{9,10},{10,1... | collective-permute-start | bytes 697352 | tf_op jit(solution)/shard_map/ppermute | solution.py:302
  2.8 6.2 %collective-permute-start.2 = (bf16[227,512]{1,0:T(8,128)(2,1)}, bf16[227,512]{1,0:T(8,128)(2,1)S(1)}, u32[]{:S(2)}, u32[]{:S(2)}) collective-permute-start(bf16[227,512]{1,0:T(8,128)(2,1)} %refs_0_.1), channel_id=1, source_target_pairs={{0,3},{1,0},{2,1},{3,2},{4,7},{5,4},{6,5},{7,6},{8,11},{9,8},{10,9... | collective-permute-start | bytes 697352 | tf_op jit(solution)/shard_map/ppermute | solution.py:302
  4.1 11.6 %collective-permute-start = (bf16[227,512]{1,0:T(8,128)(2,1)}, bf16[227,512]{1,0:T(8,128)(2,1)S(1)}, u32[]{:S(2)}, u32[]{:S(2)}) collective-permute-start(bf16[227,512]{1,0:T(8,128)(2,1)} %refs_0_.1), channel_id=1, source_target_pairs={{0,2},{1,3},{2,0},{3,1},{4,6},{5,7},{6,4},{7,5},{8,10},{9,11},{10,... | collective-permute-start | bytes 697352 | tf_op jit(solution)/shard_map/ppermute | solution.py:302
  15.7 17.5 %copy-start.1 = (bf16[227,512]{1,0:T(8,128)(2,1)}, bf16[227,512]{1,0:T(8,128)(2,1)S(1)}, u32[]{:S(2)}) copy-start(bf16[227,512]{1,0:T(8,128)(2,1)S(1)} %collective-permute-done.two_ref) | copy-start | bytes 697348
  16.9 15.6 %collective-permute-start.3 = (bf16[227,512]{1,0:T(8,128)(2,1)S(1)}, bf16[227,512]{1,0:T(8,128)(2,1)S(1)}, u32[]{:S(2)}, u32[]{:S(2)}) collective-permute-start(bf16[227,512]{1,0:T(8,128)(2,1)S(1)} %get-tuple-element.53), channel_id=1, source_target_pairs={{0,4},{4,8},{8,12},{12,16},{16,20},{20,24},{24,28},{28,32},{32,36}... | collective-permute-start | bytes 697352 | tf_op jit(solution)/shard_map/ppermute | solution.py:280
  25.7 7.4 %collective-permute-start.4 = (bf16[227,512]{1,0:T(8,128)(2,1)S(1)}, bf16[227,512]{1,0:T(8,128)(2,1)S(1)}, u32[]{:S(2)}, u32[]{:S(2)}) collective-permute-start(bf16[227,512]{1,0:T(8,128)(2,1)S(1)} %get-tuple-element.52), channel_id=1, source_target_pairs={{4,0},{8,4},{12,8},{16,12},{20,16},{24,20},{28,24},{32,28},{36,32}... | collective-permute-start | bytes 697352 | tf_op jit(solution)/shard_map/ppermute | solution.py:285
  27.8 26.0 %collective-permute-start.10 = (bf16[64,640]{1,0:T(8,128)(2,1)S(1)}, bf16[64,640]{1,0:T(8,128)(2,1)S(1)}, u32[]{:S(2)}, u32[]{:S(2)}) collective-permute-start(bf16[64,640]{1,0:T(8,128)(2,1)S(1)} %concatenate.13), channel_id=1, source_target_pairs={{0,3},{1,0},{2,1},{3,2},{4,7},{5,4},{6,5},{7,6},{8,11},{9,8},{10,9... | collective-permute-start | bytes 245768 | tf_op jit(solution)/shard_map/ppermute | solution.py:302
  31.2 22.6 %collective-permute-start.8 = (bf16[64,640]{1,0:T(8,128)(2,1)S(1)}, bf16[64,640]{1,0:T(8,128)(2,1)S(1)}, u32[]{:S(2)}, u32[]{:S(2)}) collective-permute-start(bf16[64,640]{1,0:T(8,128)(2,1)S(1)} %concatenate.13), channel_id=1, source_target_pairs={{0,1},{1,2},{2,3},{3,0},{4,5},{5,6},{6,7},{7,4},{8,9},{9,10},{10,1... | collective-permute-start | bytes 245768 | tf_op jit(solution)/shard_map/ppermute | solution.py:302
  31.2 22.6 %collective-permute-start.9 = (bf16[64,640]{1,0:T(8,128)(2,1)S(1)}, bf16[64,640]{1,0:T(8,128)(2,1)S(1)}, u32[]{:S(2)}, u32[]{:S(2)}) collective-permute-start(bf16[64,640]{1,0:T(8,128)(2,1)S(1)} %concatenate.13), channel_id=1, source_target_pairs={{0,2},{1,3},{2,0},{3,1},{4,6},{5,7},{6,4},{7,5},{8,10},{9,11},{10,... | collective-permute-start | bytes 245768 | tf_op jit(solution)/shard_map/ppermute | solution.py:302
  49.3 5.2 %collective-permute-start.5 = (bf16[64,512]{1,0:T(8,128)(2,1)}, bf16[64,512]{1,0:T(8,128)(2,1)S(1)}, u32[]{:S(2)}, u32[]{:S(2)}) collective-permute-start(bf16[64,512]{1,0:T(8,128)(2,1)} %get-tuple-element.29), channel_id=1, source_target_pairs={{0,1},{1,2},{2,3},{3,0},{4,5},{5,6},{6,7},{7,4},{8,9},{9,10},{10,1... | collective-permute-start | bytes 196616 | tf_op jit(solution)/shard_map/ppermute | solution.py:302
  51.3 5.7 %collective-permute-start.6 = (bf16[64,512]{1,0:T(8,128)(2,1)}, bf16[64,512]{1,0:T(8,128)(2,1)S(1)}, u32[]{:S(2)}, u32[]{:S(2)}) collective-permute-start(bf16[64,512]{1,0:T(8,128)(2,1)} %get-tuple-element.29), channel_id=1, source_target_pairs={{0,2},{1,3},{2,0},{3,1},{4,6},{5,7},{6,4},{7,5},{8,10},{9,11},{10,... | collective-permute-start | bytes 196616 | tf_op jit(solution)/shard_map/ppermute | solution.py:302
  53.8 3.3 %collective-permute-start.7 = (bf16[64,512]{1,0:T(8,128)(2,1)}, bf16[64,512]{1,0:T(8,128)(2,1)S(1)}, u32[]{:S(2)}, u32[]{:S(2)}) collective-permute-start(bf16[64,512]{1,0:T(8,128)(2,1)} %get-tuple-element.29), channel_id=1, source_target_pairs={{0,3},{1,0},{2,1},{3,2},{4,7},{5,4},{6,5},{7,6},{8,11},{9,8},{10,9... | collective-permute-start | bytes 196616 | tf_op jit(solution)/shard_map/ppermute | solution.py:302
  58.0 11.7 %collective-permute-start.11 = (bf16[256,1152]{1,0:T(8,128)(2,1)S(1)}, bf16[256,1152]{1,0:T(8,128)(2,1)S(1)}, u32[]{:S(2)}, u32[]{:S(2)}) collective-permute-start(bf16[256,1152]{1,0:T(8,128)(2,1)S(1)} %maximum_maximum_fusion.band_all), channel_id=1, source_target_pairs={{0,4},{1,5},{4,8},{5,9},{6,2},{7,3},{8,12},{9,13},{10,6},{11,7},{1... | collective-permute-start | bytes 1769480 | tf_op jit(solution)/shard_map/ppermute | solution.py:297
  63.0 6.4 %collective-permute-start.12 = (bf16[64,512]{1,0:T(8,128)(2,1)S(1)}, bf16[64,512]{1,0:T(8,128)(2,1)S(1)}, u32[]{:S(2)}, u32[]{:S(2)}) collective-permute-start(bf16[64,512]{1,0:T(8,128)(2,1)S(1)} %constant_dynamic-slice_fusion), channel_id=1, source_target_pairs={{2,6},{3,7},{4,0},{5,1},{6,10},{7,11},{8,4},{9,5},{10,14},{11,15},... | collective-permute-start | bytes 196616 | tf_op jit(solution)/shard_map/ppermute | solution.py:297
  88.4 27.9 %all-to-all-start = ((bf16[32,32,512]{2,1,0:T(8,128)(2,1)}), bf16[32,32,512]{2,1,0:T(8,128)(2,1)S(1)}, u32[]{:S(2)}, u32[]{:S(2)}) async-start(bf16[32,32,512]{2,1,0:T(8,128)(2,1)} %bitcast.10), calls=%async_computation | async-start | bytes 2097152 | tf_op jit(solution)/shard_map/all_to_all | solution.py:473
  110.6 15.9 %copy-start.9 = (bf16[227,512]{1,0:T(8,128)(2,1)S(1)}, bf16[227,512]{1,0:T(8,128)(2,1)}, u32[]{:S(2)}) copy-start(bf16[227,512]{1,0:T(8,128)(2,1)} %get-tuple-element.45) | copy-start | bytes 697348
  110.6 15.9 %collective-permute-start.13 = (bf16[227,512]{1,0:T(8,128)(2,1)}, bf16[227,512]{1,0:T(8,128)(2,1)S(1)}, u32[]{:S(2)}, u32[]{:S(2)}) collective-permute-start(bf16[227,512]{1,0:T(8,128)(2,1)} %get-tuple-element.41), channel_id=1, source_target_pairs={{0,4},{4,8},{8,12},{12,16},{16,20},{20,24},{24,28},{28,32},{32,36}... | collective-permute-start | bytes 697352 | tf_op jit(solution)/shard_map/ppermute | solution.py:280
  114.3 12.2 %collective-permute-start.14 = (bf16[227,512]{1,0:T(8,128)(2,1)}, bf16[227,512]{1,0:T(8,128)(2,1)S(1)}, u32[]{:S(2)}, u32[]{:S(2)}) collective-permute-start(bf16[227,512]{1,0:T(8,128)(2,1)} %get-tuple-element.42), channel_id=1, source_target_pairs={{4,0},{8,4},{12,8},{16,12},{20,16},{24,20},{28,24},{32,28},{36,32}... | collective-permute-start | bytes 697352 | tf_op jit(solution)/shard_map/ppermute | solution.py:285
  117.1 18.7 %all-to-all-start.1 = ((bf16[8,32,512]{2,1,0:T(8,128)(2,1)}), bf16[8,32,512]{2,1,0:T(8,128)(2,1)S(1)}, u32[]{:S(2)}, u32[]{:S(2)}) async-start(bf16[8,32,512]{2,1,0:T(8,128)(2,1)} %broadcast_in_dim.7), calls=%async_computation.1 | async-start | bytes 524288 | tf_op jit(solution)/shard_map/all_to_all | solution.py:273
  126.8 6.2 %collective-permute-start.15 = (bf16[227,512]{1,0:T(8,128)(2,1)S(1)}, bf16[227,512]{1,0:T(8,128)(2,1)S(1)}, u32[]{:S(2)}, u32[]{:S(2)}) collective-permute-start(bf16[227,512]{1,0:T(8,128)(2,1)S(1)} %get-tuple-element.56), channel_id=1, source_target_pairs={{0,1},{1,2},{2,3},{3,0},{4,5},{5,6},{6,7},{7,4},{8,9},{9,10},{10,1... | collective-permute-start | bytes 697352 | tf_op jit(solution)/shard_map/ppermute | solution.py:302
  128.1 5.0 %collective-permute-start.16 = (bf16[227,512]{1,0:T(8,128)(2,1)S(1)}, bf16[227,512]{1,0:T(8,128)(2,1)S(1)}, u32[]{:S(2)}, u32[]{:S(2)}) collective-permute-start(bf16[227,512]{1,0:T(8,128)(2,1)S(1)} %get-tuple-element.55), channel_id=1, source_target_pairs={{0,3},{1,0},{2,1},{3,2},{4,7},{5,4},{6,5},{7,6},{8,11},{9,8},{10,9... | collective-permute-start | bytes 697352 | tf_op jit(solution)/shard_map/ppermute | solution.py:302
  137.0 30.3 %copy-start.4 = (bf16[227,512]{1,0:T(8,128)(2,1)S(1)}, bf16[227,512]{1,0:T(8,128)(2,1)}, u32[]{:S(2)}) copy-start(bf16[227,512]{1,0:T(8,128)(2,1)} %get-tuple-element.40) | copy-start | bytes 697348
  137.0 31.3 %all-to-all-start.2 = ((bf16[32,32,512]{2,1,0:T(8,128)(2,1)}), bf16[32,32,512]{2,1,0:T(8,128)(2,1)S(1)}, u32[]{:S(2)}, u32[]{:S(2)}) async-start(bf16[32,32,512]{2,1,0:T(8,128)(2,1)} %broadcast_in_dim.8), calls=%async_computation.2 | async-start | bytes 2097152 | tf_op jit(solution)/shard_map/all_to_all | solution.py:273
  147.2 20.1 %collective-permute-start.17 = (bf16[227,512]{1,0:T(8,128)(2,1)S(1)}, bf16[227,512]{1,0:T(8,128)(2,1)S(1)}, u32[]{:S(2)}, u32[]{:S(2)}) collective-permute-start(bf16[227,512]{1,0:T(8,128)(2,1)S(1)} %get-tuple-element.54), channel_id=1, source_target_pairs={{0,2},{1,3},{2,0},{3,1},{4,6},{5,7},{6,4},{7,5},{8,10},{9,11},{10,... | collective-permute-start | bytes 697352 | tf_op jit(solution)/shard_map/ppermute | solution.py:302
  (12 other events, 74.7 us)

commit v6 on v5

--- a/solution.py
+++ b/solution.py
@@ -80,7 +80,7 @@
 def forward_kernel(
     scale,
     sub_ref, index_ref, picked_ref, two_ref, low_ref, high_ref,
-    mesh_ref, embed_ref, src_ref, dst_ref, edge_ref,
+    mesh_ref, pay_ref, embed_ref, src_ref, dst_ref, edge_ref,
     hidden_ref, hslope_ref, active_ref, bslope_ref, normed_ref, inverse_ref, mesh_out_ref,
     table, pad, embed, dest, total,
 ):
@@ -122,7 +122,9 @@
 
     @pl.when(step == pl.num_programs(0) - 1)
     def _():
-        mesh_out_ref[...] = (mesh_ref[...].astype(F32) + total[...] * scale).astype(BF)
+        latent = mesh_ref.shape[1]
+        mesh_out_ref[:, :latent] = (mesh_ref[...].astype(F32) + total[...] * scale).astype(BF)
+        mesh_out_ref[:, latent:] = pay_ref[...]
 
 
 def product_kernel(edge_ref, normed_ref, product_ref):
@@ -356,11 +358,9 @@
     place = mesh_src - (band * width - rows)
     half = 64
     spare = jnp.zeros((rows, half - mesh_count), BF)
-    cot_then, _ = lax.optimization_barrier((cotangent, last))
     pay = jnp.concatenate(
-        [cot_then, (place // rows).astype(BF), spare, (place % rows).astype(BF), spare], axis=1
+        [cotangent, (place // rows).astype(BF), spare, (place % rows).astype(BF), spare], axis=1
     )
-    pay = jnp.concatenate([pay] + [along_sub(pay, k) for k in range(1, SUBS)])
 
     hidden, hslope, active, bslope, normed, inverse, hidden_mesh = pl.pallas_call(
         functools.partial(forward_kernel, scale),
@@ -369,14 +369,18 @@
         + [whole((channels, nodes))] * 3
         + [
             whole((rows, latent)),
+            whole((rows, latent + 2 * half)),
             whole((channels, latent)),
             whole((latent, latent)),
             whole((latent, latent)),
             whole((latent, latent)),
         ],
-        out_specs=[tiled(tile, latent)] * 5 + [tiled(tile, 1), whole((rows, latent))],
+        out_specs=[tiled(tile, latent)] * 5 + [tiled(tile, 1), whole((rows, 2 * latent + 2 * half))],
         out_shape=[jax.ShapeDtypeStruct((edges, latent), BF)] * 5
-        + [jax.ShapeDtypeStruct((edges, 1), F32), jax.ShapeDtypeStruct((rows, latent), BF)],
+        + [
+            jax.ShapeDtypeStruct((edges, 1), F32),
+            jax.ShapeDtypeStruct((rows, 2 * latent + 2 * half), BF),
+        ],
         scratch_shapes=[
             pltpu.VMEM((3 * nodes, wide), BF),
             pltpu.VMEM((wide, nodes), BF),
@@ -386,10 +390,9 @@
         ],
         compiler_params=params(),
         name="encode",
-    )(sub_scalar, grid_local, picked, grid[2], grid_low, grid_high, mesh_in, w_embed, w_src, w_dst, w_edge)
+    )(sub_scalar, grid_local, picked, grid[2], grid_low, grid_high, mesh_in, pay, w_embed, w_src, w_dst, w_edge)
 
     mesh_band = jnp.concatenate([hidden_mesh] + [along_sub(hidden_mesh, k) for k in range(1, SUBS)])
-    mesh_band = jnp.concatenate([mesh_band, pay], axis=1)
     mesh_far = outwards(mesh_band, True)
     at = jnp.where(sub < SUBS // 2, sub, lax.rem(sub + 1, SUBS)) * rows
     mesh_side = outwards(lax.dynamic_slice(mesh_band, (at, 0), (rows, latent)), False)
@@ -471,20 +474,26 @@
 
     near = lax.axis_size(NEAR)
     pieces = lax.all_to_all(part.reshape(near, -1, latent), NEAR, 0, 0, tiled=True)
+    pieces, parts, part_low, part_high = lax.optimization_barrier((pieces, parts, part_low, part_high))
+    pieces = from_everyone(summed(pieces), FAR)
     from_above = bands_down(part_low)
     from_below = bands_up(part_high)
+    pieces, from_above, from_below = lax.optimization_barrier((pieces, from_above, from_below))
+    weights = from_everyone(summed(pieces), NEAR).reshape(2 * latent, latent)
     values = []
     for k in range(SUBS):
         block = lax.rem(sub + k, SUBS)
         value = parts[k].astype(F32)
         value += jnp.where(block == 0, from_below, jnp.zeros_like(from_below)).astype(F32)
         value += jnp.where(block == SUBS - 1, from_above, jnp.zeros_like(from_above)).astype(F32)
-        values.append(value.astype(BF) if k else value)
-    arrived = values[:1] + [along_sub(values[k], k) for k in range(1, SUBS)]
-    pieces = from_everyone(summed(pieces), FAR)
-    pieces, arrived[1], arrived[3] = lax.optimization_barrier((pieces, arrived[1], arrived[3]))
-    weights = from_everyone(summed(pieces), NEAR).reshape(2 * latent, latent)
-    grid_grad = functools.reduce(jnp.add, [value.astype(F32) for value in arrived])
+        values.append(value)
+    one, two = lax.optimization_barrier((values[1].astype(BF), values[2].astype(BF)))
+    ahead = along_sub(one, 1)
+    relayed = along_sub(two, -1)
+    relayed, ahead = lax.optimization_barrier((relayed, ahead))
+    behind = along_sub((values[3] + relayed.astype(F32)).astype(BF), -1)
+    weights, behind = lax.optimization_barrier((weights, behind))
+    grid_grad = values[0] + ahead.astype(F32) + behind.astype(F32)
     src_grad, edge_grad = weights[latent:].astype(F32), weights[:latent].astype(F32)
     return (mesh_out, grid_grad, src_grad, edge_grad)
 

time: 171 us -> 173 us (1.012)
  waiting for transfers between devices: 28.6 us -> 40.3 us
  starting transfers between devices: 73.4 us -> 63.1 us
    ppermute x12 -> x9, starting transfers between devices: 20 us -> 13 us  [along_sub(): lax.ppermute(value, 'sub', [(i, (i + steps) % count) for i in range(count)])]
    ppermute x2, waiting for transfers between devices: 0.69 us -> 6.75 us  [bands_down(): return lax.ppermute(value, BAND, [(i + 1, i) for i in range(count - 1)])]
    all_to_all x1, waiting for transfers between devices: 0.01 us -> 4.23 us  [body(): lax.all_to_all(part.reshape(near, -1, latent), NEAR, 0, 0, tiled=True)]
    all_to_all x2, starting transfers between devices: 19.6 us -> 16.3 us  [from_everyone(): lax.all_to_all(jnp.broadcast_to(shard[None], (devices, *shard.shape)), ax...]
    ppermute x12 -> x9, waiting for transfers between devices: 24.8 us -> 27.1 us  [along_sub(): lax.ppermute(value, 'sub', [(i, (i + steps) % count) for i in range(count)])]
    all_to_all x2, waiting for transfers between devices: 2.75 us -> 0.62 us  [from_everyone(): lax.all_to_all(jnp.broadcast_to(shard[None], (devices, *shard.shape)), ax...]
  transfers between devices with their start and end apart: 21 -> 18, of which waited for: 9 -> 15; matrix products, arithmetic and copies ran while one was open for 3% -> 3% of each run, Pallas kernels for 22% -> 12%
where the time goes in v6:
time: 173 us; the launch traced here: 172 us
  starting transfers between devices  63.1 us (36%)
  Pallas kernels  54.5 us (32%)
  waiting for transfers between devices  40.3 us (23%)
  local copies, waits for them, and re-layouts  8.28 us (5%)
  other arithmetic  5.08 us (3%)
    ppermute x9, waiting for transfers between devices, along_sub(): lax.ppermute(value, 'sub', [(i, (i + steps) % count) for i in range(count)])  27.1 us
    pallas_call x1, Pallas kernels, body(): pl.pallas_call(functools.partial(mesh_kernel, mesh_scale, scale, mesh_cou...  17.8 us
    all_to_all x2, starting transfers between devices, from_everyone(): lax.all_to_all(jnp.broadcast_to(shard[None], (devices, *shard.shape)), ax...  16.3 us
    pallas_call x1, Pallas kernels, body(): pl.pallas_call(functools.partial(forward_kernel, scale), grid=(steps,), i...  15.6 us
    ppermute x9, starting transfers between devices, along_sub(): lax.ppermute(value, 'sub', [(i, (i + steps) % count) for i in range(count)])  13 us
    pallas_call x1, Pallas kernels, body(): pl.pallas_call(grid_kernel, grid=(steps,), in_specs=[scalar(), tiled(tile...  11.8 us
    ppermute x2, starting transfers between devices, bands_up(): return lax.ppermute(value, BAND, [(i, i + 1) for i in range(count - 1)])  11.3 us
    all_to_all x1, starting transfers between devices, body(): lax.all_to_all(part.reshape(near, -1, latent), NEAR, 0, 0, tiled=True)  9.94 us
  transfers between devices with their start and end apart: 18, of which 15 were waited for; matrix products, arithmetic and copies ran while one was open for 3% of the time, Pallas kernels for 12%

profile of v6, /device:TPU:1, one launch (start us, length us, event | category | flops | bytes accessed | tf_op | source)
XLA Modules:
  0.0 172.1 jit_solution(2726501310356707733)
XLA Ops:
  0.6 2.1 %collective-permute-start.1 = (bf16[227,512]{1,0:T(8,128)(2,1)}, bf16[227,512]{1,0:T(8,128)(2,1)S(1)}, u32[]{:S(2)}, u32[]{:S(2)}) collective-permute-start(bf16[227,512]{1,0:T(8,128)(2,1)} %refs_0_.1), channel_id=1, source_target_pairs={{0,1},{1,2},{2,3},{3,0},{4,5},{5,6},{6,7},{7,4},{8,9},{9,10},{10,1... | collective-permute-start | bytes 697352 | tf_op jit(solution)/shard_map/ppermute | solution.py:304
  6.5 2.3 %reshape.26.index_ref = s32[2560,1]{1,0:T(8,128)} reshape(s32[40,64]{1,0:T(8,128)S(1)} %subtract_bitcast_fusion) | data formatting | bytes 20480 | tf_op jit(solution)/shard_map/reshape | solution.py:330
  9.6 5.1 %gather.1.picked_ref = bf16[2560,256]{1,0:T(8,128)(2,1)} custom-call(s32[1]{0:T(128)} %bitcast.sub_ref, s32[2560,1]{1,0:T(8,128)} %reshape.26.index_ref, bf16[227,512]{1,0:T(8,128)(2,1)} %refs_0_.1, bf16[227,512]{1,0:T(8,128)(2,1)} %copy-done.4, bf16[227,512]{1,0:T(8,128)(2,1)} %copy-done.5), custom_call_target="tpu_custom_call" | custom-call | flops 2013265920 | bytes 1310720 | tf_op jit(solution)/shard_map/gather/pallas_call | solution.py:333
  16.9 8.9 %collective-permute-start.3 = (bf16[227,512]{1,0:T(8,128)(2,1)S(1)}, bf16[227,512]{1,0:T(8,128)(2,1)S(1)}, u32[]{:S(2)}, u32[]{:S(2)}) collective-permute-start(bf16[227,512]{1,0:T(8,128)(2,1)S(1)} %get-tuple-element.77), channel_id=1, source_target_pairs={{0,4},{4,8},{8,12},{12,16},{16,20},{20,24},{24,28},{28,32},{32,36}... | collective-permute-start | bytes 697352 | tf_op jit(solution)/shard_map/ppermute | solution.py:282
  25.8 1.9 %collective-permute-start.4 = (bf16[227,512]{1,0:T(8,128)(2,1)S(1)}, bf16[227,512]{1,0:T(8,128)(2,1)S(1)}, u32[]{:S(2)}, u32[]{:S(2)}) collective-permute-start(bf16[227,512]{1,0:T(8,128)(2,1)S(1)} %get-tuple-element.76), channel_id=1, source_target_pairs={{4,0},{8,4},{12,8},{16,12},{20,16},{24,20},{28,24},{32,28},{36,32}... | collective-permute-start | bytes 697352 | tf_op jit(solution)/shard_map/ppermute | solution.py:287
  28.8 4.4 %collective-permute-done.4.high_ref = bf16[227,512]{1,0:T(8,128)(2,1)S(1)} collective-permute-done((bf16[227,512]{1,0:T(8,128)(2,1)S(1)}, bf16[227,512]{1,0:T(8,128)(2,1)S(1)}, u32[]{:S(2)}, u32[]{:S(2)}) %collective-permute-start.4) | collective-permute-done | bytes 232480 | tf_op jit(solution)/shard_map/ppermute | solution.py:287
  33.9 15.6 %encode.1 = (bf16[2560,512]{1,0:T(8,128)(2,1)}, bf16[2560,512]{1,0:T(8,128)(2,1)}, bf16[2560,512]{1,0:T(8,128)(2,1)}, bf16[2560,512]{1,0:T(8,128)(2,1)}, bf16[25...) custom-call(s32[1]{0:T(128)} %bitcast.sub_ref, s32[2560,1]{1,0:T(8,128)} %reshape.26.index_ref, ...), custom_call_target="tpu_custom_call" | custom-call | tf_op jit(solution)/shard_map/encode/pallas_call | solution.py:365
  49.5 4.4 %collective-permute-start.6 = (bf16[64,1152]{1,0:T(8,128)(2,1)}, bf16[64,1152]{1,0:T(8,128)(2,1)S(1)}, u32[]{:S(2)}, u32[]{:S(2)}) collective-permute-start(bf16[64,1152]{1,0:T(8,128)(2,1)} %get-tuple-element.41), channel_id=1, source_target_pairs={{0,2},{1,3},{2,0},{3,1},{4,6},{5,7},{6,4},{7,5},{8,10},{9,11},{10,... | collective-permute-start | bytes 442376 | tf_op jit(solution)/shard_map/ppermute | solution.py:304
  56.3 2.0 %collective-permute-done.6 = bf16[64,1152]{1,0:T(8,128)(2,1)S(1)} collective-permute-done((bf16[64,1152]{1,0:T(8,128)(2,1)}, bf16[64,1152]{1,0:T(8,128)(2,1)S(1)}, u32[]{:S(2)}, u32[]{:S(2)}) %collective-permute-start.6) | collective-permute-done | bytes 147488 | tf_op jit(solution)/shard_map/ppermute | solution.py:304
  58.4 5.1 %collective-permute-start.8 = (bf16[256,1152]{1,0:T(8,128)(2,1)S(1)}, bf16[256,1152]{1,0:T(8,128)(2,1)S(1)}, u32[]{:S(2)}, u32[]{:S(2)}) collective-permute-start(bf16[256,1152]{1,0:T(8,128)(2,1)S(1)} %constant_dynamic-update-slice_fusion.band_all), channel_id=1, source_target_pairs={{0,4},{1,5},{4,8},{5,9},{6,2},{7,3},{8,12},{9,13},{10,6},{11,7},{1... | collective-permute-start | bytes 1769480 | tf_op jit(solution)/shard_map/ppermute | solution.py:299
  63.6 2.1 %collective-permute-start.9 = (bf16[64,512]{1,0:T(8,128)(2,1)S(1)}, bf16[64,512]{1,0:T(8,128)(2,1)S(1)}, u32[]{:S(2)}, u32[]{:S(2)}) collective-permute-start(bf16[64,512]{1,0:T(8,128)(2,1)S(1)} %constant_dynamic-slice_fusion), channel_id=1, source_target_pairs={{2,6},{3,7},{4,0},{5,1},{6,10},{7,11},{8,4},{9,5},{10,14},{11,15},... | collective-permute-start | bytes 196616 | tf_op jit(solution)/shard_map/ppermute | solution.py:299
  65.7 4.3 %product.1.product_ref = bf16[2560,512]{1,0:T(8,128)(2,1)} custom-call(bf16[512,512]{1,0:T(8,128)(2,1)} %edge_ref.5, bf16[2560,512]{1,0:T(8,128)(2,1)} %get-tuple-element.44.normed_ref), custom_call_target="tpu_custom_call" | custom-call | flops 1342177280 | bytes 5242880 | tf_op jit(solution)/shard_map/product/pallas_call | solution.py:401
  71.2 17.8 %process.1 = (bf16[64,512]{1,0:T(8,128)(2,1)}, bf16[2560,512]{1,0:T(8,128)(2,1)}, bf16[1024,512]{1,0:T(8,128)(2,1)}) custom-call(s32[1]{0:T(128)} %bitcast.sub_ref, bf16[256,1152]{1,0:T(8,128)(2,1)} %copy-done, bf16[256,1152]{1,0:T(8,128)(2,1)} %copy-done.2, bf16[64,512]{1,0:T(8,128)(2,1)} %copy-done.12, bf16[512,512]{1,0:T(8,128)(2,1)} %proc_ref.1, ...), custom_call_target="tpu_custom_call" | custom-call | tf_op jit(solution)/shard_map/process/pallas_call | solution.py:414
  89.0 9.9 %all-to-all-start = ((bf16[32,32,512]{2,1,0:T(8,128)(2,1)}), bf16[32,32,512]{2,1,0:T(8,128)(2,1)S(1)}, u32[]{:S(2)}, u32[]{:S(2)}) async-start(bf16[32,32,512]{2,1,0:T(8,128)(2,1)} %bitcast.6), calls=%async_computation | async-start | bytes 2097152 | tf_op jit(solution)/shard_map/all_to_all | solution.py:476
  98.9 11.8 %channels.1 = (bf16[227,512]{1,0:T(8,128)(2,1)}, bf16[227,512]{1,0:T(8,128)(2,1)}, bf16[227,512]{1,0:T(8,128)(2,1)}, bf16[227,512]{1,0:T(8,128)(2,1)}, bf16[227,...) custom-call(s32[1]{0:T(128)} %bitcast.sub_ref, s32[2560,1]{1,0:T(8,128)} %reshape.26.index_ref, bf16[512,512]{1,0:T(8,128)(2,1)} %src_ref.3, ...), custom_call_target="tpu_custom_call" | custom-call | tf_op jit(solution)/shard_map/channels/pallas_call | solution.py:457
  110.7 4.2 %all-to-all-done = bf16[32,32,512]{2,1,0:T(8,128)(2,1)S(1)} async-done(((bf16[32,32,512]{2,1,0:T(8,128)(2,1)}), bf16[32,32,512]{2,1,0:T(8,128)(2,1)S(1)}, u32[]{:S(2)}, u32[]{:S(2)}) %all-to-all-start) | async-done | bytes 1048608 | tf_op jit(solution)/shard_map/all_to_all | solution.py:476
  115.8 9.0 %all-to-all-start.1 = ((bf16[8,32,512]{2,1,0:T(8,128)(2,1)}), bf16[8,32,512]{2,1,0:T(8,128)(2,1)S(1)}, u32[]{:S(2)}, u32[]{:S(2)}) async-start(bf16[8,32,512]{2,1,0:T(8,128)(2,1)} %broadcast_in_dim.7), calls=%async_computation.1 | async-start | bytes 524288 | tf_op jit(solution)/shard_map/all_to_all | solution.py:275
  124.8 3.4 %collective-permute-start.10 = (bf16[227,512]{1,0:T(8,128)(2,1)}, bf16[227,512]{1,0:T(8,128)(2,1)S(1)}, u32[]{:S(2)}, u32[]{:S(2)}) collective-permute-start(bf16[227,512]{1,0:T(8,128)(2,1)} %get-tuple-element.60), channel_id=1, source_target_pairs={{4,0},{8,4},{12,8},{16,12},{20,16},{24,20},{28,24},{32,28},{36,32}... | collective-permute-start | bytes 697352 | tf_op jit(solution)/shard_map/ppermute | solution.py:287
  128.3 2.5 %collective-permute-start.11 = (bf16[227,512]{1,0:T(8,128)(2,1)}, bf16[227,512]{1,0:T(8,128)(2,1)S(1)}, u32[]{:S(2)}, u32[]{:S(2)}) collective-permute-start(bf16[227,512]{1,0:T(8,128)(2,1)} %get-tuple-element.61), channel_id=1, source_target_pairs={{0,4},{4,8},{8,12},{12,16},{16,20},{20,24},{24,28},{28,32},{32,36}... | collective-permute-start | bytes 697352 | tf_op jit(solution)/shard_map/ppermute | solution.py:282
  130.8 2.4 %collective-permute-done.10 = bf16[227,512]{1,0:T(8,128)(2,1)S(1)} collective-permute-done((bf16[227,512]{1,0:T(8,128)(2,1)}, bf16[227,512]{1,0:T(8,128)(2,1)S(1)}, u32[]{:S(2)}, u32[]{:S(2)}) %collective-permute-start.10) | collective-permute-done | bytes 232480 | tf_op jit(solution)/shard_map/ppermute | solution.py:287
  135.9 7.3 %all-to-all-start.2 = ((bf16[32,32,512]{2,1,0:T(8,128)(2,1)}), bf16[32,32,512]{2,1,0:T(8,128)(2,1)S(1)}, u32[]{:S(2)}, u32[]{:S(2)}) async-start(bf16[32,32,512]{2,1,0:T(8,128)(2,1)} %broadcast_in_dim.8), calls=%async_computation.2 | async-start | bytes 2097152 | tf_op jit(solution)/shard_map/all_to_all | solution.py:275
  143.4 2.7 %collective-permute-start.12 = (bf16[227,512]{1,0:T(8,128)(2,1)S(1)}, bf16[227,512]{1,0:T(8,128)(2,1)S(1)}, u32[]{:S(2)}, u32[]{:S(2)}) collective-permute-start(bf16[227,512]{1,0:T(8,128)(2,1)S(1)} %get-tuple-element.66), channel_id=1, source_target_pairs={{0,3},{1,0},{2,1},{3,2},{4,7},{5,4},{6,5},{7,6},{8,11},{9,8},{10,9... | collective-permute-start | bytes 697352 | tf_op jit(solution)/shard_map/ppermute | solution.py:304
  146.1 15.6 %collective-permute-done.12 = bf16[227,512]{1,0:T(8,128)(2,1)S(1)} collective-permute-done((bf16[227,512]{1,0:T(8,128)(2,1)S(1)}, bf16[227,512]{1,0:T(8,128)(2,1)S(1)}, u32[]{:S(2)}, u32[]{:S(2)}) %collective-permute-start.12) | collective-permute-done | bytes 232480 | tf_op jit(solution)/shard_map/ppermute | solution.py:304
  163.7 5.8 %collective-permute-done.14 = bf16[227,512]{1,0:T(8,128)(2,1)S(1)} collective-permute-done((bf16[227,512]{1,0:T(8,128)(2,1)S(1)}, bf16[227,512]{1,0:T(8,128)(2,1)S(1)}, u32[]{:S(2)}, u32[]{:S(2)}) %collective-permute-start.14) | collective-permute-done | bytes 232480 | tf_op jit(solution)/shard_map/ppermute | solution.py:304
  (67 shorter events, 20.6 us)
Async XLA Ops:
  0.6 8.2 %collective-permute-start.1 = (bf16[227,512]{1,0:T(8,128)(2,1)}, bf16[227,512]{1,0:T(8,128)(2,1)S(1)}, u32[]{:S(2)}, u32[]{:S(2)}) collective-permute-start(bf16[227,512]{1,0:T(8,128)(2,1)} %refs_0_.1), channel_id=1, source_target_pairs={{0,1},{1,2},{2,3},{3,0},{4,5},{5,6},{6,7},{7,4},{8,9},{9,10},{10,1... | collective-permute-start | bytes 697352 | tf_op jit(solution)/shard_map/ppermute | solution.py:304
  2.7 6.2 %collective-permute-start.2 = (bf16[227,512]{1,0:T(8,128)(2,1)}, bf16[227,512]{1,0:T(8,128)(2,1)S(1)}, u32[]{:S(2)}, u32[]{:S(2)}) collective-permute-start(bf16[227,512]{1,0:T(8,128)(2,1)} %refs_0_.1), channel_id=1, source_target_pairs={{0,3},{1,0},{2,1},{3,2},{4,7},{5,4},{6,5},{7,6},{8,11},{9,8},{10,9... | collective-permute-start | bytes 697352 | tf_op jit(solution)/shard_map/ppermute | solution.py:304
  4.1 11.6 %collective-permute-start = (bf16[227,512]{1,0:T(8,128)(2,1)}, bf16[227,512]{1,0:T(8,128)(2,1)S(1)}, u32[]{:S(2)}, u32[]{:S(2)}) collective-permute-start(bf16[227,512]{1,0:T(8,128)(2,1)} %refs_0_.1), channel_id=1, source_target_pairs={{0,2},{1,3},{2,0},{3,1},{4,6},{5,7},{6,4},{7,5},{8,10},{9,11},{10,... | collective-permute-start | bytes 697352 | tf_op jit(solution)/shard_map/ppermute | solution.py:304
  9.6 18.1 %copy-start.14 = (s32[64,6]{0,1:T(8,128)S(1)}, s32[64,6]{0,1:T(8,128)}, u32[]{:S(2)}) copy-start(s32[64,6]{0,1:T(8,128)} %param.20) | copy-start | bytes 4612
  9.6 18.2 %copy-start.13 = (bf16[64,512]{1,0:T(8,128)(2,1)S(1)}, bf16[64,512]{1,0:T(8,128)(2,1)}, u32[]{:S(2)}) copy-start(bf16[64,512]{1,0:T(8,128)(2,1)} %param.21) | copy-start | bytes 196612
  16.9 11.9 %collective-permute-start.3 = (bf16[227,512]{1,0:T(8,128)(2,1)S(1)}, bf16[227,512]{1,0:T(8,128)(2,1)S(1)}, u32[]{:S(2)}, u32[]{:S(2)}) collective-permute-start(bf16[227,512]{1,0:T(8,128)(2,1)S(1)} %get-tuple-element.77), channel_id=1, source_target_pairs={{0,4},{4,8},{8,12},{12,16},{16,20},{20,24},{24,28},{28,32},{32,36}... | collective-permute-start | bytes 697352 | tf_op jit(solution)/shard_map/ppermute | solution.py:282
  25.8 7.4 %collective-permute-start.4 = (bf16[227,512]{1,0:T(8,128)(2,1)S(1)}, bf16[227,512]{1,0:T(8,128)(2,1)S(1)}, u32[]{:S(2)}, u32[]{:S(2)}) collective-permute-start(bf16[227,512]{1,0:T(8,128)(2,1)S(1)} %get-tuple-element.76), channel_id=1, source_target_pairs={{4,0},{8,4},{12,8},{16,12},{20,16},{24,20},{28,24},{32,28},{36,32}... | collective-permute-start | bytes 697352 | tf_op jit(solution)/shard_map/ppermute | solution.py:287
  49.4 6.9 %collective-permute-start.5 = (bf16[64,1152]{1,0:T(8,128)(2,1)}, bf16[64,1152]{1,0:T(8,128)(2,1)S(1)}, u32[]{:S(2)}, u32[]{:S(2)}) collective-permute-start(bf16[64,1152]{1,0:T(8,128)(2,1)} %get-tuple-element.41), channel_id=1, source_target_pairs={{0,1},{1,2},{2,3},{3,0},{4,5},{5,6},{6,7},{7,4},{8,9},{9,10},{10,1... | collective-permute-start | bytes 442376 | tf_op jit(solution)/shard_map/ppermute | solution.py:304
  49.5 8.8 %collective-permute-start.6 = (bf16[64,1152]{1,0:T(8,128)(2,1)}, bf16[64,1152]{1,0:T(8,128)(2,1)S(1)}, u32[]{:S(2)}, u32[]{:S(2)}) collective-permute-start(bf16[64,1152]{1,0:T(8,128)(2,1)} %get-tuple-element.41), channel_id=1, source_target_pairs={{0,2},{1,3},{2,0},{3,1},{4,6},{5,7},{6,4},{7,5},{8,10},{9,11},{10,... | collective-permute-start | bytes 442376 | tf_op jit(solution)/shard_map/ppermute | solution.py:304
  54.0 4.4 %collective-permute-start.7 = (bf16[64,1152]{1,0:T(8,128)(2,1)}, bf16[64,1152]{1,0:T(8,128)(2,1)S(1)}, u32[]{:S(2)}, u32[]{:S(2)}) collective-permute-start(bf16[64,1152]{1,0:T(8,128)(2,1)} %get-tuple-element.41), channel_id=1, source_target_pairs={{0,3},{1,0},{2,1},{3,2},{4,7},{5,4},{6,5},{7,6},{8,11},{9,8},{10,9... | collective-permute-start | bytes 442376 | tf_op jit(solution)/shard_map/ppermute | solution.py:304
  58.4 11.9 %collective-permute-start.8 = (bf16[256,1152]{1,0:T(8,128)(2,1)S(1)}, bf16[256,1152]{1,0:T(8,128)(2,1)S(1)}, u32[]{:S(2)}, u32[]{:S(2)}) collective-permute-start(bf16[256,1152]{1,0:T(8,128)(2,1)S(1)} %constant_dynamic-update-slice_fusion.band_all), channel_id=1, source_target_pairs={{0,4},{1,5},{4,8},{5,9},{6,2},{7,3},{8,12},{9,13},{10,6},{11,7},{1... | collective-permute-start | bytes 1769480 | tf_op jit(solution)/shard_map/ppermute | solution.py:299
  63.6 6.4 %collective-permute-start.9 = (bf16[64,512]{1,0:T(8,128)(2,1)S(1)}, bf16[64,512]{1,0:T(8,128)(2,1)S(1)}, u32[]{:S(2)}, u32[]{:S(2)}) collective-permute-start(bf16[64,512]{1,0:T(8,128)(2,1)S(1)} %constant_dynamic-slice_fusion), channel_id=1, source_target_pairs={{2,6},{3,7},{4,0},{5,1},{6,10},{7,11},{8,4},{9,5},{10,14},{11,15},... | collective-permute-start | bytes 196616 | tf_op jit(solution)/shard_map/ppermute | solution.py:299
  89.0 26.0 %all-to-all-start = ((bf16[32,32,512]{2,1,0:T(8,128)(2,1)}), bf16[32,32,512]{2,1,0:T(8,128)(2,1)S(1)}, u32[]{:S(2)}, u32[]{:S(2)}) async-start(bf16[32,32,512]{2,1,0:T(8,128)(2,1)} %bitcast.6), calls=%async_computation | async-start | bytes 2097152 | tf_op jit(solution)/shard_map/all_to_all | solution.py:476
  114.9 28.2 %copy-start.8 = (bf16[227,512]{1,0:T(8,128)(2,1)S(1)}, bf16[227,512]{1,0:T(8,128)(2,1)}, u32[]{:S(2)}) copy-start(bf16[227,512]{1,0:T(8,128)(2,1)} %get-tuple-element.64) | copy-start | bytes 697348
  114.9 28.2 %copy-start.9 = (bf16[227,512]{1,0:T(8,128)(2,1)S(1)}, bf16[227,512]{1,0:T(8,128)(2,1)}, u32[]{:S(2)}) copy-start(bf16[227,512]{1,0:T(8,128)(2,1)} %get-tuple-element.65) | copy-start | bytes 697348
  115.8 47.1 %copy-start.7 = (bf16[227,512]{1,0:T(8,128)(2,1)S(1)}, bf16[227,512]{1,0:T(8,128)(2,1)}, u32[]{:S(2)}) copy-start(bf16[227,512]{1,0:T(8,128)(2,1)} %get-tuple-element.70) | copy-start | bytes 697348
  115.8 18.9 %all-to-all-start.1 = ((bf16[8,32,512]{2,1,0:T(8,128)(2,1)}), bf16[8,32,512]{2,1,0:T(8,128)(2,1)S(1)}, u32[]{:S(2)}, u32[]{:S(2)}) async-start(bf16[8,32,512]{2,1,0:T(8,128)(2,1)} %broadcast_in_dim.7), calls=%async_computation.1 | async-start | bytes 524288 | tf_op jit(solution)/shard_map/all_to_all | solution.py:275
  124.8 8.3 %collective-permute-start.10 = (bf16[227,512]{1,0:T(8,128)(2,1)}, bf16[227,512]{1,0:T(8,128)(2,1)S(1)}, u32[]{:S(2)}, u32[]{:S(2)}) collective-permute-start(bf16[227,512]{1,0:T(8,128)(2,1)} %get-tuple-element.60), channel_id=1, source_target_pairs={{4,0},{8,4},{12,8},{16,12},{20,16},{24,20},{28,24},{32,28},{36,32}... | collective-permute-start | bytes 697352 | tf_op jit(solution)/shard_map/ppermute | solution.py:287
  128.3 5.8 %collective-permute-start.11 = (bf16[227,512]{1,0:T(8,128)(2,1)}, bf16[227,512]{1,0:T(8,128)(2,1)S(1)}, u32[]{:S(2)}, u32[]{:S(2)}) collective-permute-start(bf16[227,512]{1,0:T(8,128)(2,1)} %get-tuple-element.61), channel_id=1, source_target_pairs={{0,4},{4,8},{8,12},{12,16},{16,20},{20,24},{24,28},{28,32},{32,36}... | collective-permute-start | bytes 697352 | tf_op jit(solution)/shard_map/ppermute | solution.py:282
  135.9 33.7 %all-to-all-start.2 = ((bf16[32,32,512]{2,1,0:T(8,128)(2,1)}), bf16[32,32,512]{2,1,0:T(8,128)(2,1)S(1)}, u32[]{:S(2)}, u32[]{:S(2)}) async-start(bf16[32,32,512]{2,1,0:T(8,128)(2,1)} %broadcast_in_dim.8), calls=%async_computation.2 | async-start | bytes 2097152 | tf_op jit(solution)/shard_map/all_to_all | solution.py:275
  143.2 28.0 %copy-start.6 = (bf16[227,512]{1,0:T(8,128)(2,1)S(1)}, bf16[227,512]{1,0:T(8,128)(2,1)}, u32[]{:S(2)}) copy-start(bf16[227,512]{1,0:T(8,128)(2,1)} %get-tuple-element.58) | copy-start | bytes 697348
  143.4 18.3 %collective-permute-start.12 = (bf16[227,512]{1,0:T(8,128)(2,1)S(1)}, bf16[227,512]{1,0:T(8,128)(2,1)S(1)}, u32[]{:S(2)}, u32[]{:S(2)}) collective-permute-start(bf16[227,512]{1,0:T(8,128)(2,1)S(1)} %get-tuple-element.66), channel_id=1, source_target_pairs={{0,3},{1,0},{2,1},{3,2},{4,7},{5,4},{6,5},{7,6},{8,11},{9,8},{10,9... | collective-permute-start | bytes 697352 | tf_op jit(solution)/shard_map/ppermute | solution.py:304
  146.1 16.9 %collective-permute-start.13 = (bf16[227,512]{1,0:T(8,128)(2,1)S(1)}, bf16[227,512]{1,0:T(8,128)(2,1)S(1)}, u32[]{:S(2)}, u32[]{:S(2)}) collective-permute-start(bf16[227,512]{1,0:T(8,128)(2,1)S(1)} %get-tuple-element.67), channel_id=1, source_target_pairs={{0,1},{1,2},{2,3},{3,0},{4,5},{5,6},{6,7},{7,4},{8,9},{9,10},{10,1... | collective-permute-start | bytes 697352 | tf_op jit(solution)/shard_map/ppermute | solution.py:304
  163.1 6.5 %collective-permute-start.14 = (bf16[227,512]{1,0:T(8,128)(2,1)S(1)}, bf16[227,512]{1,0:T(8,128)(2,1)S(1)}, u32[]{:S(2)}, u32[]{:S(2)}) collective-permute-start(bf16[227,512]{1,0:T(8,128)(2,1)S(1)} %add_convert_fusion), channel_id=1, source_target_pairs={{0,3},{1,0},{2,1},{3,2},{4,7},{5,4},{6,5},{7,6},{8,11},{9,8},{10,9... | collective-permute-start | bytes 697352 | tf_op jit(solution)/shard_map/ppermute | solution.py:304
  (9 other events, 43.1 us)

commit v7 on v5

--- a/solution.py
+++ b/solution.py
@@ -125,16 +125,12 @@
         mesh_out_ref[...] = (mesh_ref[...].astype(F32) + total[...] * scale).astype(BF)
 
 
-def product_kernel(edge_ref, normed_ref, product_ref):
-    product_ref[...] = dot_t(normed_ref[...], edge_ref[...]).astype(BF)
-
-
 def mesh_kernel(
     mesh_scale, scale, count,
     sub_ref, band_all, far_all, side_ref, proc_ref, recv_ref, edge_ref,
-    active_ref, normed_ref, product_ref, inverse_ref, bslope_ref, hidden_ref,
+    active_ref, normed_ref, inverse_ref, bslope_ref, hidden_ref,
     out_ref, bgrad_ref, wgrad_ref,
-    receiver_all, cots, columns, lines, query_grad, centred_ref, upper_ref, through_ref, edge_total, src_total,
+    receiver_all, cots, columns, lines, query_grad, centred_ref, upper_ref, edge_total, src_total,
 ):
     step = pl.program_id(0)
     rows, latent = side_ref.shape
@@ -202,18 +198,15 @@
         upper = mesh_grad * scale
         upper_ref[...] = upper
         centred_ref[...] = upper - jnp.mean(upper, axis=-1, keepdims=True)
-        through_ref[...] = dot_t(centred_ref[...].astype(BF), edge_ref[...])
         edge_total[...] = jnp.zeros_like(edge_total)
         src_total[...] = jnp.zeros_like(src_total)
 
     normed = normed_ref[...].astype(F32).reshape(-1, rows, latent)
-    product = product_ref[...].astype(F32).reshape(-1, rows, latent)
     inverse = inverse_ref[...].reshape(-1, rows, 1)
     along = jnp.mean(upper_ref[...][None] * normed, axis=-1, keepdims=True)
     ngrad = ((centred_ref[...][None] - normed * along) * inverse).reshape(-1, latent).astype(BF)
     edge_total[...] += t_dot(active_ref[...], ngrad)
-    bgrad = ((through_ref[...][None] - product * along) * inverse).reshape(-1, latent)
-    bgrad = (bgrad * bslope_ref[...].astype(F32)).astype(BF)
+    bgrad = (dot_t(ngrad, edge_ref[...]) * bslope_ref[...].astype(F32)).astype(BF)
     bgrad_ref[...] = bgrad
     src_total[...] += t_dot(hidden_ref[...], bgrad)
 
@@ -356,11 +349,15 @@
     place = mesh_src - (band * width - rows)
     half = 64
     spare = jnp.zeros((rows, half - mesh_count), BF)
-    cot_then, _ = lax.optimization_barrier((cotangent, last))
     pay = jnp.concatenate(
-        [cot_then, (place // rows).astype(BF), spare, (place % rows).astype(BF), spare], axis=1
+        [cotangent, (place // rows).astype(BF), spare, (place % rows).astype(BF), spare], axis=1
     )
-    pay = jnp.concatenate([pay] + [along_sub(pay, k) for k in range(1, SUBS)])
+    pay = jnp.broadcast_to(pay[None], (SUBS, *pay.shape))
+    pay, grid_low, grid_high = lax.optimization_barrier((pay, grid_low, grid_high))
+    pay = lax.all_to_all(pay, "sub", 0, 0, tiled=True)
+    pay = jnp.concatenate(
+        [lax.dynamic_index_in_dim(pay, lax.rem(sub + SUBS - k, SUBS), 0, False) for k in range(SUBS)]
+    )
 
     hidden, hslope, active, bslope, normed, inverse, hidden_mesh = pl.pallas_call(
         functools.partial(forward_kernel, scale),
@@ -394,20 +391,6 @@
     at = jnp.where(sub < SUBS // 2, sub, lax.rem(sub + 1, SUBS)) * rows
     mesh_side = outwards(lax.dynamic_slice(mesh_band, (at, 0), (rows, latent)), False)
 
-    normed_then, _ = lax.optimization_barrier((normed, mesh_band))
-    product = pl.pallas_call(
-        product_kernel,
-        grid=(2,),
-        in_specs=[whole((latent, latent)), tiled(edges // 2, latent)],
-        out_specs=tiled(edges // 2, latent),
-        out_shape=jax.ShapeDtypeStruct((edges, latent), BF),
-        compiler_params=params(),
-        cost_estimate=pl.CostEstimate(
-            flops=2 * edges * latent * latent, bytes_accessed=4 * edges * latent, transcendentals=0
-        ),
-        name="product",
-    )(w_edge, normed_then)
-
     mesh_out, bgrad, part = pl.pallas_call(
         functools.partial(mesh_kernel, mesh_scale, scale, mesh_count),
         grid=(steps,),
@@ -421,7 +404,6 @@
             whole((latent, latent)),
             tiled(tile, latent),
             tiled(tile, latent),
-            tiled(tile, latent),
             tiled(tile, 1),
             tiled(tile, latent),
             tiled(tile, latent),
@@ -440,7 +422,6 @@
             pltpu.VMEM((rows, latent), F32),
             pltpu.VMEM((rows, latent), F32),
             pltpu.VMEM((rows, latent), F32),
-            pltpu.VMEM((rows, latent), F32),
             pltpu.VMEM((latent, latent), F32),
             pltpu.VMEM((latent, latent), F32),
         ],
@@ -448,7 +429,7 @@
         name="process",
     )(
         sub_scalar, mesh_band, mesh_far, mesh_side, w_proc, w_recv, w_edge,
-        active, normed, product, inverse, bslope, hidden,
+        active, normed, inverse, bslope, hidden,
     )
 
     *parts, part_low, part_high = pl.pallas_call(
@@ -480,11 +461,14 @@
         value += jnp.where(block == 0, from_below, jnp.zeros_like(from_below)).astype(F32)
         value += jnp.where(block == SUBS - 1, from_above, jnp.zeros_like(from_above)).astype(F32)
         values.append(value.astype(BF) if k else value)
-    arrived = values[:1] + [along_sub(values[k], k) for k in range(1, SUBS)]
+    ahead = along_sub(values[1], 1)
+    relayed = along_sub(values[2], -1)
     pieces = from_everyone(summed(pieces), FAR)
-    pieces, arrived[1], arrived[3] = lax.optimization_barrier((pieces, arrived[1], arrived[3]))
+    pieces, ahead, relayed = lax.optimization_barrier((pieces, ahead, relayed))
+    behind = along_sub((values[3].astype(F32) + relayed.astype(F32)).astype(BF), -1)
     weights = from_everyone(summed(pieces), NEAR).reshape(2 * latent, latent)
-    grid_grad = functools.reduce(jnp.add, [value.astype(F32) for value in arrived])
+    weights, behind = lax.optimization_barrier((weights, behind))
+    grid_grad = values[0] + ahead.astype(F32) + behind.astype(F32)
     src_grad, edge_grad = weights[latent:].astype(F32), weights[:latent].astype(F32)
     return (mesh_out, grid_grad, src_grad, edge_grad)
 

time: 171 us -> 173 us (1.012)
  waiting for transfers between devices: 28.6 us -> 35.3 us
  Pallas kernels: 54.4 us -> 50.3 us
    all_to_all x0 -> x1, starting transfers between devices: none -> 4.55 us  [body(): pay = lax.all_to_all(pay, 'sub', 0, 0, tiled=True)]
    ppermute x12 -> x9, starting transfers between devices: 20 us -> 15.6 us  [along_sub(): lax.ppermute(value, 'sub', [(i, (i + steps) % count) for i in range(count)])]
    ppermute x2, waiting for transfers between devices: 0.33 us -> 4.66 us  [outwards(): return lax.ppermute(value, ALL, pairs)]
    pallas_call x1 -> x0, Pallas kernels: 4.33 us -> none  [body(): pl.pallas_call(product_kernel, grid=(2,), in_specs=[whole((latent, latent...]
    ppermute x2, waiting for transfers between devices: 0.69 us -> 4.4 us  [bands_down(): return lax.ppermute(value, BAND, [(i + 1, i) for i in range(count - 1)])]
    ppermute x12 -> x9, waiting for transfers between devices: 24.8 us -> 22.4 us  [along_sub(): lax.ppermute(value, 'sub', [(i, (i + steps) % count) for i in range(count)])]
  transfers between devices with their start and end apart: 21 -> 19, of which waited for: 9 -> 11; matrix products, arithmetic and copies ran while one was open for 3% -> 3% of each run, Pallas kernels for 22% -> 19%
where the time goes in v7:
time: 173 us; the launch traced here: 172 us
  starting transfers between devices  73.3 us (42%)
  Pallas kernels  50.3 us (29%)
  waiting for transfers between devices  35.3 us (20%)
  local copies, waits for them, and re-layouts  6.76 us (4%)
  other arithmetic  5.97 us (3%)
    ppermute x9, waiting for transfers between devices, along_sub(): lax.ppermute(value, 'sub', [(i, (i + steps) % count) for i in range(count)])  22.4 us
    all_to_all x2, starting transfers between devices, from_everyone(): lax.all_to_all(jnp.broadcast_to(shard[None], (devices, *shard.shape)), ax...  19.3 us
    pallas_call x1, Pallas kernels, body(): pl.pallas_call(functools.partial(mesh_kernel, mesh_scale, scale, mesh_cou...  18 us
    ppermute x9, starting transfers between devices, along_sub(): lax.ppermute(value, 'sub', [(i, (i + steps) % count) for i in range(count)])  15.6 us
    pallas_call x1, Pallas kernels, body(): pl.pallas_call(functools.partial(forward_kernel, scale), grid=(steps,), i...  15.4 us
    ppermute x2, starting transfers between devices, bands_up(): return lax.ppermute(value, BAND, [(i, i + 1) for i in range(count - 1)])  12.5 us
    pallas_call x1, Pallas kernels, body(): pl.pallas_call(grid_kernel, grid=(steps,), in_specs=[scalar(), tiled(tile...  11.8 us
    all_to_all x1, starting transfers between devices, body(): lax.all_to_all(part.reshape(near, -1, latent), NEAR, 0, 0, tiled=True)  10.8 us
  transfers between devices with their start and end apart: 19, of which 11 were waited for; matrix products, arithmetic and copies ran while one was open for 3% of the time, Pallas kernels for 19%

profile of v7, /device:TPU:1, one launch (start us, length us, event | category | flops | bytes accessed | tf_op | source)
XLA Modules:
  0.0 172.4 jit_solution(7096064300807708299)
XLA Ops:
  0.6 2.1 %collective-permute-start.1 = (bf16[227,512]{1,0:T(8,128)(2,1)}, bf16[227,512]{1,0:T(8,128)(2,1)S(1)}, u32[]{:S(2)}, u32[]{:S(2)}) collective-permute-start(bf16[227,512]{1,0:T(8,128)(2,1)} %refs_0_.1), channel_id=1, source_target_pairs={{0,1},{1,2},{2,3},{3,0},{4,5},{5,6},{6,7},{7,4},{8,9},{9,10},{10,1... | collective-permute-start | bytes 697352 | tf_op jit(solution)/shard_map/ppermute | solution.py:295
  4.1 1.6 collective-permute-start
  6.5 2.4 %reshape.27.index_ref = s32[2560,1]{1,0:T(8,128)} reshape(s32[40,64]{1,0:T(8,128)S(1)} %subtract_bitcast_fusion) | data formatting | bytes 20480 | tf_op jit(solution)/shard_map/reshape | solution.py:321
  9.6 5.1 %gather.1.picked_ref = bf16[2560,256]{1,0:T(8,128)(2,1)} custom-call(s32[1]{0:T(128)} %bitcast.sub_ref, s32[2560,1]{1,0:T(8,128)} %reshape.27.index_ref, bf16[227,512]{1,0:T(8,128)(2,1)} %refs_0_.1, bf16[227,512]{1,0:T(8,128)(2,1)} %copy-done.4, bf16[227,512]{1,0:T(8,128)(2,1)} %copy-done.5), custom_call_target="tpu_custom_call" | custom-call | flops 2013265920 | bytes 1310720 | tf_op jit(solution)/shard_map/gather/pallas_call | solution.py:324
  16.9 8.9 %collective-permute-start.3 = (bf16[227,512]{1,0:T(8,128)(2,1)S(1)}, bf16[227,512]{1,0:T(8,128)(2,1)S(1)}, u32[]{:S(2)}, u32[]{:S(2)}) collective-permute-start(bf16[227,512]{1,0:T(8,128)(2,1)S(1)} %get-tuple-element.59), channel_id=1, source_target_pairs={{0,4},{4,8},{8,12},{12,16},{16,20},{20,24},{24,28},{28,32},{32,36}... | collective-permute-start | bytes 697352 | tf_op jit(solution)/shard_map/ppermute | solution.py:273
  25.8 1.9 %collective-permute-start.4 = (bf16[227,512]{1,0:T(8,128)(2,1)S(1)}, bf16[227,512]{1,0:T(8,128)(2,1)S(1)}, u32[]{:S(2)}, u32[]{:S(2)}) collective-permute-start(bf16[227,512]{1,0:T(8,128)(2,1)S(1)} %get-tuple-element.58), channel_id=1, source_target_pairs={{4,0},{8,4},{12,8},{16,12},{20,16},{24,20},{28,24},{32,28},{36,32}... | collective-permute-start | bytes 697352 | tf_op jit(solution)/shard_map/ppermute | solution.py:278
  28.8 4.4 %collective-permute-done.4.high_ref = bf16[227,512]{1,0:T(8,128)(2,1)S(1)} collective-permute-done((bf16[227,512]{1,0:T(8,128)(2,1)S(1)}, bf16[227,512]{1,0:T(8,128)(2,1)S(1)}, u32[]{:S(2)}, u32[]{:S(2)}) %collective-permute-start.4) | collective-permute-done | bytes 232480 | tf_op jit(solution)/shard_map/ppermute | solution.py:278
  34.0 4.5 %all-to-all-start = ((bf16[4,64,640]{2,1,0:T(8,128)(2,1)}), bf16[4,64,640]{2,1,0:T(8,128)(2,1)S(1)}, u32[]{:S(2)}, u32[]{:S(2)}) async-start(bf16[4,64,640]{2,1,0:T(8,128)(2,1)} %broadcast_in_dim.9), calls=%async_computation | async-start | bytes 655360 | tf_op jit(solution)/shard_map/all_to_all | solution.py:357
  38.5 15.4 %encode.1 = (bf16[2560,512]{1,0:T(8,128)(2,1)}, bf16[2560,512]{1,0:T(8,128)(2,1)}, bf16[2560,512]{1,0:T(8,128)(2,1)}, bf16[2560,512]{1,0:T(8,128)(2,1)}, bf16[25...) custom-call(s32[1]{0:T(128)} %bitcast.sub_ref, s32[2560,1]{1,0:T(8,128)} %reshape.27.index_ref, ...), custom_call_target="tpu_custom_call" | custom-call | tf_op jit(solution)/shard_map/encode/pallas_call | solution.py:362
  55.5 2.4 %collective-permute-start.6 = (bf16[64,512]{1,0:T(8,128)(2,1)}, bf16[64,512]{1,0:T(8,128)(2,1)S(1)}, u32[]{:S(2)}, u32[]{:S(2)}) collective-permute-start(bf16[64,512]{1,0:T(8,128)(2,1)} %get-tuple-element.34), channel_id=1, source_target_pairs={{0,2},{1,3},{2,0},{3,1},{4,6},{5,7},{6,4},{7,5},{8,10},{9,11},{10,... | collective-permute-start | bytes 196616 | tf_op jit(solution)/shard_map/ppermute | solution.py:295
  62.1 4.5 %collective-permute-start.8 = (bf16[256,1152]{1,0:T(8,128)(2,1)S(1)}, bf16[256,1152]{1,0:T(8,128)(2,1)S(1)}, u32[]{:S(2)}, u32[]{:S(2)}) collective-permute-start(bf16[256,1152]{1,0:T(8,128)(2,1)S(1)} %maximum_maximum_fusion.band_all), channel_id=1, source_target_pairs={{0,4},{1,5},{4,8},{5,9},{6,2},{7,3},{8,12},{9,13},{10,6},{11,7},{1... | collective-permute-start | bytes 1769480 | tf_op jit(solution)/shard_map/ppermute | solution.py:290
  66.6 2.1 %collective-permute-start.9 = (bf16[64,512]{1,0:T(8,128)(2,1)S(1)}, bf16[64,512]{1,0:T(8,128)(2,1)S(1)}, u32[]{:S(2)}, u32[]{:S(2)}) collective-permute-start(bf16[64,512]{1,0:T(8,128)(2,1)S(1)} %constant_dynamic-slice_fusion), channel_id=1, source_target_pairs={{2,6},{3,7},{4,0},{5,1},{6,10},{7,11},{8,4},{9,5},{10,14},{11,15},... | collective-permute-start | bytes 196616 | tf_op jit(solution)/shard_map/ppermute | solution.py:290
  68.8 3.5 %collective-permute-done.9.side_ref = bf16[64,512]{1,0:T(8,128)(2,1)S(1)} collective-permute-done((bf16[64,512]{1,0:T(8,128)(2,1)S(1)}, bf16[64,512]{1,0:T(8,128)(2,1)S(1)}, u32[]{:S(2)}, u32[]{:S(2)}) %collective-permute-start.9) | collective-permute-done | bytes 65568 | tf_op jit(solution)/shard_map/ppermute | solution.py:290
  74.2 18.0 %process.1 = (bf16[64,512]{1,0:T(8,128)(2,1)}, bf16[2560,512]{1,0:T(8,128)(2,1)}, bf16[1024,512]{1,0:T(8,128)(2,1)}) custom-call(s32[1]{0:T(128)} %bitcast.sub_ref, bf16[256,1152]{1,0:T(8,128)(2,1)} %copy-done, bf16[256,1152]{1,0:T(8,128)(2,1)} %copy-done.2, bf16[64,512]{1,0:T(8,128)(2,1)} %copy-done.12, bf16[512,512]{1,0:T(8,128)(2,1)} %proc_ref.1, ...), custom_call_target="tpu_custom_call" | custom-call | tf_op jit(solution)/shard_map/process/pallas_call | solution.py:394
  92.2 10.8 %all-to-all-start.1 = ((bf16[32,32,512]{2,1,0:T(8,128)(2,1)}), bf16[32,32,512]{2,1,0:T(8,128)(2,1)S(1)}, u32[]{:S(2)}, u32[]{:S(2)}) async-start(bf16[32,32,512]{2,1,0:T(8,128)(2,1)} %bitcast.14), calls=%async_computation.1 | async-start | bytes 2097152 | tf_op jit(solution)/shard_map/all_to_all | solution.py:454
  103.1 11.8 %channels.1 = (bf16[227,512]{1,0:T(8,128)(2,1)}, bf16[227,512]{1,0:T(8,128)(2,1)}, bf16[227,512]{1,0:T(8,128)(2,1)}, bf16[227,512]{1,0:T(8,128)(2,1)}, bf16[227,...) custom-call(s32[1]{0:T(128)} %bitcast.sub_ref, s32[2560,1]{1,0:T(8,128)} %reshape.27.index_ref, bf16[512,512]{1,0:T(8,128)(2,1)} %src_ref.3, ...), custom_call_target="tpu_custom_call" | custom-call | tf_op jit(solution)/shard_map/channels/pallas_call | solution.py:435
  114.8 3.7 %collective-permute-start.10 = (bf16[227,512]{1,0:T(8,128)(2,1)}, bf16[227,512]{1,0:T(8,128)(2,1)S(1)}, u32[]{:S(2)}, u32[]{:S(2)}) collective-permute-start(bf16[227,512]{1,0:T(8,128)(2,1)} %get-tuple-element.45), channel_id=1, source_target_pairs={{0,4},{4,8},{8,12},{12,16},{16,20},{20,24},{24,28},{28,32},{32,36}... | collective-permute-start | bytes 697352 | tf_op jit(solution)/shard_map/ppermute | solution.py:273
  118.5 1.9 %collective-permute-start.11 = (bf16[227,512]{1,0:T(8,128)(2,1)}, bf16[227,512]{1,0:T(8,128)(2,1)S(1)}, u32[]{:S(2)}, u32[]{:S(2)}) collective-permute-start(bf16[227,512]{1,0:T(8,128)(2,1)} %get-tuple-element.46), channel_id=1, source_target_pairs={{4,0},{8,4},{12,8},{16,12},{20,16},{24,20},{28,24},{32,28},{36,32}... | collective-permute-start | bytes 697352 | tf_op jit(solution)/shard_map/ppermute | solution.py:278
  121.4 9.2 %all-to-all-start.2 = ((bf16[8,32,512]{2,1,0:T(8,128)(2,1)}), bf16[8,32,512]{2,1,0:T(8,128)(2,1)S(1)}, u32[]{:S(2)}, u32[]{:S(2)}) async-start(bf16[8,32,512]{2,1,0:T(8,128)(2,1)} %broadcast_in_dim.10), calls=%async_computation.2 | async-start | bytes 524288 | tf_op jit(solution)/shard_map/all_to_all | solution.py:266
  133.6 3.5 %collective-permute-done.12 = bf16[227,512]{1,0:T(8,128)(2,1)S(1)} collective-permute-done((bf16[227,512]{1,0:T(8,128)(2,1)S(1)}, bf16[227,512]{1,0:T(8,128)(2,1)S(1)}, u32[]{:S(2)}, u32[]{:S(2)}) %collective-permute-start.12) | collective-permute-done | bytes 232480 | tf_op jit(solution)/shard_map/ppermute | solution.py:295
  137.1 3.0 %all-to-all-done.2 = bf16[8,32,512]{2,1,0:T(8,128)(2,1)S(1)} async-done(((bf16[8,32,512]{2,1,0:T(8,128)(2,1)}), bf16[8,32,512]{2,1,0:T(8,128)(2,1)S(1)}, u32[]{:S(2)}, u32[]{:S(2)}) %all-to-all-start.2) | async-done | bytes 262176 | tf_op jit(solution)/shard_map/all_to_all | solution.py:266
  141.2 10.1 %all-to-all-start.3 = ((bf16[32,32,512]{2,1,0:T(8,128)(2,1)}), bf16[32,32,512]{2,1,0:T(8,128)(2,1)S(1)}, u32[]{:S(2)}, u32[]{:S(2)}) async-start(bf16[32,32,512]{2,1,0:T(8,128)(2,1)} %broadcast_in_dim.11), calls=%async_computation.3 | async-start | bytes 2097152 | tf_op jit(solution)/shard_map/all_to_all | solution.py:266
  151.5 2.7 %collective-permute-start.14 = (bf16[227,512]{1,0:T(8,128)(2,1)S(1)}, bf16[227,512]{1,0:T(8,128)(2,1)S(1)}, u32[]{:S(2)}, u32[]{:S(2)}) collective-permute-start(bf16[227,512]{1,0:T(8,128)(2,1)S(1)} %add_convert_fusion), channel_id=1, source_target_pairs={{0,3},{1,0},{2,1},{3,2},{4,7},{5,4},{6,5},{7,6},{8,11},{9,8},{10,9... | collective-permute-start | bytes 697352 | tf_op jit(solution)/shard_map/ppermute | solution.py:295
  154.2 15.7 %collective-permute-done.14 = bf16[227,512]{1,0:T(8,128)(2,1)S(1)} collective-permute-done((bf16[227,512]{1,0:T(8,128)(2,1)S(1)}, bf16[227,512]{1,0:T(8,128)(2,1)S(1)}, u32[]{:S(2)}, u32[]{:S(2)}) %collective-permute-start.14) | collective-permute-done | bytes 232480 | tf_op jit(solution)/shard_map/ppermute | solution.py:295
  (67 shorter events, 22.4 us)
Async XLA Ops:
  0.6 8.2 %collective-permute-start.1 = (bf16[227,512]{1,0:T(8,128)(2,1)}, bf16[227,512]{1,0:T(8,128)(2,1)S(1)}, u32[]{:S(2)}, u32[]{:S(2)}) collective-permute-start(bf16[227,512]{1,0:T(8,128)(2,1)} %refs_0_.1), channel_id=1, source_target_pairs={{0,1},{1,2},{2,3},{3,0},{4,5},{5,6},{6,7},{7,4},{8,9},{9,10},{10,1... | collective-permute-start | bytes 697352 | tf_op jit(solution)/shard_map/ppermute | solution.py:295
  2.7 6.2 %collective-permute-start.2 = (bf16[227,512]{1,0:T(8,128)(2,1)}, bf16[227,512]{1,0:T(8,128)(2,1)S(1)}, u32[]{:S(2)}, u32[]{:S(2)}) collective-permute-start(bf16[227,512]{1,0:T(8,128)(2,1)} %refs_0_.1), channel_id=1, source_target_pairs={{0,3},{1,0},{2,1},{3,2},{4,7},{5,4},{6,5},{7,6},{8,11},{9,8},{10,9... | collective-permute-start | bytes 697352 | tf_op jit(solution)/shard_map/ppermute | solution.py:295
  4.1 11.6 %collective-permute-start = (bf16[227,512]{1,0:T(8,128)(2,1)}, bf16[227,512]{1,0:T(8,128)(2,1)S(1)}, u32[]{:S(2)}, u32[]{:S(2)}) collective-permute-start(bf16[227,512]{1,0:T(8,128)(2,1)} %refs_0_.1), channel_id=1, source_target_pairs={{0,2},{1,3},{2,0},{3,1},{4,6},{5,7},{6,4},{7,5},{8,10},{9,11},{10,... | collective-permute-start | bytes 697352 | tf_op jit(solution)/shard_map/ppermute | solution.py:295
  14.7 13.0 %copy-start.14 = (s32[64,6]{0,1:T(8,128)S(1)}, s32[64,6]{0,1:T(8,128)}, u32[]{:S(2)}) copy-start(s32[64,6]{0,1:T(8,128)} %param.20) | copy-start | bytes 4612
  14.7 13.1 %copy-start.13 = (bf16[64,512]{1,0:T(8,128)(2,1)S(1)}, bf16[64,512]{1,0:T(8,128)(2,1)}, u32[]{:S(2)}) copy-start(bf16[64,512]{1,0:T(8,128)(2,1)} %param.21) | copy-start | bytes 196612
  15.7 18.3 %copy-start.1 = (bf16[227,512]{1,0:T(8,128)(2,1)}, bf16[227,512]{1,0:T(8,128)(2,1)S(1)}, u32[]{:S(2)}) copy-start(bf16[227,512]{1,0:T(8,128)(2,1)S(1)} %collective-permute-done.two_ref) | copy-start | bytes 697348
  16.9 11.9 %collective-permute-start.3 = (bf16[227,512]{1,0:T(8,128)(2,1)S(1)}, bf16[227,512]{1,0:T(8,128)(2,1)S(1)}, u32[]{:S(2)}, u32[]{:S(2)}) collective-permute-start(bf16[227,512]{1,0:T(8,128)(2,1)S(1)} %get-tuple-element.59), channel_id=1, source_target_pairs={{0,4},{4,8},{8,12},{12,16},{16,20},{20,24},{24,28},{28,32},{32,36}... | collective-permute-start | bytes 697352 | tf_op jit(solution)/shard_map/ppermute | solution.py:273
  25.8 7.4 %collective-permute-start.4 = (bf16[227,512]{1,0:T(8,128)(2,1)S(1)}, bf16[227,512]{1,0:T(8,128)(2,1)S(1)}, u32[]{:S(2)}, u32[]{:S(2)}) collective-permute-start(bf16[227,512]{1,0:T(8,128)(2,1)S(1)} %get-tuple-element.58), channel_id=1, source_target_pairs={{4,0},{8,4},{12,8},{16,12},{20,16},{24,20},{28,24},{32,28},{36,32}... | collective-permute-start | bytes 697352 | tf_op jit(solution)/shard_map/ppermute | solution.py:278
  34.0 25.1 %all-to-all-start = ((bf16[4,64,640]{2,1,0:T(8,128)(2,1)}), bf16[4,64,640]{2,1,0:T(8,128)(2,1)S(1)}, u32[]{:S(2)}, u32[]{:S(2)}) async-start(bf16[4,64,640]{2,1,0:T(8,128)(2,1)} %broadcast_in_dim.9), calls=%async_computation | async-start | bytes 655360 | tf_op jit(solution)/shard_map/all_to_all | solution.py:357
  54.0 5.1 %collective-permute-start.5 = (bf16[64,512]{1,0:T(8,128)(2,1)}, bf16[64,512]{1,0:T(8,128)(2,1)S(1)}, u32[]{:S(2)}, u32[]{:S(2)}) collective-permute-start(bf16[64,512]{1,0:T(8,128)(2,1)} %get-tuple-element.34), channel_id=1, source_target_pairs={{0,1},{1,2},{2,3},{3,0},{4,5},{5,6},{6,7},{7,4},{8,9},{9,10},{10,1... | collective-permute-start | bytes 196616 | tf_op jit(solution)/shard_map/ppermute | solution.py:295
  55.5 5.0 %collective-permute-start.6 = (bf16[64,512]{1,0:T(8,128)(2,1)}, bf16[64,512]{1,0:T(8,128)(2,1)S(1)}, u32[]{:S(2)}, u32[]{:S(2)}) collective-permute-start(bf16[64,512]{1,0:T(8,128)(2,1)} %get-tuple-element.34), channel_id=1, source_target_pairs={{0,2},{1,3},{2,0},{3,1},{4,6},{5,7},{6,4},{7,5},{8,10},{9,11},{10,... | collective-permute-start | bytes 196616 | tf_op jit(solution)/shard_map/ppermute | solution.py:295
  57.9 3.3 %collective-permute-start.7 = (bf16[64,512]{1,0:T(8,128)(2,1)}, bf16[64,512]{1,0:T(8,128)(2,1)S(1)}, u32[]{:S(2)}, u32[]{:S(2)}) collective-permute-start(bf16[64,512]{1,0:T(8,128)(2,1)} %get-tuple-element.34), channel_id=1, source_target_pairs={{0,3},{1,0},{2,1},{3,2},{4,7},{5,4},{6,5},{7,6},{8,11},{9,8},{10,9... | collective-permute-start | bytes 196616 | tf_op jit(solution)/shard_map/ppermute | solution.py:295
  62.1 11.3 %collective-permute-start.8 = (bf16[256,1152]{1,0:T(8,128)(2,1)S(1)}, bf16[256,1152]{1,0:T(8,128)(2,1)S(1)}, u32[]{:S(2)}, u32[]{:S(2)}) collective-permute-start(bf16[256,1152]{1,0:T(8,128)(2,1)S(1)} %maximum_maximum_fusion.band_all), channel_id=1, source_target_pairs={{0,4},{1,5},{4,8},{5,9},{6,2},{7,3},{8,12},{9,13},{10,6},{11,7},{1... | collective-permute-start | bytes 1769480 | tf_op jit(solution)/shard_map/ppermute | solution.py:290
  66.6 5.6 %collective-permute-start.9 = (bf16[64,512]{1,0:T(8,128)(2,1)S(1)}, bf16[64,512]{1,0:T(8,128)(2,1)S(1)}, u32[]{:S(2)}, u32[]{:S(2)}) collective-permute-start(bf16[64,512]{1,0:T(8,128)(2,1)S(1)} %constant_dynamic-slice_fusion), channel_id=1, source_target_pairs={{2,6},{3,7},{4,0},{5,1},{6,10},{7,11},{8,4},{9,5},{10,14},{11,15},... | collective-permute-start | bytes 196616 | tf_op jit(solution)/shard_map/ppermute | solution.py:290
  92.2 28.2 %all-to-all-start.1 = ((bf16[32,32,512]{2,1,0:T(8,128)(2,1)}), bf16[32,32,512]{2,1,0:T(8,128)(2,1)S(1)}, u32[]{:S(2)}, u32[]{:S(2)}) async-start(bf16[32,32,512]{2,1,0:T(8,128)(2,1)} %bitcast.14), calls=%async_computation.1 | async-start | bytes 2097152 | tf_op jit(solution)/shard_map/all_to_all | solution.py:454
  114.8 15.8 %copy-start.8 = (bf16[227,512]{1,0:T(8,128)(2,1)S(1)}, bf16[227,512]{1,0:T(8,128)(2,1)}, u32[]{:S(2)}) copy-start(bf16[227,512]{1,0:T(8,128)(2,1)} %get-tuple-element.48) | copy-start | bytes 697348
  114.8 15.8 %copy-start.9 = (bf16[227,512]{1,0:T(8,128)(2,1)S(1)}, bf16[227,512]{1,0:T(8,128)(2,1)}, u32[]{:S(2)}) copy-start(bf16[227,512]{1,0:T(8,128)(2,1)} %get-tuple-element.49) | copy-start | bytes 697348
  114.8 15.8 %collective-permute-start.10 = (bf16[227,512]{1,0:T(8,128)(2,1)}, bf16[227,512]{1,0:T(8,128)(2,1)S(1)}, u32[]{:S(2)}, u32[]{:S(2)}) collective-permute-start(bf16[227,512]{1,0:T(8,128)(2,1)} %get-tuple-element.45), channel_id=1, source_target_pairs={{0,4},{4,8},{8,12},{12,16},{16,20},{20,24},{24,28},{28,32},{32,36}... | collective-permute-start | bytes 697352 | tf_op jit(solution)/shard_map/ppermute | solution.py:273
  118.5 12.1 %collective-permute-start.11 = (bf16[227,512]{1,0:T(8,128)(2,1)}, bf16[227,512]{1,0:T(8,128)(2,1)S(1)}, u32[]{:S(2)}, u32[]{:S(2)}) collective-permute-start(bf16[227,512]{1,0:T(8,128)(2,1)} %get-tuple-element.46), channel_id=1, source_target_pairs={{4,0},{8,4},{12,8},{16,12},{20,16},{24,20},{28,24},{32,28},{36,32}... | collective-permute-start | bytes 697352 | tf_op jit(solution)/shard_map/ppermute | solution.py:278
  121.4 18.7 %all-to-all-start.2 = ((bf16[8,32,512]{2,1,0:T(8,128)(2,1)}), bf16[8,32,512]{2,1,0:T(8,128)(2,1)S(1)}, u32[]{:S(2)}, u32[]{:S(2)}) async-start(bf16[8,32,512]{2,1,0:T(8,128)(2,1)} %broadcast_in_dim.10), calls=%async_computation.2 | async-start | bytes 524288 | tf_op jit(solution)/shard_map/all_to_all | solution.py:266
  130.9 6.2 %collective-permute-start.12 = (bf16[227,512]{1,0:T(8,128)(2,1)S(1)}, bf16[227,512]{1,0:T(8,128)(2,1)S(1)}, u32[]{:S(2)}, u32[]{:S(2)}) collective-permute-start(bf16[227,512]{1,0:T(8,128)(2,1)S(1)} %get-tuple-element.61), channel_id=1, source_target_pairs={{0,1},{1,2},{2,3},{3,0},{4,5},{5,6},{6,7},{7,4},{8,9},{9,10},{10,1... | collective-permute-start | bytes 697352 | tf_op jit(solution)/shard_map/ppermute | solution.py:295
  132.1 5.0 %collective-permute-start.13 = (bf16[227,512]{1,0:T(8,128)(2,1)S(1)}, bf16[227,512]{1,0:T(8,128)(2,1)S(1)}, u32[]{:S(2)}, u32[]{:S(2)}) collective-permute-start(bf16[227,512]{1,0:T(8,128)(2,1)S(1)} %get-tuple-element.60), channel_id=1, source_target_pairs={{0,3},{1,0},{2,1},{3,2},{4,7},{5,4},{6,5},{7,6},{8,11},{9,8},{10,9... | collective-permute-start | bytes 697352 | tf_op jit(solution)/shard_map/ppermute | solution.py:295
  141.2 28.6 %all-to-all-start.3 = ((bf16[32,32,512]{2,1,0:T(8,128)(2,1)}), bf16[32,32,512]{2,1,0:T(8,128)(2,1)S(1)}, u32[]{:S(2)}, u32[]{:S(2)}) async-start(bf16[32,32,512]{2,1,0:T(8,128)(2,1)} %broadcast_in_dim.11), calls=%async_computation.3 | async-start | bytes 2097152 | tf_op jit(solution)/shard_map/all_to_all | solution.py:266
  151.5 18.4 %collective-permute-start.14 = (bf16[227,512]{1,0:T(8,128)(2,1)S(1)}, bf16[227,512]{1,0:T(8,128)(2,1)S(1)}, u32[]{:S(2)}, u32[]{:S(2)}) collective-permute-start(bf16[227,512]{1,0:T(8,128)(2,1)S(1)} %add_convert_fusion), channel_id=1, source_target_pairs={{0,3},{1,0},{2,1},{3,2},{4,7},{5,4},{6,5},{7,6},{8,11},{9,8},{10,9... | collective-permute-start | bytes 697352 | tf_op jit(solution)/shard_map/ppermute | solution.py:295
  (10 other events, 47.5 us)

commit v8 on v7

--- a/solution.py
+++ b/solution.py
@@ -125,18 +125,55 @@
         mesh_out_ref[...] = (mesh_ref[...].astype(F32) + total[...] * scale).astype(BF)
 
 
+def sent_back(count, columns, lines, cots, receiver, own_query, total):
+    rows = own_query.shape[0]
+    lanes = lax.broadcasted_iota(jnp.int32, columns.shape, 1)
+
+    def one(j, carry):
+        column = jnp.sum(jnp.where(lanes == j, columns[...], 0), axis=1, keepdims=True)
+        value = dot(selection(column, rows), own_query) + receiver[...]
+        _, slopes = silu_and_slope(value)
+        slopes = (cots[...] * slopes).astype(BF)
+        total[...] += dot(selection_t(lines[pl.ds(j, 1), :], rows), slopes)
+        return carry
+
+    lax.fori_loop(0, count, one, 0)
+
+
+def senders(tail, wanted, rows):
+    whole_tail = tail.astype(F32).astype(jnp.int32)
+    turn = whole_tail.shape[1] // 2
+    return (whole_tail[:, :turn] - wanted) * rows + whole_tail[:, turn:]
+
+
+def near_kernel(
+    mesh_scale, count,
+    sub_ref, band_ref, proc_ref, recv_ref,
+    query_ref, receiver_ref, grad_ref,
+    cots, receiver, columns, lines,
+):
+    rows, latent = grad_ref.shape
+    hidden = band_ref[:, :latent]
+    query_ref[...] = dot(hidden, proc_ref[...]).astype(BF)
+    receiver[...] = dot(hidden, recv_ref[...])
+    receiver_ref[...] = receiver[:rows, :]
+    columns[...] = senders(band_ref[:, 2 * latent :], sub_ref[0] + 1, rows)
+    lines[...] = columns[...].T
+    cots[...] = band_ref[:, latent : 2 * latent].astype(F32) * mesh_scale
+    grad_ref[...] = jnp.zeros_like(grad_ref)
+    sent_back(count, columns, lines, cots, receiver, query_ref[:rows, :], grad_ref)
+
+
 def mesh_kernel(
     mesh_scale, scale, count,
-    sub_ref, band_all, far_all, side_ref, proc_ref, recv_ref, edge_ref,
+    sub_ref, own_ref, far_ref, side_ref, query_ref, receiver_ref, near_ref, proc_ref, recv_ref, edge_ref,
     active_ref, normed_ref, inverse_ref, bslope_ref, hidden_ref,
     out_ref, bgrad_ref, wgrad_ref,
-    receiver_all, cots, columns, lines, query_grad, centred_ref, upper_ref, edge_total, src_total,
+    far_receiver, cots, columns, lines, query_grad, upper_ref, edge_total, src_total,
 ):
     step = pl.program_id(0)
     rows, latent = side_ref.shape
-    wide = band_all.shape[0]
-    band_ref, far_ref = band_all.at[:, :latent], far_all.at[:, :latent]
-    pay_ref, far_pay_ref = band_all.at[:, latent:], far_all.at[:, latent:]
+    wide = far_ref.shape[0]
 
     @pl.when(step == 0)
     def _():
@@ -144,67 +181,48 @@
         lower = sub < SUBS // 2
         proc = proc_ref[...]
         recv = recv_ref[...]
-        own = band_ref[:rows, :]
-        window = jnp.concatenate([band_ref[...], far_ref[...], side_ref[...]], axis=0)
-        query = dot(window, proc).astype(BF)
-        receiver_all[:wide, :] = dot(band_ref[...], recv)
-        receiver_all[wide:, :] = dot(far_ref[...], recv)
-        receiver = receiver_all[:rows, :]
-
-        tail = pay_ref[:, latent:].astype(F32).astype(jnp.int32)
-        far_tail = far_pay_ref[:, latent:].astype(F32).astype(jnp.int32)
+        own = own_ref[:, :latent]
+        beyond = jnp.concatenate([far_ref[:, :latent], side_ref[...]], axis=0)
+        query = jnp.concatenate([query_ref[...], dot(beyond, proc).astype(BF)], axis=0)
+        receiver = receiver_ref[...]
+
+        tail = own_ref[:, 2 * latent :].astype(F32).astype(jnp.int32)
         turn = tail.shape[1] // 2
         block, line = tail[:, :turn], tail[:, turn:]
-        far_block, far_line = far_tail[:, :turn], far_tail[:, turn:]
-        far_wanted = jnp.where(lower, SUBS + 1 + sub, sub - SUBS + 1)
-        columns[:wide, :turn] = (block - (sub + 1)) * rows + line
-        columns[wide:, :turn] = (far_block - far_wanted) * rows + far_line
-        own_block, own_line = block[:rows], line[:rows]
-        inside = lax.rem(sub + SUBS + 1 - own_block, SUBS) * rows
+        inside = lax.rem(sub + SUBS + 1 - block, SUBS) * rows
         below = jnp.where(lower, wide + lax.rem(sub + 1, SUBS) * rows, 2 * wide)
         above = jnp.where(lower, 2 * wide, wide + sub * rows)
-        place = jnp.where(own_block == 0, below, jnp.where(own_block == SUBS + 1, above, inside))
-        place = place + own_line
-        columns[:, turn:] = jnp.zeros_like(columns[:, turn:])
-        lines[...] = columns[...].T
-        cots[:wide, :] = pay_ref[:, :latent].astype(F32) * mesh_scale
-        cots[wide:, :] = far_pay_ref[:, :latent].astype(F32) * mesh_scale
-
+        place = jnp.where(block == 0, below, jnp.where(block == SUBS + 1, above, inside)) + line
         summed = jnp.zeros((rows, latent), F32)
         slopes = jnp.zeros((rows, latent), F32)
         for j in range(count):
-            sent = dot(selection(place[:, j : j + 1], window.shape[0]), query)
+            sent = dot(selection(place[:, j : j + 1], query.shape[0]), query)
             active, slope = silu_and_slope(sent + receiver)
             summed += active
             slopes += slope
         out_ref[...] = (own.astype(F32) + summed * mesh_scale).astype(BF)
-        receiver_grad = cots[:rows, :] * slopes
-
-        own_query = query[:rows]
-        query_grad[...] = jnp.zeros_like(query_grad)
-        lanes = lax.broadcasted_iota(jnp.int32, columns.shape, 1)
-
-        def one(j, carry):
-            column = jnp.sum(jnp.where(lanes == j, columns[...], 0), axis=1, keepdims=True)
-            value = dot(selection(column, rows), own_query) + receiver_all[...]
-            _, slopes = silu_and_slope(value)
-            slopes = (cots[...] * slopes).astype(BF)
-            query_grad[...] += dot(selection_t(lines[pl.ds(j, 1), :], rows), slopes)
-            return carry
-
-        lax.fori_loop(0, count, one, 0)
-        mesh_grad = pay_ref[:rows, :latent].astype(F32) + dot_t(query_grad[...].astype(BF), proc)
+        upstream = own_ref[:, latent : 2 * latent].astype(F32)
+        receiver_grad = upstream * mesh_scale * slopes
+
+        wanted = jnp.where(lower, SUBS + 1 + sub, sub - SUBS + 1)
+        columns[...] = senders(far_ref[:, 2 * latent :], wanted, rows)
+        lines[...] = columns[...].T
+        cots[...] = far_ref[:, latent : 2 * latent].astype(F32) * mesh_scale
+        far_receiver[...] = dot(far_ref[:, :latent], recv)
+        query_grad[...] = near_ref[...]
+        sent_back(count, columns, lines, cots, far_receiver, query_ref[:rows, :], query_grad)
+        mesh_grad = upstream + dot_t(query_grad[...].astype(BF), proc)
         mesh_grad = mesh_grad + dot_t(receiver_grad.astype(BF), recv)
-        upper = mesh_grad * scale
-        upper_ref[...] = upper
-        centred_ref[...] = upper - jnp.mean(upper, axis=-1, keepdims=True)
+        upper_ref[...] = mesh_grad * scale
         edge_total[...] = jnp.zeros_like(edge_total)
         src_total[...] = jnp.zeros_like(src_total)
 
+    upper = upper_ref[...]
+    centred = upper - jnp.mean(upper, axis=-1, keepdims=True)
     normed = normed_ref[...].astype(F32).reshape(-1, rows, latent)
     inverse = inverse_ref[...].reshape(-1, rows, 1)
-    along = jnp.mean(upper_ref[...][None] * normed, axis=-1, keepdims=True)
-    ngrad = ((centred_ref[...][None] - normed * along) * inverse).reshape(-1, latent).astype(BF)
+    along = jnp.mean(upper[None] * normed, axis=-1, keepdims=True)
+    ngrad = ((centred[None] - normed * along) * inverse).reshape(-1, latent).astype(BF)
     edge_total[...] += t_dot(active_ref[...], ngrad)
     bgrad = (dot_t(ngrad, edge_ref[...]) * bslope_ref[...].astype(F32)).astype(BF)
     bgrad_ref[...] = bgrad
@@ -320,6 +338,14 @@
     grid = [grid_x] + [along_sub(grid_x, k) for k in range(1, SUBS)]
     grid_local = (g2m_src - (band * (nodes * SUBS) - nodes)).T.reshape(edges, 1)
 
+    place = mesh_src - (band * width - rows)
+    half = 64
+    spare = jnp.zeros((rows, half - mesh_count), BF)
+    pay = jnp.concatenate(
+        [cotangent, (place // rows).astype(BF), spare, (place % rows).astype(BF), spare], axis=1
+    )
+    pays = [pay] + [along_sub(pay, k) for k in range(1, SUBS)]
+
     nearest = (0, 1, 3)
     picked = pl.pallas_call(
         functools.partial(gather_kernel, nearest),
@@ -340,24 +366,11 @@
         name="gather",
     )(sub_scalar, grid_local, *[grid[k] for k in nearest])
 
-    grid[2], picked = lax.optimization_barrier((grid[2], picked))
+    grid[2], picked, *pays = lax.optimization_barrier((grid[2], picked, *pays))
     last = lax.select_n(lax.rem(sub + 1, SUBS), *grid)
     first = lax.select_n(sub, *grid)
     grid_low = bands_up(last)
     grid_high = bands_down(first)
-
-    place = mesh_src - (band * width - rows)
-    half = 64
-    spare = jnp.zeros((rows, half - mesh_count), BF)
-    pay = jnp.concatenate(
-        [cotangent, (place // rows).astype(BF), spare, (place % rows).astype(BF), spare], axis=1
-    )
-    pay = jnp.broadcast_to(pay[None], (SUBS, *pay.shape))
-    pay, grid_low, grid_high = lax.optimization_barrier((pay, grid_low, grid_high))
-    pay = lax.all_to_all(pay, "sub", 0, 0, tiled=True)
-    pay = jnp.concatenate(
-        [lax.dynamic_index_in_dim(pay, lax.rem(sub + SUBS - k, SUBS), 0, False) for k in range(SUBS)]
-    )
 
     hidden, hslope, active, bslope, normed, inverse, hidden_mesh = pl.pallas_call(
         functools.partial(forward_kernel, scale),
@@ -386,18 +399,50 @@
     )(sub_scalar, grid_local, picked, grid[2], grid_low, grid_high, mesh_in, w_embed, w_src, w_dst, w_edge)
 
     mesh_band = jnp.concatenate([hidden_mesh] + [along_sub(hidden_mesh, k) for k in range(1, SUBS)])
-    mesh_band = jnp.concatenate([mesh_band, pay], axis=1)
+    mesh_band = jnp.concatenate([mesh_band, jnp.concatenate(pays)], axis=1)
     mesh_far = outwards(mesh_band, True)
     at = jnp.where(sub < SUBS // 2, sub, lax.rem(sub + 1, SUBS)) * rows
     mesh_side = outwards(lax.dynamic_slice(mesh_band, (at, 0), (rows, latent)), False)
+
+    band_then = mesh_band
+    query_band, receiver, near_grad = pl.pallas_call(
+        functools.partial(near_kernel, mesh_scale, mesh_count),
+        grid=(1,),
+        in_specs=[
+            scalar(),
+            whole((width, 2 * latent + 2 * half)),
+            whole((latent, latent)),
+            whole((latent, latent)),
+        ],
+        out_specs=[whole((width, latent)), whole((rows, latent)), whole((rows, latent))],
+        out_shape=[
+            jax.ShapeDtypeStruct((width, latent), BF),
+            jax.ShapeDtypeStruct((rows, latent), F32),
+            jax.ShapeDtypeStruct((rows, latent), F32),
+        ],
+        scratch_shapes=[
+            pltpu.VMEM((width, latent), F32),
+            pltpu.VMEM((width, latent), F32),
+            pltpu.VMEM((width, half), jnp.int32),
+            pltpu.VMEM((half, width), jnp.int32),
+        ],
+        compiler_params=params(),
+        cost_estimate=pl.CostEstimate(
+            flops=8 * width * latent * latent, bytes_accessed=4 * width * latent, transcendentals=0
+        ),
+        name="near",
+    )(sub_scalar, band_then, w_proc, w_recv)
 
     mesh_out, bgrad, part = pl.pallas_call(
         functools.partial(mesh_kernel, mesh_scale, scale, mesh_count),
         grid=(steps,),
         in_specs=[
             scalar(),
+            whole((rows, 2 * latent + 2 * half)),
             whole((width, 2 * latent + 2 * half)),
-            whole((width, 2 * latent + 2 * half)),
+            whole((rows, latent)),
+            whole((width, latent)),
+            whole((rows, latent)),
             whole((rows, latent)),
             whole((latent, latent)),
             whole((latent, latent)),
@@ -415,11 +460,10 @@
             jax.ShapeDtypeStruct((2 * latent, latent), BF),
         ],
         scratch_shapes=[
-            pltpu.VMEM((2 * width, latent), F32),
-            pltpu.VMEM((2 * width, latent), F32),
-            pltpu.VMEM((2 * width, 2 * half), jnp.int32),
-            pltpu.VMEM((2 * half, 2 * width), jnp.int32),
-            pltpu.VMEM((rows, latent), F32),
+            pltpu.VMEM((width, latent), F32),
+            pltpu.VMEM((width, latent), F32),
+            pltpu.VMEM((width, half), jnp.int32),
+            pltpu.VMEM((half, width), jnp.int32),
             pltpu.VMEM((rows, latent), F32),
             pltpu.VMEM((rows, latent), F32),
             pltpu.VMEM((latent, latent), F32),
@@ -428,8 +472,8 @@
         compiler_params=params(),
         name="process",
     )(
-        sub_scalar, mesh_band, mesh_far, mesh_side, w_proc, w_recv, w_edge,
-        active, normed, inverse, bslope, hidden,
+        sub_scalar, mesh_band, mesh_far, mesh_side, query_band, receiver, near_grad,
+        w_proc, w_recv, w_edge, active, normed, inverse, bslope, hidden,
     )
 
     *parts, part_low, part_high = pl.pallas_call(
@@ -461,14 +505,11 @@
         value += jnp.where(block == 0, from_below, jnp.zeros_like(from_below)).astype(F32)
         value += jnp.where(block == SUBS - 1, from_above, jnp.zeros_like(from_above)).astype(F32)
         values.append(value.astype(BF) if k else value)
-    ahead = along_sub(values[1], 1)
-    relayed = along_sub(values[2], -1)
+    arrived = values[:1] + [along_sub(values[k], k) for k in range(1, SUBS)]
     pieces = from_everyone(summed(pieces), FAR)
-    pieces, ahead, relayed = lax.optimization_barrier((pieces, ahead, relayed))
-    behind = along_sub((values[3].astype(F32) + relayed.astype(F32)).astype(BF), -1)
+    pieces, arrived[1], arrived[3] = lax.optimization_barrier((pieces, arrived[1], arrived[3]))
     weights = from_everyone(summed(pieces), NEAR).reshape(2 * latent, latent)
-    weights, behind = lax.optimization_barrier((weights, behind))
-    grid_grad = values[0] + ahead.astype(F32) + behind.astype(F32)
+    grid_grad = functools.reduce(jnp.add, [value.astype(F32) for value in arrived])
     src_grad, edge_grad = weights[latent:].astype(F32), weights[:latent].astype(F32)
     return (mesh_out, grid_grad, src_grad, edge_grad)
 

time: 173 us -> 171 us (0.988)
  starting transfers between devices: 73.3 us -> 67.2 us
  Pallas kernels: 50.3 us -> 54.5 us
  waiting for transfers between devices: 35.3 us -> 33 us
    pallas_call x0 -> x1, Pallas kernels: none -> 5.79 us  [body(): pl.pallas_call(functools.partial(near_kernel, mesh_scale, mesh_count), gr...]
    ppermute x2, waiting for transfers between devices: 4.66 us -> 0.01 us  [outwards(): return lax.ppermute(value, ALL, pairs)]
    all_to_all x1 -> x0, starting transfers between devices: 4.55 us -> none  [body(): pay = lax.all_to_all(pay, 'sub', 0, 0, tiled=True)]
    ppermute x2, starting transfers between devices: 12.5 us -> 9.22 us  [bands_up(): return lax.ppermute(value, BAND, [(i, i + 1) for i in range(count - 1)])]
    ppermute x9 -> x12, starting transfers between devices: 15.6 us -> 18.3 us  [along_sub(): lax.ppermute(value, 'sub', [(i, (i + steps) % count) for i in range(count)])]
    ppermute x9 -> x12, waiting for transfers between devices: 22.4 us -> 24.6 us  [along_sub(): lax.ppermute(value, 'sub', [(i, (i + steps) % count) for i in range(count)])]
  transfers between devices with their start and end apart: 19 -> 21, of which waited for: 11 -> 7; matrix products, arithmetic and copies ran while one was open for 3% -> 4% of each run, Pallas kernels for 19% -> 13%
where the time goes in v8:
time: 171 us; the launch traced here: 170 us
  starting transfers between devices  67.2 us (39%)
  Pallas kernels  54.5 us (32%)
  waiting for transfers between devices  33 us (19%)
  local copies, waits for them, and re-layouts  8.25 us (5%)
  other arithmetic  6.04 us (4%)
    ppermute x12, waiting for transfers between devices, along_sub(): lax.ppermute(value, 'sub', [(i, (i + steps) % count) for i in range(count)])  24.6 us
    all_to_all x2, starting transfers between devices, from_everyone(): lax.all_to_all(jnp.broadcast_to(shard[None], (devices, *shard.shape)), ax...  19.3 us
    ppermute x12, starting transfers between devices, along_sub(): lax.ppermute(value, 'sub', [(i, (i + steps) % count) for i in range(count)])  18.3 us
    pallas_call x1, Pallas kernels, body(): pl.pallas_call(functools.partial(mesh_kernel, mesh_scale, scale, mesh_cou...  16.4 us
    pallas_call x1, Pallas kernels, body(): pl.pallas_call(functools.partial(forward_kernel, scale), grid=(steps,), i...  15.4 us
    pallas_call x1, Pallas kernels, body(): pl.pallas_call(grid_kernel, grid=(steps,), in_specs=[scalar(), tiled(tile...  11.8 us
    all_to_all x1, starting transfers between devices, body(): lax.all_to_all(part.reshape(near, -1, latent), NEAR, 0, 0, tiled=True)  10.2 us
    ppermute x2, starting transfers between devices, bands_up(): return lax.ppermute(value, BAND, [(i, i + 1) for i in range(count - 1)])  9.22 us
  transfers between devices with their start and end apart: 21, of which 7 were waited for; matrix products, arithmetic and copies ran while one was open for 4% of the time, Pallas kernels for 13%

profile of v8, /device:TPU:1, one launch (start us, length us, event | category | flops | bytes accessed | tf_op | source)
XLA Modules:
  0.0 169.9 jit_solution(9306820122637208940)
XLA Ops:
  0.6 2.1 %collective-permute-start.1 = (bf16[227,512]{1,0:T(8,128)(2,1)}, bf16[227,512]{1,0:T(8,128)(2,1)S(1)}, u32[]{:S(2)}, u32[]{:S(2)}) collective-permute-start(bf16[227,512]{1,0:T(8,128)(2,1)} %refs_0_.1), channel_id=1, source_target_pairs={{0,1},{1,2},{2,3},{3,0},{4,5},{5,6},{6,7},{7,4},{8,9},{9,10},{10,1... | collective-permute-start | bytes 697352 | tf_op jit(solution)/shard_map/ppermute | solution.py:313
  6.1 2.5 %collective-permute-start.4 = (bf16[64,640]{1,0:T(8,128)(2,1)S(1)}, bf16[64,640]{1,0:T(8,128)(2,1)S(1)}, u32[]{:S(2)}, u32[]{:S(2)}) collective-permute-start(bf16[64,640]{1,0:T(8,128)(2,1)S(1)} %concatenate.12), channel_id=1, source_target_pairs={{0,2},{1,3},{2,0},{3,1},{4,6},{5,7},{6,4},{7,5},{8,10},{9,11},{10,... | collective-permute-start | bytes 245768 | tf_op jit(solution)/shard_map/ppermute | solution.py:313
  9.8 2.4 %reshape.31.index_ref = s32[2560,1]{1,0:T(8,128)} reshape(s32[40,64]{1,0:T(8,128)S(1)} %subtract_bitcast_fusion) | data formatting | bytes 20480 | tf_op jit(solution)/shard_map/reshape | solution.py:339
  12.1 2.6 %collective-permute-start.5 = (bf16[64,640]{1,0:T(8,128)(2,1)S(1)}, bf16[64,640]{1,0:T(8,128)(2,1)S(1)}, u32[]{:S(2)}, u32[]{:S(2)}) collective-permute-start(bf16[64,640]{1,0:T(8,128)(2,1)S(1)} %concatenate.12), channel_id=1, source_target_pairs={{0,3},{1,0},{2,1},{3,2},{4,7},{5,4},{6,5},{7,6},{8,11},{9,8},{10,9... | collective-permute-start | bytes 245768 | tf_op jit(solution)/shard_map/ppermute | solution.py:313
  15.4 5.1 %gather.1.picked_ref = bf16[2560,256]{1,0:T(8,128)(2,1)} custom-call(s32[1]{0:T(128)} %bitcast.sub_ref, s32[2560,1]{1,0:T(8,128)} %reshape.31.index_ref, bf16[227,512]{1,0:T(8,128)(2,1)} %refs_0_.1, bf16[227,512]{1,0:T(8,128)(2,1)} %copy-done.5, bf16[227,512]{1,0:T(8,128)(2,1)} %copy-done.6), custom_call_target="tpu_custom_call" | custom-call | flops 2013265920 | bytes 1310720 | tf_op jit(solution)/shard_map/gather/pallas_call | solution.py:350
  21.7 5.6 %collective-permute-start.6 = (bf16[227,512]{1,0:T(8,128)(2,1)S(1)}, bf16[227,512]{1,0:T(8,128)(2,1)S(1)}, u32[]{:S(2)}, u32[]{:S(2)}) collective-permute-start(bf16[227,512]{1,0:T(8,128)(2,1)S(1)} %get-tuple-element.63), channel_id=1, source_target_pairs={{0,4},{4,8},{8,12},{12,16},{16,20},{20,24},{24,28},{28,32},{32,36}... | collective-permute-start | bytes 697352 | tf_op jit(solution)/shard_map/ppermute | solution.py:291
  27.3 1.9 %collective-permute-start.7 = (bf16[227,512]{1,0:T(8,128)(2,1)S(1)}, bf16[227,512]{1,0:T(8,128)(2,1)S(1)}, u32[]{:S(2)}, u32[]{:S(2)}) collective-permute-start(bf16[227,512]{1,0:T(8,128)(2,1)S(1)} %get-tuple-element.62), channel_id=1, source_target_pairs={{4,0},{8,4},{12,8},{16,12},{20,16},{24,20},{28,24},{32,28},{36,32}... | collective-permute-start | bytes 697352 | tf_op jit(solution)/shard_map/ppermute | solution.py:296
  30.3 4.4 %collective-permute-done.7.high_ref = bf16[227,512]{1,0:T(8,128)(2,1)S(1)} collective-permute-done((bf16[227,512]{1,0:T(8,128)(2,1)S(1)}, bf16[227,512]{1,0:T(8,128)(2,1)S(1)}, u32[]{:S(2)}, u32[]{:S(2)}) %collective-permute-start.7) | collective-permute-done | bytes 232480 | tf_op jit(solution)/shard_map/ppermute | solution.py:296
  35.4 15.4 %encode.1 = (bf16[2560,512]{1,0:T(8,128)(2,1)}, bf16[2560,512]{1,0:T(8,128)(2,1)}, bf16[2560,512]{1,0:T(8,128)(2,1)}, bf16[2560,512]{1,0:T(8,128)(2,1)}, bf16[25...) custom-call(s32[1]{0:T(128)} %bitcast.sub_ref, s32[2560,1]{1,0:T(8,128)} %reshape.31.index_ref, ...), custom_call_target="tpu_custom_call" | custom-call | tf_op jit(solution)/shard_map/encode/pallas_call | solution.py:375
  50.9 2.1 %collective-permute-start.10 = (bf16[64,512]{1,0:T(8,128)(2,1)}, bf16[64,512]{1,0:T(8,128)(2,1)S(1)}, u32[]{:S(2)}, u32[]{:S(2)}) collective-permute-start(bf16[64,512]{1,0:T(8,128)(2,1)} %get-tuple-element.34), channel_id=1, source_target_pairs={{0,3},{1,0},{2,1},{3,2},{4,7},{5,4},{6,5},{7,6},{8,11},{9,8},{10,9... | collective-permute-start | bytes 196616 | tf_op jit(solution)/shard_map/ppermute | solution.py:313
  55.2 3.0 %collective-permute-done.8 = bf16[64,512]{1,0:T(8,128)(2,1)S(1)} collective-permute-done((bf16[64,512]{1,0:T(8,128)(2,1)}, bf16[64,512]{1,0:T(8,128)(2,1)S(1)}, u32[]{:S(2)}, u32[]{:S(2)}) %collective-permute-start.8) | collective-permute-done | bytes 65568 | tf_op jit(solution)/shard_map/ppermute | solution.py:313
  59.1 4.2 %collective-permute-start.11 = (bf16[256,1152]{1,0:T(8,128)(2,1)S(1)}, bf16[256,1152]{1,0:T(8,128)(2,1)S(1)}, u32[]{:S(2)}, u32[]{:S(2)}) collective-permute-start(bf16[256,1152]{1,0:T(8,128)(2,1)S(1)} %maximum_maximum_fusion.band_ref.own_ref), channel_id=1, source_target_pairs={{0,4},{1,5},{4,8},{5,9},{6,2},{7,3},{8,12},{9,13},{10,6},{11,7},{1... | collective-permute-start | bytes 1769480 | tf_op jit(solution)/shard_map/ppermute | solution.py:308
  63.4 2.1 %collective-permute-start.12 = (bf16[64,512]{1,0:T(8,128)(2,1)S(1)}, bf16[64,512]{1,0:T(8,128)(2,1)S(1)}, u32[]{:S(2)}, u32[]{:S(2)}) collective-permute-start(bf16[64,512]{1,0:T(8,128)(2,1)S(1)} %constant_dynamic-slice_fusion), channel_id=1, source_target_pairs={{2,6},{3,7},{4,0},{5,1},{6,10},{7,11},{8,4},{9,5},{10,14},{11,15},... | collective-permute-start | bytes 196616 | tf_op jit(solution)/shard_map/ppermute | solution.py:308
  65.5 5.8 %near.1 = (bf16[256,512]{1,0:T(8,128)(2,1)}, f32[64,512]{1,0:T(8,128)}, f32[64,512]{1,0:T(8,128)}) custom-call(s32[1]{0:T(128)} %bitcast.sub_ref, bf16[256,1152]{1,0:T(8,128)(2,1)} %copy-done, bf16[512,512]{1,0:T(8,128)(2,1)} %proc_ref.3, bf16[512,512]{1,0:T(8,128)(2,1)} %recv_ref.3), custom_call_target="tpu_custom_call" | custom-call | flops 536870912 | bytes 524288 | tf_op jit(solution)/shard_map/near/pallas_call | solution.py:408
  72.2 16.4 %process.1 = (bf16[64,512]{1,0:T(8,128)(2,1)}, bf16[2560,512]{1,0:T(8,128)(2,1)}, bf16[1024,512]{1,0:T(8,128)(2,1)}) custom-call(s32[1]{0:T(128)} %bitcast.sub_ref, bf16[256,1152]{1,0:T(8,128)(2,1)} %copy-done, bf16[256,1152]{1,0:T(8,128)(2,1)} %copy-done.2, bf16[64,512]{1,0:T(8,128)(2,1)} %copy-done.12, bf16[256,512]{1,0:T(8,128)(2,1)} %get-tuple-element.39.query_ref, ...), custom_call_target="tpu_custom_call" | custom-call | tf_op jit(solution)/shard_map/process/pallas_call | solution.py:436
  88.6 10.2 %all-to-all-start = ((bf16[32,32,512]{2,1,0:T(8,128)(2,1)}), bf16[32,32,512]{2,1,0:T(8,128)(2,1)S(1)}, u32[]{:S(2)}, u32[]{:S(2)}) async-start(bf16[32,32,512]{2,1,0:T(8,128)(2,1)} %bitcast.10), calls=%async_computation | async-start | bytes 2097152 | tf_op jit(solution)/shard_map/all_to_all | solution.py:498
  98.8 11.8 %channels.1 = (bf16[227,512]{1,0:T(8,128)(2,1)}, bf16[227,512]{1,0:T(8,128)(2,1)}, bf16[227,512]{1,0:T(8,128)(2,1)}, bf16[227,512]{1,0:T(8,128)(2,1)}, bf16[227,...) custom-call(s32[1]{0:T(128)} %bitcast.sub_ref, s32[2560,1]{1,0:T(8,128)} %reshape.31.index_ref, bf16[512,512]{1,0:T(8,128)(2,1)} %src_ref.3, ...), custom_call_target="tpu_custom_call" | custom-call | tf_op jit(solution)/shard_map/channels/pallas_call | solution.py:479
  110.6 3.7 %collective-permute-start.13 = (bf16[227,512]{1,0:T(8,128)(2,1)}, bf16[227,512]{1,0:T(8,128)(2,1)S(1)}, u32[]{:S(2)}, u32[]{:S(2)}) collective-permute-start(bf16[227,512]{1,0:T(8,128)(2,1)} %get-tuple-element.51), channel_id=1, source_target_pairs={{0,4},{4,8},{8,12},{12,16},{16,20},{20,24},{24,28},{28,32},{32,36}... | collective-permute-start | bytes 697352 | tf_op jit(solution)/shard_map/ppermute | solution.py:291
  117.2 9.2 %all-to-all-start.1 = ((bf16[8,32,512]{2,1,0:T(8,128)(2,1)}), bf16[8,32,512]{2,1,0:T(8,128)(2,1)S(1)}, u32[]{:S(2)}, u32[]{:S(2)}) async-start(bf16[8,32,512]{2,1,0:T(8,128)(2,1)} %broadcast_in_dim.7), calls=%async_computation.1 | async-start | bytes 524288 | tf_op jit(solution)/shard_map/all_to_all | solution.py:284
  129.5 3.5 %collective-permute-done.15 = bf16[227,512]{1,0:T(8,128)(2,1)S(1)} collective-permute-done((bf16[227,512]{1,0:T(8,128)(2,1)S(1)}, bf16[227,512]{1,0:T(8,128)(2,1)S(1)}, u32[]{:S(2)}, u32[]{:S(2)}) %collective-permute-start.15) | collective-permute-done | bytes 232480 | tf_op jit(solution)/shard_map/ppermute | solution.py:313
  133.0 2.9 %all-to-all-done.1 = bf16[8,32,512]{2,1,0:T(8,128)(2,1)S(1)} async-done(((bf16[8,32,512]{2,1,0:T(8,128)(2,1)}), bf16[8,32,512]{2,1,0:T(8,128)(2,1)S(1)}, u32[]{:S(2)}, u32[]{:S(2)}) %all-to-all-start.1) | async-done | bytes 262176 | tf_op jit(solution)/shard_map/all_to_all | solution.py:284
  137.0 10.0 %all-to-all-start.2 = ((bf16[32,32,512]{2,1,0:T(8,128)(2,1)}), bf16[32,32,512]{2,1,0:T(8,128)(2,1)S(1)}, u32[]{:S(2)}, u32[]{:S(2)}) async-start(bf16[32,32,512]{2,1,0:T(8,128)(2,1)} %broadcast_in_dim.8), calls=%async_computation.2 | async-start | bytes 2097152 | tf_op jit(solution)/shard_map/all_to_all | solution.py:284
  147.1 3.0 %collective-permute-start.17 = (bf16[227,512]{1,0:T(8,128)(2,1)S(1)}, bf16[227,512]{1,0:T(8,128)(2,1)S(1)}, u32[]{:S(2)}, u32[]{:S(2)}) collective-permute-start(bf16[227,512]{1,0:T(8,128)(2,1)S(1)} %get-tuple-element.64), channel_id=1, source_target_pairs={{0,2},{1,3},{2,0},{3,1},{4,6},{5,7},{6,4},{7,5},{8,10},{9,11},{10,... | collective-permute-start | bytes 697352 | tf_op jit(solution)/shard_map/ppermute | solution.py:313
  150.1 17.1 %collective-permute-done.17 = bf16[227,512]{1,0:T(8,128)(2,1)S(1)} collective-permute-done((bf16[227,512]{1,0:T(8,128)(2,1)S(1)}, bf16[227,512]{1,0:T(8,128)(2,1)S(1)}, u32[]{:S(2)}, u32[]{:S(2)}) %collective-permute-start.17) | collective-permute-done | bytes 232480 | tf_op jit(solution)/shard_map/ppermute | solution.py:313
  (66 shorter events, 22.0 us)
Async XLA Ops:
  0.6 11.5 %collective-permute-start.1 = (bf16[227,512]{1,0:T(8,128)(2,1)}, bf16[227,512]{1,0:T(8,128)(2,1)S(1)}, u32[]{:S(2)}, u32[]{:S(2)}) collective-permute-start(bf16[227,512]{1,0:T(8,128)(2,1)} %refs_0_.1), channel_id=1, source_target_pairs={{0,1},{1,2},{2,3},{3,0},{4,5},{5,6},{6,7},{7,4},{8,9},{9,10},{10,1... | collective-permute-start | bytes 697352 | tf_op jit(solution)/shard_map/ppermute | solution.py:313
  2.7 11.9 %collective-permute-start.2 = (bf16[227,512]{1,0:T(8,128)(2,1)}, bf16[227,512]{1,0:T(8,128)(2,1)S(1)}, u32[]{:S(2)}, u32[]{:S(2)}) collective-permute-start(bf16[227,512]{1,0:T(8,128)(2,1)} %refs_0_.1), channel_id=1, source_target_pairs={{0,3},{1,0},{2,1},{3,2},{4,7},{5,4},{6,5},{7,6},{8,11},{9,8},{10,9... | collective-permute-start | bytes 697352 | tf_op jit(solution)/shard_map/ppermute | solution.py:313
  5.9 14.6 %collective-permute-start.3 = (bf16[64,640]{1,0:T(8,128)(2,1)S(1)}, bf16[64,640]{1,0:T(8,128)(2,1)S(1)}, u32[]{:S(2)}, u32[]{:S(2)}) collective-permute-start(bf16[64,640]{1,0:T(8,128)(2,1)S(1)} %concatenate.12), channel_id=1, source_target_pairs={{0,1},{1,2},{2,3},{3,0},{4,5},{5,6},{6,7},{7,4},{8,9},{9,10},{10,1... | collective-permute-start | bytes 245768 | tf_op jit(solution)/shard_map/ppermute | solution.py:313
  6.1 14.4 %collective-permute-start.4 = (bf16[64,640]{1,0:T(8,128)(2,1)S(1)}, bf16[64,640]{1,0:T(8,128)(2,1)S(1)}, u32[]{:S(2)}, u32[]{:S(2)}) collective-permute-start(bf16[64,640]{1,0:T(8,128)(2,1)S(1)} %concatenate.12), channel_id=1, source_target_pairs={{0,2},{1,3},{2,0},{3,1},{4,6},{5,7},{6,4},{7,5},{8,10},{9,11},{10,... | collective-permute-start | bytes 245768 | tf_op jit(solution)/shard_map/ppermute | solution.py:313
  8.5 12.0 %collective-permute-start = (bf16[227,512]{1,0:T(8,128)(2,1)}, bf16[227,512]{1,0:T(8,128)(2,1)S(1)}, u32[]{:S(2)}, u32[]{:S(2)}) collective-permute-start(bf16[227,512]{1,0:T(8,128)(2,1)} %refs_0_.1), channel_id=1, source_target_pairs={{0,2},{1,3},{2,0},{3,1},{4,6},{5,7},{6,4},{7,5},{8,10},{9,11},{10,... | collective-permute-start | bytes 697352 | tf_op jit(solution)/shard_map/ppermute | solution.py:313
  12.1 8.4 %collective-permute-start.5 = (bf16[64,640]{1,0:T(8,128)(2,1)S(1)}, bf16[64,640]{1,0:T(8,128)(2,1)S(1)}, u32[]{:S(2)}, u32[]{:S(2)}) collective-permute-start(bf16[64,640]{1,0:T(8,128)(2,1)S(1)} %concatenate.12), channel_id=1, source_target_pairs={{0,3},{1,0},{2,1},{3,2},{4,7},{5,4},{6,5},{7,6},{8,11},{9,8},{10,9... | collective-permute-start | bytes 245768 | tf_op jit(solution)/shard_map/ppermute | solution.py:313
  21.7 8.6 %collective-permute-start.6 = (bf16[227,512]{1,0:T(8,128)(2,1)S(1)}, bf16[227,512]{1,0:T(8,128)(2,1)S(1)}, u32[]{:S(2)}, u32[]{:S(2)}) collective-permute-start(bf16[227,512]{1,0:T(8,128)(2,1)S(1)} %get-tuple-element.63), channel_id=1, source_target_pairs={{0,4},{4,8},{8,12},{12,16},{16,20},{20,24},{24,28},{28,32},{32,36}... | collective-permute-start | bytes 697352 | tf_op jit(solution)/shard_map/ppermute | solution.py:291
  27.3 7.4 %collective-permute-start.7 = (bf16[227,512]{1,0:T(8,128)(2,1)S(1)}, bf16[227,512]{1,0:T(8,128)(2,1)S(1)}, u32[]{:S(2)}, u32[]{:S(2)}) collective-permute-start(bf16[227,512]{1,0:T(8,128)(2,1)S(1)} %get-tuple-element.62), channel_id=1, source_target_pairs={{4,0},{8,4},{12,8},{16,12},{20,16},{24,20},{28,24},{32,28},{36,32}... | collective-permute-start | bytes 697352 | tf_op jit(solution)/shard_map/ppermute | solution.py:296
  50.9 4.4 %collective-permute-start.10 = (bf16[64,512]{1,0:T(8,128)(2,1)}, bf16[64,512]{1,0:T(8,128)(2,1)S(1)}, u32[]{:S(2)}, u32[]{:S(2)}) collective-permute-start(bf16[64,512]{1,0:T(8,128)(2,1)} %get-tuple-element.34), channel_id=1, source_target_pairs={{0,3},{1,0},{2,1},{3,2},{4,7},{5,4},{6,5},{7,6},{8,11},{9,8},{10,9... | collective-permute-start | bytes 196616 | tf_op jit(solution)/shard_map/ppermute | solution.py:313
  53.0 5.2 %collective-permute-start.8 = (bf16[64,512]{1,0:T(8,128)(2,1)}, bf16[64,512]{1,0:T(8,128)(2,1)S(1)}, u32[]{:S(2)}, u32[]{:S(2)}) collective-permute-start(bf16[64,512]{1,0:T(8,128)(2,1)} %get-tuple-element.34), channel_id=1, source_target_pairs={{0,1},{1,2},{2,3},{3,0},{4,5},{5,6},{6,7},{7,4},{8,9},{9,10},{10,1... | collective-permute-start | bytes 196616 | tf_op jit(solution)/shard_map/ppermute | solution.py:313
  53.0 5.2 %collective-permute-start.9 = (bf16[64,512]{1,0:T(8,128)(2,1)}, bf16[64,512]{1,0:T(8,128)(2,1)S(1)}, u32[]{:S(2)}, u32[]{:S(2)}) collective-permute-start(bf16[64,512]{1,0:T(8,128)(2,1)} %get-tuple-element.34), channel_id=1, source_target_pairs={{0,2},{1,3},{2,0},{3,1},{4,6},{5,7},{6,4},{7,5},{8,10},{9,11},{10,... | collective-permute-start | bytes 196616 | tf_op jit(solution)/shard_map/ppermute | solution.py:313
  59.1 12.2 %collective-permute-start.11 = (bf16[256,1152]{1,0:T(8,128)(2,1)S(1)}, bf16[256,1152]{1,0:T(8,128)(2,1)S(1)}, u32[]{:S(2)}, u32[]{:S(2)}) collective-permute-start(bf16[256,1152]{1,0:T(8,128)(2,1)S(1)} %maximum_maximum_fusion.band_ref.own_ref), channel_id=1, source_target_pairs={{0,4},{1,5},{4,8},{5,9},{6,2},{7,3},{8,12},{9,13},{10,6},{11,7},{1... | collective-permute-start | bytes 1769480 | tf_op jit(solution)/shard_map/ppermute | solution.py:308
  63.4 7.9 %collective-permute-start.12 = (bf16[64,512]{1,0:T(8,128)(2,1)S(1)}, bf16[64,512]{1,0:T(8,128)(2,1)S(1)}, u32[]{:S(2)}, u32[]{:S(2)}) collective-permute-start(bf16[64,512]{1,0:T(8,128)(2,1)S(1)} %constant_dynamic-slice_fusion), channel_id=1, source_target_pairs={{2,6},{3,7},{4,0},{5,1},{6,10},{7,11},{8,4},{9,5},{10,14},{11,15},... | collective-permute-start | bytes 196616 | tf_op jit(solution)/shard_map/ppermute | solution.py:308
  88.6 27.6 %all-to-all-start = ((bf16[32,32,512]{2,1,0:T(8,128)(2,1)}), bf16[32,32,512]{2,1,0:T(8,128)(2,1)S(1)}, u32[]{:S(2)}, u32[]{:S(2)}) async-start(bf16[32,32,512]{2,1,0:T(8,128)(2,1)} %bitcast.10), calls=%async_computation | async-start | bytes 2097152 | tf_op jit(solution)/shard_map/all_to_all | solution.py:498
  110.6 15.8 %copy-start.8 = (bf16[227,512]{1,0:T(8,128)(2,1)S(1)}, bf16[227,512]{1,0:T(8,128)(2,1)}, u32[]{:S(2)}) copy-start(bf16[227,512]{1,0:T(8,128)(2,1)} %get-tuple-element.57) | copy-start | bytes 697348
  110.6 15.8 %copy-start.9 = (bf16[227,512]{1,0:T(8,128)(2,1)S(1)}, bf16[227,512]{1,0:T(8,128)(2,1)}, u32[]{:S(2)}) copy-start(bf16[227,512]{1,0:T(8,128)(2,1)} %get-tuple-element.55) | copy-start | bytes 697348
  110.6 15.8 %collective-permute-start.13 = (bf16[227,512]{1,0:T(8,128)(2,1)}, bf16[227,512]{1,0:T(8,128)(2,1)S(1)}, u32[]{:S(2)}, u32[]{:S(2)}) collective-permute-start(bf16[227,512]{1,0:T(8,128)(2,1)} %get-tuple-element.51), channel_id=1, source_target_pairs={{0,4},{4,8},{8,12},{12,16},{16,20},{20,24},{24,28},{28,32},{32,36}... | collective-permute-start | bytes 697352 | tf_op jit(solution)/shard_map/ppermute | solution.py:291
  114.3 12.1 %collective-permute-start.14 = (bf16[227,512]{1,0:T(8,128)(2,1)}, bf16[227,512]{1,0:T(8,128)(2,1)S(1)}, u32[]{:S(2)}, u32[]{:S(2)}) collective-permute-start(bf16[227,512]{1,0:T(8,128)(2,1)} %get-tuple-element.52), channel_id=1, source_target_pairs={{4,0},{8,4},{12,8},{16,12},{20,16},{24,20},{28,24},{32,28},{36,32}... | collective-permute-start | bytes 697352 | tf_op jit(solution)/shard_map/ppermute | solution.py:296
  117.2 18.7 %all-to-all-start.1 = ((bf16[8,32,512]{2,1,0:T(8,128)(2,1)}), bf16[8,32,512]{2,1,0:T(8,128)(2,1)S(1)}, u32[]{:S(2)}, u32[]{:S(2)}) async-start(bf16[8,32,512]{2,1,0:T(8,128)(2,1)} %broadcast_in_dim.7), calls=%async_computation.1 | async-start | bytes 524288 | tf_op jit(solution)/shard_map/all_to_all | solution.py:284
  126.8 6.2 %collective-permute-start.15 = (bf16[227,512]{1,0:T(8,128)(2,1)S(1)}, bf16[227,512]{1,0:T(8,128)(2,1)S(1)}, u32[]{:S(2)}, u32[]{:S(2)}) collective-permute-start(bf16[227,512]{1,0:T(8,128)(2,1)S(1)} %get-tuple-element.66), channel_id=1, source_target_pairs={{0,1},{1,2},{2,3},{3,0},{4,5},{5,6},{6,7},{7,4},{8,9},{9,10},{10,1... | collective-permute-start | bytes 697352 | tf_op jit(solution)/shard_map/ppermute | solution.py:313
  128.0 5.0 %collective-permute-start.16 = (bf16[227,512]{1,0:T(8,128)(2,1)S(1)}, bf16[227,512]{1,0:T(8,128)(2,1)S(1)}, u32[]{:S(2)}, u32[]{:S(2)}) collective-permute-start(bf16[227,512]{1,0:T(8,128)(2,1)S(1)} %get-tuple-element.65), channel_id=1, source_target_pairs={{0,3},{1,0},{2,1},{3,2},{4,7},{5,4},{6,5},{7,6},{8,11},{9,8},{10,9... | collective-permute-start | bytes 697352 | tf_op jit(solution)/shard_map/ppermute | solution.py:313
  137.0 30.1 %copy-start.4 = (bf16[227,512]{1,0:T(8,128)(2,1)S(1)}, bf16[227,512]{1,0:T(8,128)(2,1)}, u32[]{:S(2)}) copy-start(bf16[227,512]{1,0:T(8,128)(2,1)} %get-tuple-element.50) | copy-start | bytes 697348
  137.0 31.1 %all-to-all-start.2 = ((bf16[32,32,512]{2,1,0:T(8,128)(2,1)}), bf16[32,32,512]{2,1,0:T(8,128)(2,1)S(1)}, u32[]{:S(2)}, u32[]{:S(2)}) async-start(bf16[32,32,512]{2,1,0:T(8,128)(2,1)} %broadcast_in_dim.8), calls=%async_computation.2 | async-start | bytes 2097152 | tf_op jit(solution)/shard_map/all_to_all | solution.py:284
  147.1 20.1 %collective-permute-start.17 = (bf16[227,512]{1,0:T(8,128)(2,1)S(1)}, bf16[227,512]{1,0:T(8,128)(2,1)S(1)}, u32[]{:S(2)}, u32[]{:S(2)}) collective-permute-start(bf16[227,512]{1,0:T(8,128)(2,1)S(1)} %get-tuple-element.64), channel_id=1, source_target_pairs={{0,2},{1,3},{2,0},{3,1},{4,6},{5,7},{6,4},{7,5},{8,10},{9,11},{10,... | collective-permute-start | bytes 697352 | tf_op jit(solution)/shard_map/ppermute | solution.py:313
  (10 other events, 51.4 us)

commit v9 on v7

--- a/solution.py
+++ b/solution.py
@@ -127,16 +127,14 @@
 
 def mesh_kernel(
     mesh_scale, scale, count,
-    sub_ref, band_all, far_all, side_ref, proc_ref, recv_ref, edge_ref,
+    sub_ref, band_ref, far_ref, side_ref, pay_ref, far_pay_ref, proc_ref, recv_ref, edge_ref,
     active_ref, normed_ref, inverse_ref, bslope_ref, hidden_ref,
     out_ref, bgrad_ref, wgrad_ref,
-    receiver_all, cots, columns, lines, query_grad, centred_ref, upper_ref, edge_total, src_total,
+    receiver_all, cots, columns, lines, query_grad, upper_ref, edge_total, src_total,
 ):
     step = pl.program_id(0)
     rows, latent = side_ref.shape
-    wide = band_all.shape[0]
-    band_ref, far_ref = band_all.at[:, :latent], far_all.at[:, :latent]
-    pay_ref, far_pay_ref = band_all.at[:, latent:], far_all.at[:, latent:]
+    wide = band_ref.shape[0]
 
     @pl.when(step == 0)
     def _():
@@ -195,16 +193,16 @@
         lax.fori_loop(0, count, one, 0)
         mesh_grad = pay_ref[:rows, :latent].astype(F32) + dot_t(query_grad[...].astype(BF), proc)
         mesh_grad = mesh_grad + dot_t(receiver_grad.astype(BF), recv)
-        upper = mesh_grad * scale
-        upper_ref[...] = upper
-        centred_ref[...] = upper - jnp.mean(upper, axis=-1, keepdims=True)
+        upper_ref[...] = mesh_grad * scale
         edge_total[...] = jnp.zeros_like(edge_total)
         src_total[...] = jnp.zeros_like(src_total)
 
+    upper = upper_ref[...]
+    centred = upper - jnp.mean(upper, axis=-1, keepdims=True)
     normed = normed_ref[...].astype(F32).reshape(-1, rows, latent)
     inverse = inverse_ref[...].reshape(-1, rows, 1)
-    along = jnp.mean(upper_ref[...][None] * normed, axis=-1, keepdims=True)
-    ngrad = ((centred_ref[...][None] - normed * along) * inverse).reshape(-1, latent).astype(BF)
+    along = jnp.mean(upper[None] * normed, axis=-1, keepdims=True)
+    ngrad = ((centred[None] - normed * along) * inverse).reshape(-1, latent).astype(BF)
     edge_total[...] += t_dot(active_ref[...], ngrad)
     bgrad = (dot_t(ngrad, edge_ref[...]) * bslope_ref[...].astype(F32)).astype(BF)
     bgrad_ref[...] = bgrad
@@ -320,6 +318,14 @@
     grid = [grid_x] + [along_sub(grid_x, k) for k in range(1, SUBS)]
     grid_local = (g2m_src - (band * (nodes * SUBS) - nodes)).T.reshape(edges, 1)
 
+    place = mesh_src - (band * width - rows)
+    half = 64
+    spare = jnp.zeros((rows, half - mesh_count), BF)
+    pay = jnp.concatenate(
+        [cotangent, (place // rows).astype(BF), spare, (place % rows).astype(BF), spare], axis=1
+    )
+    pays = [pay] + [along_sub(pay, k) for k in range(1, SUBS)]
+
     nearest = (0, 1, 3)
     picked = pl.pallas_call(
         functools.partial(gather_kernel, nearest),
@@ -340,24 +346,13 @@
         name="gather",
     )(sub_scalar, grid_local, *[grid[k] for k in nearest])
 
-    grid[2], picked = lax.optimization_barrier((grid[2], picked))
+    grid[2], picked, *pays = lax.optimization_barrier((grid[2], picked, *pays))
     last = lax.select_n(lax.rem(sub + 1, SUBS), *grid)
     first = lax.select_n(sub, *grid)
     grid_low = bands_up(last)
     grid_high = bands_down(first)
-
-    place = mesh_src - (band * width - rows)
-    half = 64
-    spare = jnp.zeros((rows, half - mesh_count), BF)
-    pay = jnp.concatenate(
-        [cotangent, (place // rows).astype(BF), spare, (place % rows).astype(BF), spare], axis=1
-    )
-    pay = jnp.broadcast_to(pay[None], (SUBS, *pay.shape))
-    pay, grid_low, grid_high = lax.optimization_barrier((pay, grid_low, grid_high))
-    pay = lax.all_to_all(pay, "sub", 0, 0, tiled=True)
-    pay = jnp.concatenate(
-        [lax.dynamic_index_in_dim(pay, lax.rem(sub + SUBS - k, SUBS), 0, False) for k in range(SUBS)]
-    )
+    pay = jnp.concatenate(pays)
+    far_pay = outwards(pay, True)
 
     hidden, hslope, active, bslope, normed, inverse, hidden_mesh = pl.pallas_call(
         functools.partial(forward_kernel, scale),
@@ -386,19 +381,20 @@
     )(sub_scalar, grid_local, picked, grid[2], grid_low, grid_high, mesh_in, w_embed, w_src, w_dst, w_edge)
 
     mesh_band = jnp.concatenate([hidden_mesh] + [along_sub(hidden_mesh, k) for k in range(1, SUBS)])
-    mesh_band = jnp.concatenate([mesh_band, pay], axis=1)
     mesh_far = outwards(mesh_band, True)
     at = jnp.where(sub < SUBS // 2, sub, lax.rem(sub + 1, SUBS)) * rows
-    mesh_side = outwards(lax.dynamic_slice(mesh_band, (at, 0), (rows, latent)), False)
+    mesh_side = outwards(lax.dynamic_slice_in_dim(mesh_band, at, rows), False)
 
     mesh_out, bgrad, part = pl.pallas_call(
         functools.partial(mesh_kernel, mesh_scale, scale, mesh_count),
         grid=(steps,),
         in_specs=[
             scalar(),
-            whole((width, 2 * latent + 2 * half)),
-            whole((width, 2 * latent + 2 * half)),
+            whole((width, latent)),
+            whole((width, latent)),
             whole((rows, latent)),
+            whole((width, latent + 2 * half)),
+            whole((width, latent + 2 * half)),
             whole((latent, latent)),
             whole((latent, latent)),
             whole((latent, latent)),
@@ -421,14 +417,13 @@
             pltpu.VMEM((2 * half, 2 * width), jnp.int32),
             pltpu.VMEM((rows, latent), F32),
             pltpu.VMEM((rows, latent), F32),
-            pltpu.VMEM((rows, latent), F32),
             pltpu.VMEM((latent, latent), F32),
             pltpu.VMEM((latent, latent), F32),
         ],
         compiler_params=params(),
         name="process",
     )(
-        sub_scalar, mesh_band, mesh_far, mesh_side, w_proc, w_recv, w_edge,
+        sub_scalar, mesh_band, mesh_far, mesh_side, pay, far_pay, w_proc, w_recv, w_edge,
         active, normed, inverse, bslope, hidden,
     )
 
@@ -461,14 +456,11 @@
         value += jnp.where(block == 0, from_below, jnp.zeros_like(from_below)).astype(F32)
         value += jnp.where(block == SUBS - 1, from_above, jnp.zeros_like(from_above)).astype(F32)
         values.append(value.astype(BF) if k else value)
-    ahead = along_sub(values[1], 1)
-    relayed = along_sub(values[2], -1)
+    arrived = values[:1] + [along_sub(values[k], k) for k in range(1, SUBS)]
     pieces = from_everyone(summed(pieces), FAR)
-    pieces, ahead, relayed = lax.optimization_barrier((pieces, ahead, relayed))
-    behind = along_sub((values[3].astype(F32) + relayed.astype(F32)).astype(BF), -1)
+    pieces, arrived[1], arrived[3] = lax.optimization_barrier((pieces, arrived[1], arrived[3]))
     weights = from_everyone(summed(pieces), NEAR).reshape(2 * latent, latent)
-    weights, behind = lax.optimization_barrier((weights, behind))
-    grid_grad = values[0] + ahead.astype(F32) + behind.astype(F32)
+    grid_grad = functools.reduce(jnp.add, [value.astype(F32) for value in arrived])
     src_grad, edge_grad = weights[latent:].astype(F32), weights[:latent].astype(F32)
     return (mesh_out, grid_grad, src_grad, edge_grad)
 

time: 173 us -> 169 us (0.977)
  waiting for transfers between devices: 35.3 us -> 30.1 us
  starting transfers between devices: 73.3 us -> 70.8 us
  local copies, waits for them, and re-layouts: 6.76 us -> 9.13 us
    all_to_all x1 -> x0, starting transfers between devices: 4.55 us -> none  [body(): pay = lax.all_to_all(pay, 'sub', 0, 0, tiled=True)]
    ppermute x2, starting transfers between devices: 12.5 us -> 9.08 us  [bands_up(): return lax.ppermute(value, BAND, [(i, i + 1) for i in range(count - 1)])]
    ppermute x2 -> x3, starting transfers between devices: 6.58 us -> 9.58 us  [outwards(): return lax.ppermute(value, ALL, pairs)]
    ppermute x2, waiting for transfers between devices: 4.4 us -> 1.74 us  [bands_down(): return lax.ppermute(value, BAND, [(i + 1, i) for i in range(count - 1)])]
    ppermute x9 -> x12, starting transfers between devices: 15.6 us -> 18.2 us  [along_sub(): lax.ppermute(value, 'sub', [(i, (i + steps) % count) for i in range(count)])]
    all_to_all x1, starting transfers between devices: 10.8 us -> 8.42 us  [body(): lax.all_to_all(part.reshape(near, -1, latent), NEAR, 0, 0, tiled=True)]
    all_to_all x2, starting transfers between devices: 19.3 us -> 21.7 us  [from_everyone(): lax.all_to_all(jnp.broadcast_to(shard[None], (devices, *shard.shape)), ax...]
    unnamed x31, local copies, waits for them, and re-layouts: 1.66 us -> 3.88 us
  transfers between devices with their start and end apart: 19 -> 22, of which waited for: 11 -> 8; matrix products, arithmetic and copies ran while one was open for 3% -> 5% of each run, Pallas kernels for 19% -> 19%
where the time goes in v9:
time: 169 us; the launch traced here: 168 us
  starting transfers between devices  70.8 us (42%)
  Pallas kernels  50.2 us (30%)
  waiting for transfers between devices  30.1 us (18%)
  local copies, waits for them, and re-layouts  9.13 us (5%)
  other arithmetic  6.36 us (4%)
    ppermute x12, waiting for transfers between devices, along_sub(): lax.ppermute(value, 'sub', [(i, (i + steps) % count) for i in range(count)])  23 us
    all_to_all x2, starting transfers between devices, from_everyone(): lax.all_to_all(jnp.broadcast_to(shard[None], (devices, *shard.shape)), ax...  21.7 us
    ppermute x12, starting transfers between devices, along_sub(): lax.ppermute(value, 'sub', [(i, (i + steps) % count) for i in range(count)])  18.2 us
    pallas_call x1, Pallas kernels, body(): pl.pallas_call(functools.partial(mesh_kernel, mesh_scale, scale, mesh_cou...  17.9 us
    pallas_call x1, Pallas kernels, body(): pl.pallas_call(functools.partial(forward_kernel, scale), grid=(steps,), i...  15.4 us
    pallas_call x1, Pallas kernels, body(): pl.pallas_call(grid_kernel, grid=(steps,), in_specs=[scalar(), tiled(tile...  11.8 us
    ppermute x3, starting transfers between devices, outwards(): return lax.ppermute(value, ALL, pairs)  9.58 us
    ppermute x2, starting transfers between devices, bands_up(): return lax.ppermute(value, BAND, [(i, i + 1) for i in range(count - 1)])  9.08 us
  transfers between devices with their start and end apart: 22, of which 8 were waited for; matrix products, arithmetic and copies ran while one was open for 5% of the time, Pallas kernels for 19%

profile of v9, /device:TPU:1, one launch (start us, length us, event | category | flops | bytes accessed | tf_op | source)
XLA Modules:
  0.0 167.6 jit_solution(17395397520795429938)
XLA Ops:
  0.6 2.1 %collective-permute-start.1 = (bf16[227,512]{1,0:T(8,128)(2,1)}, bf16[227,512]{1,0:T(8,128)(2,1)S(1)}, u32[]{:S(2)}, u32[]{:S(2)}) collective-permute-start(bf16[227,512]{1,0:T(8,128)(2,1)} %refs_0_.1), channel_id=1, source_target_pairs={{0,1},{1,2},{2,3},{3,0},{4,5},{5,6},{6,7},{7,4},{8,9},{9,10},{10,1... | collective-permute-start | bytes 697352 | tf_op jit(solution)/shard_map/ppermute | solution.py:293
  6.1 2.5 %collective-permute-start.4 = (bf16[64,640]{1,0:T(8,128)(2,1)S(1)}, bf16[64,640]{1,0:T(8,128)(2,1)S(1)}, u32[]{:S(2)}, u32[]{:S(2)}) collective-permute-start(bf16[64,640]{1,0:T(8,128)(2,1)S(1)} %concatenate.9), channel_id=1, source_target_pairs={{0,2},{1,3},{2,0},{3,1},{4,6},{5,7},{6,4},{7,5},{8,10},{9,11},{10,... | collective-permute-start | bytes 245768 | tf_op jit(solution)/shard_map/ppermute | solution.py:293
  9.8 2.4 %reshape.31.index_ref = s32[2560,1]{1,0:T(8,128)} reshape(s32[40,64]{1,0:T(8,128)S(1)} %subtract_bitcast_fusion) | data formatting | bytes 20480 | tf_op jit(solution)/shard_map/reshape | solution.py:319
  12.1 2.6 %collective-permute-start.5 = (bf16[64,640]{1,0:T(8,128)(2,1)S(1)}, bf16[64,640]{1,0:T(8,128)(2,1)S(1)}, u32[]{:S(2)}, u32[]{:S(2)}) collective-permute-start(bf16[64,640]{1,0:T(8,128)(2,1)S(1)} %concatenate.9), channel_id=1, source_target_pairs={{0,3},{1,0},{2,1},{3,2},{4,7},{5,4},{6,5},{7,6},{8,11},{9,8},{10,9... | collective-permute-start | bytes 245768 | tf_op jit(solution)/shard_map/ppermute | solution.py:293
  15.4 5.1 %gather.1.picked_ref = bf16[2560,256]{1,0:T(8,128)(2,1)} custom-call(s32[1]{0:T(128)} %bitcast.sub_ref, s32[2560,1]{1,0:T(8,128)} %reshape.31.index_ref, bf16[227,512]{1,0:T(8,128)(2,1)} %refs_0_.1, bf16[227,512]{1,0:T(8,128)(2,1)} %copy-done.7, bf16[227,512]{1,0:T(8,128)(2,1)} %copy-done.8), custom_call_target="tpu_custom_call" | custom-call | flops 2013265920 | bytes 1310720 | tf_op jit(solution)/shard_map/gather/pallas_call | solution.py:330
  21.7 5.5 %collective-permute-start.6 = (bf16[227,512]{1,0:T(8,128)(2,1)S(1)}, bf16[227,512]{1,0:T(8,128)(2,1)S(1)}, u32[]{:S(2)}, u32[]{:S(2)}) collective-permute-start(bf16[227,512]{1,0:T(8,128)(2,1)S(1)} %get-tuple-element.57), channel_id=1, source_target_pairs={{0,4},{4,8},{8,12},{12,16},{16,20},{20,24},{24,28},{28,32},{32,36}... | collective-permute-start | bytes 697352 | tf_op jit(solution)/shard_map/ppermute | solution.py:271
  27.3 1.9 %collective-permute-start.7 = (bf16[227,512]{1,0:T(8,128)(2,1)S(1)}, bf16[227,512]{1,0:T(8,128)(2,1)S(1)}, u32[]{:S(2)}, u32[]{:S(2)}) collective-permute-start(bf16[227,512]{1,0:T(8,128)(2,1)S(1)} %get-tuple-element.56), channel_id=1, source_target_pairs={{4,0},{8,4},{12,8},{16,12},{20,16},{24,20},{28,24},{32,28},{36,32}... | collective-permute-start | bytes 697352 | tf_op jit(solution)/shard_map/ppermute | solution.py:276
  29.3 3.6 %collective-permute-start.13 = (bf16[256,640]{1,0:T(8,128)(2,1)S(1)}, bf16[256,640]{1,0:T(8,128)(2,1)S(1)}, u32[]{:S(2)}, u32[]{:S(2)}) collective-permute-start(bf16[256,640]{1,0:T(8,128)(2,1)S(1)} %constant_dynamic-update-slice_fusion.4.pay_ref), channel_id=1, source_target_pairs={{0,4},{1,5},{4,8},{5,9},{6,2},{7,3},{8,12},{9,13},{10,6},{11,7},{1... | collective-permute-start | bytes 983048 | tf_op jit(solution)/shard_map/ppermute | solution.py:288
  33.0 1.7 %collective-permute-done.7.high_ref = bf16[227,512]{1,0:T(8,128)(2,1)S(1)} collective-permute-done((bf16[227,512]{1,0:T(8,128)(2,1)S(1)}, bf16[227,512]{1,0:T(8,128)(2,1)S(1)}, u32[]{:S(2)}, u32[]{:S(2)}) %collective-permute-start.7) | collective-permute-done | bytes 232480 | tf_op jit(solution)/shard_map/ppermute | solution.py:276
  35.4 15.4 %encode.1 = (bf16[2560,512]{1,0:T(8,128)(2,1)}, bf16[2560,512]{1,0:T(8,128)(2,1)}, bf16[2560,512]{1,0:T(8,128)(2,1)}, bf16[2560,512]{1,0:T(8,128)(2,1)}, bf16[25...) custom-call(s32[1]{0:T(128)} %bitcast.sub_ref, s32[2560,1]{1,0:T(8,128)} %reshape.31.index_ref, ...), custom_call_target="tpu_custom_call" | custom-call | tf_op jit(solution)/shard_map/encode/pallas_call | solution.py:357
  51.0 3.2 %collective-permute-start.9 = (bf16[64,512]{1,0:T(8,128)(2,1)}, bf16[64,512]{1,0:T(8,128)(2,1)S(1)}, u32[]{:S(2)}, u32[]{:S(2)}) collective-permute-start(bf16[64,512]{1,0:T(8,128)(2,1)} %get-tuple-element.31), channel_id=1, source_target_pairs={{0,2},{1,3},{2,0},{3,1},{4,6},{5,7},{6,4},{7,5},{8,10},{9,11},{10,... | collective-permute-start | bytes 196616 | tf_op jit(solution)/shard_map/ppermute | solution.py:293
  57.5 4.0 %collective-permute-start.11 = (bf16[256,512]{1,0:T(8,128)(2,1)S(1)}, bf16[256,512]{1,0:T(8,128)(2,1)S(1)}, u32[]{:S(2)}, u32[]{:S(2)}) collective-permute-start(bf16[256,512]{1,0:T(8,128)(2,1)S(1)} %constant_dynamic-update-slice_fusion.band_ref), channel_id=1, source_target_pairs={{0,4},{1,5},{4,8},{5,9},{6,2},{7,3},{8,12},{9,13},{10,6},{11,7},{1... | collective-permute-start | bytes 786440 | tf_op jit(solution)/shard_map/ppermute | solution.py:288
  61.6 1.9 %collective-permute-start.12 = (bf16[64,512]{1,0:T(8,128)(2,1)S(1)}, bf16[64,512]{1,0:T(8,128)(2,1)S(1)}, u32[]{:S(2)}, u32[]{:S(2)}) collective-permute-start(bf16[64,512]{1,0:T(8,128)(2,1)S(1)} %constant_dynamic-slice_fusion), channel_id=1, source_target_pairs={{2,6},{3,7},{4,0},{5,1},{6,10},{7,11},{8,4},{9,5},{10,14},{11,15},... | collective-permute-start | bytes 196616 | tf_op jit(solution)/shard_map/ppermute | solution.py:288
  63.5 3.6 %collective-permute-done.12.side_ref = bf16[64,512]{1,0:T(8,128)(2,1)S(1)} collective-permute-done((bf16[64,512]{1,0:T(8,128)(2,1)S(1)}, bf16[64,512]{1,0:T(8,128)(2,1)S(1)}, u32[]{:S(2)}, u32[]{:S(2)}) %collective-permute-start.12) | collective-permute-done | bytes 65568 | tf_op jit(solution)/shard_map/ppermute | solution.py:288
  67.9 17.9 %process.1 = (bf16[64,512]{1,0:T(8,128)(2,1)}, bf16[2560,512]{1,0:T(8,128)(2,1)}, bf16[1024,512]{1,0:T(8,128)(2,1)}) custom-call(s32[1]{0:T(128)} %bitcast.sub_ref, bf16[256,512]{1,0:T(8,128)(2,1)} %copy-done.1, bf16[256,512]{1,0:T(8,128)(2,1)} %copy-done.4, bf16[64,512]{1,0:T(8,128)(2,1)} %copy-done.11, bf16[256,640]{1,0:T(8,128)(2,1)} %copy-done.2, ...), custom_call_target="tpu_custom_call" | custom-call | tf_op jit(solution)/shard_map/process/pallas_call | solution.py:388
  85.8 8.4 %all-to-all-start = ((bf16[32,32,512]{2,1,0:T(8,128)(2,1)}), bf16[32,32,512]{2,1,0:T(8,128)(2,1)S(1)}, u32[]{:S(2)}, u32[]{:S(2)}) async-start(bf16[32,32,512]{2,1,0:T(8,128)(2,1)} %bitcast.10), calls=%async_computation | async-start | bytes 2097152 | tf_op jit(solution)/shard_map/all_to_all | solution.py:449
  94.2 11.8 %channels.1 = (bf16[227,512]{1,0:T(8,128)(2,1)}, bf16[227,512]{1,0:T(8,128)(2,1)}, bf16[227,512]{1,0:T(8,128)(2,1)}, bf16[227,512]{1,0:T(8,128)(2,1)}, bf16[227,...) custom-call(s32[1]{0:T(128)} %bitcast.sub_ref, s32[2560,1]{1,0:T(8,128)} %reshape.31.index_ref, bf16[512,512]{1,0:T(8,128)(2,1)} %src_ref.3, ...), custom_call_target="tpu_custom_call" | custom-call | tf_op jit(solution)/shard_map/channels/pallas_call | solution.py:430
  106.0 3.5 %collective-permute-start.14 = (bf16[227,512]{1,0:T(8,128)(2,1)}, bf16[227,512]{1,0:T(8,128)(2,1)S(1)}, u32[]{:S(2)}, u32[]{:S(2)}) collective-permute-start(bf16[227,512]{1,0:T(8,128)(2,1)} %get-tuple-element.45), channel_id=1, source_target_pairs={{0,4},{4,8},{8,12},{12,16},{16,20},{20,24},{24,28},{28,32},{32,36}... | collective-permute-start | bytes 697352 | tf_op jit(solution)/shard_map/ppermute | solution.py:271
  109.6 1.9 %collective-permute-start.15 = (bf16[227,512]{1,0:T(8,128)(2,1)}, bf16[227,512]{1,0:T(8,128)(2,1)S(1)}, u32[]{:S(2)}, u32[]{:S(2)}) collective-permute-start(bf16[227,512]{1,0:T(8,128)(2,1)} %get-tuple-element.46), channel_id=1, source_target_pairs={{4,0},{8,4},{12,8},{16,12},{20,16},{24,20},{28,24},{32,28},{36,32}... | collective-permute-start | bytes 697352 | tf_op jit(solution)/shard_map/ppermute | solution.py:276
  112.4 11.8 %all-to-all-start.1 = ((bf16[8,32,512]{2,1,0:T(8,128)(2,1)}), bf16[8,32,512]{2,1,0:T(8,128)(2,1)S(1)}, u32[]{:S(2)}, u32[]{:S(2)}) async-start(bf16[8,32,512]{2,1,0:T(8,128)(2,1)} %broadcast_in_dim.7), calls=%async_computation.1 | async-start | bytes 524288 | tf_op jit(solution)/shard_map/all_to_all | solution.py:264
  128.5 3.5 %collective-permute-done.16 = bf16[227,512]{1,0:T(8,128)(2,1)S(1)} collective-permute-done((bf16[227,512]{1,0:T(8,128)(2,1)S(1)}, bf16[227,512]{1,0:T(8,128)(2,1)S(1)}, u32[]{:S(2)}, u32[]{:S(2)}) %collective-permute-start.16) | collective-permute-done | bytes 232480 | tf_op jit(solution)/shard_map/ppermute | solution.py:293
  134.8 9.9 %all-to-all-start.2 = ((bf16[32,32,512]{2,1,0:T(8,128)(2,1)}), bf16[32,32,512]{2,1,0:T(8,128)(2,1)S(1)}, u32[]{:S(2)}, u32[]{:S(2)}) async-start(bf16[32,32,512]{2,1,0:T(8,128)(2,1)} %broadcast_in_dim.8), calls=%async_computation.2 | async-start | bytes 2097152 | tf_op jit(solution)/shard_map/all_to_all | solution.py:264
  144.7 3.0 %collective-permute-start.18 = (bf16[227,512]{1,0:T(8,128)(2,1)S(1)}, bf16[227,512]{1,0:T(8,128)(2,1)S(1)}, u32[]{:S(2)}, u32[]{:S(2)}) collective-permute-start(bf16[227,512]{1,0:T(8,128)(2,1)S(1)} %get-tuple-element.58), channel_id=1, source_target_pairs={{0,2},{1,3},{2,0},{3,1},{4,6},{5,7},{6,4},{7,5},{8,10},{9,11},{10,... | collective-permute-start | bytes 697352 | tf_op jit(solution)/shard_map/ppermute | solution.py:293
  147.7 17.1 %collective-permute-done.18 = bf16[227,512]{1,0:T(8,128)(2,1)S(1)} collective-permute-done((bf16[227,512]{1,0:T(8,128)(2,1)S(1)}, bf16[227,512]{1,0:T(8,128)(2,1)S(1)}, u32[]{:S(2)}, u32[]{:S(2)}) %collective-permute-start.18) | collective-permute-done | bytes 232480 | tf_op jit(solution)/shard_map/ppermute | solution.py:293
  (72 shorter events, 22.1 us)
Async XLA Ops:
  0.6 11.5 %collective-permute-start.1 = (bf16[227,512]{1,0:T(8,128)(2,1)}, bf16[227,512]{1,0:T(8,128)(2,1)S(1)}, u32[]{:S(2)}, u32[]{:S(2)}) collective-permute-start(bf16[227,512]{1,0:T(8,128)(2,1)} %refs_0_.1), channel_id=1, source_target_pairs={{0,1},{1,2},{2,3},{3,0},{4,5},{5,6},{6,7},{7,4},{8,9},{9,10},{10,1... | collective-permute-start | bytes 697352 | tf_op jit(solution)/shard_map/ppermute | solution.py:293
  2.7 12.0 %collective-permute-start.2 = (bf16[227,512]{1,0:T(8,128)(2,1)}, bf16[227,512]{1,0:T(8,128)(2,1)S(1)}, u32[]{:S(2)}, u32[]{:S(2)}) collective-permute-start(bf16[227,512]{1,0:T(8,128)(2,1)} %refs_0_.1), channel_id=1, source_target_pairs={{0,3},{1,0},{2,1},{3,2},{4,7},{5,4},{6,5},{7,6},{8,11},{9,8},{10,9... | collective-permute-start | bytes 697352 | tf_op jit(solution)/shard_map/ppermute | solution.py:293
  5.9 14.6 %collective-permute-start.3 = (bf16[64,640]{1,0:T(8,128)(2,1)S(1)}, bf16[64,640]{1,0:T(8,128)(2,1)S(1)}, u32[]{:S(2)}, u32[]{:S(2)}) collective-permute-start(bf16[64,640]{1,0:T(8,128)(2,1)S(1)} %concatenate.9), channel_id=1, source_target_pairs={{0,1},{1,2},{2,3},{3,0},{4,5},{5,6},{6,7},{7,4},{8,9},{9,10},{10,1... | collective-permute-start | bytes 245768 | tf_op jit(solution)/shard_map/ppermute | solution.py:293
  6.1 14.4 %collective-permute-start.4 = (bf16[64,640]{1,0:T(8,128)(2,1)S(1)}, bf16[64,640]{1,0:T(8,128)(2,1)S(1)}, u32[]{:S(2)}, u32[]{:S(2)}) collective-permute-start(bf16[64,640]{1,0:T(8,128)(2,1)S(1)} %concatenate.9), channel_id=1, source_target_pairs={{0,2},{1,3},{2,0},{3,1},{4,6},{5,7},{6,4},{7,5},{8,10},{9,11},{10,... | collective-permute-start | bytes 245768 | tf_op jit(solution)/shard_map/ppermute | solution.py:293
  8.5 12.0 %collective-permute-start = (bf16[227,512]{1,0:T(8,128)(2,1)}, bf16[227,512]{1,0:T(8,128)(2,1)S(1)}, u32[]{:S(2)}, u32[]{:S(2)}) collective-permute-start(bf16[227,512]{1,0:T(8,128)(2,1)} %refs_0_.1), channel_id=1, source_target_pairs={{0,2},{1,3},{2,0},{3,1},{4,6},{5,7},{6,4},{7,5},{8,10},{9,11},{10,... | collective-permute-start | bytes 697352 | tf_op jit(solution)/shard_map/ppermute | solution.py:293
  12.1 8.3 %collective-permute-start.5 = (bf16[64,640]{1,0:T(8,128)(2,1)S(1)}, bf16[64,640]{1,0:T(8,128)(2,1)S(1)}, u32[]{:S(2)}, u32[]{:S(2)}) collective-permute-start(bf16[64,640]{1,0:T(8,128)(2,1)S(1)} %concatenate.9), channel_id=1, source_target_pairs={{0,3},{1,0},{2,1},{3,2},{4,7},{5,4},{6,5},{7,6},{8,11},{9,8},{10,9... | collective-permute-start | bytes 245768 | tf_op jit(solution)/shard_map/ppermute | solution.py:293
  21.7 11.2 %collective-permute-start.6 = (bf16[227,512]{1,0:T(8,128)(2,1)S(1)}, bf16[227,512]{1,0:T(8,128)(2,1)S(1)}, u32[]{:S(2)}, u32[]{:S(2)}) collective-permute-start(bf16[227,512]{1,0:T(8,128)(2,1)S(1)} %get-tuple-element.57), channel_id=1, source_target_pairs={{0,4},{4,8},{8,12},{12,16},{16,20},{20,24},{24,28},{28,32},{32,36}... | collective-permute-start | bytes 697352 | tf_op jit(solution)/shard_map/ppermute | solution.py:271
  27.3 7.4 %collective-permute-start.7 = (bf16[227,512]{1,0:T(8,128)(2,1)S(1)}, bf16[227,512]{1,0:T(8,128)(2,1)S(1)}, u32[]{:S(2)}, u32[]{:S(2)}) collective-permute-start(bf16[227,512]{1,0:T(8,128)(2,1)S(1)} %get-tuple-element.56), channel_id=1, source_target_pairs={{4,0},{8,4},{12,8},{16,12},{20,16},{24,20},{28,24},{32,28},{36,32}... | collective-permute-start | bytes 697352 | tf_op jit(solution)/shard_map/ppermute | solution.py:276
  29.3 25.8 %copy-start.2 = (bf16[256,640]{1,0:T(8,128)(2,1)}, bf16[256,640]{1,0:T(8,128)(2,1)S(1)}, u32[]{:S(2)}) copy-start(bf16[256,640]{1,0:T(8,128)(2,1)S(1)} %constant_dynamic-update-slice_fusion.4.pay_ref) | copy-start | bytes 983044
  29.3 34.2 %collective-permute-start.13 = (bf16[256,640]{1,0:T(8,128)(2,1)S(1)}, bf16[256,640]{1,0:T(8,128)(2,1)S(1)}, u32[]{:S(2)}, u32[]{:S(2)}) collective-permute-start(bf16[256,640]{1,0:T(8,128)(2,1)S(1)} %constant_dynamic-update-slice_fusion.4.pay_ref), channel_id=1, source_target_pairs={{0,4},{1,5},{4,8},{5,9},{6,2},{7,3},{8,12},{9,13},{10,6},{11,7},{1... | collective-permute-start | bytes 983048 | tf_op jit(solution)/shard_map/ppermute | solution.py:288
  50.9 4.6 %collective-permute-start.8 = (bf16[64,512]{1,0:T(8,128)(2,1)}, bf16[64,512]{1,0:T(8,128)(2,1)S(1)}, u32[]{:S(2)}, u32[]{:S(2)}) collective-permute-start(bf16[64,512]{1,0:T(8,128)(2,1)} %get-tuple-element.31), channel_id=1, source_target_pairs={{0,1},{1,2},{2,3},{3,0},{4,5},{5,6},{6,7},{7,4},{8,9},{9,10},{10,1... | collective-permute-start | bytes 196616 | tf_op jit(solution)/shard_map/ppermute | solution.py:293
  51.0 5.8 %collective-permute-start.9 = (bf16[64,512]{1,0:T(8,128)(2,1)}, bf16[64,512]{1,0:T(8,128)(2,1)S(1)}, u32[]{:S(2)}, u32[]{:S(2)}) collective-permute-start(bf16[64,512]{1,0:T(8,128)(2,1)} %get-tuple-element.31), channel_id=1, source_target_pairs={{0,2},{1,3},{2,0},{3,1},{4,6},{5,7},{6,4},{7,5},{8,10},{9,11},{10,... | collective-permute-start | bytes 196616 | tf_op jit(solution)/shard_map/ppermute | solution.py:293
  54.2 3.3 %collective-permute-start.10 = (bf16[64,512]{1,0:T(8,128)(2,1)}, bf16[64,512]{1,0:T(8,128)(2,1)S(1)}, u32[]{:S(2)}, u32[]{:S(2)}) collective-permute-start(bf16[64,512]{1,0:T(8,128)(2,1)} %get-tuple-element.31), channel_id=1, source_target_pairs={{0,3},{1,0},{2,1},{3,2},{4,7},{5,4},{6,5},{7,6},{8,11},{9,8},{10,9... | collective-permute-start | bytes 196616 | tf_op jit(solution)/shard_map/ppermute | solution.py:293
  57.5 9.6 %collective-permute-start.11 = (bf16[256,512]{1,0:T(8,128)(2,1)S(1)}, bf16[256,512]{1,0:T(8,128)(2,1)S(1)}, u32[]{:S(2)}, u32[]{:S(2)}) collective-permute-start(bf16[256,512]{1,0:T(8,128)(2,1)S(1)} %constant_dynamic-update-slice_fusion.band_ref), channel_id=1, source_target_pairs={{0,4},{1,5},{4,8},{5,9},{6,2},{7,3},{8,12},{9,13},{10,6},{11,7},{1... | collective-permute-start | bytes 786440 | tf_op jit(solution)/shard_map/ppermute | solution.py:288
  61.6 5.6 %collective-permute-start.12 = (bf16[64,512]{1,0:T(8,128)(2,1)S(1)}, bf16[64,512]{1,0:T(8,128)(2,1)S(1)}, u32[]{:S(2)}, u32[]{:S(2)}) collective-permute-start(bf16[64,512]{1,0:T(8,128)(2,1)S(1)} %constant_dynamic-slice_fusion), channel_id=1, source_target_pairs={{2,6},{3,7},{4,0},{5,1},{6,10},{7,11},{8,4},{9,5},{10,14},{11,15},... | collective-permute-start | bytes 196616 | tf_op jit(solution)/shard_map/ppermute | solution.py:288
  85.8 25.7 %all-to-all-start = ((bf16[32,32,512]{2,1,0:T(8,128)(2,1)}), bf16[32,32,512]{2,1,0:T(8,128)(2,1)S(1)}, u32[]{:S(2)}, u32[]{:S(2)}) async-start(bf16[32,32,512]{2,1,0:T(8,128)(2,1)} %bitcast.10), calls=%async_computation | async-start | bytes 2097152 | tf_op jit(solution)/shard_map/all_to_all | solution.py:449
  106.0 18.2 %collective-permute-start.14 = (bf16[227,512]{1,0:T(8,128)(2,1)}, bf16[227,512]{1,0:T(8,128)(2,1)S(1)}, u32[]{:S(2)}, u32[]{:S(2)}) collective-permute-start(bf16[227,512]{1,0:T(8,128)(2,1)} %get-tuple-element.45), channel_id=1, source_target_pairs={{0,4},{4,8},{8,12},{12,16},{16,20},{20,24},{24,28},{28,32},{32,36}... | collective-permute-start | bytes 697352 | tf_op jit(solution)/shard_map/ppermute | solution.py:271
  109.6 14.6 %collective-permute-start.15 = (bf16[227,512]{1,0:T(8,128)(2,1)}, bf16[227,512]{1,0:T(8,128)(2,1)S(1)}, u32[]{:S(2)}, u32[]{:S(2)}) collective-permute-start(bf16[227,512]{1,0:T(8,128)(2,1)} %get-tuple-element.46), channel_id=1, source_target_pairs={{4,0},{8,4},{12,8},{16,12},{20,16},{24,20},{28,24},{32,28},{36,32}... | collective-permute-start | bytes 697352 | tf_op jit(solution)/shard_map/ppermute | solution.py:276
  112.4 21.2 %all-to-all-start.1 = ((bf16[8,32,512]{2,1,0:T(8,128)(2,1)}), bf16[8,32,512]{2,1,0:T(8,128)(2,1)S(1)}, u32[]{:S(2)}, u32[]{:S(2)}) async-start(bf16[8,32,512]{2,1,0:T(8,128)(2,1)} %broadcast_in_dim.7), calls=%async_computation.1 | async-start | bytes 524288 | tf_op jit(solution)/shard_map/all_to_all | solution.py:264
  124.2 40.6 %copy-start.6 = (bf16[227,512]{1,0:T(8,128)(2,1)S(1)}, bf16[227,512]{1,0:T(8,128)(2,1)}, u32[]{:S(2)}) copy-start(bf16[227,512]{1,0:T(8,128)(2,1)} %get-tuple-element.44) | copy-start | bytes 697348
  125.7 6.2 %collective-permute-start.16 = (bf16[227,512]{1,0:T(8,128)(2,1)S(1)}, bf16[227,512]{1,0:T(8,128)(2,1)S(1)}, u32[]{:S(2)}, u32[]{:S(2)}) collective-permute-start(bf16[227,512]{1,0:T(8,128)(2,1)S(1)} %get-tuple-element.60), channel_id=1, source_target_pairs={{0,1},{1,2},{2,3},{3,0},{4,5},{5,6},{6,7},{7,4},{8,9},{9,10},{10,1... | collective-permute-start | bytes 697352 | tf_op jit(solution)/shard_map/ppermute | solution.py:293
  127.0 5.0 %collective-permute-start.17 = (bf16[227,512]{1,0:T(8,128)(2,1)S(1)}, bf16[227,512]{1,0:T(8,128)(2,1)S(1)}, u32[]{:S(2)}, u32[]{:S(2)}) collective-permute-start(bf16[227,512]{1,0:T(8,128)(2,1)S(1)} %get-tuple-element.59), channel_id=1, source_target_pairs={{0,3},{1,0},{2,1},{3,2},{4,7},{5,4},{6,5},{7,6},{8,11},{9,8},{10,9... | collective-permute-start | bytes 697352 | tf_op jit(solution)/shard_map/ppermute | solution.py:293
  134.8 31.0 %all-to-all-start.2 = ((bf16[32,32,512]{2,1,0:T(8,128)(2,1)}), bf16[32,32,512]{2,1,0:T(8,128)(2,1)S(1)}, u32[]{:S(2)}, u32[]{:S(2)}) async-start(bf16[32,32,512]{2,1,0:T(8,128)(2,1)} %broadcast_in_dim.8), calls=%async_computation.2 | async-start | bytes 2097152 | tf_op jit(solution)/shard_map/all_to_all | solution.py:264
  144.7 20.1 %collective-permute-start.18 = (bf16[227,512]{1,0:T(8,128)(2,1)S(1)}, bf16[227,512]{1,0:T(8,128)(2,1)S(1)}, u32[]{:S(2)}, u32[]{:S(2)}) collective-permute-start(bf16[227,512]{1,0:T(8,128)(2,1)S(1)} %get-tuple-element.58), channel_id=1, source_target_pairs={{0,2},{1,3},{2,0},{3,1},{4,6},{5,7},{6,4},{7,5},{8,10},{9,11},{10,... | collective-permute-start | bytes 697352 | tf_op jit(solution)/shard_map/ppermute | solution.py:293
  (10 other events, 39.7 us)

commit v10 on v9

--- a/solution.py
+++ b/solution.py
@@ -429,14 +429,14 @@
 
     *parts, part_low, part_high = pl.pallas_call(
         grid_kernel,
-        grid=(steps,),
+        grid=(steps // 2,),
         in_specs=[
             scalar(),
-            tiled(tile, 1),
+            tiled(2 * tile, 1),
             whole((latent, latent)),
             whole((channels, latent)),
-            tiled(tile, latent),
-            tiled(tile, latent),
+            tiled(2 * tile, latent),
+            tiled(2 * tile, latent),
         ],
         out_specs=[whole((channels, nodes))] * (SUBS + 2),
         out_shape=[jax.ShapeDtypeStruct((channels, nodes), BF)] * (SUBS + 2),
@@ -460,8 +460,9 @@
     pieces = from_everyone(summed(pieces), FAR)
     pieces, arrived[1], arrived[3] = lax.optimization_barrier((pieces, arrived[1], arrived[3]))
     weights = from_everyone(summed(pieces), NEAR).reshape(2 * latent, latent)
+    src_grad, edge_grad = weights[latent:].astype(F32), weights[:latent].astype(F32)
+    src_grad, edge_grad, arrived[2] = lax.optimization_barrier((src_grad, edge_grad, arrived[2]))
     grid_grad = functools.reduce(jnp.add, [value.astype(F32) for value in arrived])
-    src_grad, edge_grad = weights[latent:].astype(F32), weights[:latent].astype(F32)
     return (mesh_out, grid_grad, src_grad, edge_grad)
 
 

time: 169 us -> 166 us (0.982)
  waiting for transfers between devices: 30.1 us -> 28.3 us
    ppermute x12, waiting for transfers between devices: 23 us -> 8.06 us  [along_sub(): lax.ppermute(value, 'sub', [(i, (i + steps) % count) for i in range(count)])]
    all_to_all x2, waiting for transfers between devices: 1.68 us -> 14.9 us  [from_everyone(): lax.all_to_all(jnp.broadcast_to(shard[None], (devices, *shard.shape)), ax...]
  transfers between devices with their start and end apart: 22 -> 22, of which waited for: 8 -> 9; matrix products, arithmetic and copies ran while one was open for 5% -> 6% of each run, Pallas kernels for 19% -> 19%
where the time goes in v10:
time: 166 us; the launch traced here: 165 us
  starting transfers between devices  70.8 us (43%)
  Pallas kernels  49.1 us (30%)
  waiting for transfers between devices  28.3 us (17%)
  local copies, waits for them, and re-layouts  9.13 us (6%)
  other arithmetic  6.32 us (4%)
    all_to_all x2, starting transfers between devices, from_everyone(): lax.all_to_all(jnp.broadcast_to(shard[None], (devices, *shard.shape)), ax...  21.7 us
    ppermute x12, starting transfers between devices, along_sub(): lax.ppermute(value, 'sub', [(i, (i + steps) % count) for i in range(count)])  18.2 us
    pallas_call x1, Pallas kernels, body(): pl.pallas_call(functools.partial(mesh_kernel, mesh_scale, scale, mesh_cou...  17.9 us
    pallas_call x1, Pallas kernels, body(): pl.pallas_call(functools.partial(forward_kernel, scale), grid=(steps,), i...  15.4 us
    all_to_all x2, waiting for transfers between devices, from_everyone(): lax.all_to_all(jnp.broadcast_to(shard[None], (devices, *shard.shape)), ax...  14.9 us
    pallas_call x1, Pallas kernels, body(): pl.pallas_call(grid_kernel, grid=(steps // 2,), in_specs=[scalar(), tiled...  10.7 us
    ppermute x3, starting transfers between devices, outwards(): return lax.ppermute(value, ALL, pairs)  9.58 us
    ppermute x2, starting transfers between devices, bands_up(): return lax.ppermute(value, BAND, [(i, i + 1) for i in range(count - 1)])  9.08 us
  transfers between devices with their start and end apart: 22, of which 9 were waited for; matrix products, arithmetic and copies ran while one was open for 6% of the time, Pallas kernels for 19%

profile of v10, /device:TPU:1, one launch (start us, length us, event | category | flops | bytes accessed | tf_op | source)
XLA Modules:
  0.0 164.6 jit_solution(819611431035266534)
XLA Ops:
  0.6 2.1 %collective-permute-start.1 = (bf16[227,512]{1,0:T(8,128)(2,1)}, bf16[227,512]{1,0:T(8,128)(2,1)S(1)}, u32[]{:S(2)}, u32[]{:S(2)}) collective-permute-start(bf16[227,512]{1,0:T(8,128)(2,1)} %refs_0_.1), channel_id=1, source_target_pairs={{0,1},{1,2},{2,3},{3,0},{4,5},{5,6},{6,7},{7,4},{8,9},{9,10},{10,1... | collective-permute-start | bytes 697352 | tf_op jit(solution)/shard_map/ppermute | solution.py:293
  6.1 2.5 %collective-permute-start.4 = (bf16[64,640]{1,0:T(8,128)(2,1)S(1)}, bf16[64,640]{1,0:T(8,128)(2,1)S(1)}, u32[]{:S(2)}, u32[]{:S(2)}) collective-permute-start(bf16[64,640]{1,0:T(8,128)(2,1)S(1)} %concatenate.9), channel_id=1, source_target_pairs={{0,2},{1,3},{2,0},{3,1},{4,6},{5,7},{6,4},{7,5},{8,10},{9,11},{10,... | collective-permute-start | bytes 245768 | tf_op jit(solution)/shard_map/ppermute | solution.py:293
  9.8 2.4 %reshape.31.index_ref = s32[2560,1]{1,0:T(8,128)} reshape(s32[40,64]{1,0:T(8,128)S(1)} %subtract_bitcast_fusion) | data formatting | bytes 20480 | tf_op jit(solution)/shard_map/reshape | solution.py:319
  12.1 2.6 %collective-permute-start.5 = (bf16[64,640]{1,0:T(8,128)(2,1)S(1)}, bf16[64,640]{1,0:T(8,128)(2,1)S(1)}, u32[]{:S(2)}, u32[]{:S(2)}) collective-permute-start(bf16[64,640]{1,0:T(8,128)(2,1)S(1)} %concatenate.9), channel_id=1, source_target_pairs={{0,3},{1,0},{2,1},{3,2},{4,7},{5,4},{6,5},{7,6},{8,11},{9,8},{10,9... | collective-permute-start | bytes 245768 | tf_op jit(solution)/shard_map/ppermute | solution.py:293
  15.4 5.1 %gather.1.picked_ref = bf16[2560,256]{1,0:T(8,128)(2,1)} custom-call(s32[1]{0:T(128)} %bitcast.sub_ref, s32[2560,1]{1,0:T(8,128)} %reshape.31.index_ref, bf16[227,512]{1,0:T(8,128)(2,1)} %refs_0_.1, bf16[227,512]{1,0:T(8,128)(2,1)} %copy-done.7, bf16[227,512]{1,0:T(8,128)(2,1)} %copy-done.8), custom_call_target="tpu_custom_call" | custom-call | flops 2013265920 | bytes 1310720 | tf_op jit(solution)/shard_map/gather/pallas_call | solution.py:330
  21.7 5.5 %collective-permute-start.6 = (bf16[227,512]{1,0:T(8,128)(2,1)S(1)}, bf16[227,512]{1,0:T(8,128)(2,1)S(1)}, u32[]{:S(2)}, u32[]{:S(2)}) collective-permute-start(bf16[227,512]{1,0:T(8,128)(2,1)S(1)} %get-tuple-element.63), channel_id=1, source_target_pairs={{0,4},{4,8},{8,12},{12,16},{16,20},{20,24},{24,28},{28,32},{32,36}... | collective-permute-start | bytes 697352 | tf_op jit(solution)/shard_map/ppermute | solution.py:271
  27.3 1.9 %collective-permute-start.7 = (bf16[227,512]{1,0:T(8,128)(2,1)S(1)}, bf16[227,512]{1,0:T(8,128)(2,1)S(1)}, u32[]{:S(2)}, u32[]{:S(2)}) collective-permute-start(bf16[227,512]{1,0:T(8,128)(2,1)S(1)} %get-tuple-element.62), channel_id=1, source_target_pairs={{4,0},{8,4},{12,8},{16,12},{20,16},{24,20},{28,24},{32,28},{36,32}... | collective-permute-start | bytes 697352 | tf_op jit(solution)/shard_map/ppermute | solution.py:276
  29.3 3.6 %collective-permute-start.13 = (bf16[256,640]{1,0:T(8,128)(2,1)S(1)}, bf16[256,640]{1,0:T(8,128)(2,1)S(1)}, u32[]{:S(2)}, u32[]{:S(2)}) collective-permute-start(bf16[256,640]{1,0:T(8,128)(2,1)S(1)} %constant_dynamic-update-slice_fusion.4.pay_ref), channel_id=1, source_target_pairs={{0,4},{1,5},{4,8},{5,9},{6,2},{7,3},{8,12},{9,13},{10,6},{11,7},{1... | collective-permute-start | bytes 983048 | tf_op jit(solution)/shard_map/ppermute | solution.py:288
  35.4 15.4 %encode.1 = (bf16[2560,512]{1,0:T(8,128)(2,1)}, bf16[2560,512]{1,0:T(8,128)(2,1)}, bf16[2560,512]{1,0:T(8,128)(2,1)}, bf16[2560,512]{1,0:T(8,128)(2,1)}, bf16[25...) custom-call(s32[1]{0:T(128)} %bitcast.sub_ref, s32[2560,1]{1,0:T(8,128)} %reshape.31.index_ref, ...), custom_call_target="tpu_custom_call" | custom-call | tf_op jit(solution)/shard_map/encode/pallas_call | solution.py:357
  51.0 3.2 %collective-permute-start.9 = (bf16[64,512]{1,0:T(8,128)(2,1)}, bf16[64,512]{1,0:T(8,128)(2,1)S(1)}, u32[]{:S(2)}, u32[]{:S(2)}) collective-permute-start(bf16[64,512]{1,0:T(8,128)(2,1)} %get-tuple-element.34), channel_id=1, source_target_pairs={{0,2},{1,3},{2,0},{3,1},{4,6},{5,7},{6,4},{7,5},{8,10},{9,11},{10,... | collective-permute-start | bytes 196616 | tf_op jit(solution)/shard_map/ppermute | solution.py:293
  57.5 4.0 %collective-permute-start.11 = (bf16[256,512]{1,0:T(8,128)(2,1)S(1)}, bf16[256,512]{1,0:T(8,128)(2,1)S(1)}, u32[]{:S(2)}, u32[]{:S(2)}) collective-permute-start(bf16[256,512]{1,0:T(8,128)(2,1)S(1)} %constant_dynamic-update-slice_fusion.band_ref), channel_id=1, source_target_pairs={{0,4},{1,5},{4,8},{5,9},{6,2},{7,3},{8,12},{9,13},{10,6},{11,7},{1... | collective-permute-start | bytes 786440 | tf_op jit(solution)/shard_map/ppermute | solution.py:288
  61.6 1.9 %collective-permute-start.12 = (bf16[64,512]{1,0:T(8,128)(2,1)S(1)}, bf16[64,512]{1,0:T(8,128)(2,1)S(1)}, u32[]{:S(2)}, u32[]{:S(2)}) collective-permute-start(bf16[64,512]{1,0:T(8,128)(2,1)S(1)} %constant_dynamic-slice_fusion), channel_id=1, source_target_pairs={{2,6},{3,7},{4,0},{5,1},{6,10},{7,11},{8,4},{9,5},{10,14},{11,15},... | collective-permute-start | bytes 196616 | tf_op jit(solution)/shard_map/ppermute | solution.py:288
  63.5 3.6 %collective-permute-done.12.side_ref = bf16[64,512]{1,0:T(8,128)(2,1)S(1)} collective-permute-done((bf16[64,512]{1,0:T(8,128)(2,1)S(1)}, bf16[64,512]{1,0:T(8,128)(2,1)S(1)}, u32[]{:S(2)}, u32[]{:S(2)}) %collective-permute-start.12) | collective-permute-done | bytes 65568 | tf_op jit(solution)/shard_map/ppermute | solution.py:288
  67.9 17.9 %process.1 = (bf16[64,512]{1,0:T(8,128)(2,1)}, bf16[2560,512]{1,0:T(8,128)(2,1)}, bf16[1024,512]{1,0:T(8,128)(2,1)}) custom-call(s32[1]{0:T(128)} %bitcast.sub_ref, bf16[256,512]{1,0:T(8,128)(2,1)} %copy-done.1, bf16[256,512]{1,0:T(8,128)(2,1)} %copy-done.4, bf16[64,512]{1,0:T(8,128)(2,1)} %copy-done.11, bf16[256,640]{1,0:T(8,128)(2,1)} %copy-done.2, ...), custom_call_target="tpu_custom_call" | custom-call | tf_op jit(solution)/shard_map/process/pallas_call | solution.py:388
  85.8 8.4 %all-to-all-start = ((bf16[32,32,512]{2,1,0:T(8,128)(2,1)}), bf16[32,32,512]{2,1,0:T(8,128)(2,1)S(1)}, u32[]{:S(2)}, u32[]{:S(2)}) async-start(bf16[32,32,512]{2,1,0:T(8,128)(2,1)} %bitcast.10), calls=%async_computation | async-start | bytes 2097152 | tf_op jit(solution)/shard_map/all_to_all | solution.py:449
  94.2 10.7 %channels.1 = (bf16[227,512]{1,0:T(8,128)(2,1)}, bf16[227,512]{1,0:T(8,128)(2,1)}, bf16[227,512]{1,0:T(8,128)(2,1)}, bf16[227,512]{1,0:T(8,128)(2,1)}, bf16[227,...) custom-call(s32[1]{0:T(128)} %bitcast.sub_ref, s32[2560,1]{1,0:T(8,128)} %reshape.31.index_ref, bf16[512,512]{1,0:T(8,128)(2,1)} %src_ref.3, ...), custom_call_target="tpu_custom_call" | custom-call | tf_op jit(solution)/shard_map/channels/pallas_call | solution.py:430
  104.9 3.5 %collective-permute-start.14 = (bf16[227,512]{1,0:T(8,128)(2,1)}, bf16[227,512]{1,0:T(8,128)(2,1)S(1)}, u32[]{:S(2)}, u32[]{:S(2)}) collective-permute-start(bf16[227,512]{1,0:T(8,128)(2,1)} %get-tuple-element.48), channel_id=1, source_target_pairs={{0,4},{4,8},{8,12},{12,16},{16,20},{20,24},{24,28},{28,32},{32,36}... | collective-permute-start | bytes 697352 | tf_op jit(solution)/shard_map/ppermute | solution.py:271
  108.4 1.9 %collective-permute-start.15 = (bf16[227,512]{1,0:T(8,128)(2,1)}, bf16[227,512]{1,0:T(8,128)(2,1)S(1)}, u32[]{:S(2)}, u32[]{:S(2)}) collective-permute-start(bf16[227,512]{1,0:T(8,128)(2,1)} %get-tuple-element.49), channel_id=1, source_target_pairs={{4,0},{8,4},{12,8},{16,12},{20,16},{24,20},{28,24},{32,28},{36,32}... | collective-permute-start | bytes 697352 | tf_op jit(solution)/shard_map/ppermute | solution.py:276
  111.3 11.8 %all-to-all-start.1 = ((bf16[8,32,512]{2,1,0:T(8,128)(2,1)}), bf16[8,32,512]{2,1,0:T(8,128)(2,1)S(1)}, u32[]{:S(2)}, u32[]{:S(2)}) async-start(bf16[8,32,512]{2,1,0:T(8,128)(2,1)} %broadcast_in_dim.7), calls=%async_computation.1 | async-start | bytes 524288 | tf_op jit(solution)/shard_map/all_to_all | solution.py:264
  127.3 3.5 %collective-permute-done.16 = bf16[227,512]{1,0:T(8,128)(2,1)S(1)} collective-permute-done((bf16[227,512]{1,0:T(8,128)(2,1)S(1)}, bf16[227,512]{1,0:T(8,128)(2,1)S(1)}, u32[]{:S(2)}, u32[]{:S(2)}) %collective-permute-start.16) | collective-permute-done | bytes 232480 | tf_op jit(solution)/shard_map/ppermute | solution.py:293
  133.6 9.9 %all-to-all-start.2 = ((bf16[32,32,512]{2,1,0:T(8,128)(2,1)}), bf16[32,32,512]{2,1,0:T(8,128)(2,1)S(1)}, u32[]{:S(2)}, u32[]{:S(2)}) async-start(bf16[32,32,512]{2,1,0:T(8,128)(2,1)} %broadcast_in_dim.8), calls=%async_computation.2 | async-start | bytes 2097152 | tf_op jit(solution)/shard_map/all_to_all | solution.py:264
  143.6 3.0 %collective-permute-start.18 = (bf16[227,512]{1,0:T(8,128)(2,1)S(1)}, bf16[227,512]{1,0:T(8,128)(2,1)S(1)}, u32[]{:S(2)}, u32[]{:S(2)}) collective-permute-start(bf16[227,512]{1,0:T(8,128)(2,1)S(1)} %get-tuple-element.64), channel_id=1, source_target_pairs={{0,2},{1,3},{2,0},{3,1},{4,6},{5,7},{6,4},{7,5},{8,10},{9,11},{10,... | collective-permute-start | bytes 697352 | tf_op jit(solution)/shard_map/ppermute | solution.py:293
  146.6 13.1 %all-to-all-done.2 = bf16[32,32,512]{2,1,0:T(8,128)(2,1)S(1)} async-done(((bf16[32,32,512]{2,1,0:T(8,128)(2,1)}), bf16[32,32,512]{2,1,0:T(8,128)(2,1)S(1)}, u32[]{:S(2)}, u32[]{:S(2)}) %all-to-all-start.2) | async-done | bytes 1048608 | tf_op jit(solution)/shard_map/all_to_all | solution.py:264
  161.5 2.2 %collective-permute-done.18 = bf16[227,512]{1,0:T(8,128)(2,1)S(1)} collective-permute-done((bf16[227,512]{1,0:T(8,128)(2,1)S(1)}, bf16[227,512]{1,0:T(8,128)(2,1)S(1)}, u32[]{:S(2)}, u32[]{:S(2)}) %collective-permute-start.18) | collective-permute-done | bytes 232480 | tf_op jit(solution)/shard_map/ppermute | solution.py:293
  (72 shorter events, 23.9 us)
Async XLA Ops:
  0.6 11.5 %collective-permute-start.1 = (bf16[227,512]{1,0:T(8,128)(2,1)}, bf16[227,512]{1,0:T(8,128)(2,1)S(1)}, u32[]{:S(2)}, u32[]{:S(2)}) collective-permute-start(bf16[227,512]{1,0:T(8,128)(2,1)} %refs_0_.1), channel_id=1, source_target_pairs={{0,1},{1,2},{2,3},{3,0},{4,5},{5,6},{6,7},{7,4},{8,9},{9,10},{10,1... | collective-permute-start | bytes 697352 | tf_op jit(solution)/shard_map/ppermute | solution.py:293
  2.7 12.0 %collective-permute-start.2 = (bf16[227,512]{1,0:T(8,128)(2,1)}, bf16[227,512]{1,0:T(8,128)(2,1)S(1)}, u32[]{:S(2)}, u32[]{:S(2)}) collective-permute-start(bf16[227,512]{1,0:T(8,128)(2,1)} %refs_0_.1), channel_id=1, source_target_pairs={{0,3},{1,0},{2,1},{3,2},{4,7},{5,4},{6,5},{7,6},{8,11},{9,8},{10,9... | collective-permute-start | bytes 697352 | tf_op jit(solution)/shard_map/ppermute | solution.py:293
  5.9 14.6 %collective-permute-start.3 = (bf16[64,640]{1,0:T(8,128)(2,1)S(1)}, bf16[64,640]{1,0:T(8,128)(2,1)S(1)}, u32[]{:S(2)}, u32[]{:S(2)}) collective-permute-start(bf16[64,640]{1,0:T(8,128)(2,1)S(1)} %concatenate.9), channel_id=1, source_target_pairs={{0,1},{1,2},{2,3},{3,0},{4,5},{5,6},{6,7},{7,4},{8,9},{9,10},{10,1... | collective-permute-start | bytes 245768 | tf_op jit(solution)/shard_map/ppermute | solution.py:293
  6.1 14.4 %collective-permute-start.4 = (bf16[64,640]{1,0:T(8,128)(2,1)S(1)}, bf16[64,640]{1,0:T(8,128)(2,1)S(1)}, u32[]{:S(2)}, u32[]{:S(2)}) collective-permute-start(bf16[64,640]{1,0:T(8,128)(2,1)S(1)} %concatenate.9), channel_id=1, source_target_pairs={{0,2},{1,3},{2,0},{3,1},{4,6},{5,7},{6,4},{7,5},{8,10},{9,11},{10,... | collective-permute-start | bytes 245768 | tf_op jit(solution)/shard_map/ppermute | solution.py:293
  8.5 12.0 %collective-permute-start = (bf16[227,512]{1,0:T(8,128)(2,1)}, bf16[227,512]{1,0:T(8,128)(2,1)S(1)}, u32[]{:S(2)}, u32[]{:S(2)}) collective-permute-start(bf16[227,512]{1,0:T(8,128)(2,1)} %refs_0_.1), channel_id=1, source_target_pairs={{0,2},{1,3},{2,0},{3,1},{4,6},{5,7},{6,4},{7,5},{8,10},{9,11},{10,... | collective-permute-start | bytes 697352 | tf_op jit(solution)/shard_map/ppermute | solution.py:293
  12.1 8.3 %collective-permute-start.5 = (bf16[64,640]{1,0:T(8,128)(2,1)S(1)}, bf16[64,640]{1,0:T(8,128)(2,1)S(1)}, u32[]{:S(2)}, u32[]{:S(2)}) collective-permute-start(bf16[64,640]{1,0:T(8,128)(2,1)S(1)} %concatenate.9), channel_id=1, source_target_pairs={{0,3},{1,0},{2,1},{3,2},{4,7},{5,4},{6,5},{7,6},{8,11},{9,8},{10,9... | collective-permute-start | bytes 245768 | tf_op jit(solution)/shard_map/ppermute | solution.py:293
  21.7 11.2 %collective-permute-start.6 = (bf16[227,512]{1,0:T(8,128)(2,1)S(1)}, bf16[227,512]{1,0:T(8,128)(2,1)S(1)}, u32[]{:S(2)}, u32[]{:S(2)}) collective-permute-start(bf16[227,512]{1,0:T(8,128)(2,1)S(1)} %get-tuple-element.63), channel_id=1, source_target_pairs={{0,4},{4,8},{8,12},{12,16},{16,20},{20,24},{24,28},{28,32},{32,36}... | collective-permute-start | bytes 697352 | tf_op jit(solution)/shard_map/ppermute | solution.py:271
  27.3 7.4 %collective-permute-start.7 = (bf16[227,512]{1,0:T(8,128)(2,1)S(1)}, bf16[227,512]{1,0:T(8,128)(2,1)S(1)}, u32[]{:S(2)}, u32[]{:S(2)}) collective-permute-start(bf16[227,512]{1,0:T(8,128)(2,1)S(1)} %get-tuple-element.62), channel_id=1, source_target_pairs={{4,0},{8,4},{12,8},{16,12},{20,16},{24,20},{28,24},{32,28},{36,32}... | collective-permute-start | bytes 697352 | tf_op jit(solution)/shard_map/ppermute | solution.py:276
  29.3 25.8 %copy-start.2 = (bf16[256,640]{1,0:T(8,128)(2,1)}, bf16[256,640]{1,0:T(8,128)(2,1)S(1)}, u32[]{:S(2)}) copy-start(bf16[256,640]{1,0:T(8,128)(2,1)S(1)} %constant_dynamic-update-slice_fusion.4.pay_ref) | copy-start | bytes 983044
  29.3 34.2 %collective-permute-start.13 = (bf16[256,640]{1,0:T(8,128)(2,1)S(1)}, bf16[256,640]{1,0:T(8,128)(2,1)S(1)}, u32[]{:S(2)}, u32[]{:S(2)}) collective-permute-start(bf16[256,640]{1,0:T(8,128)(2,1)S(1)} %constant_dynamic-update-slice_fusion.4.pay_ref), channel_id=1, source_target_pairs={{0,4},{1,5},{4,8},{5,9},{6,2},{7,3},{8,12},{9,13},{10,6},{11,7},{1... | collective-permute-start | bytes 983048 | tf_op jit(solution)/shard_map/ppermute | solution.py:288
  50.9 4.6 %collective-permute-start.8 = (bf16[64,512]{1,0:T(8,128)(2,1)}, bf16[64,512]{1,0:T(8,128)(2,1)S(1)}, u32[]{:S(2)}, u32[]{:S(2)}) collective-permute-start(bf16[64,512]{1,0:T(8,128)(2,1)} %get-tuple-element.34), channel_id=1, source_target_pairs={{0,1},{1,2},{2,3},{3,0},{4,5},{5,6},{6,7},{7,4},{8,9},{9,10},{10,1... | collective-permute-start | bytes 196616 | tf_op jit(solution)/shard_map/ppermute | solution.py:293
  51.0 5.8 %collective-permute-start.9 = (bf16[64,512]{1,0:T(8,128)(2,1)}, bf16[64,512]{1,0:T(8,128)(2,1)S(1)}, u32[]{:S(2)}, u32[]{:S(2)}) collective-permute-start(bf16[64,512]{1,0:T(8,128)(2,1)} %get-tuple-element.34), channel_id=1, source_target_pairs={{0,2},{1,3},{2,0},{3,1},{4,6},{5,7},{6,4},{7,5},{8,10},{9,11},{10,... | collective-permute-start | bytes 196616 | tf_op jit(solution)/shard_map/ppermute | solution.py:293
  54.2 3.3 %collective-permute-start.10 = (bf16[64,512]{1,0:T(8,128)(2,1)}, bf16[64,512]{1,0:T(8,128)(2,1)S(1)}, u32[]{:S(2)}, u32[]{:S(2)}) collective-permute-start(bf16[64,512]{1,0:T(8,128)(2,1)} %get-tuple-element.34), channel_id=1, source_target_pairs={{0,3},{1,0},{2,1},{3,2},{4,7},{5,4},{6,5},{7,6},{8,11},{9,8},{10,9... | collective-permute-start | bytes 196616 | tf_op jit(solution)/shard_map/ppermute | solution.py:293
  57.5 9.6 %collective-permute-start.11 = (bf16[256,512]{1,0:T(8,128)(2,1)S(1)}, bf16[256,512]{1,0:T(8,128)(2,1)S(1)}, u32[]{:S(2)}, u32[]{:S(2)}) collective-permute-start(bf16[256,512]{1,0:T(8,128)(2,1)S(1)} %constant_dynamic-update-slice_fusion.band_ref), channel_id=1, source_target_pairs={{0,4},{1,5},{4,8},{5,9},{6,2},{7,3},{8,12},{9,13},{10,6},{11,7},{1... | collective-permute-start | bytes 786440 | tf_op jit(solution)/shard_map/ppermute | solution.py:288
  61.6 5.6 %collective-permute-start.12 = (bf16[64,512]{1,0:T(8,128)(2,1)S(1)}, bf16[64,512]{1,0:T(8,128)(2,1)S(1)}, u32[]{:S(2)}, u32[]{:S(2)}) collective-permute-start(bf16[64,512]{1,0:T(8,128)(2,1)S(1)} %constant_dynamic-slice_fusion), channel_id=1, source_target_pairs={{2,6},{3,7},{4,0},{5,1},{6,10},{7,11},{8,4},{9,5},{10,14},{11,15},... | collective-permute-start | bytes 196616 | tf_op jit(solution)/shard_map/ppermute | solution.py:288
  85.8 24.6 %all-to-all-start = ((bf16[32,32,512]{2,1,0:T(8,128)(2,1)}), bf16[32,32,512]{2,1,0:T(8,128)(2,1)S(1)}, u32[]{:S(2)}, u32[]{:S(2)}) async-start(bf16[32,32,512]{2,1,0:T(8,128)(2,1)} %bitcast.10), calls=%async_computation | async-start | bytes 2097152 | tf_op jit(solution)/shard_map/all_to_all | solution.py:449
  104.9 18.1 %collective-permute-start.14 = (bf16[227,512]{1,0:T(8,128)(2,1)}, bf16[227,512]{1,0:T(8,128)(2,1)S(1)}, u32[]{:S(2)}, u32[]{:S(2)}) collective-permute-start(bf16[227,512]{1,0:T(8,128)(2,1)} %get-tuple-element.48), channel_id=1, source_target_pairs={{0,4},{4,8},{8,12},{12,16},{16,20},{20,24},{24,28},{28,32},{32,36}... | collective-permute-start | bytes 697352 | tf_op jit(solution)/shard_map/ppermute | solution.py:271
  108.4 14.6 %collective-permute-start.15 = (bf16[227,512]{1,0:T(8,128)(2,1)}, bf16[227,512]{1,0:T(8,128)(2,1)S(1)}, u32[]{:S(2)}, u32[]{:S(2)}) collective-permute-start(bf16[227,512]{1,0:T(8,128)(2,1)} %get-tuple-element.49), channel_id=1, source_target_pairs={{4,0},{8,4},{12,8},{16,12},{20,16},{24,20},{28,24},{32,28},{36,32}... | collective-permute-start | bytes 697352 | tf_op jit(solution)/shard_map/ppermute | solution.py:276
  111.3 21.2 %all-to-all-start.1 = ((bf16[8,32,512]{2,1,0:T(8,128)(2,1)}), bf16[8,32,512]{2,1,0:T(8,128)(2,1)S(1)}, u32[]{:S(2)}, u32[]{:S(2)}) async-start(bf16[8,32,512]{2,1,0:T(8,128)(2,1)} %broadcast_in_dim.7), calls=%async_computation.1 | async-start | bytes 524288 | tf_op jit(solution)/shard_map/all_to_all | solution.py:264
  124.5 6.2 %collective-permute-start.16 = (bf16[227,512]{1,0:T(8,128)(2,1)S(1)}, bf16[227,512]{1,0:T(8,128)(2,1)S(1)}, u32[]{:S(2)}, u32[]{:S(2)}) collective-permute-start(bf16[227,512]{1,0:T(8,128)(2,1)S(1)} %get-tuple-element.66), channel_id=1, source_target_pairs={{0,1},{1,2},{2,3},{3,0},{4,5},{5,6},{6,7},{7,4},{8,9},{9,10},{10,1... | collective-permute-start | bytes 697352 | tf_op jit(solution)/shard_map/ppermute | solution.py:293
  125.8 5.0 %collective-permute-start.17 = (bf16[227,512]{1,0:T(8,128)(2,1)S(1)}, bf16[227,512]{1,0:T(8,128)(2,1)S(1)}, u32[]{:S(2)}, u32[]{:S(2)}) collective-permute-start(bf16[227,512]{1,0:T(8,128)(2,1)S(1)} %get-tuple-element.65), channel_id=1, source_target_pairs={{0,3},{1,0},{2,1},{3,2},{4,7},{5,4},{6,5},{7,6},{8,11},{9,8},{10,9... | collective-permute-start | bytes 697352 | tf_op jit(solution)/shard_map/ppermute | solution.py:293
  133.6 26.1 %all-to-all-start.2 = ((bf16[32,32,512]{2,1,0:T(8,128)(2,1)}), bf16[32,32,512]{2,1,0:T(8,128)(2,1)S(1)}, u32[]{:S(2)}, u32[]{:S(2)}) async-start(bf16[32,32,512]{2,1,0:T(8,128)(2,1)} %broadcast_in_dim.8), calls=%async_computation.2 | async-start | bytes 2097152 | tf_op jit(solution)/shard_map/all_to_all | solution.py:264
  143.6 20.1 %copy-start.6 = (bf16[227,512]{1,0:T(8,128)(2,1)S(1)}, bf16[227,512]{1,0:T(8,128)(2,1)}, u32[]{:S(2)}) copy-start(bf16[227,512]{1,0:T(8,128)(2,1)} %get-tuple-element.47) | copy-start | bytes 697348
  143.6 20.1 %collective-permute-start.18 = (bf16[227,512]{1,0:T(8,128)(2,1)S(1)}, bf16[227,512]{1,0:T(8,128)(2,1)S(1)}, u32[]{:S(2)}, u32[]{:S(2)}) collective-permute-start(bf16[227,512]{1,0:T(8,128)(2,1)S(1)} %get-tuple-element.64), channel_id=1, source_target_pairs={{0,2},{1,3},{2,0},{3,1},{4,6},{5,7},{6,4},{7,5},{8,10},{9,11},{10,... | collective-permute-start | bytes 697352 | tf_op jit(solution)/shard_map/ppermute | solution.py:293
  (10 other events, 39.7 us)

commit v11 on v10

--- a/solution.py
+++ b/solution.py
@@ -60,17 +60,22 @@
     return scratch[...]
 
 
-def gather_kernel(blocks, sub_ref, index_ref, *refs):
-    *sources, picked_ref, table, pad = refs
+def gather_kernel(blocks, sub_ref, base_ref, edges_ref, *refs):
+    *sources, picked_ref, index_ref, table, pad = refs
     nodes = sources[0].shape[1]
     sub = sub_ref[0]
-
-    @pl.when(pl.program_id(0) == 0)
-    def _():
+    step = pl.program_id(0)
+
+    @pl.when(step == 0)
+    def _():
+        local = edges_ref[...] - base_ref[0]
+        columns = [local[:, k : k + 1] for k in range(local.shape[1])]
+        index_ref[...] = jnp.concatenate(columns, axis=0)
         for place, source in enumerate(sources):
             table[place * nodes : (place + 1) * nodes, :] = padded_rows(source, pad).T
 
-    column = index_ref[...]
+    edges = picked_ref.shape[0]
+    column = index_ref[pl.ds(pl.multiple_of(step * edges, edges), edges), :]
     chosen = [
         selection(column - (lax.rem(sub + SUBS - k, SUBS) + 1) * nodes, nodes) for k in blocks
     ]
@@ -316,7 +321,7 @@
     mesh_scale = 1.0 / math.sqrt(mesh_count)
 
     grid = [grid_x] + [along_sub(grid_x, k) for k in range(1, SUBS)]
-    grid_local = (g2m_src - (band * (nodes * SUBS) - nodes)).T.reshape(edges, 1)
+    grid_base = (band * (nodes * SUBS) - nodes).astype(jnp.int32).reshape(1)
 
     place = mesh_src - (band * width - rows)
     half = 64
@@ -327,12 +332,16 @@
     pays = [pay] + [along_sub(pay, k) for k in range(1, SUBS)]
 
     nearest = (0, 1, 3)
-    picked = pl.pallas_call(
+    picked, grid_local = pl.pallas_call(
         functools.partial(gather_kernel, nearest),
         grid=(2,),
-        in_specs=[scalar(), tiled(edges // 2, 1)] + [whole((channels, nodes))] * len(nearest),
-        out_specs=tiled(edges // 2, wide),
-        out_shape=jax.ShapeDtypeStruct((edges, wide), BF),
+        in_specs=[scalar(), scalar(), whole((rows, enc_count))]
+        + [whole((channels, nodes))] * len(nearest),
+        out_specs=[tiled(edges // 2, wide), whole((edges, 1))],
+        out_shape=[
+            jax.ShapeDtypeStruct((edges, wide), BF),
+            jax.ShapeDtypeStruct((edges, 1), jnp.int32),
+        ],
         scratch_shapes=[
             pltpu.VMEM((len(nearest) * nodes, wide), BF),
             pltpu.VMEM((wide, nodes), BF),
@@ -344,7 +353,7 @@
             transcendentals=0,
         ),
         name="gather",
-    )(sub_scalar, grid_local, *[grid[k] for k in nearest])
+    )(sub_scalar, grid_base, g2m_src, *[grid[k] for k in nearest])
 
     grid[2], picked, *pays = lax.optimization_barrier((grid[2], picked, *pays))
     last = lax.select_n(lax.rem(sub + 1, SUBS), *grid)

time: 166 us -> 166 us (level)
    reshape x1 -> x0, local copies, waits for them, and re-layouts: 2.36 us -> none  [body(): grid_local = (g2m_src - (band * (nodes * SUBS) - nodes)).T.reshape(edges, 1)]
    unnamed x31 -> x32, local copies, waits for them, and re-layouts: 3.88 us -> 5.29 us
  transfers between devices with their start and end apart: 22 -> 22, of which waited for: 9 -> 9; matrix products, arithmetic and copies ran while one was open for 6% -> 5% of each run, Pallas kernels for 19% -> 19%
where the time goes in v11:
time: 166 us; the launch traced here: 165 us
  starting transfers between devices  72.3 us (44%)
  Pallas kernels  49.3 us (30%)
  waiting for transfers between devices  28.6 us (17%)
  local copies, waits for them, and re-layouts  8.18 us (5%)
  other arithmetic  5.59 us (3%)
    all_to_all x2, starting transfers between devices, from_everyone(): lax.all_to_all(jnp.broadcast_to(shard[None], (devices, *shard.shape)), ax...  21.6 us
    ppermute x12, starting transfers between devices, along_sub(): lax.ppermute(value, 'sub', [(i, (i + steps) % count) for i in range(count)])  19.3 us
    pallas_call x1, Pallas kernels, body(): pl.pallas_call(functools.partial(mesh_kernel, mesh_scale, scale, mesh_cou...  17.9 us
    pallas_call x1, Pallas kernels, body(): pl.pallas_call(functools.partial(forward_kernel, scale), grid=(steps,), i...  15.4 us
    all_to_all x2, waiting for transfers between devices, from_everyone(): lax.all_to_all(jnp.broadcast_to(shard[None], (devices, *shard.shape)), ax...  14.9 us
    pallas_call x1, Pallas kernels, body(): pl.pallas_call(grid_kernel, grid=(steps // 2,), in_specs=[scalar(), tiled...  10.6 us
    ppermute x2, starting transfers between devices, bands_up(): return lax.ppermute(value, BAND, [(i, i + 1) for i in range(count - 1)])  9.63 us
    ppermute x3, starting transfers between devices, outwards(): return lax.ppermute(value, ALL, pairs)  8.91 us
  transfers between devices with their start and end apart: 22, of which 9 were waited for; matrix products, arithmetic and copies ran while one was open for 5% of the time, Pallas kernels for 19%

profile of v11, /device:TPU:1, one launch (start us, length us, event | category | flops | bytes accessed | tf_op | source)
XLA Modules:
  0.0 165.0 jit_solution(17308353244856125618)
XLA Ops:
  0.6 2.1 %collective-permute-start = (bf16[227,512]{1,0:T(8,128)(2,1)}, bf16[227,512]{1,0:T(8,128)(2,1)S(1)}, u32[]{:S(2)}, u32[]{:S(2)}) collective-permute-start(bf16[227,512]{1,0:T(8,128)(2,1)} %refs_0_.1), channel_id=1, source_target_pairs={{0,1},{1,2},{2,3},{3,0},{4,5},{5,6},{6,7},{7,4},{8,9},{9,10},{10,1... | collective-permute-start | bytes 697352 | tf_op jit(solution)/shard_map/ppermute | solution.py:298
  7.9 1.7 %collective-permute-start.4 = (bf16[64,640]{1,0:T(8,128)(2,1)S(1)}, bf16[64,640]{1,0:T(8,128)(2,1)S(1)}, u32[]{:S(2)}, u32[]{:S(2)}) collective-permute-start(bf16[64,640]{1,0:T(8,128)(2,1)S(1)} %concatenate.9), channel_id=1, source_target_pairs={{0,2},{1,3},{2,0},{3,1},{4,6},{5,7},{6,4},{7,5},{8,10},{9,11},{10,... | collective-permute-start | bytes 245768 | tf_op jit(solution)/shard_map/ppermute | solution.py:298
  13.1 5.3 %gather.1 = (bf16[2560,256]{1,0:T(8,128)(2,1)}, s32[2560,1]{1,0:T(8,128)}) custom-call(s32[1]{0:T(128)} %bitcast.sub_ref, s32[1]{0:T(128)} %bitcast.1.base_ref, s32[64,40]{1,0:T(8,128)} %copy.15.edges_ref, bf16[227,512]{1,0:T(8,128)(2,1)} %refs_0_.1, bf16[227,512]{1,0:T(8,128)(2,1)} %copy-done.7, bf16[227,512]{1,0:T(8,128)(2,1)} %copy-done.8), custom_call_target="tpu_custom_call" | custom-call | flops 2013265920 | bytes 1310720 | tf_op jit(solution)/shard_map/gather/pallas_call | solution.py:335
  20.2 6.1 %collective-permute-start.6 = (bf16[227,512]{1,0:T(8,128)(2,1)S(1)}, bf16[227,512]{1,0:T(8,128)(2,1)S(1)}, u32[]{:S(2)}, u32[]{:S(2)}) collective-permute-start(bf16[227,512]{1,0:T(8,128)(2,1)S(1)} %get-tuple-element.67), channel_id=1, source_target_pairs={{0,4},{4,8},{8,12},{12,16},{16,20},{20,24},{24,28},{28,32},{32,36}... | collective-permute-start | bytes 697352 | tf_op jit(solution)/shard_map/ppermute | solution.py:276
  26.3 2.6 %collective-permute-start.7 = (bf16[227,512]{1,0:T(8,128)(2,1)S(1)}, bf16[227,512]{1,0:T(8,128)(2,1)S(1)}, u32[]{:S(2)}, u32[]{:S(2)}) collective-permute-start(bf16[227,512]{1,0:T(8,128)(2,1)S(1)} %get-tuple-element.66), channel_id=1, source_target_pairs={{4,0},{8,4},{12,8},{16,12},{20,16},{24,20},{28,24},{32,28},{36,32}... | collective-permute-start | bytes 697352 | tf_op jit(solution)/shard_map/ppermute | solution.py:281
  29.0 3.0 %collective-permute-start.13 = (bf16[256,640]{1,0:T(8,128)(2,1)S(1)}, bf16[256,640]{1,0:T(8,128)(2,1)S(1)}, u32[]{:S(2)}, u32[]{:S(2)}) collective-permute-start(bf16[256,640]{1,0:T(8,128)(2,1)S(1)} %constant_dynamic-update-slice_fusion.4.pay_ref), channel_id=1, source_target_pairs={{0,4},{1,5},{4,8},{5,9},{6,2},{7,3},{8,12},{9,13},{10,6},{11,7},{1... | collective-permute-start | bytes 983048 | tf_op jit(solution)/shard_map/ppermute | solution.py:293
  32.0 1.7 %collective-permute-done.7.high_ref = bf16[227,512]{1,0:T(8,128)(2,1)S(1)} collective-permute-done((bf16[227,512]{1,0:T(8,128)(2,1)S(1)}, bf16[227,512]{1,0:T(8,128)(2,1)S(1)}, u32[]{:S(2)}, u32[]{:S(2)}) %collective-permute-start.7) | collective-permute-done | bytes 232480 | tf_op jit(solution)/shard_map/ppermute | solution.py:281
  34.4 15.4 %encode.1 = (bf16[2560,512]{1,0:T(8,128)(2,1)}, bf16[2560,512]{1,0:T(8,128)(2,1)}, bf16[2560,512]{1,0:T(8,128)(2,1)}, bf16[2560,512]{1,0:T(8,128)(2,1)}, bf16[25...) custom-call(s32[1]{0:T(128)} %bitcast.sub_ref, s32[2560,1]{1,0:T(8,128)} %get-tuple-element.34.index_ref, ...), custom_call_target="tpu_custom_call" | custom-call | tf_op jit(solution)/shard_map/encode/pallas_call | solution.py:366
  50.0 4.9 %collective-permute-start.9 = (bf16[64,512]{1,0:T(8,128)(2,1)}, bf16[64,512]{1,0:T(8,128)(2,1)S(1)}, u32[]{:S(2)}, u32[]{:S(2)}) collective-permute-start(bf16[64,512]{1,0:T(8,128)(2,1)} %get-tuple-element.38), channel_id=1, source_target_pairs={{0,2},{1,3},{2,0},{3,1},{4,6},{5,7},{6,4},{7,5},{8,10},{9,11},{10,... | collective-permute-start | bytes 196616 | tf_op jit(solution)/shard_map/ppermute | solution.py:298
  58.2 3.8 %collective-permute-start.11 = (bf16[256,512]{1,0:T(8,128)(2,1)S(1)}, bf16[256,512]{1,0:T(8,128)(2,1)S(1)}, u32[]{:S(2)}, u32[]{:S(2)}) collective-permute-start(bf16[256,512]{1,0:T(8,128)(2,1)S(1)} %constant_dynamic-update-slice_fusion.band_ref), channel_id=1, source_target_pairs={{0,4},{1,5},{4,8},{5,9},{6,2},{7,3},{8,12},{9,13},{10,6},{11,7},{1... | collective-permute-start | bytes 786440 | tf_op jit(solution)/shard_map/ppermute | solution.py:293
  62.1 2.1 %collective-permute-start.12 = (bf16[64,512]{1,0:T(8,128)(2,1)S(1)}, bf16[64,512]{1,0:T(8,128)(2,1)S(1)}, u32[]{:S(2)}, u32[]{:S(2)}) collective-permute-start(bf16[64,512]{1,0:T(8,128)(2,1)S(1)} %constant_dynamic-slice_fusion), channel_id=1, source_target_pairs={{2,6},{3,7},{4,0},{5,1},{6,10},{7,11},{8,4},{9,5},{10,14},{11,15},... | collective-permute-start | bytes 196616 | tf_op jit(solution)/shard_map/ppermute | solution.py:293
  64.2 3.5 %collective-permute-done.12.side_ref = bf16[64,512]{1,0:T(8,128)(2,1)S(1)} collective-permute-done((bf16[64,512]{1,0:T(8,128)(2,1)S(1)}, bf16[64,512]{1,0:T(8,128)(2,1)S(1)}, u32[]{:S(2)}, u32[]{:S(2)}) %collective-permute-start.12) | collective-permute-done | bytes 65568 | tf_op jit(solution)/shard_map/ppermute | solution.py:293
  68.4 17.9 %process.1 = (bf16[64,512]{1,0:T(8,128)(2,1)}, bf16[2560,512]{1,0:T(8,128)(2,1)}, bf16[1024,512]{1,0:T(8,128)(2,1)}) custom-call(s32[1]{0:T(128)} %bitcast.sub_ref, bf16[256,512]{1,0:T(8,128)(2,1)} %copy-done.1, bf16[256,512]{1,0:T(8,128)(2,1)} %copy-done.4, bf16[64,512]{1,0:T(8,128)(2,1)} %copy-done.11, bf16[256,640]{1,0:T(8,128)(2,1)} %copy-done.2, ...), custom_call_target="tpu_custom_call" | custom-call | tf_op jit(solution)/shard_map/process/pallas_call | solution.py:397
  86.3 8.4 %all-to-all-start = ((bf16[32,32,512]{2,1,0:T(8,128)(2,1)}), bf16[32,32,512]{2,1,0:T(8,128)(2,1)S(1)}, u32[]{:S(2)}, u32[]{:S(2)}) async-start(bf16[32,32,512]{2,1,0:T(8,128)(2,1)} %bitcast.9), calls=%async_computation | async-start | bytes 2097152 | tf_op jit(solution)/shard_map/all_to_all | solution.py:458
  94.7 10.6 %channels.1 = (bf16[227,512]{1,0:T(8,128)(2,1)}, bf16[227,512]{1,0:T(8,128)(2,1)}, bf16[227,512]{1,0:T(8,128)(2,1)}, bf16[227,512]{1,0:T(8,128)(2,1)}, bf16[227,...) custom-call(s32[1]{0:T(128)} %bitcast.sub_ref, s32[2560,1]{1,0:T(8,128)} %get-tuple-element.34.index_ref, ...), custom_call_target="tpu_custom_call" | custom-call | tf_op jit(solution)/shard_map/channels/pallas_call | solution.py:439
  105.4 3.5 %collective-permute-start.14 = (bf16[227,512]{1,0:T(8,128)(2,1)}, bf16[227,512]{1,0:T(8,128)(2,1)S(1)}, u32[]{:S(2)}, u32[]{:S(2)}) collective-permute-start(bf16[227,512]{1,0:T(8,128)(2,1)} %get-tuple-element.52), channel_id=1, source_target_pairs={{0,4},{4,8},{8,12},{12,16},{16,20},{20,24},{24,28},{28,32},{32,36}... | collective-permute-start | bytes 697352 | tf_op jit(solution)/shard_map/ppermute | solution.py:276
  108.9 1.9 %collective-permute-start.15 = (bf16[227,512]{1,0:T(8,128)(2,1)}, bf16[227,512]{1,0:T(8,128)(2,1)S(1)}, u32[]{:S(2)}, u32[]{:S(2)}) collective-permute-start(bf16[227,512]{1,0:T(8,128)(2,1)} %get-tuple-element.53), channel_id=1, source_target_pairs={{4,0},{8,4},{12,8},{16,12},{20,16},{24,20},{28,24},{32,28},{36,32}... | collective-permute-start | bytes 697352 | tf_op jit(solution)/shard_map/ppermute | solution.py:281
  111.8 11.6 %all-to-all-start.1 = ((bf16[8,32,512]{2,1,0:T(8,128)(2,1)}), bf16[8,32,512]{2,1,0:T(8,128)(2,1)S(1)}, u32[]{:S(2)}, u32[]{:S(2)}) async-start(bf16[8,32,512]{2,1,0:T(8,128)(2,1)} %broadcast_in_dim.7), calls=%async_computation.1 | async-start | bytes 524288 | tf_op jit(solution)/shard_map/all_to_all | solution.py:269
  127.6 3.5 %collective-permute-done.16 = bf16[227,512]{1,0:T(8,128)(2,1)S(1)} collective-permute-done((bf16[227,512]{1,0:T(8,128)(2,1)S(1)}, bf16[227,512]{1,0:T(8,128)(2,1)S(1)}, u32[]{:S(2)}, u32[]{:S(2)}) %collective-permute-start.16) | collective-permute-done | bytes 232480 | tf_op jit(solution)/shard_map/ppermute | solution.py:298
  131.1 1.7 %all-to-all-done.1 = bf16[8,32,512]{2,1,0:T(8,128)(2,1)S(1)} async-done(((bf16[8,32,512]{2,1,0:T(8,128)(2,1)}), bf16[8,32,512]{2,1,0:T(8,128)(2,1)S(1)}, u32[]{:S(2)}, u32[]{:S(2)}) %all-to-all-start.1) | async-done | bytes 262176 | tf_op jit(solution)/shard_map/all_to_all | solution.py:269
  134.0 9.9 %all-to-all-start.2 = ((bf16[32,32,512]{2,1,0:T(8,128)(2,1)}), bf16[32,32,512]{2,1,0:T(8,128)(2,1)S(1)}, u32[]{:S(2)}, u32[]{:S(2)}) async-start(bf16[32,32,512]{2,1,0:T(8,128)(2,1)} %broadcast_in_dim.8), calls=%async_computation.2 | async-start | bytes 2097152 | tf_op jit(solution)/shard_map/all_to_all | solution.py:269
  144.0 3.0 %collective-permute-start.18 = (bf16[227,512]{1,0:T(8,128)(2,1)S(1)}, bf16[227,512]{1,0:T(8,128)(2,1)S(1)}, u32[]{:S(2)}, u32[]{:S(2)}) collective-permute-start(bf16[227,512]{1,0:T(8,128)(2,1)S(1)} %get-tuple-element.68), channel_id=1, source_target_pairs={{0,2},{1,3},{2,0},{3,1},{4,6},{5,7},{6,4},{7,5},{8,10},{9,11},{10,... | collective-permute-start | bytes 697352 | tf_op jit(solution)/shard_map/ppermute | solution.py:298
  146.9 13.1 %all-to-all-done.2 = bf16[32,32,512]{2,1,0:T(8,128)(2,1)S(1)} async-done(((bf16[32,32,512]{2,1,0:T(8,128)(2,1)}), bf16[32,32,512]{2,1,0:T(8,128)(2,1)S(1)}, u32[]{:S(2)}, u32[]{:S(2)}) %all-to-all-start.2) | async-done | bytes 1048608 | tf_op jit(solution)/shard_map/all_to_all | solution.py:269
  161.9 2.2 %collective-permute-done.18 = bf16[227,512]{1,0:T(8,128)(2,1)S(1)} collective-permute-done((bf16[227,512]{1,0:T(8,128)(2,1)S(1)}, bf16[227,512]{1,0:T(8,128)(2,1)S(1)}, u32[]{:S(2)}, u32[]{:S(2)}) %collective-permute-start.18) | collective-permute-done | bytes 232480 | tf_op jit(solution)/shard_map/ppermute | solution.py:298
  (71 shorter events, 24.3 us)
Async XLA Ops:
  0.6 10.4 %collective-permute-start = (bf16[227,512]{1,0:T(8,128)(2,1)}, bf16[227,512]{1,0:T(8,128)(2,1)S(1)}, u32[]{:S(2)}, u32[]{:S(2)}) collective-permute-start(bf16[227,512]{1,0:T(8,128)(2,1)} %refs_0_.1), channel_id=1, source_target_pairs={{0,1},{1,2},{2,3},{3,0},{4,5},{5,6},{6,7},{7,4},{8,9},{9,10},{10,1... | collective-permute-start | bytes 697352 | tf_op jit(solution)/shard_map/ppermute | solution.py:298
  2.7 9.7 %collective-permute-start.1 = (bf16[227,512]{1,0:T(8,128)(2,1)}, bf16[227,512]{1,0:T(8,128)(2,1)S(1)}, u32[]{:S(2)}, u32[]{:S(2)}) collective-permute-start(bf16[227,512]{1,0:T(8,128)(2,1)} %refs_0_.1), channel_id=1, source_target_pairs={{0,3},{1,0},{2,1},{3,2},{4,7},{5,4},{6,5},{7,6},{8,11},{9,8},{10,9... | collective-permute-start | bytes 697352 | tf_op jit(solution)/shard_map/ppermute | solution.py:298
  4.1 14.8 %collective-permute-start.2 = (bf16[227,512]{1,0:T(8,128)(2,1)}, bf16[227,512]{1,0:T(8,128)(2,1)S(1)}, u32[]{:S(2)}, u32[]{:S(2)}) collective-permute-start(bf16[227,512]{1,0:T(8,128)(2,1)} %refs_0_.1), channel_id=1, source_target_pairs={{0,2},{1,3},{2,0},{3,1},{4,6},{5,7},{6,4},{7,5},{8,10},{9,11},{10,... | collective-permute-start | bytes 697352 | tf_op jit(solution)/shard_map/ppermute | solution.py:298
  7.5 10.9 %collective-permute-start.3 = (bf16[64,640]{1,0:T(8,128)(2,1)S(1)}, bf16[64,640]{1,0:T(8,128)(2,1)S(1)}, u32[]{:S(2)}, u32[]{:S(2)}) collective-permute-start(bf16[64,640]{1,0:T(8,128)(2,1)S(1)} %concatenate.9), channel_id=1, source_target_pairs={{0,1},{1,2},{2,3},{3,0},{4,5},{5,6},{6,7},{7,4},{8,9},{9,10},{10,1... | collective-permute-start | bytes 245768 | tf_op jit(solution)/shard_map/ppermute | solution.py:298
  7.9 11.0 %collective-permute-start.4 = (bf16[64,640]{1,0:T(8,128)(2,1)S(1)}, bf16[64,640]{1,0:T(8,128)(2,1)S(1)}, u32[]{:S(2)}, u32[]{:S(2)}) collective-permute-start(bf16[64,640]{1,0:T(8,128)(2,1)S(1)} %concatenate.9), channel_id=1, source_target_pairs={{0,2},{1,3},{2,0},{3,1},{4,6},{5,7},{6,4},{7,5},{8,10},{9,11},{10,... | collective-permute-start | bytes 245768 | tf_op jit(solution)/shard_map/ppermute | solution.py:298
  11.1 7.9 %collective-permute-start.5 = (bf16[64,640]{1,0:T(8,128)(2,1)S(1)}, bf16[64,640]{1,0:T(8,128)(2,1)S(1)}, u32[]{:S(2)}, u32[]{:S(2)}) collective-permute-start(bf16[64,640]{1,0:T(8,128)(2,1)S(1)} %concatenate.9), channel_id=1, source_target_pairs={{0,3},{1,0},{2,1},{3,2},{4,7},{5,4},{6,5},{7,6},{8,11},{9,8},{10,9... | collective-permute-start | bytes 245768 | tf_op jit(solution)/shard_map/ppermute | solution.py:298
  20.2 11.8 %collective-permute-start.6 = (bf16[227,512]{1,0:T(8,128)(2,1)S(1)}, bf16[227,512]{1,0:T(8,128)(2,1)S(1)}, u32[]{:S(2)}, u32[]{:S(2)}) collective-permute-start(bf16[227,512]{1,0:T(8,128)(2,1)S(1)} %get-tuple-element.67), channel_id=1, source_target_pairs={{0,4},{4,8},{8,12},{12,16},{16,20},{20,24},{24,28},{28,32},{32,36}... | collective-permute-start | bytes 697352 | tf_op jit(solution)/shard_map/ppermute | solution.py:276
  26.3 7.4 %collective-permute-start.7 = (bf16[227,512]{1,0:T(8,128)(2,1)S(1)}, bf16[227,512]{1,0:T(8,128)(2,1)S(1)}, u32[]{:S(2)}, u32[]{:S(2)}) collective-permute-start(bf16[227,512]{1,0:T(8,128)(2,1)S(1)} %get-tuple-element.66), channel_id=1, source_target_pairs={{4,0},{8,4},{12,8},{16,12},{20,16},{24,20},{28,24},{32,28},{36,32}... | collective-permute-start | bytes 697352 | tf_op jit(solution)/shard_map/ppermute | solution.py:281
  29.0 26.8 %copy-start.2 = (bf16[256,640]{1,0:T(8,128)(2,1)}, bf16[256,640]{1,0:T(8,128)(2,1)S(1)}, u32[]{:S(2)}) copy-start(bf16[256,640]{1,0:T(8,128)(2,1)S(1)} %constant_dynamic-update-slice_fusion.4.pay_ref) | copy-start | bytes 983044
  29.0 35.2 %collective-permute-start.13 = (bf16[256,640]{1,0:T(8,128)(2,1)S(1)}, bf16[256,640]{1,0:T(8,128)(2,1)S(1)}, u32[]{:S(2)}, u32[]{:S(2)}) collective-permute-start(bf16[256,640]{1,0:T(8,128)(2,1)S(1)} %constant_dynamic-update-slice_fusion.4.pay_ref), channel_id=1, source_target_pairs={{0,4},{1,5},{4,8},{5,9},{6,2},{7,3},{8,12},{9,13},{10,6},{11,7},{1... | collective-permute-start | bytes 983048 | tf_op jit(solution)/shard_map/ppermute | solution.py:293
  49.9 5.9 %collective-permute-start.8 = (bf16[64,512]{1,0:T(8,128)(2,1)}, bf16[64,512]{1,0:T(8,128)(2,1)S(1)}, u32[]{:S(2)}, u32[]{:S(2)}) collective-permute-start(bf16[64,512]{1,0:T(8,128)(2,1)} %get-tuple-element.38), channel_id=1, source_target_pairs={{0,1},{1,2},{2,3},{3,0},{4,5},{5,6},{6,7},{7,4},{8,9},{9,10},{10,1... | collective-permute-start | bytes 196616 | tf_op jit(solution)/shard_map/ppermute | solution.py:298
  50.0 7.5 %collective-permute-start.9 = (bf16[64,512]{1,0:T(8,128)(2,1)}, bf16[64,512]{1,0:T(8,128)(2,1)S(1)}, u32[]{:S(2)}, u32[]{:S(2)}) collective-permute-start(bf16[64,512]{1,0:T(8,128)(2,1)} %get-tuple-element.38), channel_id=1, source_target_pairs={{0,2},{1,3},{2,0},{3,1},{4,6},{5,7},{6,4},{7,5},{8,10},{9,11},{10,... | collective-permute-start | bytes 196616 | tf_op jit(solution)/shard_map/ppermute | solution.py:298
  54.9 3.3 %collective-permute-start.10 = (bf16[64,512]{1,0:T(8,128)(2,1)}, bf16[64,512]{1,0:T(8,128)(2,1)S(1)}, u32[]{:S(2)}, u32[]{:S(2)}) collective-permute-start(bf16[64,512]{1,0:T(8,128)(2,1)} %get-tuple-element.38), channel_id=1, source_target_pairs={{0,3},{1,0},{2,1},{3,2},{4,7},{5,4},{6,5},{7,6},{8,11},{9,8},{10,9... | collective-permute-start | bytes 196616 | tf_op jit(solution)/shard_map/ppermute | solution.py:298
  58.2 9.5 %collective-permute-start.11 = (bf16[256,512]{1,0:T(8,128)(2,1)S(1)}, bf16[256,512]{1,0:T(8,128)(2,1)S(1)}, u32[]{:S(2)}, u32[]{:S(2)}) collective-permute-start(bf16[256,512]{1,0:T(8,128)(2,1)S(1)} %constant_dynamic-update-slice_fusion.band_ref), channel_id=1, source_target_pairs={{0,4},{1,5},{4,8},{5,9},{6,2},{7,3},{8,12},{9,13},{10,6},{11,7},{1... | collective-permute-start | bytes 786440 | tf_op jit(solution)/shard_map/ppermute | solution.py:293
  62.1 5.6 %collective-permute-start.12 = (bf16[64,512]{1,0:T(8,128)(2,1)S(1)}, bf16[64,512]{1,0:T(8,128)(2,1)S(1)}, u32[]{:S(2)}, u32[]{:S(2)}) collective-permute-start(bf16[64,512]{1,0:T(8,128)(2,1)S(1)} %constant_dynamic-slice_fusion), channel_id=1, source_target_pairs={{2,6},{3,7},{4,0},{5,1},{6,10},{7,11},{8,4},{9,5},{10,14},{11,15},... | collective-permute-start | bytes 196616 | tf_op jit(solution)/shard_map/ppermute | solution.py:293
  86.3 24.6 %all-to-all-start = ((bf16[32,32,512]{2,1,0:T(8,128)(2,1)}), bf16[32,32,512]{2,1,0:T(8,128)(2,1)S(1)}, u32[]{:S(2)}, u32[]{:S(2)}) async-start(bf16[32,32,512]{2,1,0:T(8,128)(2,1)} %bitcast.9), calls=%async_computation | async-start | bytes 2097152 | tf_op jit(solution)/shard_map/all_to_all | solution.py:458
  105.4 18.0 %collective-permute-start.14 = (bf16[227,512]{1,0:T(8,128)(2,1)}, bf16[227,512]{1,0:T(8,128)(2,1)S(1)}, u32[]{:S(2)}, u32[]{:S(2)}) collective-permute-start(bf16[227,512]{1,0:T(8,128)(2,1)} %get-tuple-element.52), channel_id=1, source_target_pairs={{0,4},{4,8},{8,12},{12,16},{16,20},{20,24},{24,28},{28,32},{32,36}... | collective-permute-start | bytes 697352 | tf_op jit(solution)/shard_map/ppermute | solution.py:276
  108.9 14.5 %collective-permute-start.15 = (bf16[227,512]{1,0:T(8,128)(2,1)}, bf16[227,512]{1,0:T(8,128)(2,1)S(1)}, u32[]{:S(2)}, u32[]{:S(2)}) collective-permute-start(bf16[227,512]{1,0:T(8,128)(2,1)} %get-tuple-element.53), channel_id=1, source_target_pairs={{4,0},{8,4},{12,8},{16,12},{20,16},{24,20},{28,24},{32,28},{36,32}... | collective-permute-start | bytes 697352 | tf_op jit(solution)/shard_map/ppermute | solution.py:281
  111.8 21.1 %all-to-all-start.1 = ((bf16[8,32,512]{2,1,0:T(8,128)(2,1)}), bf16[8,32,512]{2,1,0:T(8,128)(2,1)S(1)}, u32[]{:S(2)}, u32[]{:S(2)}) async-start(bf16[8,32,512]{2,1,0:T(8,128)(2,1)} %broadcast_in_dim.7), calls=%async_computation.1 | async-start | bytes 524288 | tf_op jit(solution)/shard_map/all_to_all | solution.py:269
  124.9 6.2 %collective-permute-start.16 = (bf16[227,512]{1,0:T(8,128)(2,1)S(1)}, bf16[227,512]{1,0:T(8,128)(2,1)S(1)}, u32[]{:S(2)}, u32[]{:S(2)}) collective-permute-start(bf16[227,512]{1,0:T(8,128)(2,1)S(1)} %get-tuple-element.70), channel_id=1, source_target_pairs={{0,1},{1,2},{2,3},{3,0},{4,5},{5,6},{6,7},{7,4},{8,9},{9,10},{10,1... | collective-permute-start | bytes 697352 | tf_op jit(solution)/shard_map/ppermute | solution.py:298
  126.1 5.0 %collective-permute-start.17 = (bf16[227,512]{1,0:T(8,128)(2,1)S(1)}, bf16[227,512]{1,0:T(8,128)(2,1)S(1)}, u32[]{:S(2)}, u32[]{:S(2)}) collective-permute-start(bf16[227,512]{1,0:T(8,128)(2,1)S(1)} %get-tuple-element.69), channel_id=1, source_target_pairs={{0,3},{1,0},{2,1},{3,2},{4,7},{5,4},{6,5},{7,6},{8,11},{9,8},{10,9... | collective-permute-start | bytes 697352 | tf_op jit(solution)/shard_map/ppermute | solution.py:298
  134.0 26.1 %all-to-all-start.2 = ((bf16[32,32,512]{2,1,0:T(8,128)(2,1)}), bf16[32,32,512]{2,1,0:T(8,128)(2,1)S(1)}, u32[]{:S(2)}, u32[]{:S(2)}) async-start(bf16[32,32,512]{2,1,0:T(8,128)(2,1)} %broadcast_in_dim.8), calls=%async_computation.2 | async-start | bytes 2097152 | tf_op jit(solution)/shard_map/all_to_all | solution.py:269
  143.9 20.1 %copy-start.6 = (bf16[227,512]{1,0:T(8,128)(2,1)S(1)}, bf16[227,512]{1,0:T(8,128)(2,1)}, u32[]{:S(2)}) copy-start(bf16[227,512]{1,0:T(8,128)(2,1)} %get-tuple-element.51) | copy-start | bytes 697348
  144.0 20.1 %collective-permute-start.18 = (bf16[227,512]{1,0:T(8,128)(2,1)S(1)}, bf16[227,512]{1,0:T(8,128)(2,1)S(1)}, u32[]{:S(2)}, u32[]{:S(2)}) collective-permute-start(bf16[227,512]{1,0:T(8,128)(2,1)S(1)} %get-tuple-element.68), channel_id=1, source_target_pairs={{0,2},{1,3},{2,0},{3,1},{4,6},{5,7},{6,4},{7,5},{8,10},{9,11},{10,... | collective-permute-start | bytes 697352 | tf_op jit(solution)/shard_map/ppermute | solution.py:298
  (10 other events, 39.4 us)

commit v12 on v10

--- a/solution.py
+++ b/solution.py
@@ -387,7 +387,7 @@
 
     mesh_out, bgrad, part = pl.pallas_call(
         functools.partial(mesh_kernel, mesh_scale, scale, mesh_count),
-        grid=(steps,),
+        grid=(steps // 2,),
         in_specs=[
             scalar(),
             whole((width, latent)),
@@ -398,13 +398,13 @@
             whole((latent, latent)),
             whole((latent, latent)),
             whole((latent, latent)),
-            tiled(tile, latent),
-            tiled(tile, latent),
-            tiled(tile, 1),
-            tiled(tile, latent),
-            tiled(tile, latent),
-        ],
-        out_specs=[whole((rows, latent)), tiled(tile, latent), whole((2 * latent, latent))],
+            tiled(2 * tile, latent),
+            tiled(2 * tile, latent),
+            tiled(2 * tile, 1),
+            tiled(2 * tile, latent),
+            tiled(2 * tile, latent),
+        ],
+        out_specs=[whole((rows, latent)), tiled(2 * tile, latent), whole((2 * latent, latent))],
         out_shape=[
             jax.ShapeDtypeStruct((rows, latent), BF),
             jax.ShapeDtypeStruct((edges, latent), BF),
@@ -429,14 +429,14 @@
 
     *parts, part_low, part_high = pl.pallas_call(
         grid_kernel,
-        grid=(steps // 2,),
+        grid=(1,),
         in_specs=[
             scalar(),
-            tiled(2 * tile, 1),
+            tiled(edges, 1),
             whole((latent, latent)),
             whole((channels, latent)),
-            tiled(2 * tile, latent),
-            tiled(2 * tile, latent),
+            tiled(edges, latent),
+            tiled(edges, latent),
         ],
         out_specs=[whole((channels, nodes))] * (SUBS + 2),
         out_shape=[jax.ShapeDtypeStruct((channels, nodes), BF)] * (SUBS + 2),

time: 166 us -> 165 us (level)
  transfers between devices with their start and end apart: 22 -> 22, of which waited for: 9 -> 10; matrix products, arithmetic and copies ran while one was open for 6% -> 6% of each run, Pallas kernels for 19% -> 19%
where the time goes in v12:
time: 165 us; the launch traced here: 164 us
  starting transfers between devices  70.9 us (43%)
  Pallas kernels  48.7 us (30%)
  waiting for transfers between devices  28.2 us (17%)
  local copies, waits for them, and re-layouts  9.13 us (6%)
  other arithmetic  6.32 us (4%)
    all_to_all x2, starting transfers between devices, from_everyone(): lax.all_to_all(jnp.broadcast_to(shard[None], (devices, *shard.shape)), ax...  21.6 us
    ppermute x12, starting transfers between devices, along_sub(): lax.ppermute(value, 'sub', [(i, (i + steps) % count) for i in range(count)])  18.4 us
    pallas_call x1, Pallas kernels, body(): pl.pallas_call(functools.partial(mesh_kernel, mesh_scale, scale, mesh_cou...  17.8 us
    pallas_call x1, Pallas kernels, body(): pl.pallas_call(functools.partial(forward_kernel, scale), grid=(steps,), i...  15.4 us
    all_to_all x2, waiting for transfers between devices, from_everyone(): lax.all_to_all(jnp.broadcast_to(shard[None], (devices, *shard.shape)), ax...  14.7 us
    pallas_call x1, Pallas kernels, body(): pl.pallas_call(grid_kernel, grid=(1,), in_specs=[scalar(), tiled(edges, 1...  10.4 us
    ppermute x3, starting transfers between devices, outwards(): return lax.ppermute(value, ALL, pairs)  9.58 us
    ppermute x2, starting transfers between devices, bands_up(): return lax.ppermute(value, BAND, [(i, i + 1) for i in range(count - 1)])  9.07 us
  transfers between devices with their start and end apart: 22, of which 10 were waited for; matrix products, arithmetic and copies ran while one was open for 6% of the time, Pallas kernels for 19%

profile of v12, /device:TPU:1, one launch (start us, length us, event | category | flops | bytes accessed | tf_op | source)
XLA Modules:
  0.0 164.3 jit_solution(385869160563401017)
XLA Ops:
  0.6 2.1 %collective-permute-start.1 = (bf16[227,512]{1,0:T(8,128)(2,1)}, bf16[227,512]{1,0:T(8,128)(2,1)S(1)}, u32[]{:S(2)}, u32[]{:S(2)}) collective-permute-start(bf16[227,512]{1,0:T(8,128)(2,1)} %refs_0_.1), channel_id=1, source_target_pairs={{0,1},{1,2},{2,3},{3,0},{4,5},{5,6},{6,7},{7,4},{8,9},{9,10},{10,1... | collective-permute-start | bytes 697352 | tf_op jit(solution)/shard_map/ppermute | solution.py:293
  6.1 2.5 %collective-permute-start.4 = (bf16[64,640]{1,0:T(8,128)(2,1)S(1)}, bf16[64,640]{1,0:T(8,128)(2,1)S(1)}, u32[]{:S(2)}, u32[]{:S(2)}) collective-permute-start(bf16[64,640]{1,0:T(8,128)(2,1)S(1)} %concatenate.9), channel_id=1, source_target_pairs={{0,2},{1,3},{2,0},{3,1},{4,6},{5,7},{6,4},{7,5},{8,10},{9,11},{10,... | collective-permute-start | bytes 245768 | tf_op jit(solution)/shard_map/ppermute | solution.py:293
  9.8 2.4 %reshape.31.index_ref = s32[2560,1]{1,0:T(8,128)} reshape(s32[40,64]{1,0:T(8,128)S(1)} %subtract_bitcast_fusion) | data formatting | bytes 20480 | tf_op jit(solution)/shard_map/reshape | solution.py:319
  12.1 2.6 %collective-permute-start.5 = (bf16[64,640]{1,0:T(8,128)(2,1)S(1)}, bf16[64,640]{1,0:T(8,128)(2,1)S(1)}, u32[]{:S(2)}, u32[]{:S(2)}) collective-permute-start(bf16[64,640]{1,0:T(8,128)(2,1)S(1)} %concatenate.9), channel_id=1, source_target_pairs={{0,3},{1,0},{2,1},{3,2},{4,7},{5,4},{6,5},{7,6},{8,11},{9,8},{10,9... | collective-permute-start | bytes 245768 | tf_op jit(solution)/shard_map/ppermute | solution.py:293
  15.4 5.0 %gather.1.picked_ref = bf16[2560,256]{1,0:T(8,128)(2,1)} custom-call(s32[1]{0:T(128)} %bitcast.sub_ref, s32[2560,1]{1,0:T(8,128)} %reshape.31.index_ref, bf16[227,512]{1,0:T(8,128)(2,1)} %refs_0_.1, bf16[227,512]{1,0:T(8,128)(2,1)} %copy-done.7, bf16[227,512]{1,0:T(8,128)(2,1)} %copy-done.8), custom_call_target="tpu_custom_call" | custom-call | flops 2013265920 | bytes 1310720 | tf_op jit(solution)/shard_map/gather/pallas_call | solution.py:330
  21.7 5.5 %collective-permute-start.6 = (bf16[227,512]{1,0:T(8,128)(2,1)S(1)}, bf16[227,512]{1,0:T(8,128)(2,1)S(1)}, u32[]{:S(2)}, u32[]{:S(2)}) collective-permute-start(bf16[227,512]{1,0:T(8,128)(2,1)S(1)} %get-tuple-element.63), channel_id=1, source_target_pairs={{0,4},{4,8},{8,12},{12,16},{16,20},{20,24},{24,28},{28,32},{32,36}... | collective-permute-start | bytes 697352 | tf_op jit(solution)/shard_map/ppermute | solution.py:271
  27.3 1.9 %collective-permute-start.7 = (bf16[227,512]{1,0:T(8,128)(2,1)S(1)}, bf16[227,512]{1,0:T(8,128)(2,1)S(1)}, u32[]{:S(2)}, u32[]{:S(2)}) collective-permute-start(bf16[227,512]{1,0:T(8,128)(2,1)S(1)} %get-tuple-element.62), channel_id=1, source_target_pairs={{4,0},{8,4},{12,8},{16,12},{20,16},{24,20},{28,24},{32,28},{36,32}... | collective-permute-start | bytes 697352 | tf_op jit(solution)/shard_map/ppermute | solution.py:276
  29.3 3.6 %collective-permute-start.13 = (bf16[256,640]{1,0:T(8,128)(2,1)S(1)}, bf16[256,640]{1,0:T(8,128)(2,1)S(1)}, u32[]{:S(2)}, u32[]{:S(2)}) collective-permute-start(bf16[256,640]{1,0:T(8,128)(2,1)S(1)} %constant_dynamic-update-slice_fusion.4.pay_ref), channel_id=1, source_target_pairs={{0,4},{1,5},{4,8},{5,9},{6,2},{7,3},{8,12},{9,13},{10,6},{11,7},{1... | collective-permute-start | bytes 983048 | tf_op jit(solution)/shard_map/ppermute | solution.py:288
  35.4 15.4 %encode.1 = (bf16[2560,512]{1,0:T(8,128)(2,1)}, bf16[2560,512]{1,0:T(8,128)(2,1)}, bf16[2560,512]{1,0:T(8,128)(2,1)}, bf16[2560,512]{1,0:T(8,128)(2,1)}, bf16[25...) custom-call(s32[1]{0:T(128)} %bitcast.sub_ref, s32[2560,1]{1,0:T(8,128)} %reshape.31.index_ref, ...), custom_call_target="tpu_custom_call" | custom-call | tf_op jit(solution)/shard_map/encode/pallas_call | solution.py:357
  50.9 3.2 %collective-permute-start.9 = (bf16[64,512]{1,0:T(8,128)(2,1)}, bf16[64,512]{1,0:T(8,128)(2,1)S(1)}, u32[]{:S(2)}, u32[]{:S(2)}) collective-permute-start(bf16[64,512]{1,0:T(8,128)(2,1)} %get-tuple-element.34), channel_id=1, source_target_pairs={{0,2},{1,3},{2,0},{3,1},{4,6},{5,7},{6,4},{7,5},{8,10},{9,11},{10,... | collective-permute-start | bytes 196616 | tf_op jit(solution)/shard_map/ppermute | solution.py:293
  57.5 4.0 %collective-permute-start.11 = (bf16[256,512]{1,0:T(8,128)(2,1)S(1)}, bf16[256,512]{1,0:T(8,128)(2,1)S(1)}, u32[]{:S(2)}, u32[]{:S(2)}) collective-permute-start(bf16[256,512]{1,0:T(8,128)(2,1)S(1)} %constant_dynamic-update-slice_fusion.band_ref), channel_id=1, source_target_pairs={{0,4},{1,5},{4,8},{5,9},{6,2},{7,3},{8,12},{9,13},{10,6},{11,7},{1... | collective-permute-start | bytes 786440 | tf_op jit(solution)/shard_map/ppermute | solution.py:288
  61.5 1.9 %collective-permute-start.12 = (bf16[64,512]{1,0:T(8,128)(2,1)S(1)}, bf16[64,512]{1,0:T(8,128)(2,1)S(1)}, u32[]{:S(2)}, u32[]{:S(2)}) collective-permute-start(bf16[64,512]{1,0:T(8,128)(2,1)S(1)} %constant_dynamic-slice_fusion), channel_id=1, source_target_pairs={{2,6},{3,7},{4,0},{5,1},{6,10},{7,11},{8,4},{9,5},{10,14},{11,15},... | collective-permute-start | bytes 196616 | tf_op jit(solution)/shard_map/ppermute | solution.py:288
  63.5 3.6 %collective-permute-done.12.side_ref = bf16[64,512]{1,0:T(8,128)(2,1)S(1)} collective-permute-done((bf16[64,512]{1,0:T(8,128)(2,1)S(1)}, bf16[64,512]{1,0:T(8,128)(2,1)S(1)}, u32[]{:S(2)}, u32[]{:S(2)}) %collective-permute-start.12) | collective-permute-done | bytes 65568 | tf_op jit(solution)/shard_map/ppermute | solution.py:288
  67.8 17.8 %process.1 = (bf16[64,512]{1,0:T(8,128)(2,1)}, bf16[2560,512]{1,0:T(8,128)(2,1)}, bf16[1024,512]{1,0:T(8,128)(2,1)}) custom-call(s32[1]{0:T(128)} %bitcast.sub_ref, bf16[256,512]{1,0:T(8,128)(2,1)} %copy-done.1, bf16[256,512]{1,0:T(8,128)(2,1)} %copy-done.4, bf16[64,512]{1,0:T(8,128)(2,1)} %copy-done.11, bf16[256,640]{1,0:T(8,128)(2,1)} %copy-done.2, ...), custom_call_target="tpu_custom_call" | custom-call | tf_op jit(solution)/shard_map/process/pallas_call | solution.py:388
  85.7 8.4 %all-to-all-start = ((bf16[32,32,512]{2,1,0:T(8,128)(2,1)}), bf16[32,32,512]{2,1,0:T(8,128)(2,1)S(1)}, u32[]{:S(2)}, u32[]{:S(2)}) async-start(bf16[32,32,512]{2,1,0:T(8,128)(2,1)} %bitcast.10), calls=%async_computation | async-start | bytes 2097152 | tf_op jit(solution)/shard_map/all_to_all | solution.py:449
  94.1 10.4 %channels.1 = (bf16[227,512]{1,0:T(8,128)(2,1)}, bf16[227,512]{1,0:T(8,128)(2,1)}, bf16[227,512]{1,0:T(8,128)(2,1)}, bf16[227,512]{1,0:T(8,128)(2,1)}, bf16[227,...) custom-call(s32[1]{0:T(128)} %bitcast.sub_ref, s32[2560,1]{1,0:T(8,128)} %reshape.31.index_ref, bf16[512,512]{1,0:T(8,128)(2,1)} %src_ref.3, ...), custom_call_target="tpu_custom_call" | custom-call | tf_op jit(solution)/shard_map/channels/pallas_call | solution.py:430
  104.5 3.5 %collective-permute-start.14 = (bf16[227,512]{1,0:T(8,128)(2,1)}, bf16[227,512]{1,0:T(8,128)(2,1)S(1)}, u32[]{:S(2)}, u32[]{:S(2)}) collective-permute-start(bf16[227,512]{1,0:T(8,128)(2,1)} %get-tuple-element.48), channel_id=1, source_target_pairs={{0,4},{4,8},{8,12},{12,16},{16,20},{20,24},{24,28},{28,32},{32,36}... | collective-permute-start | bytes 697352 | tf_op jit(solution)/shard_map/ppermute | solution.py:271
  108.1 1.9 %collective-permute-start.15 = (bf16[227,512]{1,0:T(8,128)(2,1)}, bf16[227,512]{1,0:T(8,128)(2,1)S(1)}, u32[]{:S(2)}, u32[]{:S(2)}) collective-permute-start(bf16[227,512]{1,0:T(8,128)(2,1)} %get-tuple-element.49), channel_id=1, source_target_pairs={{4,0},{8,4},{12,8},{16,12},{20,16},{24,20},{28,24},{32,28},{36,32}... | collective-permute-start | bytes 697352 | tf_op jit(solution)/shard_map/ppermute | solution.py:276
  111.0 11.8 %all-to-all-start.1 = ((bf16[8,32,512]{2,1,0:T(8,128)(2,1)}), bf16[8,32,512]{2,1,0:T(8,128)(2,1)S(1)}, u32[]{:S(2)}, u32[]{:S(2)}) async-start(bf16[8,32,512]{2,1,0:T(8,128)(2,1)} %broadcast_in_dim.7), calls=%async_computation.1 | async-start | bytes 524288 | tf_op jit(solution)/shard_map/all_to_all | solution.py:264
  127.2 3.5 %collective-permute-done.16 = bf16[227,512]{1,0:T(8,128)(2,1)S(1)} collective-permute-done((bf16[227,512]{1,0:T(8,128)(2,1)S(1)}, bf16[227,512]{1,0:T(8,128)(2,1)S(1)}, u32[]{:S(2)}, u32[]{:S(2)}) %collective-permute-start.16) | collective-permute-done | bytes 232480 | tf_op jit(solution)/shard_map/ppermute | solution.py:293
  133.4 9.8 %all-to-all-start.2 = ((bf16[32,32,512]{2,1,0:T(8,128)(2,1)}), bf16[32,32,512]{2,1,0:T(8,128)(2,1)S(1)}, u32[]{:S(2)}, u32[]{:S(2)}) async-start(bf16[32,32,512]{2,1,0:T(8,128)(2,1)} %broadcast_in_dim.8), calls=%async_computation.2 | async-start | bytes 2097152 | tf_op jit(solution)/shard_map/all_to_all | solution.py:264
  143.2 3.0 %collective-permute-start.18 = (bf16[227,512]{1,0:T(8,128)(2,1)S(1)}, bf16[227,512]{1,0:T(8,128)(2,1)S(1)}, u32[]{:S(2)}, u32[]{:S(2)}) collective-permute-start(bf16[227,512]{1,0:T(8,128)(2,1)S(1)} %get-tuple-element.64), channel_id=1, source_target_pairs={{0,2},{1,3},{2,0},{3,1},{4,6},{5,7},{6,4},{7,5},{8,10},{9,11},{10,... | collective-permute-start | bytes 697352 | tf_op jit(solution)/shard_map/ppermute | solution.py:293
  146.2 13.1 %all-to-all-done.2 = bf16[32,32,512]{2,1,0:T(8,128)(2,1)S(1)} async-done(((bf16[32,32,512]{2,1,0:T(8,128)(2,1)}), bf16[32,32,512]{2,1,0:T(8,128)(2,1)S(1)}, u32[]{:S(2)}, u32[]{:S(2)}) %all-to-all-start.2) | async-done | bytes 1048608 | tf_op jit(solution)/shard_map/all_to_all | solution.py:264
  161.1 2.2 %collective-permute-done.18 = bf16[227,512]{1,0:T(8,128)(2,1)S(1)} collective-permute-done((bf16[227,512]{1,0:T(8,128)(2,1)S(1)}, bf16[227,512]{1,0:T(8,128)(2,1)S(1)}, u32[]{:S(2)}, u32[]{:S(2)}) %collective-permute-start.18) | collective-permute-done | bytes 232480 | tf_op jit(solution)/shard_map/ppermute | solution.py:293
  (72 shorter events, 24.0 us)
Async XLA Ops:
  0.6 11.5 %collective-permute-start.1 = (bf16[227,512]{1,0:T(8,128)(2,1)}, bf16[227,512]{1,0:T(8,128)(2,1)S(1)}, u32[]{:S(2)}, u32[]{:S(2)}) collective-permute-start(bf16[227,512]{1,0:T(8,128)(2,1)} %refs_0_.1), channel_id=1, source_target_pairs={{0,1},{1,2},{2,3},{3,0},{4,5},{5,6},{6,7},{7,4},{8,9},{9,10},{10,1... | collective-permute-start | bytes 697352 | tf_op jit(solution)/shard_map/ppermute | solution.py:293
  2.7 12.0 %collective-permute-start.2 = (bf16[227,512]{1,0:T(8,128)(2,1)}, bf16[227,512]{1,0:T(8,128)(2,1)S(1)}, u32[]{:S(2)}, u32[]{:S(2)}) collective-permute-start(bf16[227,512]{1,0:T(8,128)(2,1)} %refs_0_.1), channel_id=1, source_target_pairs={{0,3},{1,0},{2,1},{3,2},{4,7},{5,4},{6,5},{7,6},{8,11},{9,8},{10,9... | collective-permute-start | bytes 697352 | tf_op jit(solution)/shard_map/ppermute | solution.py:293
  5.9 14.5 %collective-permute-start.3 = (bf16[64,640]{1,0:T(8,128)(2,1)S(1)}, bf16[64,640]{1,0:T(8,128)(2,1)S(1)}, u32[]{:S(2)}, u32[]{:S(2)}) collective-permute-start(bf16[64,640]{1,0:T(8,128)(2,1)S(1)} %concatenate.9), channel_id=1, source_target_pairs={{0,1},{1,2},{2,3},{3,0},{4,5},{5,6},{6,7},{7,4},{8,9},{9,10},{10,1... | collective-permute-start | bytes 245768 | tf_op jit(solution)/shard_map/ppermute | solution.py:293
  6.1 14.4 %collective-permute-start.4 = (bf16[64,640]{1,0:T(8,128)(2,1)S(1)}, bf16[64,640]{1,0:T(8,128)(2,1)S(1)}, u32[]{:S(2)}, u32[]{:S(2)}) collective-permute-start(bf16[64,640]{1,0:T(8,128)(2,1)S(1)} %concatenate.9), channel_id=1, source_target_pairs={{0,2},{1,3},{2,0},{3,1},{4,6},{5,7},{6,4},{7,5},{8,10},{9,11},{10,... | collective-permute-start | bytes 245768 | tf_op jit(solution)/shard_map/ppermute | solution.py:293
  8.5 11.9 %collective-permute-start = (bf16[227,512]{1,0:T(8,128)(2,1)}, bf16[227,512]{1,0:T(8,128)(2,1)S(1)}, u32[]{:S(2)}, u32[]{:S(2)}) collective-permute-start(bf16[227,512]{1,0:T(8,128)(2,1)} %refs_0_.1), channel_id=1, source_target_pairs={{0,2},{1,3},{2,0},{3,1},{4,6},{5,7},{6,4},{7,5},{8,10},{9,11},{10,... | collective-permute-start | bytes 697352 | tf_op jit(solution)/shard_map/ppermute | solution.py:293
  12.1 8.3 %collective-permute-start.5 = (bf16[64,640]{1,0:T(8,128)(2,1)S(1)}, bf16[64,640]{1,0:T(8,128)(2,1)S(1)}, u32[]{:S(2)}, u32[]{:S(2)}) collective-permute-start(bf16[64,640]{1,0:T(8,128)(2,1)S(1)} %concatenate.9), channel_id=1, source_target_pairs={{0,3},{1,0},{2,1},{3,2},{4,7},{5,4},{6,5},{7,6},{8,11},{9,8},{10,9... | collective-permute-start | bytes 245768 | tf_op jit(solution)/shard_map/ppermute | solution.py:293
  21.7 11.2 %collective-permute-start.6 = (bf16[227,512]{1,0:T(8,128)(2,1)S(1)}, bf16[227,512]{1,0:T(8,128)(2,1)S(1)}, u32[]{:S(2)}, u32[]{:S(2)}) collective-permute-start(bf16[227,512]{1,0:T(8,128)(2,1)S(1)} %get-tuple-element.63), channel_id=1, source_target_pairs={{0,4},{4,8},{8,12},{12,16},{16,20},{20,24},{24,28},{28,32},{32,36}... | collective-permute-start | bytes 697352 | tf_op jit(solution)/shard_map/ppermute | solution.py:271
  27.3 7.4 %collective-permute-start.7 = (bf16[227,512]{1,0:T(8,128)(2,1)S(1)}, bf16[227,512]{1,0:T(8,128)(2,1)S(1)}, u32[]{:S(2)}, u32[]{:S(2)}) collective-permute-start(bf16[227,512]{1,0:T(8,128)(2,1)S(1)} %get-tuple-element.62), channel_id=1, source_target_pairs={{4,0},{8,4},{12,8},{16,12},{20,16},{24,20},{28,24},{32,28},{36,32}... | collective-permute-start | bytes 697352 | tf_op jit(solution)/shard_map/ppermute | solution.py:276
  29.3 25.8 %copy-start.2 = (bf16[256,640]{1,0:T(8,128)(2,1)}, bf16[256,640]{1,0:T(8,128)(2,1)S(1)}, u32[]{:S(2)}) copy-start(bf16[256,640]{1,0:T(8,128)(2,1)S(1)} %constant_dynamic-update-slice_fusion.4.pay_ref) | copy-start | bytes 983044
  29.3 34.2 %collective-permute-start.13 = (bf16[256,640]{1,0:T(8,128)(2,1)S(1)}, bf16[256,640]{1,0:T(8,128)(2,1)S(1)}, u32[]{:S(2)}, u32[]{:S(2)}) collective-permute-start(bf16[256,640]{1,0:T(8,128)(2,1)S(1)} %constant_dynamic-update-slice_fusion.4.pay_ref), channel_id=1, source_target_pairs={{0,4},{1,5},{4,8},{5,9},{6,2},{7,3},{8,12},{9,13},{10,6},{11,7},{1... | collective-permute-start | bytes 983048 | tf_op jit(solution)/shard_map/ppermute | solution.py:288
  50.8 4.6 %collective-permute-start.8 = (bf16[64,512]{1,0:T(8,128)(2,1)}, bf16[64,512]{1,0:T(8,128)(2,1)S(1)}, u32[]{:S(2)}, u32[]{:S(2)}) collective-permute-start(bf16[64,512]{1,0:T(8,128)(2,1)} %get-tuple-element.34), channel_id=1, source_target_pairs={{0,1},{1,2},{2,3},{3,0},{4,5},{5,6},{6,7},{7,4},{8,9},{9,10},{10,1... | collective-permute-start | bytes 196616 | tf_op jit(solution)/shard_map/ppermute | solution.py:293
  50.9 5.8 %collective-permute-start.9 = (bf16[64,512]{1,0:T(8,128)(2,1)}, bf16[64,512]{1,0:T(8,128)(2,1)S(1)}, u32[]{:S(2)}, u32[]{:S(2)}) collective-permute-start(bf16[64,512]{1,0:T(8,128)(2,1)} %get-tuple-element.34), channel_id=1, source_target_pairs={{0,2},{1,3},{2,0},{3,1},{4,6},{5,7},{6,4},{7,5},{8,10},{9,11},{10,... | collective-permute-start | bytes 196616 | tf_op jit(solution)/shard_map/ppermute | solution.py:293
  54.1 3.3 %collective-permute-start.10 = (bf16[64,512]{1,0:T(8,128)(2,1)}, bf16[64,512]{1,0:T(8,128)(2,1)S(1)}, u32[]{:S(2)}, u32[]{:S(2)}) collective-permute-start(bf16[64,512]{1,0:T(8,128)(2,1)} %get-tuple-element.34), channel_id=1, source_target_pairs={{0,3},{1,0},{2,1},{3,2},{4,7},{5,4},{6,5},{7,6},{8,11},{9,8},{10,9... | collective-permute-start | bytes 196616 | tf_op jit(solution)/shard_map/ppermute | solution.py:293
  57.5 9.6 %collective-permute-start.11 = (bf16[256,512]{1,0:T(8,128)(2,1)S(1)}, bf16[256,512]{1,0:T(8,128)(2,1)S(1)}, u32[]{:S(2)}, u32[]{:S(2)}) collective-permute-start(bf16[256,512]{1,0:T(8,128)(2,1)S(1)} %constant_dynamic-update-slice_fusion.band_ref), channel_id=1, source_target_pairs={{0,4},{1,5},{4,8},{5,9},{6,2},{7,3},{8,12},{9,13},{10,6},{11,7},{1... | collective-permute-start | bytes 786440 | tf_op jit(solution)/shard_map/ppermute | solution.py:288
  61.5 5.6 %collective-permute-start.12 = (bf16[64,512]{1,0:T(8,128)(2,1)S(1)}, bf16[64,512]{1,0:T(8,128)(2,1)S(1)}, u32[]{:S(2)}, u32[]{:S(2)}) collective-permute-start(bf16[64,512]{1,0:T(8,128)(2,1)S(1)} %constant_dynamic-slice_fusion), channel_id=1, source_target_pairs={{2,6},{3,7},{4,0},{5,1},{6,10},{7,11},{8,4},{9,5},{10,14},{11,15},... | collective-permute-start | bytes 196616 | tf_op jit(solution)/shard_map/ppermute | solution.py:288
  85.7 24.5 %all-to-all-start = ((bf16[32,32,512]{2,1,0:T(8,128)(2,1)}), bf16[32,32,512]{2,1,0:T(8,128)(2,1)S(1)}, u32[]{:S(2)}, u32[]{:S(2)}) async-start(bf16[32,32,512]{2,1,0:T(8,128)(2,1)} %bitcast.10), calls=%async_computation | async-start | bytes 2097152 | tf_op jit(solution)/shard_map/all_to_all | solution.py:449
  104.5 18.2 %collective-permute-start.14 = (bf16[227,512]{1,0:T(8,128)(2,1)}, bf16[227,512]{1,0:T(8,128)(2,1)S(1)}, u32[]{:S(2)}, u32[]{:S(2)}) collective-permute-start(bf16[227,512]{1,0:T(8,128)(2,1)} %get-tuple-element.48), channel_id=1, source_target_pairs={{0,4},{4,8},{8,12},{12,16},{16,20},{20,24},{24,28},{28,32},{32,36}... | collective-permute-start | bytes 697352 | tf_op jit(solution)/shard_map/ppermute | solution.py:271
  108.1 14.7 %collective-permute-start.15 = (bf16[227,512]{1,0:T(8,128)(2,1)}, bf16[227,512]{1,0:T(8,128)(2,1)S(1)}, u32[]{:S(2)}, u32[]{:S(2)}) collective-permute-start(bf16[227,512]{1,0:T(8,128)(2,1)} %get-tuple-element.49), channel_id=1, source_target_pairs={{4,0},{8,4},{12,8},{16,12},{20,16},{24,20},{28,24},{32,28},{36,32}... | collective-permute-start | bytes 697352 | tf_op jit(solution)/shard_map/ppermute | solution.py:276
  111.0 21.2 %all-to-all-start.1 = ((bf16[8,32,512]{2,1,0:T(8,128)(2,1)}), bf16[8,32,512]{2,1,0:T(8,128)(2,1)S(1)}, u32[]{:S(2)}, u32[]{:S(2)}) async-start(bf16[8,32,512]{2,1,0:T(8,128)(2,1)} %broadcast_in_dim.7), calls=%async_computation.1 | async-start | bytes 524288 | tf_op jit(solution)/shard_map/all_to_all | solution.py:264
  124.3 6.5 %collective-permute-start.16 = (bf16[227,512]{1,0:T(8,128)(2,1)S(1)}, bf16[227,512]{1,0:T(8,128)(2,1)S(1)}, u32[]{:S(2)}, u32[]{:S(2)}) collective-permute-start(bf16[227,512]{1,0:T(8,128)(2,1)S(1)} %get-tuple-element.66), channel_id=1, source_target_pairs={{0,1},{1,2},{2,3},{3,0},{4,5},{5,6},{6,7},{7,4},{8,9},{9,10},{10,1... | collective-permute-start | bytes 697352 | tf_op jit(solution)/shard_map/ppermute | solution.py:293
  125.6 5.1 %collective-permute-start.17 = (bf16[227,512]{1,0:T(8,128)(2,1)S(1)}, bf16[227,512]{1,0:T(8,128)(2,1)S(1)}, u32[]{:S(2)}, u32[]{:S(2)}) collective-permute-start(bf16[227,512]{1,0:T(8,128)(2,1)S(1)} %get-tuple-element.65), channel_id=1, source_target_pairs={{0,3},{1,0},{2,1},{3,2},{4,7},{5,4},{6,5},{7,6},{8,11},{9,8},{10,9... | collective-permute-start | bytes 697352 | tf_op jit(solution)/shard_map/ppermute | solution.py:293
  133.4 26.0 %all-to-all-start.2 = ((bf16[32,32,512]{2,1,0:T(8,128)(2,1)}), bf16[32,32,512]{2,1,0:T(8,128)(2,1)S(1)}, u32[]{:S(2)}, u32[]{:S(2)}) async-start(bf16[32,32,512]{2,1,0:T(8,128)(2,1)} %broadcast_in_dim.8), calls=%async_computation.2 | async-start | bytes 2097152 | tf_op jit(solution)/shard_map/all_to_all | solution.py:264
  143.2 20.1 %copy-start.6 = (bf16[227,512]{1,0:T(8,128)(2,1)S(1)}, bf16[227,512]{1,0:T(8,128)(2,1)}, u32[]{:S(2)}) copy-start(bf16[227,512]{1,0:T(8,128)(2,1)} %get-tuple-element.47) | copy-start | bytes 697348
  143.2 20.1 %collective-permute-start.18 = (bf16[227,512]{1,0:T(8,128)(2,1)S(1)}, bf16[227,512]{1,0:T(8,128)(2,1)S(1)}, u32[]{:S(2)}, u32[]{:S(2)}) collective-permute-start(bf16[227,512]{1,0:T(8,128)(2,1)S(1)} %get-tuple-element.64), channel_id=1, source_target_pairs={{0,2},{1,3},{2,0},{3,1},{4,6},{5,7},{6,4},{7,5},{8,10},{9,11},{10,... | collective-permute-start | bytes 697352 | tf_op jit(solution)/shard_map/ppermute | solution.py:293
  (10 other events, 39.7 us)
